TPU v7x, 32 devices: a whole 2x2x4 slice. The times are simulated.
32 devices in a mesh: dp: 8 (over y, x, core), tensor: 4 (over z).
Axes of the slice: x: 2, y: 2, z: 4, core: 2. Of those that a mesh axis runs over, the one named last changes fastest.
Arguments:
- tokens: bfloat16 [32768, 768], P(('dp', 'tensor')), may hold values from -6 to 6
- cotangent: bfloat16 [32768, 768], P(('dp', 'tensor')), may hold values from -6 to 6
- source: int32 [32768], P(('dp', 'tensor')), may hold values from 0 to 32767, as said below
- target: int32 [32768], P(('dp', 'tensor')), may hold values from 0 to 32767, as said below
- lengths: int32 [8, 3], P('dp'), may hold values from 1 to 2048, as said below
- ln_gain: float32 [768], P(('dp', 'tensor')), may hold values from 0.5 to 1.5
- ln_bias: float32 [768], P(('dp', 'tensor')), may hold values from -1.75 to 1.75
- w_fwd: bfloat16 [768, 1536], P('dp', 'tensor'), may hold values from -0.21875 to 0.21875
- b_fwd: float32 [1536], P(('dp', 'tensor')), may hold values from -3 to 3
- w_bwd: bfloat16 [768, 1536], P('dp', 'tensor'), may hold values from -0.21875 to 0.21875
- b_bwd: float32 [1536], P(('dp', 'tensor')), may hold values from -3 to 3
- w_gate: bfloat16 [768, 2, 1536], P('dp', None, 'tensor'), may hold values from -0.21875 to 0.21875
- b_gate: float32 [2, 1536], P(None, ('dp', 'tensor')), may hold values from -3 to 3
- w_out: bfloat16 [2, 1536, 768], P(None, 'tensor', 'dp'), may hold values from -0.109375 to 0.109375
- b_out: float32 [768], P(('dp', 'tensor')), may hold values from -1.75 to 1.75
- log_dt: float32 [2, 1536], P(None, ('dp', 'tensor')), may hold values from -6.9 to -2.3
- log_rate: float32 [2, 1536, 64], P(None, ('dp', 'tensor')), may hold values from -0.7 to 4.2
- ssm_b: float32 [2, 1536, 64], P(None, ('dp', 'tensor')), may hold values from -6 to 6
- ssm_c: float32 [2, 1536, 64], P(None, ('dp', 'tensor')), may hold values from -6 to 6
- ssm_d: float32 [2, 1536], P(None, ('dp', 'tensor')), may hold values from -6 to 6
Outputs:
- layer_out: bfloat16 [32768, 768], P(('dp', 'tensor'))
- input_grad: bfloat16 [32768, 768], P(('dp', 'tensor'))
- ln_gain_grad: float32 [768], P(('dp', 'tensor'))
- ln_bias_grad: float32 [768], P(('dp', 'tensor'))
- w_fwd_grad: float32 [768, 1536], P('dp', 'tensor')
- b_fwd_grad: float32 [1536], P(('dp', 'tensor'))
- w_bwd_grad: float32 [768, 1536], P('dp', 'tensor')
- b_bwd_grad: float32 [1536], P(('dp', 'tensor'))
- w_gate_grad: float32 [768, 2, 1536], P('dp', None, 'tensor')
- b_gate_grad: float32 [2, 1536], P(None, ('dp', 'tensor'))
- w_out_grad: float32 [2, 1536, 768], P(None, 'tensor', 'dp')
- b_out_grad: float32 [768], P(('dp', 'tensor'))
- log_dt_grad: float32 [2, 1536], P(None, ('dp', 'tensor'))
- log_rate_grad: float32 [2, 1536, 64], P(None, ('dp', 'tensor'))
- ssm_b_grad: float32 [2, 1536, 64], P(None, ('dp', 'tensor'))
- ssm_c_grad: float32 [2, 1536, 64], P(None, ('dp', 'tensor'))
- ssm_d_grad: float32 [2, 1536], P(None, ('dp', 'tensor'))
Inputs may be any that keep to these rules, and one draw needn't show every extreme that they name: Row q of the dealt order takes row source[q] of the given order. Both orders are cut into blocks of 1024 rows, one a device in the order of the dp+tensor placement; a row moves only between devices with the same tensor index, and exactly 1024 / (devices of dp) rows move from each such device to each such device. The inverse of source: source[target[r]] = r. `lengths`: the slots of a group's sequences, each rounded up to a multiple of 128 rows, fit in its 4096 rows; every group has a sequence of exactly 2048 rows.
All inputs are finite; a program needn't handle non-finite values.
Results may differ from a plain program's by a relative error of at most 0.012.
Values may be sent and summed in bfloat16 or wider, within the bound.
A program may use at most 448 MiB of HBM per device.

v0:
```python
from functools import partial

import jax
import jax.numpy as jnp
from jax import lax
from jax.sharding import PartitionSpec as P

BLK = 128


epsilon = 1e-05
highest = lax.Precision.HIGHEST


def group_layout(seq_lens, group_tok):
    slot_len = (seq_lens + BLK - 1) // BLK * BLK
    slot_end = jnp.cumsum(slot_len)
    slot_begin = slot_end - slot_len
    positions = jnp.arange(group_tok, dtype=jnp.int32)
    inside = (positions[:, None] >= slot_begin[None, :]) & (
        positions[:, None] < (slot_begin + seq_lens)[None, :]
    )
    live_rows = jnp.sum(inside.astype(jnp.float32), axis=1)
    block_heads = jnp.arange(group_tok // BLK, dtype=jnp.int32) * BLK
    resets = jnp.any(block_heads[:, None] == slot_begin[None, :], axis=1) | (
        block_heads >= slot_end[-1]
    )
    finish = jnp.concatenate([resets[1:], jnp.ones((1,), bool)])
    return (live_rows, 1.0 - resets.astype(jnp.float32), jnp.flip(1.0 - finish.astype(jnp.float32)))


def ssm_blocks(inputs, keep_flags, step_log, rate_log, in_coef, out_coef, skip_coef):
    block_count = inputs.shape[0] // BLK
    chan_count = inputs.shape[1]
    rate_val = jnp.exp(rate_log)
    log_decay = -jnp.exp(step_log)[:, None] * rate_val
    drive = (1.0 - jnp.exp(log_decay)) / rate_val * in_coef
    steps = jnp.arange(BLK + 1, dtype=jnp.float32)
    powers = jnp.exp(steps[:, None, None] * log_decay[None])
    kernel = jnp.einsum("lcn,cn->cl", powers[:BLK], out_coef * drive, precision=highest)
    lag_idx = jnp.arange(BLK)[:, None] - jnp.arange(BLK)[None, :]
    toeplitz = jnp.where(lag_idx[None] >= 0, kernel[:, jnp.clip(lag_idx, 0, BLK - 1)], 0.0)
    blocks = inputs.reshape(block_count, BLK, chan_count)
    intra = jnp.einsum("cts,bsc->btc", toeplitz, blocks, precision=highest)
    inflows = jnp.einsum(
        "bsc,scn->bcn", blocks, powers[BLK - 1 :: -1] * drive[None], precision=highest
    )
    decay = powers[BLK]

    def advance(state, entry):
        inflow, hold_flag = entry
        before = hold_flag * state
        return (before * decay + inflow, before)

    unused, entering = lax.scan(advance, jnp.zeros_like(decay), (inflows, keep_flags))
    carried = jnp.einsum("bcn,tcn->btc", entering, powers[1:] * out_coef[None], precision=highest)
    return (intra + carried).reshape(inputs.shape) + skip_coef * inputs


def mixer(
    live_rows,
    fwd_keep,
    rev_keep,
    pre_fwd,
    pre_bwd,
    pre_gate,
    step_log,
    rate_log,
    in_coef,
    out_coef,
    skip_coef,
):
    fwd_input = live_rows[:, None] * jax.nn.gelu(pre_fwd)
    bwd_input = live_rows[:, None] * jax.nn.gelu(pre_bwd)
    forward_out = ssm_blocks(
        fwd_input, fwd_keep, step_log[0], rate_log[0], in_coef[0], out_coef[0], skip_coef[0]
    )
    behind = jnp.flip(
        ssm_blocks(
            jnp.flip(bwd_input, 0),
            rev_keep,
            step_log[1],
            rate_log[1],
            in_coef[1],
            out_coef[1],
            skip_coef[1],
        ),
        0,
    )
    return jnp.stack([forward_out, behind], axis=1) * jax.nn.gelu(pre_gate)


def local(
    tokens,
    cotangent,
    source,
    target,
    lengths,
    ln_gain,
    ln_bias,
    w_fwd,
    b_fwd,
    w_bwd,
    b_bwd,
    w_gate,
    b_gate,
    w_out,
    b_out,
    log_dt,
    log_rate,
    ssm_b,
    ssm_c,
    ssm_d,
):
    row_count = tokens.shape[0]
    feat_width = tokens.shape[1]
    shares = lax.axis_size("tensor")
    my_share = lax.axis_index("tensor")
    group_tok = row_count * shares
    channels = w_fwd.shape[1]
    contract_rows = (((0,), (0,)), ((), ()))
    contract_cols = (((1,), (1,)), ((), ()))
    send_order = jnp.argsort(target)
    arrived = (
        lax.all_to_all(tokens[send_order], "dp", split_axis=0, concat_axis=0, tiled=True),
        lax.all_to_all(cotangent[send_order], "dp", split_axis=0, concat_axis=0, tiled=True),
    )
    anchor = source // group_tok
    recv_order = jnp.argsort(anchor * row_count + jnp.arange(row_count, dtype=jnp.int32))
    placing = jnp.argsort(recv_order)
    x_dealt = arrived[0][placing].astype(jnp.float32)
    dout_dealt = arrived[1][placing].astype(jnp.float32)
    wf_all, wb_all, wg_all, wo_all = (
        lax.all_gather(w_fwd, "dp", axis=0, tiled=True),
        lax.all_gather(w_bwd, "dp", axis=0, tiled=True),
        lax.all_gather(w_gate, "dp", axis=0, tiled=True),
        lax.all_gather(w_out, "dp", axis=2, tiled=True),
    )
    vectors = (
        lax.all_gather(ln_gain, ("dp", "tensor"), axis=0, tiled=True),
        lax.all_gather(ln_bias, ("dp", "tensor"), axis=0, tiled=True),
        lax.all_gather(b_out, ("dp", "tensor"), axis=0, tiled=True),
        lax.all_gather(b_fwd, ("dp", "tensor"), axis=0, tiled=True),
        lax.all_gather(b_bwd, ("dp", "tensor"), axis=0, tiled=True),
        lax.all_gather(b_gate, ("dp", "tensor"), axis=1, tiled=True),
        lax.all_gather(log_dt, ("dp", "tensor"), axis=1, tiled=True),
        lax.all_gather(log_rate, ("dp", "tensor"), axis=1, tiled=True),
        lax.all_gather(ssm_b, ("dp", "tensor"), axis=1, tiled=True),
        lax.all_gather(ssm_c, ("dp", "tensor"), axis=1, tiled=True),
        lax.all_gather(ssm_d, ("dp", "tensor"), axis=1, tiled=True),
    )
    first_chan = my_share * channels

    def own_slice(values, along):
        return lax.dynamic_slice_in_dim(values, first_chan, channels, along)

    def spread(piece, whole_shape, along):
        return lax.dynamic_update_slice_in_dim(
            jnp.zeros(whole_shape, jnp.float32), piece, first_chan, along
        )

    gain_all = vectors[0]
    shift_all = vectors[1]
    bias_out = vectors[2]
    bias_fwd = own_slice(vectors[3], 0)
    bias_bwd = own_slice(vectors[4], 0)
    bias_gate = own_slice(vectors[5], 1)
    step_log = own_slice(vectors[6], 1)
    rate_log = own_slice(vectors[7], 1)
    in_coef = own_slice(vectors[8], 1)
    out_coef = own_slice(vectors[9], 1)
    skip_coef = own_slice(vectors[10], 1)
    live_group, fwd_keep, rev_keep = group_layout(lengths[0], group_tok)
    live_local = lax.dynamic_slice_in_dim(live_group, my_share * row_count, row_count, 0)
    mean_val = jnp.mean(x_dealt, axis=1, keepdims=True)
    centred = x_dealt - mean_val
    inv_std = lax.rsqrt(jnp.mean(centred * centred, axis=1, keepdims=True) + epsilon)
    x_hat = centred * inv_std
    normed = (x_hat * gain_all + shift_all).astype(jnp.bfloat16)
    mix_fn = partial(mixer, live_group, fwd_keep, rev_keep)

    def project(gathered_rows):
        pre_fwd = jnp.dot(gathered_rows, wf_all, preferred_element_type=jnp.float32) + bias_fwd
        pre_bwd = jnp.dot(gathered_rows, wb_all, preferred_element_type=jnp.float32) + bias_bwd
        pre_gate = (
            jnp.einsum("td,dkc->tkc", gathered_rows, wg_all, preferred_element_type=jnp.float32)
            + bias_gate
        )
        return (pre_fwd, pre_bwd, pre_gate)

    gathered = lax.all_gather(normed, "tensor", axis=0, tiled=True)
    pre_fwd, pre_bwd, pre_gate = project(gathered)
    mixed_val = mix_fn(pre_fwd, pre_bwd, pre_gate, step_log, rate_log, in_coef, out_coef, skip_coef)
    mixed_low = mixed_val.astype(jnp.bfloat16).reshape(group_tok, 2 * channels)
    wo_flat = wo_all.reshape(2 * channels, feat_width)
    branch = lax.psum_scatter(
        jnp.dot(mixed_low, wo_flat, preferred_element_type=jnp.float32).astype(jnp.bfloat16),
        "tensor",
        scatter_dimension=0,
        tiled=True,
    ).astype(jnp.float32)
    layer_out = x_dealt + live_local[:, None] * (branch + bias_out)
    g_branch = live_local[:, None] * dout_dealt
    g_bias_out = jnp.sum(g_branch, axis=0)
    g_low = g_branch.astype(jnp.bfloat16)
    incoming = lax.all_gather(g_low, "tensor", axis=0, tiled=True)
    partial_rows = lax.dot_general(
        incoming, wo_flat, contract_cols, preferred_element_type=jnp.float32
    )
    g_mixed = partial_rows
    g_wout = lax.dot_general(mixed_low, incoming, contract_rows, preferred_element_type=jnp.float32)
    g_mixed, g_wout = (g_mixed, g_wout)
    gathered = lax.all_gather(normed, "tensor", axis=0, tiled=True)
    pre_fwd, pre_bwd, pre_gate = project(gathered)
    unused, mix_back = jax.vjp(
        mix_fn, pre_fwd, pre_bwd, pre_gate, step_log, rate_log, in_coef, out_coef, skip_coef
    )
    grads_mix = mix_back(g_mixed.reshape(group_tok, 2, channels))
    g_fwd = grads_mix[0].astype(jnp.bfloat16)
    g_bwd = grads_mix[1].astype(jnp.bfloat16)
    g_gate = grads_mix[2].astype(jnp.bfloat16).reshape(group_tok, 2 * channels)
    wg_flat = wg_all.reshape(feat_width, 2 * channels)
    total = lax.dot_general(g_fwd, wf_all, contract_cols, preferred_element_type=jnp.float32)
    total = total + lax.dot_general(
        g_bwd, wb_all, contract_cols, preferred_element_type=jnp.float32
    )
    g_normed = lax.psum_scatter(
        (
            total
            + lax.dot_general(g_gate, wg_flat, contract_cols, preferred_element_type=jnp.float32)
        ).astype(jnp.bfloat16),
        "tensor",
        scatter_dimension=0,
        tiled=True,
    ).astype(jnp.float32)
    gw_fwd = lax.dot_general(gathered, g_fwd, contract_rows, preferred_element_type=jnp.float32)
    gw_bwd = lax.dot_general(gathered, g_bwd, contract_rows, preferred_element_type=jnp.float32)
    gw_gate = lax.dot_general(
        gathered, g_gate, contract_rows, preferred_element_type=jnp.float32
    ).reshape(feat_width, 2, channels)
    gw_out = g_wout.reshape(2, channels, feat_width)
    gb_fwd = jnp.sum(g_fwd.astype(jnp.float32), axis=0)
    gb_bwd = jnp.sum(g_bwd.astype(jnp.float32), axis=0)
    gb_gate = jnp.sum(g_gate.astype(jnp.float32), axis=0).reshape(2, channels)
    g_gain = jnp.sum(g_normed * x_hat, axis=0)
    g_shift = jnp.sum(g_normed, axis=0)
    g_hat = g_normed * gain_all
    in_dealt = dout_dealt + inv_std * (
        g_hat
        - jnp.mean(g_hat, axis=1, keepdims=True)
        - x_hat * jnp.mean(g_hat * x_hat, axis=1, keepdims=True)
    )
    owned = (
        lax.psum_scatter(gw_fwd.astype(jnp.bfloat16), "dp", scatter_dimension=0, tiled=True).astype(
            jnp.float32
        ),
        lax.psum_scatter(gw_bwd.astype(jnp.bfloat16), "dp", scatter_dimension=0, tiled=True).astype(
            jnp.float32
        ),
        lax.psum_scatter(
            gw_gate.astype(jnp.bfloat16), "dp", scatter_dimension=0, tiled=True
        ).astype(jnp.float32),
        lax.psum_scatter(gw_out.astype(jnp.bfloat16), "dp", scatter_dimension=2, tiled=True).astype(
            jnp.float32
        ),
    )
    summed = (
        lax.psum_scatter(g_gain, ("dp", "tensor"), scatter_dimension=0, tiled=True),
        lax.psum_scatter(g_shift, ("dp", "tensor"), scatter_dimension=0, tiled=True),
        lax.psum_scatter(g_bias_out, ("dp", "tensor"), scatter_dimension=0, tiled=True),
        lax.psum_scatter(
            spread(gb_fwd, vectors[3].shape, 0), ("dp", "tensor"), scatter_dimension=0, tiled=True
        ),
        lax.psum_scatter(
            spread(gb_bwd, vectors[4].shape, 0), ("dp", "tensor"), scatter_dimension=0, tiled=True
        ),
        lax.psum_scatter(
            spread(gb_gate, vectors[5].shape, 1), ("dp", "tensor"), scatter_dimension=1, tiled=True
        ),
        lax.psum_scatter(
            spread(grads_mix[3], vectors[6].shape, 1),
            ("dp", "tensor"),
            scatter_dimension=1,
            tiled=True,
        ),
        lax.psum_scatter(
            spread(grads_mix[4], vectors[7].shape, 1),
            ("dp", "tensor"),
            scatter_dimension=1,
            tiled=True,
        ),
        lax.psum_scatter(
            spread(grads_mix[5], vectors[8].shape, 1),
            ("dp", "tensor"),
            scatter_dimension=1,
            tiled=True,
        ),
        lax.psum_scatter(
            spread(grads_mix[6], vectors[9].shape, 1),
            ("dp", "tensor"),
            scatter_dimension=1,
            tiled=True,
        ),
        lax.psum_scatter(
            spread(grads_mix[7], vectors[10].shape, 1),
            ("dp", "tensor"),
            scatter_dimension=1,
            tiled=True,
        ),
    )
    returned = (
        lax.all_to_all(
            layer_out.astype(jnp.bfloat16)[recv_order],
            "dp",
            split_axis=0,
            concat_axis=0,
            tiled=True,
        ),
        lax.all_to_all(
            in_dealt.astype(jnp.bfloat16)[recv_order], "dp", split_axis=0, concat_axis=0, tiled=True
        ),
    )
    restore = jnp.argsort(send_order)
    return (
        returned[0][restore],
        returned[1][restore],
        summed[0],
        summed[1],
        owned[0],
        summed[3],
        owned[1],
        summed[4],
        owned[2],
        summed[5],
        owned[3],
        summed[2],
        summed[6],
        summed[7],
        summed[8],
        summed[9],
        summed[10],
    )


def solution(mesh):
    return jax.shard_map(
        local,
        mesh=mesh,
        in_specs=(
            P(("dp", "tensor"), None),
            P(("dp", "tensor"), None),
            P(("dp", "tensor")),
            P(("dp", "tensor")),
            P("dp", None),
            P(("dp", "tensor")),
            P(("dp", "tensor")),
            P("dp", "tensor"),
            P(("dp", "tensor")),
            P("dp", "tensor"),
            P(("dp", "tensor")),
            P("dp", None, "tensor"),
            P(None, ("dp", "tensor")),
            P(None, "tensor", "dp"),
            P(("dp", "tensor")),
            P(None, ("dp", "tensor")),
            P(None, ("dp", "tensor"), None),
            P(None, ("dp", "tensor"), None),
            P(None, ("dp", "tensor"), None),
            P(None, ("dp", "tensor")),
        ),
        out_specs=(
            P(("dp", "tensor"), None),
            P(("dp", "tensor"), None),
            P(("dp", "tensor")),
            P(("dp", "tensor")),
            P("dp", "tensor"),
            P(("dp", "tensor")),
            P("dp", "tensor"),
            P(("dp", "tensor")),
            P("dp", None, "tensor"),
            P(None, ("dp", "tensor")),
            P(None, "tensor", "dp"),
            P(("dp", "tensor")),
            P(None, ("dp", "tensor")),
            P(None, ("dp", "tensor"), None),
            P(None, ("dp", "tensor"), None),
            P(None, ("dp", "tensor"), None),
            P(None, ("dp", "tensor")),
        ),
        check_vma=False,
    )
```

profile of v0, /device:TPU:1, one launch (start us, length us, event | category | flops | bytes accessed | tf_op | source)
XLA Modules:
  0.0 3676.3 jit_solution(5048482560316226244)
XLA Ops:
  33.3 43.4 %all-reduce.29 = (f32[768]{0:T(1024)S(1)}, f32[768]{0:T(1024)S(1)}, f32[1536]{0:T(1024)S(1)}, f32[1536]{0:T(1024)S(1)}) all-reduce(f32[768]{0:T(1024)S(1)} %dynamic-update-slice.1, f32[768]{0:T(1024)S(1)} %dynamic-update-slice, f32[1536]{0:T(1024)S(1)} %dynamic-update-slice.3, ...), channel_id=1, replica_groups=mesh['dp'=8,'tensor'=4] {'dp','tensor'}, use_global_device_ids=true, to_apply=%add.19 | all-reduce | flops 4608 | bytes 36864
  120.5 118.2 %all_gather.60 = f32[2,1536,64]{2,1,0:T(8,128)} all-gather(f32[2,48,64]{2,1,0:T(8,128)S(1)} %copy-done.68), channel_id=1, replica_groups=mesh['dp'=8,'tensor'=4] {'dp','tensor'}, dimensions={1}, use_global_device_ids=true | all-gather | bytes 811008 | tf_op jit(solution)/shard_map/all_gather | solution.py:148
  238.7 107.1 %all_gather.58 = f32[2,1536,64]{2,1,0:T(8,128)S(1)} all-gather(f32[2,48,64]{2,1,0:T(8,128)S(1)} %copy-done.69), channel_id=1, replica_groups=mesh['dp'=8,'tensor'=4] {'dp','tensor'}, dimensions={1}, use_global_device_ids=true | all-gather | bytes 811008 | tf_op jit(solution)/shard_map/all_gather | solution.py:147
  345.8 70.1 %all-gather = f32[32,48,2]{1,2,0:T(2,128)S(1)} all-gather(f32[1,48,2]{1,2,0:T(2,128)S(1)} %bitcast.578), channel_id=1, replica_groups=mesh['dp'=8,'tensor'=4] {'dp','tensor'}, dimensions={0}, use_global_device_ids=true | all-gather | bytes 12672 | tf_op jit(solution)/shard_map/all_gather | solution.py:146
  416.0 64.3 %all-gather.1 = f32[32,48,2]{1,2,0:T(2,128)S(1)} all-gather(f32[1,48,2]{1,2,0:T(2,128)S(1)} %bitcast.579), channel_id=1, replica_groups=mesh['dp'=8,'tensor'=4] {'dp','tensor'}, dimensions={0}, use_global_device_ids=true | all-gather | bytes 12672 | tf_op jit(solution)/shard_map/all_gather | solution.py:150
  565.7 60.3 %all-gather.2 = f32[32,48,2]{1,2,0:T(2,128)S(1)} all-gather(f32[1,48,2]{1,2,0:T(2,128)S(1)} %bitcast.580), channel_id=1, replica_groups=mesh['dp'=8,'tensor'=4] {'dp','tensor'}, dimensions={0}, use_global_device_ids=true | all-gather | bytes 12672 | tf_op jit(solution)/shard_map/all_gather | solution.py:145
  626.7 76.6 %all_gather.59 = f32[2,1536,64]{2,1,0:T(8,128)S(1)} all-gather(f32[2,48,64]{2,1,0:T(8,128)S(1)} %copy-done.70), channel_id=1, replica_groups=mesh['dp'=8,'tensor'=4] {'dp','tensor'}, dimensions={1}, use_global_device_ids=true | all-gather | bytes 811008 | tf_op jit(solution)/shard_map/all_gather | solution.py:149
  776.5 63.3 %gather_fusion.2 = f32[16384,384]{1,0:T(8,128)} fusion(f32[384,128]{0,1:T(8,128)S(1)} %bitcast.504, s32[16384]{0:T(1024)S(1)} %broadcast_clamp_fusion), kind=kCustom, calls=%fused_computation.2 | custom fusion | bytes 50397184 | tf_op jit(solution)/shard_map/gather | solution.py:42
  839.8 24.8 copy.145
  897.5 63.3 %gather_fusion.3 = f32[16384,384]{1,0:T(8,128)} fusion(f32[384,128]{0,1:T(8,128)S(1)} %bitcast.503, s32[16384]{0:T(1024)S(1)} %broadcast_clamp_fusion), kind=kCustom, calls=%fused_computation.3 | custom fusion | bytes 50397184 | tf_op jit(solution)/shard_map/gather | solution.py:42
  960.9 24.8 copy.152
  1023.5 137.2 %while.74 = (s32[]{:T(128)}, f32[384,64]{1,0:T(8,128)S(1)}, f32[32,384,64]{2,1,0:T(8,128)}, f32[32]{0:T(128)S(1)}, f32[384,64]{1,0:T(8,128)S(1)}, /*index=5*/f32[32,384,64]{2,0,1:T(8,128)}, s32[]{:T(128)}, s32[]{:T(128)}) while((s32[]{:T(128)}, f32[384,64]{1,0:T(8,128)S(1)}, f32[32,384,64]{2,1,0:T(8,128)}, f32[32]{0:T(128)S(1)}, ...), condition=%wide.region_9.10_spmd.clone, body=%wide.region_8.9_spmd.clone.sunk | while | flops 147459 | bytes 885376 | solution.py:55
  1181.6 42.8 %bitcast_add_fusion.6 = f32[32,128,384]{1,0,2:T(8,128)S(1)} fusion(f32[384,128,32]{1,2,0:T(8,128)S(1)} %fusion.43, f32[32,128,384]{1,0,2:T(8,128)} %bitcast.508, f32[128,128,384]{1,0,2:T(8,128)} %copy.145, pred[128,128]{1,0:T(8,128)(4,1)S(1)} %copy-done.37), kind=kOutput, calls=%fused_computation.149 | convolution fusion | flops 2423783424 | bytes 44056576 | tf_op jit(solution)/shard_map/cts,bsc->btc/dot_general | solution.py:44
  1240.1 51.1 %rev.36 = f32[4096,384]{0,1:T(8,128)} reverse(f32[4096,384]{0,1:T(8,128)} %get-tuple-element.850), dimensions={0} | reverse | bytes 12582912 | tf_op jit(solution)/shard_map/jit(_flip)/rev | solution.py:80
  1295.3 26.0 fusion.129
  1324.8 137.1 %while.75 = (s32[]{:T(128)}, f32[384,64]{1,0:T(8,128)S(1)}, f32[32,384,64]{2,1,0:T(8,128)}, f32[32]{0:T(128)S(1)}, f32[384,64]{1,0:T(8,128)S(1)}, /*index=5*/f32[32,384,64]{2,0,1:T(8,128)}, s32[]{:T(128)}, s32[]{:T(128)}) while((s32[]{:T(128)}, f32[384,64]{1,0:T(8,128)S(1)}, f32[32,384,64]{2,1,0:T(8,128)}, f32[32]{0:T(128)S(1)}, ...), condition=%wide.region_11.12_spmd.clone, body=%wide.region_10.11_spmd.clone.sunk | while | flops 147459 | bytes 885376 | solution.py:55
  1483.1 43.4 %bitcast_add_fusion.5 = f32[32,128,384]{1,0,2:T(8,128)S(1)} fusion(f32[384,128,32]{1,2,0:T(8,128)} %fusion.45, f32[32,128,384]{1,0,2:T(8,128)} %bitcast.512, f32[128,128,384]{1,0,2:T(8,128)} %copy.152, pred[128,128]{1,0:T(8,128)(4,1)S(1)} %copy-done.37), kind=kOutput, calls=%fused_computation.148 | convolution fusion | flops 2423783424 | bytes 44056576 | tf_op jit(solution)/shard_map/cts,bsc->btc/dot_general | solution.py:44
  1535.7 51.0 %rev.39 = f32[4096,384]{0,1:T(8,128)} reverse(f32[4096,384]{0,1:T(8,128)} %bitcast_add_fusion.3), dimensions={0} | reverse | bytes 12582912 | tf_op jit(solution)/shard_map/jit(_flip)/rev | solution.py:78
  1597.0 26.8 convert_reduce_fusion
  1634.5 51.0 %rev.40 = f32[4096,384]{0,1:T(8,128)} reverse(f32[4096,384]{0,1:T(8,128)} %get-tuple-element.826), dimensions={0} | reverse | bytes 12582912 | tf_op jit(solution)/shard_map/transpose(jvp(jit(_flip)))/rev | solution.py:78
  1689.7 28.4 fusion.2
  1718.1 27.5 fusion.120
  1747.0 28.2 fusion.6
  1775.1 27.5 fusion.123
  1806.0 146.0 %while.77 = (s32[]{:T(128)}, f32[384,64]{1,0:T(8,128)S(1)}, f32[384,64]{1,0:T(8,128)S(1)}, f32[32,384,64]{2,1,0:T(8,128)}, f32[32,384,64]{2,1,0:T(8,128)}, /*ind...) while((s32[]{:T(128)}, f32[384,64]{1,0:T(8,128)S(1)}, ...), condition=%wide.region_17.18_spmd.clone, body=%wide.region_16.17_spmd.clone.sunk | while | flops 196612 | bytes 1179816 | solution.py:55
  1984.2 51.1 %rev.41 = f32[4096,384]{0,1:T(8,128)} reverse(f32[4096,384]{0,1:T(8,128)} %get-tuple-element.829), dimensions={0} | reverse | bytes 12582912 | tf_op jit(solution)/shard_map/transpose(jvp(jit(_flip)))/rev | solution.py:80
  2038.8 146.0 %while.76 = (s32[]{:T(128)}, f32[384,64]{1,0:T(8,128)S(1)}, f32[384,64]{1,0:T(8,128)S(1)}, f32[32,384,64]{2,1,0:T(8,128)}, f32[32,384,64]{2,1,0:T(8,128)}, /*ind...) while((s32[]{:T(128)}, f32[384,64]{1,0:T(8,128)S(1)}, ...), condition=%wide.region_15.16_spmd.clone, body=%wide.region_14.15_spmd.clone.sunk | while | flops 196612 | bytes 1179816 | solution.py:55
  2254.1 45.1 %select_bitcast_fusion.1 = f32[128,128,384]{1,0,2:T(8,128)} fusion(pred[128,128]{1,0:T(8,128)(4,1)S(1)} %copy-done.37, f32[32,128,384]{1,0,2:T(8,128)} %bitcast.513, f32[32,128,384]{1,0,2:T(8,128)} %bitcast.523), kind=kOutput, calls=%fused_computation.41 | convolution fusion | flops 2422210560 | bytes 37765120 | tf_op jit(solution)/shard_map/transpose(jvp(cts,bsc->btc))/dot_general | solution.py:44
  2299.2 25.0 copy.206
  2324.2 104.1 %scatter_custom_fusion = f32[384,128]{0,1:T(8,128)S(1)} fusion(s32[16384]{0:T(1024)S(1)} %fusion.184, f32[16384,384]{1,0:T(8,128)} %bitcast.544, f32[]{:T(128)} %constant.182.clone.1), kind=kCustom, calls=%fused_computation.271 | custom fusion | flops 6291456 | bytes 197120 | tf_op jit(solution)/shard_map/transpose(jvp())/scatter-add | solution.py:42
  2439.2 35.0 fusion.23
  2500.1 44.8 %select_bitcast_fusion = f32[128,128,384]{1,0,2:T(8,128)} fusion(pred[128,128]{1,0:T(8,128)(4,1)S(1)} %copy-done.37, f32[32,128,384]{1,0,2:T(8,128)} %bitcast.509, f32[32,128,384]{1,0,2:T(8,128)} %bitcast.517), kind=kOutput, calls=%fused_computation.39 | convolution fusion | flops 2422210560 | bytes 37765120 | tf_op jit(solution)/shard_map/transpose(jvp(cts,bsc->btc))/dot_general | solution.py:44
  2544.9 24.8 copy.209
  2569.7 104.1 %scatter_custom_fusion.1 = f32[384,128]{0,1:T(8,128)S(1)} fusion(s32[16384]{0:T(1024)S(1)} %fusion.184, f32[16384,384]{1,0:T(8,128)} %bitcast.543, f32[]{:T(128)} %constant.182.clone.1), kind=kCustom, calls=%fused_computation.269 | custom fusion | flops 6291456 | bytes 197120 | tf_op jit(solution)/shard_map/transpose(jvp())/scatter-add | solution.py:42
  2674.9 34.4 fusion.21
  2794.3 39.4 %fusion.24 = (f32[384,64]{1,0:T(8,128)S(1)}, f32[128,384,64]{0,2,1:T(8,128)}) fusion(f32[129,384,64]{0,2,1:T(8,128)} %multiply_exponential_fusion, f32[384,64]{1,0:T(8,128)S(1)} %copy-done.32, f32[32,384,64]{2,1,0:T(8,128)} %get-tuple-element.1172, f32[32,128,384]{1,0,2:T(8,128)} %bitcast.524), kind=kOutput, calls=%fused_computation.69 | convolution fusion | flops 1217372160 | bytes 34799616 | tf_op jit(solution)/shard_map/transpose(jvp(bcn,tcn->btc))/dot_general | solution.py:56
  2833.8 39.1 %fusion.22 = (f32[384,64]{1,0:T(8,128)S(1)}, f32[128,384,64]{0,2,1:T(8,128)}) fusion(f32[129,384,64]{0,2,1:T(8,128)} %multiply_exponential_fusion.1, f32[384,64]{1,0:T(8,128)S(1)} %copy-done.30, f32[32,384,64]{2,1,0:T(8,128)} %get-tuple-element.1171, f32[32,128,384]{1,0,2:T(8,128)S(1)} %bitcast.520), kind=kOutput, calls=%fused_computation.63 | convolution fusion | flops 1217372160 | bytes 34799616 | tf_op jit(solution)/shard_map/transpose(jvp(bcn,tcn->btc))/dot_general | solution.py:56
  2895.0 22.3 multiply_reduce_fusion
  2969.3 37.2 %all-reduce.28 = (f32[768]{0:T(1024)}, f32[768]{0:T(1024)}, f32[768]{0:T(1024)}, f32[1536]{0:T(1024)}, f32[1536]{0:T(1024)}, /*index=5*/f32[768]{0:T(1024)}) all-reduce(f32[768]{0:T(1024)} %copy-done.87, f32[768]{0:T(1024)S(1)} %get-tuple-element.717, f32[768]{0:T(1024)S(1)} %get-tuple-element.722, ...), channel_id=1, replica_groups=mesh['dp'=8,'tensor'=4] {'dp','tensor'}, use_global_device_ids=true, to_apply=%add.22 | all-reduce | flops 6144 | bytes 49152
  3053.0 56.2 %reduce-scatter.39.cloned.1.call-done = f32[48,2]{1,0:T(8,128)} async-done(((f32[1536,2]{1,0:T(8,128)}), f32[48,2]{1,0:T(8,128)}) %reduce-scatter.39.cloned.1.call-update) | async-done | bytes 400
  3110.5 98.3 %reduce-scatter.41.cloned.1.call-done = f32[48,2]{1,0:T(8,128)} async-done(((f32[1536,2]{1,0:T(8,128)}), f32[48,2]{1,0:T(8,128)}) %reduce-scatter.41.cloned.1.call-update) | async-done | bytes 400
  3210.2 36.2 reduce-scatter.23.cloned.1.call-done
  3248.0 36.0 reduce-scatter.25.cloned.1.call-done
  3285.5 38.7 %reduce-scatter.27.cloned.1.call-done = bf16[96,2,384]{2,0,1:T(8,128)(2,1)} async-done(((bf16[768,2,384]{2,0,1:T(8,128)(2,1)}), bf16[96,2,384]{2,0,1:T(8,128)(2,1)}) %reduce-scatter.27.cloned.1.call-update) | async-done | bytes 147472 | tf_op jit(solution)/shard_map/reduce_scatter | solution.py:260
  3326.0 38.6 %reduce-scatter.29.cloned.1.call-done = bf16[2,384,96]{1,2,0:T(8,128)(2,1)} async-done(((bf16[2,384,768]{1,2,0:T(8,128)(2,1)}), bf16[2,384,96]{1,2,0:T(8,128)(2,1)}) %reduce-scatter.29.cloned.1.call-update) | async-done | bytes 147472 | tf_op jit(solution)/shard_map/reduce_scatter | solution.py:263
  3383.0 82.8 %reduce-scatter.31.cloned.1.call-done = f32[2,48,64]{2,1,0:T(8,128)} async-done(((f32[2,1536,64]{2,1,0:T(8,128)}), f32[2,48,64]{2,1,0:T(8,128)}) %reduce-scatter.31.cloned.1.call-update) | async-done | bytes 24592 | tf_op jit(solution)/shard_map/reduce_scatter | solution.py:286
  3465.8 101.8 %reduce-scatter.33.cloned.1.call-done = f32[2,48,64]{2,1,0:T(8,128)} async-done(((f32[2,1536,64]{2,1,0:T(8,128)}), f32[2,48,64]{2,1,0:T(8,128)}) %reduce-scatter.33.cloned.1.call-update) | async-done | bytes 24592 | tf_op jit(solution)/shard_map/reduce_scatter | solution.py:292
  3567.6 101.8 %reduce-scatter.35.cloned.1.call-done = f32[2,48,64]{2,1,0:T(8,128)} async-done(((f32[2,1536,64]{2,1,0:T(8,128)}), f32[2,48,64]{2,1,0:T(8,128)}) %reduce-scatter.35.cloned.1.call-update) | async-done | bytes 24592 | tf_op jit(solution)/shard_map/reduce_scatter | solution.py:298
  (978 shorter events, 1341.0 us)
Async XLA Ops:
  18.4 58.4 %all-to-all-start = ((bf16[8,128,768]{2,1,0:T(8,128)(2,1)}), bf16[8,128,768]{2,1,0:T(8,128)(2,1)S(1)}, u32[]{:S(2)}, u32[]{:S(2)}) async-start(bf16[8,128,768]{2,1,0:T(8,128)(2,1)} %bitcast), calls=%async_computation | async-start | bytes 3145728 | tf_op jit(solution)/shard_map/all_to_all | solution.py:125
  23.6 962.1 %all-gather.8.cloned.1.call-start = ((), (), s32[]{:S(2)}) async-start(), calls=%async_computation.16 | async-start | bytes 7864320 | tf_op jit(solution)/shard_map/all_gather | solution.py:191
  84.2 1502.5 %all-gather.12.cloned.1.call-start = ((), (), s32[]{:S(2)}) async-start(), calls=%async_computation.18 | async-start | bytes 1327104 | tf_op jit(solution)/shard_map/all_gather | solution.py:137
  90.2 22.6 all-to-all-start.2
  95.2 1491.5 %all-gather.14.cloned.1.call-start = ((), (), s32[]{:S(2)}) async-start(), calls=%async_computation.20 | async-start | bytes 7864320 | tf_op jit(solution)/shard_map/all_gather | solution.py:206
  116.8 375.9 %copy-start.18 = (bf16[1024,768]{1,0:T(8,128)(2,1)}, bf16[1024,768]{1,0:T(8,128)(2,1)S(1)}, u32[]{:S(2)}) copy-start(bf16[1024,768]{1,0:T(8,128)(2,1)S(1)} %gather_fusion.7) | copy-start | bytes 4718596
  116.8 121.9 %copy-start.69 = (f32[2,48,64]{2,1,0:T(8,128)S(1)}, f32[2,48,64]{2,1,0:T(8,128)}, u32[]{:S(2)}) copy-start(f32[2,48,64]{2,1,0:T(8,128)} %param.44) | copy-start | bytes 73732
  116.8 229.0 %copy-start.95 = (f32[2,48]{1,0:T(2,128)S(1)}, f32[2,48]{1,0:T(2,128)}, u32[]{:S(2)}) copy-start(f32[2,48]{1,0:T(2,128)} %param.43) | copy-start | bytes 1156
  116.8 299.2 %copy-start.96 = (f32[2,48]{1,0:T(2,128)S(1)}, f32[2,48]{1,0:T(2,128)}, u32[]{:S(2)}) copy-start(f32[2,48]{1,0:T(2,128)} %param.47) | copy-start | bytes 1156
  119.1 1477.9 %all-gather.10.cloned.1.call-start = ((), (), s32[]{:S(2)}) async-start(), calls=%async_computation.17 | async-start | bytes 1327104 | tf_op jit(solution)/shard_map/all_gather | solution.py:136
  119.8 2845.3 %reduce-scatter.21.cloned.1.call-start = ((), (), s32[]{:S(2)}) async-start(), calls=%async_computation.21 | async-start | bytes 7864320 | tf_op jit(solution)/shard_map/reduce_scatter | solution.py:227
  345.8 357.5 %copy-start.26 = (f32[2,1536,64]{2,1,0:T(8,128)}, f32[2,1536,64]{2,1,0:T(8,128)S(1)}, u32[]{:S(2)}) copy-start(f32[2,1536,64]{2,1,0:T(8,128)S(1)} %all_gather.58) | copy-start | bytes 2359300
  481.1 222.2 %copy-start.64 = (f32[384]{0:T(512)}, f32[384]{0:T(512)S(1)}, u32[]{:S(2)}) copy-start(f32[384]{0:T(512)S(1)} %get-tuple-element.725) | copy-start | bytes 4612
  481.1 222.2 %copy-start.66 = (f32[384]{0:T(512)}, f32[384]{0:T(512)S(1)}, u32[]{:S(2)}) copy-start(f32[384]{0:T(512)S(1)} %get-tuple-element.726) | copy-start | bytes 4612
  537.9 88.8 %copy-start.70 = (f32[2,48,64]{2,1,0:T(8,128)S(1)}, f32[2,48,64]{2,1,0:T(8,128)}, u32[]{:S(2)}) copy-start(f32[2,48,64]{2,1,0:T(8,128)} %param.46) | copy-start | bytes 73732
  705.3 58.0 %copy-start.46 = (f32[384,64]{1,0:T(8,128)}, f32[384,64]{1,0:T(8,128)S(1)}, u32[]{:S(2)}) copy-start(f32[384,64]{1,0:T(8,128)S(1)} %get-tuple-element.803) | copy-start | bytes 294916
  705.3 179.0 %copy-start.48 = (f32[384,64]{1,0:T(8,128)}, f32[384,64]{1,0:T(8,128)S(1)}, u32[]{:S(2)}) copy-start(f32[384,64]{1,0:T(8,128)S(1)} %get-tuple-element.830) | copy-start | bytes 294916
  1020.1 140.7 %copy-start.28 = (f32[384,64]{1,0:T(8,128)S(1)}, f32[384,64]{1,0:T(8,128)}, u32[]{:S(2)}) copy-start(f32[384,64]{1,0:T(8,128)} %get-tuple-element.804) | copy-start | bytes 294916
  1160.8 68.6 %slice-start.7 = ((s8[6291456]{0:T(1024)(128)(4,1)}), s8[2097152]{0:T(1024)(128)(4,1)S(1)}, s32[]{:S(2)}) async-start(s8[6291456]{0:T(1024)(128)(4,1)} %bitcast.534), calls=%async_computation.39 | async-start | bytes 4194304
  1181.5 42.9 %copy-start.38 = (bf16[768,384]{1,0:T(8,128)(2,1)S(1)}, bf16[768,384]{1,0:T(8,128)(2,1)}, u32[]{:S(2)}) copy-start(bf16[768,384]{1,0:T(8,128)(2,1)} %all_gather.62) | copy-start | bytes 1769476
  1181.6 42.9 %copy-start.93 = (f32[384]{0:T(512)S(1)}, f32[384]{0:T(512)}, u32[]{:S(2)}) copy-start(f32[384]{0:T(512)} %dynamic_slice.106) | copy-start | bytes 4612
  1181.6 47.8 %slice-start.8 = ((s8[6291456]{0:T(1024)(128)(4,1)}), s8[4194304]{0:T(1024)(128)(4,1)S(1)}, s32[]{:S(2)}) async-start(s8[6291456]{0:T(1024)(128)(4,1)} %bitcast.534), calls=%async_computation.40 | async-start | bytes 8388608
  1321.4 140.6 %copy-start.31 = (f32[384,64]{1,0:T(8,128)S(1)}, f32[384,64]{1,0:T(8,128)}, u32[]{:S(2)}) copy-start(f32[384,64]{1,0:T(8,128)} %get-tuple-element.831) | copy-start | bytes 294916
  1462.0 64.5 %slice-start.5 = ((s8[6291456]{0:T(1024)(128)(4,1)}), s8[4194304]{0:T(1024)(128)(4,1)S(1)}, s32[]{:S(2)}) async-start(s8[6291456]{0:T(1024)(128)(4,1)} %bitcast.530), calls=%async_computation.37 | async-start | bytes 8388608
  1483.0 43.4 %slice-start.6 = ((s8[6291456]{0:T(1024)(128)(4,1)}), s8[2097152]{0:T(1024)(128)(4,1)S(1)}, s32[]{:S(2)}) async-start(s8[6291456]{0:T(1024)(128)(4,1)} %bitcast.530), calls=%async_computation.38 | async-start | bytes 4194304
  1483.0 43.4 %copy-start.82 = (f32[384]{0:T(512)S(1)}, f32[384]{0:T(512)}, u32[]{:S(2)}) copy-start(f32[384]{0:T(512)} %get-tuple-element.724) | copy-start | bytes 4612
  1685.5 60.2 %slice-start.9 = ((s8[6291456]{0:T(1024)(128)(4,1)}), s8[4194304]{0:T(1024)(128)(4,1)S(1)}, s32[]{:S(2)}) async-start(s8[6291456]{0:T(1024)(128)(4,1)} %bitcast.545), calls=%async_computation.41 | async-start | bytes 8388608
  1689.7 55.9 %slice-start.10 = ((s8[6291456]{0:T(1024)(128)(4,1)}), s8[2097152]{0:T(1024)(128)(4,1)S(1)}, s32[]{:S(2)}) async-start(s8[6291456]{0:T(1024)(128)(4,1)} %bitcast.545), calls=%async_computation.42 | async-start | bytes 4194304
  1806.0 146.0 %copy-start.36 = (f32[384,64]{1,0:T(8,128)S(1)}, f32[384,64]{1,0:T(8,128)}, u32[]{:S(2)}) copy-start(f32[384,64]{1,0:T(8,128)} %get-tuple-element.837) | copy-start | bytes 294916
  2038.8 146.0 %copy-start.34 = (f32[384,64]{1,0:T(8,128)S(1)}, f32[384,64]{1,0:T(8,128)}, u32[]{:S(2)}) copy-start(f32[384,64]{1,0:T(8,128)} %get-tuple-element.836) | copy-start | bytes 294916
  2252.8 753.7 %reduce-scatter.19.cloned.1.call-start = ((), (), s32[]{:S(2)}) async-start(), calls=%async_computation.19 | async-start | bytes 7864320 | tf_op jit(solution)/shard_map/reduce_scatter | solution.py:196
  2299.2 129.9 %copy-start.101 = (bf16[2,384,768]{1,2,0:T(8,128)(2,1)S(1)}, bf16[2,384,768]{1,2,0:T(8,128)(2,1)}, u32[]{:S(2)}) copy-start(bf16[2,384,768]{1,2,0:T(8,128)(2,1)} %all-gather.12.cloned.1.call-done) | copy-start | bytes 3538948
  2439.1 612.5 %reduce-scatter.37.cloned.1.call-start = ((), (), s32[]{:S(2)}) async-start(), calls=%async_computation.29 | async-start | bytes 811008
  2787.2 46.6 %slice-start.3 = ((s8[6291456]{0:T(1024)(128)(4,1)}), s8[4194304]{0:T(1024)(128)(4,1)S(1)}, s32[]{:S(2)}) async-start(s8[6291456]{0:T(1024)(128)(4,1)} %bitcast.518), calls=%async_computation.35 | async-start | bytes 8388608
  2794.3 39.4 %slice-start.4 = ((s8[6291456]{0:T(1024)(128)(4,1)}), s8[2097152]{0:T(1024)(128)(4,1)S(1)}, s32[]{:S(2)}) async-start(s8[6291456]{0:T(1024)(128)(4,1)} %bitcast.518), calls=%async_computation.36 | async-start | bytes 4194304
  2919.7 189.5 %reduce-scatter.39.cloned.1.call-start = ((), (), s32[]{:S(2)}) async-start(), calls=%async_computation.30 | async-start | bytes 811008
  2921.0 287.8 %reduce-scatter.41.cloned.1.call-start = ((), (), s32[]{:S(2)}) async-start(), calls=%async_computation.31 | async-start | bytes 811008
  2922.3 324.1 %reduce-scatter.23.cloned.1.call-start = ((), (), s32[]{:S(2)}) async-start(), calls=%async_computation.22 | async-start | bytes 663552 | tf_op jit(solution)/shard_map/reduce_scatter | solution.py:254
  2930.5 353.5 %reduce-scatter.25.cloned.1.call-start = ((), (), s32[]{:S(2)}) async-start(), calls=%async_computation.23 | async-start | bytes 663552 | tf_op jit(solution)/shard_map/reduce_scatter | solution.py:257
  2938.6 385.7 %reduce-scatter.27.cloned.1.call-start = ((), (), s32[]{:S(2)}) async-start(), calls=%async_computation.24 | async-start | bytes 1327104 | tf_op jit(solution)/shard_map/reduce_scatter | solution.py:260
  2950.6 414.1 %reduce-scatter.29.cloned.1.call-start = ((), (), s32[]{:S(2)}) async-start(), calls=%async_computation.25 | async-start | bytes 1327104 | tf_op jit(solution)/shard_map/reduce_scatter | solution.py:263
  2960.6 45.9 %copy-start.74 = (f32[1024]{0:T(1024)S(1)}, f32[1024]{0:T(1024)}, u32[]{:S(2)}) copy-start(f32[1024]{0:T(1024)} %copy-done.73) | copy-start | bytes 12292
  2960.7 505.1 %reduce-scatter.31.cloned.1.call-start = ((), (), s32[]{:S(2)}) async-start(), calls=%async_computation.26 | async-start | bytes 1622016 | tf_op jit(solution)/shard_map/reduce_scatter | solution.py:286
  3015.9 22.3 all-to-all-start.1
  3020.6 547.0 %reduce-scatter.33.cloned.1.call-start = ((), (), s32[]{:S(2)}) async-start(), calls=%async_computation.27 | async-start | bytes 1622016 | tf_op jit(solution)/shard_map/reduce_scatter | solution.py:292
  3038.2 339.6 %all-to-all-start.3 = ((bf16[8,128,768]{2,1,0:T(8,128)(2,1)}), bf16[8,128,768]{2,1,0:T(8,128)(2,1)S(1)}, u32[]{:S(2)}, u32[]{:S(2)}) async-start(bf16[8,128,768]{2,1,0:T(8,128)(2,1)} %bitcast.559), calls=%async_computation.5 | async-start | bytes 3145728 | tf_op jit(solution)/shard_map/all_to_all | solution.py:319
  3045.1 624.2 %reduce-scatter.35.cloned.1.call-start = ((), (), s32[]{:S(2)}) async-start(), calls=%async_computation.28 | async-start | bytes 1622016 | tf_op jit(solution)/shard_map/reduce_scatter | solution.py:298
  3377.8 291.5 %copy-start.1 = (bf16[1024,768]{1,0:T(8,128)(2,1)S(1)}, bf16[1024,768]{1,0:T(8,128)(2,1)}, u32[]{:S(2)}) copy-start(bf16[1024,768]{1,0:T(8,128)(2,1)} %param.28) | copy-start | bytes 4718596
  (92 other events, 1151.4 us)
Sparse Core Ops, SparseCore 0:
  84.3 141.8 all-gather.7
  228.1 22.9 all-gather.11
  252.7 137.1 all-gather.13
  392.2 23.9 all-gather.9
  2252.9 107.5 reduce-scatter.20
  2439.2 107.2 reduce-scatter.18
  2919.8 89.6 reduce-scatter.36
  3014.6 94.5 reduce-scatter.38
  3114.3 94.5 reduce-scatter.40
  3211.8 34.5 reduce-scatter.22
  3249.6 34.3 reduce-scatter.24
  3287.1 37.1 reduce-scatter.26
  3327.8 36.7 reduce-scatter.28
  3370.3 95.4 reduce-scatter.30
  3471.5 96.0 reduce-scatter.32
  3573.2 96.0 reduce-scatter.34
where the time goes:
time: 3710 us; the launch traced here: 3680 us
  local copies, waits for them, and re-layouts  968 us (26%)
  matrix products  758 us (20%)
  other arithmetic  680 us (18%)
  waiting for transfers between devices  618 us (17%)
  blocking collectives  612 us (16%)
    dynamic_slice x256, local copies, waits for them, and re-layouts, ssm_blocks(): lax.scan(advance, jnp.zeros_like(decay), (inflows, keep_flags))  273 us
    dot_general x6, matrix products, ssm_blocks(): intra = jnp.einsum('cts,bsc->btc', toeplitz, blocks, precision=highest)  233 us
    scatter-add x2, other arithmetic, ssm_blocks(): kernel[:, jnp.clip(lag_idx, 0, BLK - 1)]  208 us
    gather x4, local copies, waits for them, and re-layouts, ssm_blocks(): kernel[:, jnp.clip(lag_idx, 0, BLK - 1)]  176 us
    dot_general x6, matrix products, ssm_blocks(): jnp.einsum('bcn,tcn->btc', entering, powers[1:] * out_coef[None], precisi...  175 us
    dot_general x6, matrix products, ssm_blocks(): jnp.einsum('bsc,scn->bcn', blocks, powers[BLK - 1::-1] * drive[None], pre...  156 us
    unnamed x19, waiting for transfers between devices  155 us
    dynamic_update_slice x128, other arithmetic, ssm_blocks(): lax.scan(advance, jnp.zeros_like(decay), (inflows, keep_flags))  130 us
  transfers between devices with their start and end apart: 20, of which 11 were waited for; matrix products, arithmetic and copies ran while one was open for 47% of the time, Pallas kernels for 0%

commit v1 on v0

v1 whole, which is shorter than its diff:
```python
from functools import partial

import jax
import jax.numpy as jnp
import numpy as np
from jax import lax
from jax.experimental import pallas as pl
from jax.experimental.pallas import tpu as pltpu
from jax.sharding import PartitionSpec as P

BLK = 128
BIG = 256
MOST = 2048
LAGS = MOST // BIG
STATE = 64
epsilon = 1e-05
log2e = 1.4426950408889634
f32 = jnp.float32
bf16 = jnp.bfloat16
MIB = 2**20


def nn(a, b):
    return lax.dot_general(a, b, (((1,), (0,)), ((), ())), preferred_element_type=f32)


def nt(a, b):
    return lax.dot_general(a, b, (((1,), (1,)), ((), ())), preferred_element_type=f32)


def params(limit):
    return pltpu.CompilerParams(vmem_limit_bytes=limit * MIB)


def cost(flops, moved, trans=0):
    return pl.CostEstimate(flops=int(flops), bytes_accessed=int(moved), transcendentals=int(trans))


def halves(x):
    high = x.astype(bf16)
    return high, (x - high.astype(f32)).astype(bf16)


def wave_table():
    pos = np.arange(BIG)[:, None]
    freq = np.arange(BIG)[None, :]
    angle = 2 * np.pi * ((2 * freq + 1) * pos % (4 * BIG)) / (4 * BIG)
    return np.concatenate([np.cos(angle), np.sin(angle)], 1).astype(np.float32)


def chunk_of(channels, most):
    best = 16
    for size in range(16, most + 1, 16):
        if channels % size == 0:
            best = size
    return best


def permute_row_body(count, rank_ref, *refs):
    rows = rank_ref.shape[1]
    spot = lax.broadcasted_iota(jnp.int32, (rows, rows), 0)
    pick = jnp.where(spot == rank_ref[...], 1.0, 0.0).astype(bf16)
    for at in range(count):
        refs[count + at][...] = nn(pick, refs[at][...]).astype(bf16)


def permute_to(rank, arrays):
    rows, width = arrays[0].shape
    count = len(arrays)
    return pl.pallas_call(
        partial(permute_row_body, count),
        out_shape=[jax.ShapeDtypeStruct((rows, width), bf16)] * count,
        compiler_params=params(48),
        cost_estimate=cost(2 * count * rows * rows * width, 4 * count * rows * width),
    )(rank.reshape(1, rows), *arrays)


def permute_col_body(rank_ref, x_ref, o_ref):
    rows = x_ref.shape[0]
    spot = lax.broadcasted_iota(jnp.int32, (rows, rows), 1)
    pick = jnp.where(spot == rank_ref[...], 1.0, 0.0).astype(bf16)
    o_ref[...] = nn(pick, x_ref[...]).astype(bf16)


def permute_from(rank, x):
    rows, width = x.shape
    return pl.pallas_call(
        permute_col_body,
        out_shape=jax.ShapeDtypeStruct((rows, width), bf16),
        compiler_params=params(48),
        cost_estimate=cost(2 * rows * rows * width, 4 * rows * width),
    )(rank.reshape(rows, 1), x)


def deal_body(place_ref, x_ref, g_ref, live_ref, gain_ref, shift_ref, xt_ref, gt_ref, xd_ref, gd_ref, bo_ref):
    step = pl.program_id(0)
    rows = x_ref.shape[0]
    spot = lax.broadcasted_iota(jnp.int32, (BLK, rows), 1)
    pick = jnp.where(spot == place_ref[...], 1.0, 0.0).astype(bf16)
    live = live_ref[0]
    x = nn(pick, x_ref[...]).T
    xd_ref[0] = x.astype(bf16)
    centred = x - jnp.mean(x, axis=0, keepdims=True)
    inv_std = lax.rsqrt(jnp.mean(centred * centred, axis=0, keepdims=True) + epsilon)
    xt_ref[0] = (centred * inv_std * gain_ref[...] + shift_ref[...]).astype(bf16)
    g = nn(pick, g_ref[...]).T
    gd_ref[0] = g.astype(bf16)
    g = g * live
    gt_ref[0] = g.astype(bf16)

    @pl.when(step == 0)
    def _():
        bo_ref[...] = jnp.zeros_like(bo_ref)

    bo_ref[...] += g


def deal_rows(place, x, g, live, gain, shift):
    rows, width = x.shape
    blocks = rows // BLK
    whole = pl.BlockSpec((rows, width), lambda i: (0, 0))
    wide = pl.BlockSpec((width, BLK), lambda i: (0, 0))
    out = pl.BlockSpec((1, width, BLK), lambda i: (i, 0, 0))
    return pl.pallas_call(
        deal_body,
        grid=(blocks,),
        in_specs=[
            pl.BlockSpec((BLK, 1), lambda i: (i, 0)),
            whole,
            whole,
            pl.BlockSpec((1, 1, BLK), lambda i: (i, 0, 0)),
            wide,
            wide,
        ],
        out_specs=[out, out, out, out, wide],
        out_shape=[jax.ShapeDtypeStruct((blocks, width, BLK), bf16)] * 4
        + [jax.ShapeDtypeStruct((width, BLK), f32)],
        compiler_params=params(40),
        cost_estimate=cost(4 * rows * rows * width, 12 * rows * width),
    )(place.reshape(rows, 1), x, g, live, gain, shift)


def send_back(place_ref, out_s, o_ref):
    rows = out_s.shape[0]
    spot = lax.broadcasted_iota(jnp.int32, (rows, rows), 0)
    pick = jnp.where(spot == place_ref[...], 1.0, 0.0).astype(bf16)
    o_ref[...] = nn(pick, out_s[...]).astype(bf16)


def layer_body(place_ref, br_ref, xd_ref, live_ref, bias_ref, o_ref, out_s):
    for at in range(br_ref.shape[0]):
        y = xd_ref[at].astype(f32) + live_ref[at] * (br_ref[at].astype(f32) + bias_ref[...])
        out_s[at * BLK : (at + 1) * BLK, :] = y.T.astype(bf16)
    send_back(place_ref, out_s, o_ref)


def layer_rows(place, branch, xd, live, bias):
    blocks, width, _ = xd.shape
    rows = blocks * BLK
    return pl.pallas_call(
        layer_body,
        out_shape=jax.ShapeDtypeStruct((rows, width), bf16),
        scratch_shapes=[pltpu.VMEM((rows, width), bf16)],
        compiler_params=params(48),
        cost_estimate=cost(2 * rows * rows * width, 6 * rows * width),
    )(place.reshape(1, rows), branch, xd, live, bias)


def input_body(place_ref, gn_ref, xd_ref, gd_ref, gain_ref, o_ref, sums_ref, out_s):
    g_gain = jnp.zeros(gain_ref.shape, f32)
    g_shift = jnp.zeros(gain_ref.shape, f32)
    for at in range(gn_ref.shape[0]):
        x = xd_ref[at].astype(f32)
        centred = x - jnp.mean(x, axis=0, keepdims=True)
        inv_std = lax.rsqrt(jnp.mean(centred * centred, axis=0, keepdims=True) + epsilon)
        x_hat = centred * inv_std
        g = gn_ref[at].astype(f32)
        g_gain = g_gain + g * x_hat
        g_shift = g_shift + g
        hat = g * gain_ref[...]
        back = inv_std * (
            hat
            - jnp.mean(hat, axis=0, keepdims=True)
            - x_hat * jnp.mean(hat * x_hat, axis=0, keepdims=True)
        )
        out_s[at * BLK : (at + 1) * BLK, :] = (gd_ref[at].astype(f32) + back).T.astype(bf16)
    sums_ref[0] = g_gain
    sums_ref[1] = g_shift
    send_back(place_ref, out_s, o_ref)


def input_rows(place, gn, xd, gd, gain):
    blocks, width, _ = xd.shape
    rows = blocks * BLK
    return pl.pallas_call(
        input_body,
        out_shape=[
            jax.ShapeDtypeStruct((rows, width), bf16),
            jax.ShapeDtypeStruct((2, width, BLK), f32),
        ],
        scratch_shapes=[pltpu.VMEM((rows, width), bf16)],
        compiler_params=params(48),
        cost_estimate=cost(2 * rows * rows * width, 8 * rows * width),
    )(place.reshape(1, rows), gn, xd, gd, gain)


def project_body(ch, x_ref, g_ref, live_ref, wt_ref, bias_ref, u_ref, v_ref, gg_ref, gq_ref, da_ref, pre_s, gm_s):
    x = jnp.concatenate([x_ref[0], x_ref[1]], axis=1)
    g = jnp.concatenate([g_ref[0], g_ref[1]], axis=1)
    pre_s[...] = nn(wt_ref[0 : 4 * ch, :], x)
    gm_s[...] = nn(wt_ref[4 * ch : 6 * ch, :], g)
    live = live_ref[0]
    step = 32
    root = 0.7978845608028654

    def act(pre):
        square = pre * pre
        bent = jnp.tanh(root * pre * (1.0 + 0.044715 * square))
        rise = 0.5 + 0.5 * bent
        slope = rise + (0.5 * root) * pre * (1.0 - bent * bent) * (1.0 + 0.134145 * square)
        return pre * rise, slope

    def put(ref, k, at, value):
        value = value.astype(bf16)
        ref[k, 0, at, :] = value[:, :BLK]
        ref[k, 1, at, :] = value[:, BLK:]

    def chunk(i, carry):
        at = pl.ds(pl.multiple_of(i * step, step), step)
        for k in range(2):
            row = pl.ds(pl.multiple_of(k * ch + i * step, step), step)
            gate = pl.ds(pl.multiple_of((2 + k) * ch + i * step, step), step)
            bias = bias_ref[row, :]
            value, slope = act(pre_s[row, :] + jnp.concatenate([bias, bias], axis=1))
            put(u_ref if k == 0 else v_ref, k, at, live * value)
            put(da_ref, k, at, live * slope)
            bias = bias_ref[gate, :]
            value, slope = act(pre_s[gate, :] + jnp.concatenate([bias, bias], axis=1))
            gm = gm_s[row, :]
            put(gg_ref, k, at, value)
            put(v_ref if k == 0 else u_ref, k, at, gm * value)
            put(gq_ref, k, at, gm * slope)
        return carry

    lax.fori_loop(0, ch // step, chunk, 0)


def project(xt, gt, live, wt, bias):
    nb, width, _ = xt.shape
    ch = wt.shape[0] // 6
    rows = pl.BlockSpec((2, width, BLK), lambda i: (i, 0, 0))
    out = pl.BlockSpec((2, 2, ch, BLK), lambda i: (0, i, 0, 0))
    tok = nb * BLK
    return pl.pallas_call(
        partial(project_body, ch),
        grid=(nb // 2,),
        in_specs=[
            rows,
            rows,
            pl.BlockSpec((1, 1, BIG), lambda i: (i, 0, 0)),
            pl.BlockSpec((6 * ch, width), lambda i: (0, 0)),
            pl.BlockSpec((4 * ch, BLK), lambda i: (0, 0)),
        ],
        out_specs=[out] * 5,
        out_shape=[jax.ShapeDtypeStruct((2, nb, ch, BLK), bf16)] * 5,
        scratch_shapes=[pltpu.VMEM((4 * ch, BIG), f32), pltpu.VMEM((2 * ch, BIG), f32)],
        compiler_params=params(56),
        cost_estimate=cost(12 * tok * width * ch, 4 * tok * width + 20 * tok * ch, 4 * tok * ch),
    )(xt, gt, live, wt, bias)


def spectra_body(cc, ld_ref, w_ref, d_ref, wave_ref, kh_ref, k_s):
    t = lax.broadcasted_iota(jnp.int32, (BLK, BLK), 0).astype(f32)
    block = lax.broadcasted_iota(jnp.int32, (2 * LAGS, BLK), 0).astype(f32) * float(BLK)
    low = lax.broadcasted_iota(jnp.int32, (2 * LAGS, BLK), 1) < STATE
    count = 2 * LAGS

    def one(p, carry):
        ld = ld_ref[0, pl.ds(p, 1), :]
        decay = jnp.exp2(t * ld)
        scale = w_ref[0, pl.ds(p, 1), :] * jnp.exp2(block * ld)
        lhs = jnp.concatenate([jnp.where(low, scale, 0.0), jnp.where(low, 0.0, scale)], axis=0)
        lhs_high, lhs_low = halves(lhs)
        high, rest = halves(decay)
        k = nt(jnp.concatenate([lhs_high, lhs_low], axis=0), high)
        k = k[0 : 2 * count] + k[2 * count : 4 * count] + nt(lhs_high, rest)
        k_s[pl.ds(2 * p, count, stride=cc), :] = k[0:count]
        k_s[pl.ds(2 * p + 1, count, stride=cc), :] = k[count : 2 * count]
        return carry

    lax.fori_loop(0, cc // 2, one, 0, unroll=4)
    sign = jnp.where(lax.broadcasted_iota(jnp.int32, (cc, BIG), 1) % 2 == 0, 1.0, -1.0)
    before = None
    for big in range(LAGS):
        rows = jnp.concatenate(
            [k_s[pl.ds(2 * big * cc, cc), :], k_s[pl.ds((2 * big + 1) * cc, cc), :]], axis=1
        )
        high, rest = halves(rows)
        x = nn(high, wave_ref[...]) + nn(rest, wave_ref[...])
        xc, xs = x[:, :BIG], x[:, BIG:]
        if big == 0:
            kh_ref[0, 0, :, :BIG] = xc + d_ref[0][:, 0:1]
            kh_ref[0, 0, :, BIG:] = xs
        else:
            kh_ref[0, big, :, :BIG] = xc + sign * before[1]
            kh_ref[0, big, :, BIG:] = xs - sign * before[0]
        before = (xc, xs)


def spectra(ld, w, d, wave):
    ch = 2 * ld.shape[1]
    cc = chunk_of(ch, 128)
    return pl.pallas_call(
        partial(spectra_body, cc),
        grid=(2, ch // cc),
        in_specs=[pl.BlockSpec((1, cc // 2, BLK), lambda k, i: (k, i, 0))] * 2
        + [
            pl.BlockSpec((1, cc, BLK), lambda k, i: (k, i, 0)),
            pl.BlockSpec((BIG, 2 * BIG), lambda k, i: (0, 0)),
        ],
        out_specs=pl.BlockSpec((1, LAGS, cc, 2 * BIG), lambda k, i: (k, 0, i, 0)),
        out_shape=jax.ShapeDtypeStruct((2, LAGS, ch, 2 * BIG), f32),
        scratch_shapes=[pltpu.VMEM((2 * LAGS * cc, BLK), f32)],
        compiler_params=params(40),
        cost_estimate=cost(2 * ch * 40e6, 2 * ch * LAGS * 2 * BIG * 4),
    )(ld, w, d, wave)


def moments_body(cc, ld_ref, gh_ref, back_ref, s0_ref, s1_ref, g0_ref, g_s):
    sign = jnp.where(lax.broadcasted_iota(jnp.int32, (cc, BIG), 1) % 2 == 0, 1.0, -1.0)
    count = 2 * LAGS
    for big in range(LAGS):
        c = gh_ref[0, big, :, :BIG]
        s = gh_ref[0, big, :, BIG:]
        if big < LAGS - 1:
            c, s = c - sign * gh_ref[0, big + 1, :, BIG:], s + sign * gh_ref[0, big + 1, :, :BIG]
        high, rest = halves(jnp.concatenate([c, s], axis=1))
        g = nn(high, back_ref[...]) + nn(rest, back_ref[...])
        g_s[pl.ds(2 * big * cc, cc), :] = g[:, :BLK]
        g_s[pl.ds((2 * big + 1) * cc, cc), :] = g[:, BLK:]
        if big == 0:
            g0_ref[0] = g[:, :BLK]
    t = lax.broadcasted_iota(jnp.int32, (BLK, BLK), 0).astype(f32)
    lane = lax.broadcasted_iota(jnp.int32, (count, BLK), 1)
    lag = lane.astype(f32)
    block = lax.broadcasted_iota(jnp.int32, (count, BLK), 0).astype(f32) * float(BLK)
    low = lane < STATE

    def one(p, carry):
        ld = ld_ref[0, pl.ds(p, 1), :]
        decay = jnp.exp2(t * ld).astype(bf16)
        far = jnp.exp2(block * ld)
        ga = g_s[pl.ds(2 * p, count, stride=cc), :]
        gb = g_s[pl.ds(2 * p + 1, count, stride=cc), :]
        high, rest = halves(jnp.concatenate([ga, gb, ga * lag, gb * lag], axis=0))
        m = nn(jnp.concatenate([high, rest], axis=0), decay)
        m = m[0 : 4 * count] + m[4 * count : 8 * count]
        m0 = jnp.where(low, m[0:count], m[count : 2 * count])
        m1 = jnp.where(low, m[2 * count : 3 * count], m[3 * count : 4 * count]) + block * m0
        s0_ref[0, pl.ds(p, 1), :] = jnp.sum(far * m0, axis=0, keepdims=True)
        s1_ref[0, pl.ds(p, 1), :] = jnp.sum(far * m1, axis=0, keepdims=True)
        return carry

    lax.fori_loop(0, cc // 2, one, 0, unroll=4)


def moments(ld, gh, back):
    ch = gh.shape[2]
    cc = chunk_of(ch, 128)
    row = pl.BlockSpec((1, cc // 2, BLK), lambda k, i: (k, i, 0))
    return pl.pallas_call(
        partial(moments_body, cc),
        grid=(2, ch // cc),
        in_specs=[
            row,
            pl.BlockSpec((1, LAGS, cc, 2 * BIG), lambda k, i: (k, 0, i, 0)),
            pl.BlockSpec((2 * BIG, BIG), lambda k, i: (0, 0)),
        ],
        out_specs=[row, row, pl.BlockSpec((1, cc, BLK), lambda k, i: (k, i, 0))],
        out_shape=[jax.ShapeDtypeStruct((2, ch // 2, BLK), f32)] * 2
        + [jax.ShapeDtypeStruct((2, ch, BLK), f32)],
        scratch_shapes=[pltpu.VMEM((2 * LAGS * cc, BLK), f32)],
        compiler_params=params(40),
        cost_estimate=cost(2 * ch * 40e6, 2 * ch * LAGS * 2 * BIG * 4),
    )(ld, gh, back)


def ssm_body(
    nb, nseq, cc, rg, tab_ref, seq_ref, u_ref, v_ref, kh_ref, wave_ref, back_ref, gg_ref, gq_ref, da_ref,
    mix_ref, gpg_ref, gp_ref, gh_ref, bs_ref, in_s, uh_s, vh_s, ph_s, qh_s, p_s, q_s,
):
    pieces = (nb + nseq) // 2

    def load(src, dst):
        for h in range(pieces):
            first = tab_ref[0, h]
            whole = tab_ref[1, h].astype(f32)
            in_s[pl.ds(h * cc, cc), 0:BLK] = src[0, first]
            after = src[0, jnp.minimum(first + 1, nb - 1)].astype(f32) * whole
            in_s[pl.ds(h * cc, cc), BLK:BIG] = after.astype(bf16)
        for h in range(pieces):
            at = pl.ds(h * cc, cc)
            dst[at, :] = nn(in_s[at, :], wave_ref[...])

    load(u_ref, uh_s)
    load(v_ref, vh_s)
    qh_s[...] = jnp.zeros_like(qh_s)
    gh_ref[...] = jnp.zeros_like(gh_ref)
    zero = jnp.zeros((rg, BIG), f32)

    def group(r, carry):
        off = pl.multiple_of(r * rg, rg)
        for s in range(nseq):
            base = seq_ref[0, s]
            count = seq_ref[1, s]

            def outer(i, carry):
                at = pl.ds(pl.multiple_of((base + i) * cc + off, rg), rg)
                vc = vh_s[at, :BIG]
                vs = vh_s[at, BIG:]

                def inner(j, acc):
                    pc, ps = acc
                    m = pl.ds(pl.multiple_of((base + i - j) * cc + off, rg), rg)
                    rows = pl.ds(off, rg)
                    uc = uh_s[m, :BIG]
                    us = uh_s[m, BIG:]
                    kc = kh_ref[0, j, rows, :BIG]
                    ks = kh_ref[0, j, rows, BIG:]
                    pc = pc + kc * uc - ks * us
                    ps = ps + kc * us + ks * uc
                    qh_s[m, :BIG] += kc * vc + ks * vs
                    qh_s[m, BIG:] += kc * vs - ks * vc
                    gh_ref[0, j, rows, :BIG] += uc * vc + us * vs
                    gh_ref[0, j, rows, BIG:] += uc * vs - us * vc
                    return (pc, ps)

                pc, ps = lax.fori_loop(0, i + 1, inner, (zero, zero))
                ph_s[at, :BIG] = pc.astype(bf16)
                ph_s[at, BIG:] = ps.astype(bf16)
                return carry

            lax.fori_loop(0, count, outer, 0)
        return carry

    lax.fori_loop(0, cc // rg, group, 0)

    for h in range(pieces):
        at = pl.ds(h * cc, cc)
        p_s[at, :] = nn(ph_s[at, :], back_ref[...])
        q_s[at, :] = nn(qh_s[at, :].astype(bf16), back_ref[...])

    none = jnp.zeros((cc, BLK), f32)

    def finish(y_s, gx_s):
        def one(b, y, gx, carry):
            s0, s1 = carry
            mix_ref[0, b] = (y * gg_ref[0, b].astype(f32)).astype(bf16)
            gpg = (y * gq_ref[0, b].astype(f32)).astype(bf16)
            gpg_ref[0, b] = gpg
            gp = (gx * da_ref[0, b].astype(f32)).astype(bf16)
            gp_ref[0, b] = gp
            return (s0 + gpg.astype(f32), s1 + gp.astype(f32))

        def last(h, carry):
            b = tab_ref[0, h]
            at = pl.ds(pl.multiple_of(h * cc, cc), cc)
            carry = one(b, y_s[at, 0:BLK], gx_s[at, 0:BLK], carry)

            def more(kept):
                return one(b + 1, y_s[at, BLK:], gx_s[at, BLK:], kept)

            return lax.cond(tab_ref[1, h] == 1, more, lambda kept: kept, carry)

        s0, s1 = lax.fori_loop(0, seq_ref[1, nseq], last, (none, none))
        bs_ref[0, :, 0:BLK] = s0
        bs_ref[0, :, BLK:] = s1

    @pl.when(pl.program_id(0) == 0)
    def _():
        finish(p_s, q_s)

    @pl.when(pl.program_id(0) == 1)
    def _():
        finish(q_s, p_s)

    nothing = jnp.zeros((cc, BLK), bf16)

    def fill(b, carry):
        mix_ref[0, b] = nothing
        gpg_ref[0, b] = nothing
        gp_ref[0, b] = nothing
        return carry

    lax.fori_loop(seq_ref[0, nseq], nb, fill, 0)


def ssm(tab, seq, u, v, kh, wave, back, gg, gq, da):
    _, nb, ch, _ = u.shape
    nseq = seq.shape[1] - 1
    pieces = (nb + nseq) // 2
    cc = chunk_of(ch, 128 if nb <= 32 else 64)
    rg = 16
    size = pieces * cc
    big = pl.BlockSpec((1, nb, cc, BLK), lambda k, i: (k, 0, i, 0))
    spec = pl.BlockSpec((1, LAGS, cc, 2 * BIG), lambda k, i: (k, 0, i, 0))
    smem = pl.BlockSpec(memory_space=pltpu.SMEM)
    pairs = 2 * LAGS * (LAGS + 1) // 2
    return pl.pallas_call(
        partial(ssm_body, nb, nseq, cc, rg),
        grid=(2, ch // cc),
        in_specs=[
            smem,
            smem,
            big,
            big,
            spec,
            pl.BlockSpec((BIG, 2 * BIG), lambda k, i: (0, 0)),
            pl.BlockSpec((2 * BIG, BIG), lambda k, i: (0, 0)),
            big,
            big,
            big,
        ],
        out_specs=[big, big, big, spec, pl.BlockSpec((1, cc, 2 * BLK), lambda k, i: (k, i, 0))],
        out_shape=[jax.ShapeDtypeStruct(u.shape, bf16)] * 3
        + [
            jax.ShapeDtypeStruct((2, LAGS, ch, 2 * BIG), f32),
            jax.ShapeDtypeStruct((2, ch, 2 * BLK), f32),
        ],
        scratch_shapes=[
            pltpu.VMEM((size, BIG), bf16),
            pltpu.VMEM((size, 2 * BIG), f32),
            pltpu.VMEM((size, 2 * BIG), f32),
            pltpu.VMEM((size, 2 * BIG), bf16),
            pltpu.VMEM((size, 2 * BIG), f32),
            pltpu.VMEM((size, BIG), f32),
            pltpu.VMEM((size, BIG), f32),
        ],
        compiler_params=params(60),
        cost_estimate=cost(2 * ch * pairs * BIG * 300, 2 * ch * nb * BLK * 16),
    )(tab, seq, u, v, kh, wave, back, gg, gq, da)


def stack_pair(refs):
    return jnp.concatenate(
        [jnp.concatenate([ref[k, 0], ref[k, 1]], axis=1) for ref in refs for k in range(2)], axis=0
    )


def mul_body(count, w_ref, *refs):
    out = nn(w_ref[...], stack_pair(refs[:count])).astype(bf16)
    refs[count][0] = out[:, :BLK]
    refs[count][1] = out[:, BLK:]


def mul_rows(w, arrays):
    width, deep = w.shape
    _, nb, ch, _ = arrays[0].shape
    count = len(arrays)
    return pl.pallas_call(
        partial(mul_body, count),
        grid=(nb // 2,),
        in_specs=[pl.BlockSpec((width, deep), lambda i: (0, 0))]
        + [pl.BlockSpec((2, 2, ch, BLK), lambda i: (0, i, 0, 0))] * count,
        out_specs=pl.BlockSpec((2, width, BLK), lambda i: (i, 0, 0)),
        out_shape=jax.ShapeDtypeStruct((nb, width, BLK), bf16),
        compiler_params=params(40),
        cost_estimate=cost(2 * nb * BLK * width * deep, 2 * nb * BLK * (width + deep)),
    )(w, *arrays)


def outer_body(ch, many, x_ref, g_ref, gp_ref, gpg_ref, mix_ref, o_ref, acc_s):
    step = pl.program_id(0)

    def flat(ref):
        return jnp.concatenate([ref[b] for b in range(many)], axis=1)

    def part(ref, k):
        return jnp.concatenate([ref[k, b] for b in range(many)], axis=1)

    @pl.when(step == 0)
    def _():
        acc_s[...] = jnp.zeros_like(acc_s)

    x = flat(x_ref)
    g = flat(g_ref)
    for at, (left, ref, k) in enumerate(
        [(x, gp_ref, 0), (x, gp_ref, 1), (x, gpg_ref, 0), (x, gpg_ref, 1), (g, mix_ref, 0), (g, mix_ref, 1)]
    ):
        acc_s[at] += nt(left, part(ref, k))

    @pl.when(step == pl.num_programs(0) - 1)
    def _():
        for at in range(6):
            o_ref[at] = acc_s[at].astype(bf16)


def outer_sums(xt, gt, gp, gpg, mix):
    nb, width, _ = xt.shape
    ch = gp.shape[2]
    many = 8
    rows = pl.BlockSpec((many, width, BLK), lambda i: (i, 0, 0))
    chan = pl.BlockSpec((2, many, ch, BLK), lambda i: (0, i, 0, 0))
    tok = nb * BLK
    return pl.pallas_call(
        partial(outer_body, ch, many),
        grid=(nb // many,),
        in_specs=[rows, rows, chan, chan, chan],
        out_specs=pl.BlockSpec((6, width, ch), lambda i: (0, 0, 0)),
        out_shape=jax.ShapeDtypeStruct((6, width, ch), bf16),
        scratch_shapes=[pltpu.VMEM((6, width, ch), f32)],
        compiler_params=params(56),
        cost_estimate=cost(12 * tok * width * ch, tok * (4 * width + 12 * ch)),
    )(xt, gt, gp, gpg, mix)


def sequence_tables(lens, nb):
    nseq = lens.shape[0]
    blocks = (lens + BLK - 1) // BLK
    start = jnp.cumsum(blocks) - blocks
    bigs = (blocks + 1) // 2
    first_big = jnp.cumsum(bigs) - bigs
    h = jnp.arange((nb + nseq) // 2, dtype=jnp.int32)
    owner = (h[:, None] >= first_big[None, :]).astype(jnp.int32).sum(axis=1) - 1
    mine = owner[:, None] == jnp.arange(nseq, dtype=jnp.int32)[None, :]

    def at_owner(values):
        return jnp.sum(jnp.where(mine, values[None, :], 0), axis=1)

    rel = h - at_owner(first_big)
    first = jnp.minimum(at_owner(start) + 2 * rel, nb - 1)
    whole = (2 * rel + 1 < at_owner(blocks)).astype(jnp.int32)
    tab = jnp.stack([first, whole]).astype(jnp.int32)
    seq = jnp.stack(
        [jnp.append(first_big, jnp.sum(blocks)), jnp.append(bigs, jnp.sum(bigs))]
    ).astype(jnp.int32)
    return tab, seq


def live_rows(lens, rows):
    slot = (lens + BLK - 1) // BLK * BLK
    begin = jnp.cumsum(slot) - slot
    pos = jnp.arange(rows, dtype=jnp.int32)
    inside = (pos[:, None] >= begin[None, :]) & (pos[:, None] < (begin + lens)[None, :])
    return jnp.sum(inside.astype(f32), axis=1)


def rank_of(keys):
    return jnp.sum((keys[None, :] < keys[:, None]).astype(jnp.int32), axis=1)


def local(
    n_dp, n_t, wave, tokens, cotangent, source, target, lengths, ln_gain, ln_bias, w_fwd, b_fwd, w_bwd, b_bwd,
    w_gate, b_gate, w_out, b_out, log_dt, log_rate, ssm_b, ssm_c, ssm_d,
):
    rows, width = tokens.shape
    share = lax.axis_index("tensor")
    group = rows * n_t
    nb = group // BLK
    ch = w_fwd.shape[1]
    own = b_fwd.shape[0]
    both = ("dp", "tensor")
    back = (wave.T / BIG).astype(bf16)
    wave = wave.astype(bf16)

    rank = rank_of(target)
    sender = source // group
    place = rank_of(sender * rows + jnp.arange(rows, dtype=jnp.int32))
    sent_x, sent_g = permute_to(rank, [tokens, cotangent])

    def swap(x):
        return lax.all_to_all(x, "dp", split_axis=0, concat_axis=0, tiled=True)

    got_x = swap(sent_x)
    got_g = swap(sent_g)

    perm = [(f, (f % n_dp) * n_t + f // n_dp) for f in range(n_dp * n_t)]
    unperm = [(b, a) for a, b in perm]
    chan = jnp.concatenate(
        [log_rate[0], log_rate[1], ssm_b[0], ssm_b[1], ssm_c[0], ssm_c[1]]
        + [jnp.stack([log_dt[0], log_dt[1], ssm_d[0], ssm_d[1], b_fwd, b_bwd, b_gate[0], b_gate[1]], axis=1)],
        axis=1,
    )
    chan = lax.ppermute(chan, both, perm)
    norm = lax.all_gather(jnp.stack([ln_gain, ln_bias, b_out]), "tensor", axis=1, tiled=True)
    flat = jnp.concatenate([chan.reshape(-1), norm.reshape(-1)])
    flat = lax.all_gather(flat.reshape(1, -1), "dp", axis=0, tiled=True)
    chan_all = flat[:, : chan.size].reshape(n_dp * own, chan.shape[1])
    norm_all = flat[:, chan.size :].reshape(n_dp, 3, width // n_dp).transpose(1, 0, 2).reshape(3, width)

    def lanes(column):
        return jnp.broadcast_to(column[..., None], column.shape + (BLK,))

    gain = lanes(norm_all[0])
    shift = lanes(norm_all[1])
    bias_out = lanes(norm_all[2])
    small = chan_all[:, 6 * STATE :]
    bias_in = lanes(small[:, 4:8].T.reshape(-1))

    def pick(at):
        return jnp.stack([chan_all[:, at * STATE : (at + 1) * STATE], chan_all[:, (at + 1) * STATE : (at + 2) * STATE]])

    def decays(log_dt, log_rate, ssm_b):
        rate = jnp.exp(log_rate)
        ld = -jnp.exp(log_dt)[..., None] * rate
        return rate, ld, (1.0 - jnp.exp(ld)) / rate * ssm_b

    _, ld_all, drive_all = decays(small[:, 0:2].T, pick(0), pick(2))
    ld_pairs = (ld_all * log2e).reshape(2, ch // 2, 2 * STATE)
    w_pairs = (pick(4) * drive_all).reshape(2, ch // 2, 2 * STATE)
    kh = spectra(ld_pairs, w_pairs, lanes(small[:, 2:4].T), wave)

    pack = jnp.concatenate(
        [w_fwd, w_bwd, w_gate.reshape(-1, 2 * ch), w_out.transpose(2, 0, 1).reshape(-1, 2 * ch)], axis=1
    )
    w_all = lax.all_gather(pack, "dp", axis=0, tiled=True)
    w_t = w_all.T

    live = live_rows(lengths[0], group)
    live_own = lax.dynamic_slice_in_dim(live, share * rows, rows, 0).reshape(rows // BLK, 1, BLK)
    tab, seq = sequence_tables(lengths[0], nb)

    xt, gt, xd, gd, g_bias_out = deal_rows(place, got_x, got_g, live_own, gain, shift)
    xt_all = lax.all_gather(xt, "tensor", axis=0, tiled=True)
    gt_all = lax.all_gather(gt, "tensor", axis=0, tiled=True)
    u, v, gg, gq, da = project(xt_all, gt_all, live.reshape(nb // 2, 1, BIG), w_t, bias_in)
    mix, gpg, gp, gh, bsum = ssm(tab, seq, u, v, kh, wave, back, gg, gq, da)

    def to_owner(x):
        return lax.psum_scatter(x, "tensor", scatter_dimension=0, tiled=True)

    g_normed = to_owner(mul_rows(w_all[:, : 4 * ch], [gp, gpg]))
    branch = to_owner(mul_rows(w_all[:, 4 * ch :], [mix]))
    gw = outer_sums(xt_all, gt_all, gp, gpg, mix)
    gw = gw.reshape(6, n_dp, width // n_dp, ch).transpose(1, 0, 2, 3)
    gw = lax.psum_scatter(gw, "dp", scatter_dimension=0, tiled=True)[0].astype(f32)
    s0, s1, g0 = moments(ld_pairs, gh, back)

    sent_in, norm_sums = input_rows(place, g_normed, xd, gd, gain)
    in_grad = permute_from(rank, swap(sent_in))
    sent_out = layer_rows(place, branch, xd, live_own, bias_out)
    layer_out = permute_from(rank, swap(sent_out))

    s0 = s0.reshape(2, ch, STATE)
    s1 = s1.reshape(2, ch, STATE)
    gb_gate = jnp.sum(bsum[:, :, :BLK], axis=2)
    gb_in = jnp.sum(bsum[:, :, BLK:], axis=2)
    sums = jnp.concatenate(
        [s0[0], s0[1], s1[0], s1[1], jnp.concatenate([g0[:, :, 0], gb_gate, gb_in], axis=0).T], axis=1
    )
    norm_sums = jnp.sum(jnp.concatenate([norm_sums, g_bias_out[None]], axis=0), axis=2)
    norm_sums = norm_sums.reshape(3, n_dp, width // n_dp).transpose(1, 0, 2).reshape(n_dp, -1)
    flat = jnp.concatenate([sums.reshape(n_dp, -1), norm_sums], axis=1)
    flat = lax.psum_scatter(flat, "dp", scatter_dimension=0, tiled=True)[0]
    cut = own * sums.shape[1]
    norm_sums = lax.psum_scatter(
        flat[cut:].reshape(3, width // n_dp), "tensor", scatter_dimension=1, tiled=True
    )
    sums = lax.ppermute(flat[:cut].reshape(own, -1), both, unperm)
    s0 = jnp.stack([sums[:, :STATE], sums[:, STATE : 2 * STATE]])
    s1 = jnp.stack([sums[:, 2 * STATE : 3 * STATE], sums[:, 3 * STATE : 4 * STATE]])
    tail = sums[:, 4 * STATE :].T
    step = jnp.exp(log_dt)[..., None]
    rate, ld, drive = decays(log_dt, log_rate, ssm_b)
    g_c = s0 * drive
    g_drive = s0 * ssm_c
    g_b = g_drive * (1.0 - jnp.exp(ld)) / rate
    g_ld = s1 * ssm_c * drive - g_drive * ssm_b / rate * jnp.exp(ld)
    g_rate = -g_drive * drive / rate - g_ld * step
    g_dt = jnp.sum(g_ld * ld, axis=2)
    return (
        layer_out,
        in_grad,
        norm_sums[0],
        norm_sums[1],
        gw[0],
        tail[4],
        gw[1],
        tail[5],
        jnp.stack([gw[2], gw[3]], axis=1),
        tail[2:4],
        jnp.stack([gw[4].T, gw[5].T]),
        norm_sums[2],
        g_dt,
        g_rate * rate,
        g_b,
        g_c,
        tail[0:2],
    )


def solution(mesh):
    n_dp, n_t = mesh.shape["dp"], mesh.shape["tensor"]
    both = P(("dp", "tensor"))
    rows = P(("dp", "tensor"), None)
    pair = P(None, ("dp", "tensor"))
    state = P(None, ("dp", "tensor"), None)
    proj = P("dp", "tensor")
    gate = P("dp", None, "tensor")
    out = P(None, "tensor", "dp")
    wave = wave_table()

    def run(*args):
        return local(n_dp, n_t, jnp.asarray(wave), *args)

    return jax.shard_map(
        run,
        mesh=mesh,
        in_specs=(
            rows, rows, both, both, P("dp", None), both, both, proj, both, proj, both, gate, pair, out, both,
            pair, state, state, state, pair,
        ),
        out_specs=(
            rows, rows, both, both, proj, both, proj, both, gate, pair, out, both, pair, state, state, state, pair,
        ),
        check_vma=False,
    )
```

time: 3710 us -> 925 us (0.25)
  local copies, waits for them, and re-layouts: 968 us -> 74.2 us
  matrix products: 758 us -> 0 us
  other arithmetic: 680 us -> 17.7 us
  blocking collectives: 612 us -> 48.4 us
  Pallas kernels: 0 us -> 265 us
  waiting for transfers between devices: 618 us -> 469 us
    dot_general x34 -> x0, matrix products: 758 us -> none  [the longest x6 233 us: ssm_blocks(): intra = jnp.einsum('cts,bsc->btc', toeplitz, blocks, precision=highest)]
    all_gather x8 -> x1, blocking collectives: 531 us -> 10.5 us  [local(): lax.all_gather(jnp.stack([ln_gain, ln_bias, b_out]), 'tensor', axis=1, ti...]
    rev x8 -> x0, local copies, waits for them, and re-layouts: 281 us -> none  [the longest x2 102 us: mixer(): jnp.flip(bwd_input, 0)]
    dynamic_slice x261 -> x1, local copies, waits for them, and re-layouts: 275 us -> 0.01 us  [local(): lax.dynamic_slice_in_dim(live, share * rows, rows, 0)]
    pallas_call x0 -> x13, Pallas kernels: none -> 265 us  [the longest x1 84.5 us: ssm(): pl.pallas_call(partial(ssm_body, nb, nseq, cc, rg), grid=(2, ch // cc), i...]
    reduce_scatter x9 -> x3, waiting for transfers between devices: 436 us -> 185 us  [the longest x2 185 us: to_owner(): return lax.psum_scatter(x, 'tensor', scatter_dimension=0, tiled=True)]
    gather x12 -> x0, local copies, waits for them, and re-layouts: 216 us -> none  [the longest x4 176 us: ssm_blocks(): kernel[:, jnp.clip(lag_idx, 0, BLK - 1)]]
    scatter-add x2 -> x0, other arithmetic: 208 us -> none  [ssm_blocks(): kernel[:, jnp.clip(lag_idx, 0, BLK - 1)]]
  transfers between devices with their start and end apart: 20 -> 13, of which waited for: 11 -> 7; matrix products, arithmetic and copies ran while one was open for 47% -> 6% of each run, Pallas kernels for 0% -> 12%
where the time goes in v1:
time: 925 us; the launch traced here: 915 us
  waiting for transfers between devices  469 us (51%)
  Pallas kernels  265 us (29%)
  local copies, waits for them, and re-layouts  74.2 us (8%)
  blocking collectives  48.4 us (5%)
  starting transfers between devices  23.8 us (3%)
  other arithmetic  17.7 us (2%)
  between operations  16.5 us (2%)
    reduce_scatter x2, waiting for transfers between devices, to_owner(): return lax.psum_scatter(x, 'tensor', scatter_dimension=0, tiled=True)  185 us
    all_gather x1, waiting for transfers between devices, local(): xt_all = lax.all_gather(xt, 'tensor', axis=0, tiled=True)  116 us
    pallas_call x1, Pallas kernels, ssm(): pl.pallas_call(partial(ssm_body, nb, nseq, cc, rg), grid=(2, ch // cc), i...  84.5 us
    all_gather x1, waiting for transfers between devices, local(): gt_all = lax.all_gather(gt, 'tensor', axis=0, tiled=True)  83.5 us
    unnamed x10, waiting for transfers between devices  75.1 us
    pallas_call x1, Pallas kernels, project(): pl.pallas_call(partial(project_body, ch), grid=(nb // 2,), in_specs=[rows...  41.3 us
    pallas_call x1, Pallas kernels, spectra(): pl.pallas_call(partial(spectra_body, cc), grid=(2, ch // cc), in_specs=[p...  33.6 us
    unnamed x79, local copies, waits for them, and re-layouts  33.2 us
  transfers between devices with their start and end apart: 13, of which 7 were waited for; matrix products, arithmetic and copies ran while one was open for 6% of the time, Pallas kernels for 12%

profile of v1, /device:TPU:1, one launch (start us, length us, event | category | flops | bytes accessed | tf_op | source)
XLA Modules:
  0.0 915.2 jit_solution(13235608140551750817)
XLA Ops:
  13.4 4.5 collective-permute-start
  18.6 10.5 %all-gather.1 = f32[4,24,3]{1,2,0:T(4,128)S(1)} all-gather(f32[1,24,3]{1,2,0:T(4,128)S(1)} %maximum_bitcast_fusion), channel_id=1, replica_groups=mesh['dp'=8,'tensor'=4] {'tensor'}, dimensions={0}, use_global_device_ids=true | all-gather | bytes 1440 | tf_op jit(solution)/shard_map/all_gather | solution.py:685
  31.2 1.3 fusion.21
  34.6 1.8 pad_maximum_fusion
  37.0 4.8 shard_map.332
  41.8 28.2 %all_to_all.44 = bf16[8,128,768]{2,1,0:T(8,128)(2,1)S(1)} all-to-all(bf16[8,128,768]{2,1,0:T(8,128)(2,1)S(1)} %bitcast.170), channel_id=1, replica_groups=mesh['dp'=8,'tensor'=4] {'dp'}, dimensions={0} | all-to-all | bytes 3145728 | tf_op jit(solution)/shard_map/all_to_all | solution.py:672
  70.0 4.9 all-to-all-start.1
  77.8 21.9 %all-reduce.6.cloned.1.call-done = f32[152832]{0:T(1024)} async-done(((f32[152832]{0:T(1024)}), f32[152832]{0:T(1024)}) %all-reduce.6.cloned.1.call-update) | async-done | bytes 611344
  99.7 2.2 reshape.374
  106.2 7.9 shard_map.333
  116.0 1.2 copy-done.18
  121.9 1.4 add_bitcast_fusion
  126.6 33.6 %shard_map.335.kh_ref = f32[2,8,384,512]{3,2,1,0:T(8,128)S(1)} custom-call(f32[2,192,128]{2,1,0:T(8,128)S(1)} %get-tuple-element.176.ld_ref, f32[2,192,128]{2,1,0:T(8,128)S(1)} %get-tuple-element.175.w_ref, f32[2,384,128]{2,1,0:T(8,128)S(1)} %broadcast_in_dim.92.d_ref, bf16[256,512]{1,0:T(8,128)(2,1)S(1)} %copy-done.10), custom_call_target="tpu_custom_call" | custom-call | flops 30720000000 | bytes 12582912 | tf_op jit(solution)/shard_map/pallas_call | solution.py:313
  160.3 4.5 copy-done
  164.7 5.8 copy.142.wt_ref
  170.5 83.5 %all-gather.10.cloned.1.call-done.g_ref = bf16[32,768,128]{2,1,0:T(8,128)(2,1)} async-done(((bf16[8,768,128]{2,1,0:T(8,128)(2,1)}), bf16[32,768,128]{2,1,0:T(8,128)(2,1)}) %all-gather.10.cloned.1.call-update) | async-done | bytes 6291472 | tf_op jit(solution)/shard_map/all_gather | solution.py:725
  254.0 115.8 %all-gather.8.cloned.1.call-done.x_ref = bf16[32,768,128]{2,1,0:T(8,128)(2,1)} async-done(((bf16[8,768,128]{2,1,0:T(8,128)(2,1)}), bf16[32,768,128]{2,1,0:T(8,128)(2,1)}) %all-gather.8.cloned.1.call-update) | async-done | bytes 6291472 | tf_op jit(solution)/shard_map/all_gather | solution.py:724
  370.9 41.3 %shard_map.334 = (bf16[2,32,384,128]{3,2,1,0:T(8,128)(2,1)}, bf16[2,32,384,128]{3,2,1,0:T(8,128)(2,1)}, bf16[2,32,384,128]{3,2,1,0:T(8,128)(2,1)}, bf16[2,32,384...) custom-call(bf16[32,768,128]{2,1,0:T(8,128)(2,1)} %all-gather.8.cloned.1.call-done.x_ref, ...), custom_call_target="tpu_custom_call" | custom-call | flops 14495514624 | bytes 44040192 | tf_op jit(solution)/shard_map/pallas_call | solution.py:254
  412.2 84.5 %shard_map.336 = (bf16[2,32,384,128]{3,2,1,0:T(8,128)(2,1)}, bf16[2,32,384,128]{3,2,1,0:T(8,128)(2,1)}, bf16[2,32,384,128]{3,2,1,0:T(8,128)(2,1)}, f32[2,8,384,512]{3,2,1,0:T(8,128)}, f32[2,384,256]{2,1,0:T(8,128)}) custom-call(s32[2,17]{1,0:T(2,128)} %pad_add_fusion.tab_ref, s32[2,4]{1,0:T(2,128)} %pad_add_fusion.1.seq_ref, ...), custom_call_target="tpu_custom_call" | custom-call | flops 4246732800 | bytes 50331648 | tf_op jit(solution)/shard_map/pallas_call | solution.py:509
  496.8 26.5 %shard_map.344 = bf16[6,768,384]{2,1,0:T(8,128)(2,1)} custom-call(bf16[32,768,128]{2,1,0:T(8,128)(2,1)} %all-gather.8.cloned.1.call-done.x_ref, bf16[32,768,128]{2,1,0:T(8,128)(2,1)} %all-gather.10.cloned.1.call-done.g_ref, bf16[2,32,384,128]{3,2,1,0:T(8,128)(2,1)} %get-tuple-element.50.refs_0_.gp_ref, ...), custom_call_target="tpu_custom_call" | custom-call | flops 14495514624 | bytes 31457280 | tf_op jit(solution)/shard_map/pallas_call | solution.py:605
  523.3 4.3 copy.158
  527.7 1.8 slice.254.w_ref
  529.5 16.7 %shard_map.340 = bf16[32,768,128]{2,1,0:T(8,128)(2,1)S(1)} custom-call(bf16[768,1536]{1,0:T(8,128)(2,1)S(1)} %slice.254.w_ref, bf16[2,32,384,128]{3,2,1,0:T(8,128)(2,1)} %get-tuple-element.50.refs_0_.gp_ref, bf16[2,32,384,128]{3,2,1,0:T(8,128)(2,1)} %get-tuple-element.51.refs_1_.gpg_ref), custom_call_target="tpu_custom_call" | custom-call | flops 9663676416 | bytes 18874368 | tf_op jit(solution)/shard_map/pallas_call | solution.py:560
  546.2 2.6 copy-done.2
  548.8 1.3 slice.239.w_ref
  550.2 2.8 copy-done.12
  553.0 8.2 shard_map.337
  561.2 2.6 copy-done.1
  567.4 4.9 copy-done.11
  572.3 25.3 %shard_map.343 = (f32[2,192,128]{2,1,0:T(8,128)S(1)}, f32[2,192,128]{2,1,0:T(8,128)S(1)}, f32[2,384,128]{2,1,0:T(8,128)S(1)}) custom-call(f32[2,192,128]{2,1,0:T(8,128)S(1)} %get-tuple-element.176.ld_ref, f32[2,8,384,512]{3,2,1,0:T(8,128)S(1)} %copy-done.11, bf16[512,256]{1,0:T(8,128)(2,1)S(1)} %copy-done.9), custom_call_target="tpu_custom_call" | custom-call | flops 30720000000 | bytes 12582912 | tf_op jit(solution)/shard_map/pallas_call | solution.py:371
  604.2 87.8 %reduce-scatter.7.cloned.1.call-done.gn_ref = bf16[8,768,128]{2,1,0:T(8,128)(2,1)} async-done(((bf16[32,768,128]{2,1,0:T(8,128)(2,1)}), bf16[8,768,128]{2,1,0:T(8,128)(2,1)}) %reduce-scatter.7.cloned.1.call-update) | async-done | bytes 1572880 | tf_op jit(solution)/shard_map/reduce_scatter | solution.py:730
  692.0 1.4 copy-done.15
  693.4 7.3 shard_map.341
  701.2 4.3 all-to-all-start.3
  705.5 1.8 pad_maximum_fusion.1
  708.3 97.4 %reduce-scatter.5.cloned.1.call-done.br_ref = bf16[8,768,128]{2,1,0:T(8,128)(2,1)} async-done(((bf16[32,768,128]{2,1,0:T(8,128)(2,1)}), bf16[8,768,128]{2,1,0:T(8,128)(2,1)}) %reduce-scatter.5.cloned.1.call-update) | async-done | bytes 1572880 | tf_op jit(solution)/shard_map/reduce_scatter | solution.py:730
  805.9 1.4 copy-done.14
  807.3 3.3 shard_map.338
  810.6 52.6 %all-reduce.8.cloned.1.call-done = f32[8,12864]{1,0:T(8,128)} async-done(((f32[8,12864]{1,0:T(8,128)}), f32[8,12864]{1,0:T(8,128)}) %all-reduce.8.cloned.1.call-update) | async-done | bytes 411664
  863.2 1.8 dynamic-slice_reduce_fusion
  865.1 3.7 collective-permute-start.1
  868.9 1.4 dynamic-slice_reduce_fusion.1
  870.4 9.7 %all-reduce.2 = f32[3,96]{1,0:T(4,128)S(1)} all-reduce(f32[3,96]{1,0:T(4,128)S(1)} %reshape.371), channel_id=6, replica_groups=mesh['dp'=8,'tensor'=4] {'tensor'}, use_global_device_ids=true, to_apply=%region_18.19.clone | all-reduce | flops 288 | bytes 2304
  880.2 6.1 all-to-all-start.2
  889.0 1.4 subtract_multiply_fusion
  891.4 3.0 shard_map.342
  894.4 9.4 %all-to-all-done.2 = bf16[8,128,768]{2,1,0:T(8,128)(2,1)S(1)} async-done(((bf16[8,128,768]{2,1,0:T(8,128)(2,1)}), bf16[8,128,768]{2,1,0:T(8,128)(2,1)S(1)}, u32[]{:S(2)}, u32[]{:S(2)}) %all-to-all-start.2) | async-done | bytes 1572896 | tf_op jit(solution)/shard_map/all_to_all | solution.py:672
  904.9 3.0 shard_map.339
  (193 shorter events, 45.1 us)
Async XLA Ops:
  7.2 29.2 %copy-start.25 = (s32[1024]{0:T(1024)S(1)}, s32[1024]{0:T(1024)}, u32[]{:S(2)}) copy-start(s32[1024]{0:T(1024)} %param.24) | copy-start | bytes 12292
  7.2 29.8 %copy-start.13 = (bf16[1024,768]{1,0:T(8,128)(2,1)S(1)}, bf16[1024,768]{1,0:T(8,128)(2,1)}, u32[]{:S(2)}) copy-start(bf16[1024,768]{1,0:T(8,128)(2,1)} %refs_0_.1) | copy-start | bytes 4718596
  7.2 92.5 %all-reduce.6.cloned.1.call-start = ((), (), s32[]{:S(2)}) async-start(), calls=%async_computation.13 | async-start | bytes 1228800
  13.4 19.8 %collective-permute-start = (f32[48,392]{1,0:T(8,128)S(1)}, f32[48,392]{1,0:T(8,128)S(1)}, u32[]{:S(2)}, u32[]{:S(2)}) collective-permute-start(f32[48,392]{1,0:T(8,128)S(1)} %concatenate.35), channel_id=1, source_target_pairs={{0,0},{1,4},{2,8},{3,12},{4,16},{5,20},{6,24},{7,28},{8,1},{9,5},{... | collective-permute-start | bytes 225800 | tf_op jit(solution)/shard_map/ppermute | solution.py:684
  33.7 0.8 copy-start.19
  34.6 130.2 %all-gather.6.cloned.1.call-start = ((), (), s32[]{:S(2)}) async-start(), calls=%async_computation.7 | async-start | bytes 3981312 | tf_op jit(solution)/shard_map/all_gather | solution.py:716
  41.8 28.2 %copy-start.3 = (bf16[1024,768]{1,0:T(8,128)(2,1)}, bf16[1024,768]{1,0:T(8,128)(2,1)S(1)}, u32[]{:S(2)}) copy-start(bf16[1024,768]{1,0:T(8,128)(2,1)S(1)} %get-tuple-element.40) | copy-start | bytes 4718596
  41.8 33.1 %copy-start.30 = (s32[1,3]{1,0:T(1,128)S(1)}, s32[1,3]{1,0:T(1,128)}, u32[]{:S(2)}) copy-start(s32[1,3]{1,0:T(1,128)} %param.25) | copy-start | bytes 40
  41.8 33.7 %copy-start.29 = (s32[1024]{0:T(1024)S(1)}, s32[1024]{0:T(1024)}, u32[]{:S(2)}) copy-start(s32[1024]{0:T(1024)} %param.23) | copy-start | bytes 12292
  70.0 34.1 %all-to-all-start.1 = ((bf16[8,128,768]{2,1,0:T(8,128)(2,1)}), bf16[8,128,768]{2,1,0:T(8,128)(2,1)S(1)}, u32[]{:S(2)}, u32[]{:S(2)}) async-start(bf16[8,128,768]{2,1,0:T(8,128)(2,1)} %bitcast.168), calls=%async_computation.1 | async-start | bytes 3145728 | tf_op jit(solution)/shard_map/all_to_all | solution.py:672
  74.9 179.1 %all-gather.10.cloned.1.call-start = ((), (), s32[]{:S(2)}) async-start(), calls=%async_computation.9 | async-start | bytes 7864320 | tf_op jit(solution)/shard_map/all_gather | solution.py:725
  75.0 2.7 copy-start.32
  75.5 2.1 copy-start.33
  77.8 24.2 %copy-start.24 = (f32[4096]{0:T(1024)}, f32[4096]{0:T(1024)S(1)}, u32[]{:S(2)}) copy-start(f32[4096]{0:T(1024)S(1)} %convert_reduce_fusion.2) | copy-start | bytes 49156
  105.1 1.0 copy-start.6
  106.2 11.7 %copy-start.31 = (s32[1,3]{1,0:T(1,128)S(1)}, s32[1,3]{1,0:T(1,128)}, u32[]{:S(2)}) copy-start(s32[1,3]{1,0:T(1,128)} %param.25) | copy-start | bytes 40
  114.1 0.8 copy-start.7
  114.8 1.2 copy-start.16
  116.0 1.2 copy-start.18
  117.2 6.7 slice-start
  117.2 252.5 %all-gather.8.cloned.1.call-start = ((), (), s32[]{:S(2)}) async-start(), calls=%async_computation.8 | async-start | bytes 7864320 | tf_op jit(solution)/shard_map/all_gather | solution.py:724
  117.8 483.8 %reduce-scatter.9.cloned.1.call-start = ((), (), s32[]{:S(2)}) async-start(), calls=%async_computation.12 | async-start | bytes 3981312 | tf_op jit(solution)/shard_map/reduce_scatter | solution.py:736
  124.8 1.7 copy-start.10
  160.2 4.5 copy-start
  527.6 164.4 %reduce-scatter.7.cloned.1.call-start = ((), (), s32[]{:S(2)}) async-start(), calls=%async_computation.11 | async-start | bytes 7864320 | tf_op jit(solution)/shard_map/reduce_scatter | solution.py:730
  546.2 2.6 copy-start.2
  548.8 257.0 %reduce-scatter.5.cloned.1.call-start = ((), (), s32[]{:S(2)}) async-start(), calls=%async_computation.10 | async-start | bytes 7864320 | tf_op jit(solution)/shard_map/reduce_scatter | solution.py:730
  550.2 2.8 copy-start.12
  561.2 2.6 copy-start.1
  563.8 2.9 copy-start.28
  563.8 3.5 copy-start.26
  563.8 3.6 copy-start.9
  567.4 4.9 copy-start.11
  572.3 25.5 %copy-start.20 = (f32[2,384,256]{2,1,0:T(8,128)S(1)}, f32[2,384,256]{2,1,0:T(8,128)}, u32[]{:S(2)}) copy-start(f32[2,384,256]{2,1,0:T(8,128)} %get-tuple-element.58) | copy-start | bytes 2359300
  598.5 93.5 %copy-start.17 = (bf16[8,768,128]{2,1,0:T(8,128)(2,1)S(1)}, bf16[8,768,128]{2,1,0:T(8,128)(2,1)}, u32[]{:S(2)}) copy-start(bf16[8,768,128]{2,1,0:T(8,128)(2,1)} %copy-done.16) | copy-start | bytes 4718596
  603.5 97.2 %copy-start.8 = (f32[768,128]{1,0:T(8,128)S(1)}, f32[768,128]{1,0:T(8,128)}, u32[]{:S(2)}) copy-start(f32[768,128]{1,0:T(8,128)} %copy-done.7) | copy-start | bytes 1179652
  692.0 1.4 copy-start.15
  701.2 179.0 %all-to-all-start.3 = ((bf16[8,128,768]{2,1,0:T(8,128)(2,1)}), bf16[8,128,768]{2,1,0:T(8,128)(2,1)S(1)}, u32[]{:S(2)}, u32[]{:S(2)}) async-start(bf16[8,128,768]{2,1,0:T(8,128)(2,1)} %bitcast.57), calls=%async_computation.5 | async-start | bytes 3145728 | tf_op jit(solution)/shard_map/all_to_all | solution.py:672
  705.5 157.7 %all-reduce.8.cloned.1.call-start = ((), (), s32[]{:S(2)}) async-start(), calls=%async_computation.14 | async-start | bytes 827392
  805.9 1.4 copy-start.14
  807.3 81.6 %copy-start.21 = (f32[2,48,64]{2,1,0:T(8,128)S(1)}, f32[2,48,64]{2,1,0:T(8,128)}, u32[]{:S(2)}) copy-start(f32[2,48,64]{2,1,0:T(8,128)} %param.37) | copy-start | bytes 73732
  807.3 81.6 %copy-start.22 = (f32[2,48,64]{2,1,0:T(8,128)S(1)}, f32[2,48,64]{2,1,0:T(8,128)}, u32[]{:S(2)}) copy-start(f32[2,48,64]{2,1,0:T(8,128)} %param.39) | copy-start | bytes 73732
  807.3 81.7 %copy-start.23 = (f32[2,48,64]{2,1,0:T(8,128)S(1)}, f32[2,48,64]{2,1,0:T(8,128)}, u32[]{:S(2)}) copy-start(f32[2,48,64]{2,1,0:T(8,128)} %param.38) | copy-start | bytes 73732
  807.3 81.7 %copy-start.27 = (f32[2,48]{1,0:T(2,128)S(1)}, f32[2,48]{1,0:T(2,128)}, u32[]{:S(2)}) copy-start(f32[2,48]{1,0:T(2,128)} %get-tuple-element.201) | copy-start | bytes 1156
  865.1 21.7 %collective-permute-start.1 = (f32[48,262]{1,0:T(8,128)S(1)}, f32[48,262]{1,0:T(8,128)S(1)}, u32[]{:S(2)}, u32[]{:S(2)}) collective-permute-start(f32[48,262]{1,0:T(8,128)S(1)} %reshape.373), channel_id=1, source_target_pairs={{0,0},{4,1},{8,2},{12,3},{16,4},{20,5},{24,6},{28,7},{1,8},{5,9},{... | collective-permute-start | bytes 150920 | tf_op jit(solution)/shard_map/ppermute | solution.py:759
  880.2 23.7 %all-to-all-start.2 = ((bf16[8,128,768]{2,1,0:T(8,128)(2,1)}), bf16[8,128,768]{2,1,0:T(8,128)(2,1)S(1)}, u32[]{:S(2)}, u32[]{:S(2)}) async-start(bf16[8,128,768]{2,1,0:T(8,128)(2,1)} %bitcast.55), calls=%async_computation.3 | async-start | bytes 3145728 | tf_op jit(solution)/shard_map/all_to_all | solution.py:672
  890.4 1.0 copy-start.4
  903.8 1.0 copy-start.5
  (1 other events, 0.7 us)
Sparse Core Ops, SparseCore 0:
  34.7 65.0 all-reduce.5
  101.8 34.7 all-gather.5
  138.8 115.1 all-gather.9
  256.1 113.6 all-gather.7
  527.7 51.0 reduce-scatter.8
  581.1 110.8 reduce-scatter.6
  694.4 111.3 reduce-scatter.4
  809.2 53.9 all-reduce.7

commit v2 on v1

v2 whole, which is shorter than its diff:
```python
from functools import partial

import jax
import jax.numpy as jnp
import numpy as np
from jax import lax
from jax.experimental import pallas as pl
from jax.experimental.pallas import tpu as pltpu
from jax.sharding import PartitionSpec as P

BLK = 128
BIG = 256
MOST = 2048
LAGS = MOST // BIG
STATE = 64
epsilon = 1e-05
log2e = 1.4426950408889634
f32 = jnp.float32
bf16 = jnp.bfloat16
MIB = 2**20


def nn(a, b):
    return lax.dot_general(a, b, (((1,), (0,)), ((), ())), preferred_element_type=f32)


def nt(a, b):
    return lax.dot_general(a, b, (((1,), (1,)), ((), ())), preferred_element_type=f32)


def params(limit):
    return pltpu.CompilerParams(vmem_limit_bytes=limit * MIB)


def cost(flops, moved, trans=0):
    return pl.CostEstimate(flops=int(flops), bytes_accessed=int(moved), transcendentals=int(trans))


def halves(x):
    high = x.astype(bf16)
    return high, (x - high.astype(f32)).astype(bf16)


def wave_table():
    pos = np.arange(BIG)[:, None]
    freq = np.arange(BIG)[None, :]
    angle = 2 * np.pi * ((2 * freq + 1) * pos % (4 * BIG)) / (4 * BIG)
    return np.concatenate([np.cos(angle), np.sin(angle)], 1).astype(np.float32)


def chunk_of(channels, most):
    best = 16
    for size in range(16, most + 1, 16):
        if channels % size == 0:
            best = size
    return best


def permute_row_body(count, rank_ref, *refs):
    rows = rank_ref.shape[1]
    spot = lax.broadcasted_iota(jnp.int32, (rows, rows), 0)
    pick = jnp.where(spot == rank_ref[...], 1.0, 0.0).astype(bf16)
    for at in range(count):
        refs[count + at][...] = nn(pick, refs[at][...]).astype(bf16)


def permute_to(rank, arrays):
    rows, width = arrays[0].shape
    count = len(arrays)
    return pl.pallas_call(
        partial(permute_row_body, count),
        out_shape=[jax.ShapeDtypeStruct((rows, width), bf16)] * count,
        compiler_params=params(48),
        cost_estimate=cost(2 * count * rows * rows * width, 4 * count * rows * width),
    )(rank.reshape(1, rows), *arrays)


def permute_col_body(rank_ref, x_ref, o_ref):
    rows = x_ref.shape[0]
    spot = lax.broadcasted_iota(jnp.int32, (rows, rows), 1)
    pick = jnp.where(spot == rank_ref[...], 1.0, 0.0).astype(bf16)
    o_ref[...] = nn(pick, x_ref[...]).astype(bf16)


def permute_from(rank, x):
    rows, width = x.shape
    return pl.pallas_call(
        permute_col_body,
        out_shape=jax.ShapeDtypeStruct((rows, width), bf16),
        compiler_params=params(48),
        cost_estimate=cost(2 * rows * rows * width, 4 * rows * width),
    )(rank.reshape(rows, 1), x)


def pick_rows(place_ref, x_ref):
    spot = lax.broadcasted_iota(jnp.int32, (BLK, x_ref.shape[0]), 1)
    pick = jnp.where(spot == place_ref[...], 1.0, 0.0).astype(bf16)
    return nn(pick, x_ref[...]).T


def deal_x_body(place_ref, x_ref, gain_ref, shift_ref, xt_ref, xd_ref):
    x = pick_rows(place_ref, x_ref)
    xd_ref[0] = x.astype(bf16)
    centred = x - jnp.mean(x, axis=0, keepdims=True)
    inv_std = lax.rsqrt(jnp.mean(centred * centred, axis=0, keepdims=True) + epsilon)
    xt_ref[0] = (centred * inv_std * gain_ref[...] + shift_ref[...]).astype(bf16)


def deal_g_body(place_ref, g_ref, live_ref, gt_ref, gd_ref, bo_ref):
    g = pick_rows(place_ref, g_ref)
    gd_ref[0] = g.astype(bf16)
    g = g * live_ref[0]
    gt_ref[0] = g.astype(bf16)

    @pl.when(pl.program_id(0) == 0)
    def _():
        bo_ref[...] = jnp.zeros_like(bo_ref)

    bo_ref[...] += g


def deal_specs(rows, width):
    place = pl.BlockSpec((BLK, 1), lambda i: (i, 0))
    whole = pl.BlockSpec((rows, width), lambda i: (0, 0))
    wide = pl.BlockSpec((width, BLK), lambda i: (0, 0))
    out = pl.BlockSpec((1, width, BLK), lambda i: (i, 0, 0))
    return place, whole, wide, out


def deal_x(place, x, gain, shift):
    rows, width = x.shape
    blocks = rows // BLK
    spot, whole, wide, out = deal_specs(rows, width)
    return pl.pallas_call(
        deal_x_body,
        grid=(blocks,),
        in_specs=[spot, whole, wide, wide],
        out_specs=[out, out],
        out_shape=[jax.ShapeDtypeStruct((blocks, width, BLK), bf16)] * 2,
        compiler_params=params(40),
        cost_estimate=cost(2 * rows * rows * width, 6 * rows * width),
    )(place.reshape(rows, 1), x, gain, shift)


def deal_g(place, g, live):
    rows, width = g.shape
    blocks = rows // BLK
    spot, whole, wide, out = deal_specs(rows, width)
    return pl.pallas_call(
        deal_g_body,
        grid=(blocks,),
        in_specs=[spot, whole, pl.BlockSpec((1, 1, BLK), lambda i: (i, 0, 0))],
        out_specs=[out, out, wide],
        out_shape=[jax.ShapeDtypeStruct((blocks, width, BLK), bf16)] * 2
        + [jax.ShapeDtypeStruct((width, BLK), f32)],
        compiler_params=params(40),
        cost_estimate=cost(2 * rows * rows * width, 6 * rows * width),
    )(place.reshape(rows, 1), g, live)


def send_back(place_ref, out_s, o_ref):
    rows = out_s.shape[0]
    spot = lax.broadcasted_iota(jnp.int32, (rows, rows), 0)
    pick = jnp.where(spot == place_ref[...], 1.0, 0.0).astype(bf16)
    o_ref[...] = nn(pick, out_s[...]).astype(bf16)


def total(refs, at):
    value = refs[0][at].astype(f32)
    for ref in refs[1:]:
        value = value + ref[at].astype(f32)
    return value


def layer_body(place_ref, xd_ref, live_ref, bias_ref, *refs):
    o_ref, out_s = refs[-2:]
    for at in range(xd_ref.shape[0]):
        y = xd_ref[at].astype(f32) + live_ref[at] * (total(refs[:-2], at) + bias_ref[...])
        out_s[at * BLK : (at + 1) * BLK, :] = y.T.astype(bf16)
    send_back(place_ref, out_s, o_ref)


def layer_rows(place, parts, xd, live, bias):
    blocks, width, _ = xd.shape
    rows = blocks * BLK
    return pl.pallas_call(
        layer_body,
        out_shape=jax.ShapeDtypeStruct((rows, width), bf16),
        scratch_shapes=[pltpu.VMEM((rows, width), bf16)],
        compiler_params=params(48),
        cost_estimate=cost(2 * rows * rows * width, 6 * rows * width),
    )(place.reshape(1, rows), xd, live, bias, *parts)


def input_body(place_ref, xd_ref, gd_ref, gain_ref, *refs):
    o_ref, sums_ref, out_s = refs[-3:]
    g_gain = jnp.zeros(gain_ref.shape, f32)
    g_shift = jnp.zeros(gain_ref.shape, f32)
    for at in range(xd_ref.shape[0]):
        x = xd_ref[at].astype(f32)
        centred = x - jnp.mean(x, axis=0, keepdims=True)
        inv_std = lax.rsqrt(jnp.mean(centred * centred, axis=0, keepdims=True) + epsilon)
        x_hat = centred * inv_std
        g = total(refs[:-3], at)
        g_gain = g_gain + g * x_hat
        g_shift = g_shift + g
        hat = g * gain_ref[...]
        back = inv_std * (
            hat
            - jnp.mean(hat, axis=0, keepdims=True)
            - x_hat * jnp.mean(hat * x_hat, axis=0, keepdims=True)
        )
        out_s[at * BLK : (at + 1) * BLK, :] = (gd_ref[at].astype(f32) + back).T.astype(bf16)
    sums_ref[0] = g_gain
    sums_ref[1] = g_shift
    send_back(place_ref, out_s, o_ref)


def input_rows(place, parts, xd, gd, gain):
    blocks, width, _ = xd.shape
    rows = blocks * BLK
    return pl.pallas_call(
        input_body,
        out_shape=[
            jax.ShapeDtypeStruct((rows, width), bf16),
            jax.ShapeDtypeStruct((2, width, BLK), f32),
        ],
        scratch_shapes=[pltpu.VMEM((rows, width), bf16)],
        compiler_params=params(48),
        cost_estimate=cost(2 * rows * rows * width, 8 * rows * width),
    )(place.reshape(1, rows), xd, gd, gain, *parts)


def project_body(ch, many, start_ref, x_ref, live_ref, wt_ref, bias_ref, *refs):
    a_ref, da_ref, gg_ref, dg_ref, pre_s = refs[-5:]
    x = jnp.concatenate([x_ref[0], x_ref[1]], axis=1)
    pre_s[...] = nn(wt_ref[...], x)
    live = live_ref[0]
    step = 32
    root = 0.7978845608028654

    def act(pre):
        square = pre * pre
        bent = jnp.tanh(root * pre * (1.0 + 0.044715 * square))
        rise = 0.5 + 0.5 * bent
        slope = rise + (0.5 * root) * pre * (1.0 - bent * bent) * (1.0 + 0.134145 * square)
        return pre * rise, slope

    def put(ref, k, at, value):
        value = value.astype(bf16)
        ref[k, 0, at, :] = value[:, :BLK]
        ref[k, 1, at, :] = value[:, BLK:]

    def chunk(i, carry):
        at = pl.ds(pl.multiple_of(i * step, step), step)
        for k in range(2):
            row = pl.ds(pl.multiple_of(k * ch + i * step, step), step)
            gate = pl.ds(pl.multiple_of((2 + k) * ch + i * step, step), step)
            bias = bias_ref[row, :]
            value, slope = act(pre_s[row, :] + jnp.concatenate([bias, bias], axis=1))
            put(a_ref, k, at, live * value)
            put(da_ref, k, at, live * slope)
            bias = bias_ref[gate, :]
            value, slope = act(pre_s[gate, :] + jnp.concatenate([bias, bias], axis=1))
            put(gg_ref, k, at, value)
            put(dg_ref, k, at, slope)
        return carry

    lax.fori_loop(0, ch // step, chunk, 0)


def chained(body, grid, in_specs, out_specs, shapes, scratch, limit, estimate, start, operands, kept):
    kept = [] if kept is None else list(kept)
    specs = list(in_specs) + [pl.BlockSpec(memory_space=pl.ANY)] * len(kept)
    first = 1 + len(operands)
    return pl.pallas_call(
        body,
        grid_spec=pltpu.PrefetchScalarGridSpec(
            num_scalar_prefetch=1, grid=grid, in_specs=specs, out_specs=out_specs, scratch_shapes=scratch
        ),
        out_shape=shapes,
        input_output_aliases={first + at: at for at in range(len(kept))},
        compiler_params=params(limit),
        cost_estimate=estimate,
    )(start, *operands, *kept)


def project(xt, start, nb, live, wt, bias, kept):
    many, width, _ = xt.shape
    ch = wt.shape[0] // 4
    out = pl.BlockSpec((2, 2, ch, BLK), lambda i, at: (0, at[0] + i, 0, 0))
    tok = many * BLK
    return chained(
        partial(project_body, ch, many),
        (many // 2,),
        [
            pl.BlockSpec((2, width, BLK), lambda i, at: (i, 0, 0)),
            pl.BlockSpec((1, 1, BIG), lambda i, at: (at[0] + i, 0, 0)),
            pl.BlockSpec((4 * ch, width), lambda i, at: (0, 0)),
            pl.BlockSpec((4 * ch, BLK), lambda i, at: (0, 0)),
        ],
        [out] * 4,
        [jax.ShapeDtypeStruct((2, nb, ch, BLK), bf16)] * 4,
        [pltpu.VMEM((4 * ch, BIG), f32)],
        48,
        cost(8 * tok * width * ch, 2 * tok * width + 16 * tok * ch, 4 * tok * ch),
        start // 2,
        [xt, live, wt, bias],
        kept,
    )


def gate_grad_body(ch, start_ref, g_ref, wt_ref, *refs):
    o_ref = refs[-1]
    gm = nn(wt_ref[...], jnp.concatenate([g_ref[0], g_ref[1]], axis=1)).astype(bf16)
    for k in range(2):
        for h in range(2):
            o_ref[k, h] = gm[k * ch : (k + 1) * ch, h * BLK : (h + 1) * BLK]


def gate_grad(gt, start, nb, wt, kept):
    many, width, _ = gt.shape
    ch = wt.shape[0] // 2
    tok = many * BLK
    return chained(
        partial(gate_grad_body, ch),
        (many // 2,),
        [
            pl.BlockSpec((2, width, BLK), lambda i, at: (i, 0, 0)),
            pl.BlockSpec((2 * ch, width), lambda i, at: (0, 0)),
        ],
        [pl.BlockSpec((2, 2, ch, BLK), lambda i, at: (0, at[0] + i, 0, 0))],
        [jax.ShapeDtypeStruct((2, nb, ch, BLK), bf16)],
        [],
        40,
        cost(4 * tok * width * ch, 2 * tok * width + 4 * tok * ch),
        start // 2,
        [gt, wt],
        kept,
    )


def spectra_body(cc, ld_ref, w_ref, d_ref, wave_ref, kh_ref, k_s):
    t = lax.broadcasted_iota(jnp.int32, (BLK, BLK), 0).astype(f32)
    block = lax.broadcasted_iota(jnp.int32, (2 * LAGS, BLK), 0).astype(f32) * float(BLK)
    low = lax.broadcasted_iota(jnp.int32, (2 * LAGS, BLK), 1) < STATE
    count = 2 * LAGS

    def one(p, carry):
        ld = ld_ref[0, pl.ds(p, 1), :]
        decay = jnp.exp2(t * ld)
        scale = w_ref[0, pl.ds(p, 1), :] * jnp.exp2(block * ld)
        lhs = jnp.concatenate([jnp.where(low, scale, 0.0), jnp.where(low, 0.0, scale)], axis=0)
        lhs_high, lhs_low = halves(lhs)
        high, rest = halves(decay)
        k = nt(jnp.concatenate([lhs_high, lhs_low], axis=0), high)
        k = k[0 : 2 * count] + k[2 * count : 4 * count] + nt(lhs_high, rest)
        k_s[pl.ds(2 * p, count, stride=cc), :] = k[0:count]
        k_s[pl.ds(2 * p + 1, count, stride=cc), :] = k[count : 2 * count]
        return carry

    lax.fori_loop(0, cc // 2, one, 0, unroll=4)
    sign = jnp.where(lax.broadcasted_iota(jnp.int32, (cc, BIG), 1) % 2 == 0, 1.0, -1.0)
    before = None
    for big in range(LAGS):
        rows = jnp.concatenate(
            [k_s[pl.ds(2 * big * cc, cc), :], k_s[pl.ds((2 * big + 1) * cc, cc), :]], axis=1
        )
        high, rest = halves(rows)
        x = nn(high, wave_ref[...]) + nn(rest, wave_ref[...])
        xc, xs = x[:, :BIG], x[:, BIG:]
        if big == 0:
            kh_ref[0, 0, :, :BIG] = xc + d_ref[0][:, 0:1]
            kh_ref[0, 0, :, BIG:] = xs
        else:
            kh_ref[0, big, :, :BIG] = xc + sign * before[1]
            kh_ref[0, big, :, BIG:] = xs - sign * before[0]
        before = (xc, xs)


def spectra(ld, w, d, wave):
    ch = 2 * ld.shape[1]
    cc = chunk_of(ch, 128)
    return pl.pallas_call(
        partial(spectra_body, cc),
        grid=(2, ch // cc),
        in_specs=[pl.BlockSpec((1, cc // 2, BLK), lambda k, i: (k, i, 0))] * 2
        + [
            pl.BlockSpec((1, cc, BLK), lambda k, i: (k, i, 0)),
            pl.BlockSpec((BIG, 2 * BIG), lambda k, i: (0, 0)),
        ],
        out_specs=pl.BlockSpec((1, LAGS, cc, 2 * BIG), lambda k, i: (k, 0, i, 0)),
        out_shape=jax.ShapeDtypeStruct((2, LAGS, ch, 2 * BIG), f32),
        scratch_shapes=[pltpu.VMEM((2 * LAGS * cc, BLK), f32)],
        compiler_params=params(40),
        cost_estimate=cost(2 * ch * 40e6, 2 * ch * LAGS * 2 * BIG * 4),
    )(ld, w, d, wave)


def moments_body(cc, ld_ref, gh_ref, back_ref, s0_ref, s1_ref, g0_ref, g_s):
    sign = jnp.where(lax.broadcasted_iota(jnp.int32, (cc, BIG), 1) % 2 == 0, 1.0, -1.0)
    count = 2 * LAGS
    for big in range(LAGS):
        c = gh_ref[0, big, :, :BIG]
        s = gh_ref[0, big, :, BIG:]
        if big < LAGS - 1:
            c, s = c - sign * gh_ref[0, big + 1, :, BIG:], s + sign * gh_ref[0, big + 1, :, :BIG]
        high, rest = halves(jnp.concatenate([c, s], axis=1))
        g = nn(high, back_ref[...]) + nn(rest, back_ref[...])
        g_s[pl.ds(2 * big * cc, cc), :] = g[:, :BLK]
        g_s[pl.ds((2 * big + 1) * cc, cc), :] = g[:, BLK:]
        if big == 0:
            g0_ref[0] = g[:, :BLK]
    t = lax.broadcasted_iota(jnp.int32, (BLK, BLK), 0).astype(f32)
    lane = lax.broadcasted_iota(jnp.int32, (count, BLK), 1)
    lag = lane.astype(f32)
    block = lax.broadcasted_iota(jnp.int32, (count, BLK), 0).astype(f32) * float(BLK)
    low = lane < STATE

    def one(p, carry):
        ld = ld_ref[0, pl.ds(p, 1), :]
        decay = jnp.exp2(t * ld).astype(bf16)
        far = jnp.exp2(block * ld)
        ga = g_s[pl.ds(2 * p, count, stride=cc), :]
        gb = g_s[pl.ds(2 * p + 1, count, stride=cc), :]
        high, rest = halves(jnp.concatenate([ga, gb, ga * lag, gb * lag], axis=0))
        m = nn(jnp.concatenate([high, rest], axis=0), decay)
        m = m[0 : 4 * count] + m[4 * count : 8 * count]
        m0 = jnp.where(low, m[0:count], m[count : 2 * count])
        m1 = jnp.where(low, m[2 * count : 3 * count], m[3 * count : 4 * count]) + block * m0
        s0_ref[0, pl.ds(p, 1), :] = jnp.sum(far * m0, axis=0, keepdims=True)
        s1_ref[0, pl.ds(p, 1), :] = jnp.sum(far * m1, axis=0, keepdims=True)
        return carry

    lax.fori_loop(0, cc // 2, one, 0, unroll=4)


def moments(ld, gh, back):
    ch = gh.shape[2]
    cc = chunk_of(ch, 128)
    row = pl.BlockSpec((1, cc // 2, BLK), lambda k, i: (k, i, 0))
    return pl.pallas_call(
        partial(moments_body, cc),
        grid=(2, ch // cc),
        in_specs=[
            row,
            pl.BlockSpec((1, LAGS, cc, 2 * BIG), lambda k, i: (k, 0, i, 0)),
            pl.BlockSpec((2 * BIG, BIG), lambda k, i: (0, 0)),
        ],
        out_specs=[row, row, pl.BlockSpec((1, cc, BLK), lambda k, i: (k, i, 0))],
        out_shape=[jax.ShapeDtypeStruct((2, ch // 2, BLK), f32)] * 2
        + [jax.ShapeDtypeStruct((2, ch, BLK), f32)],
        scratch_shapes=[pltpu.VMEM((2 * LAGS * cc, BLK), f32)],
        compiler_params=params(40),
        cost_estimate=cost(2 * ch * 40e6, 2 * ch * LAGS * 2 * BIG * 4),
    )(ld, gh, back)


def load_pieces(nb, pieces, cc, tab_ref, block, in_s, wave_ref, dst):
    for h in range(pieces):
        first = tab_ref[0, h]
        whole = tab_ref[1, h].astype(f32)
        in_s[pl.ds(h * cc, cc), 0:BLK] = block(first).astype(bf16)
        in_s[pl.ds(h * cc, cc), BLK:BIG] = (block(jnp.minimum(first + 1, nb - 1)) * whole).astype(bf16)
    for h in range(pieces):
        at = pl.ds(h * cc, cc)
        dst[at, :] = nn(in_s[at, :], wave_ref[...])


def over_pieces(nseq, cc, rg, seq_ref, piece):
    def group(r, carry):
        off = pl.multiple_of(r * rg, rg)
        for s in range(nseq):
            base = seq_ref[0, s]
            count = seq_ref[1, s]

            def outer(i, carry):
                piece(i, count, base, off)
                return carry

            lax.fori_loop(0, count, outer, 0)
        return carry

    lax.fori_loop(0, cc // rg, group, 0)


def scan_body(
    nb, nseq, cc, rg, tab_ref, seq_ref, a_ref, kh_ref, wave_ref, back_ref, gg_ref, y_ref, mix_ref, in_s, ah_s, yh_s, y_s
):
    pieces = (nb + nseq) // 2
    load_pieces(nb, pieces, cc, tab_ref, lambda b: a_ref[0, b].astype(f32), in_s, wave_ref, ah_s)
    zero = jnp.zeros((rg, BIG), f32)

    def products(flip):
        def piece(i, count, base, off):
            def inner(j, acc):
                yc, ys = acc
                other = (base + i + j) if flip else (base + i - j)
                m = pl.ds(pl.multiple_of(other * cc + off, rg), rg)
                rows = pl.ds(off, rg)
                ac = ah_s[m, :BIG]
                as_ = ah_s[m, BIG:]
                kc = kh_ref[0, j, rows, :BIG]
                ks = kh_ref[0, j, rows, BIG:]
                if flip:
                    return (yc + kc * ac + ks * as_, ys + kc * as_ - ks * ac)
                return (yc + kc * ac - ks * as_, ys + kc * as_ + ks * ac)

            yc, ys = lax.fori_loop(0, (count - i) if flip else (i + 1), inner, (zero, zero))
            at = pl.ds(pl.multiple_of((base + i) * cc + off, rg), rg)
            yh_s[at, :BIG] = yc.astype(bf16)
            yh_s[at, BIG:] = ys.astype(bf16)

        over_pieces(nseq, cc, rg, seq_ref, piece)

    @pl.when(pl.program_id(0) == 0)
    def _():
        products(False)

    @pl.when(pl.program_id(0) == 1)
    def _():
        products(True)

    for h in range(pieces):
        at = pl.ds(h * cc, cc)
        y_s[at, :] = nn(yh_s[at, :], back_ref[...])

    def one(b, y):
        y_ref[0, b] = y.astype(bf16)
        mix_ref[0, b] = (y * gg_ref[0, b].astype(f32)).astype(bf16)

    def last(h, carry):
        b = tab_ref[0, h]
        at = pl.ds(pl.multiple_of(h * cc, cc), cc)
        one(b, y_s[at, 0:BLK])

        @pl.when(tab_ref[1, h] == 1)
        def _():
            one(b + 1, y_s[at, BLK:])

        return carry

    lax.fori_loop(0, seq_ref[1, nseq], last, 0)
    nothing = jnp.zeros((cc, BLK), bf16)

    def fill(b, carry):
        y_ref[0, b] = nothing
        mix_ref[0, b] = nothing
        return carry

    lax.fori_loop(seq_ref[0, nseq], nb, fill, 0)


def back_body(
    nb, nseq, cc, rg, tab_ref, seq_ref, a_ref, gm_ref, kh_ref, wave_ref, back_ref, gg_ref, y_ref, dg_ref, da_ref,
    gpg_ref, gp_ref, gh_ref, bs_ref, in_s, ah_s, gh_s, xh_s, x_s,
):
    pieces = (nb + nseq) // 2
    load_pieces(nb, pieces, cc, tab_ref, lambda b: a_ref[0, b].astype(f32), in_s, wave_ref, ah_s)
    load_pieces(
        nb, pieces, cc, tab_ref, lambda b: gm_ref[0, b].astype(f32) * gg_ref[0, b].astype(f32), in_s, wave_ref, gh_s
    )
    gh_ref[...] = jnp.zeros_like(gh_ref)
    zero = jnp.zeros((rg, BIG), f32)

    def products(flip):
        def piece(i, count, base, off):
            at = pl.ds(pl.multiple_of((base + i) * cc + off, rg), rg)
            ac = ah_s[at, :BIG]
            as_ = ah_s[at, BIG:]

            def inner(j, acc):
                xc, xs = acc
                other = (base + i - j) if flip else (base + i + j)
                m = pl.ds(pl.multiple_of(other * cc + off, rg), rg)
                rows = pl.ds(off, rg)
                gc = gh_s[m, :BIG]
                gs = gh_s[m, BIG:]
                kc = kh_ref[0, j, rows, :BIG]
                ks = kh_ref[0, j, rows, BIG:]
                gh_ref[0, j, rows, :BIG] += ac * gc + as_ * gs
                if flip:
                    gh_ref[0, j, rows, BIG:] += gc * as_ - gs * ac
                    return (xc + kc * gc - ks * gs, xs + kc * gs + ks * gc)
                gh_ref[0, j, rows, BIG:] += ac * gs - as_ * gc
                return (xc + kc * gc + ks * gs, xs + kc * gs - ks * gc)

            xc, xs = lax.fori_loop(0, (i + 1) if flip else (count - i), inner, (zero, zero))
            xh_s[at, :BIG] = xc.astype(bf16)
            xh_s[at, BIG:] = xs.astype(bf16)

        over_pieces(nseq, cc, rg, seq_ref, piece)

    @pl.when(pl.program_id(0) == 0)
    def _():
        products(False)

    @pl.when(pl.program_id(0) == 1)
    def _():
        products(True)

    for h in range(pieces):
        at = pl.ds(h * cc, cc)
        x_s[at, :] = nn(xh_s[at, :], back_ref[...])

    none = jnp.zeros((cc, BLK), f32)

    def one(b, gx, carry):
        s0, s1 = carry
        gpg = (y_ref[0, b].astype(f32) * gm_ref[0, b].astype(f32) * dg_ref[0, b].astype(f32)).astype(bf16)
        gpg_ref[0, b] = gpg
        gp = (gx * da_ref[0, b].astype(f32)).astype(bf16)
        gp_ref[0, b] = gp
        return (s0 + gpg.astype(f32), s1 + gp.astype(f32))

    def last(h, carry):
        b = tab_ref[0, h]
        at = pl.ds(pl.multiple_of(h * cc, cc), cc)
        carry = one(b, x_s[at, 0:BLK], carry)

        def more(kept):
            return one(b + 1, x_s[at, BLK:], kept)

        return lax.cond(tab_ref[1, h] == 1, more, lambda kept: kept, carry)

    s0, s1 = lax.fori_loop(0, seq_ref[1, nseq], last, (none, none))
    bs_ref[0, :, 0:BLK] = s0
    bs_ref[0, :, BLK:] = s1
    nothing = jnp.zeros((cc, BLK), bf16)

    def fill(b, carry):
        gpg_ref[0, b] = nothing
        gp_ref[0, b] = nothing
        return carry

    lax.fori_loop(seq_ref[0, nseq], nb, fill, 0)


def ssm_specs(shape, seq):
    _, nb, ch, _ = shape
    nseq = seq.shape[1] - 1
    pieces = (nb + nseq) // 2
    cc = chunk_of(ch, 128 if nb <= 32 else 64)
    big = pl.BlockSpec((1, nb, cc, BLK), lambda k, i: (k, 0, i, 0))
    spec = pl.BlockSpec((1, LAGS, cc, 2 * BIG), lambda k, i: (k, 0, i, 0))
    smem = pl.BlockSpec(memory_space=pltpu.SMEM)
    head = [smem, smem]
    tables = [pl.BlockSpec((BIG, 2 * BIG), lambda k, i: (0, 0)), pl.BlockSpec((2 * BIG, BIG), lambda k, i: (0, 0))]
    return nb, nseq, ch, cc, pieces * cc, big, spec, head, tables


def ssm_scan(tab, seq, a, kh, wave, back, gg):
    nb, nseq, ch, cc, size, big, spec, head, tables = ssm_specs(a.shape, seq)
    return pl.pallas_call(
        partial(scan_body, nb, nseq, cc, 32),
        grid=(2, ch // cc),
        in_specs=head + [big, spec] + tables + [big],
        out_specs=[big, big],
        out_shape=[jax.ShapeDtypeStruct(a.shape, bf16)] * 2,
        scratch_shapes=[
            pltpu.VMEM((size, BIG), bf16),
            pltpu.VMEM((size, 2 * BIG), f32),
            pltpu.VMEM((size, 2 * BIG), bf16),
            pltpu.VMEM((size, BIG), f32),
        ],
        compiler_params=params(56),
        cost_estimate=cost(2 * ch * 50e6, 2 * ch * nb * BLK * 8),
    )(tab, seq, a, kh, wave, back, gg)


def ssm_back(tab, seq, a, gm, kh, wave, back, gg, y, dg, da):
    nb, nseq, ch, cc, size, big, spec, head, tables = ssm_specs(a.shape, seq)
    return pl.pallas_call(
        partial(back_body, nb, nseq, cc, 16),
        grid=(2, ch // cc),
        in_specs=head + [big, big, spec] + tables + [big] * 4,
        out_specs=[big, big, spec, pl.BlockSpec((1, cc, 2 * BLK), lambda k, i: (k, i, 0))],
        out_shape=[jax.ShapeDtypeStruct(a.shape, bf16)] * 2
        + [
            jax.ShapeDtypeStruct((2, LAGS, ch, 2 * BIG), f32),
            jax.ShapeDtypeStruct((2, ch, 2 * BLK), f32),
        ],
        scratch_shapes=[
            pltpu.VMEM((size, BIG), bf16),
            pltpu.VMEM((size, 2 * BIG), f32),
            pltpu.VMEM((size, 2 * BIG), f32),
            pltpu.VMEM((size, 2 * BIG), bf16),
            pltpu.VMEM((size, BIG), f32),
        ],
        compiler_params=params(60),
        cost_estimate=cost(2 * ch * 80e6, 2 * ch * nb * BLK * 16),
    )(tab, seq, a, gm, kh, wave, back, gg, y, dg, da)


def stack_pair(refs):
    return jnp.concatenate(
        [jnp.concatenate([ref[k, 0], ref[k, 1]], axis=1) for ref in refs for k in range(2)], axis=0
    )


def mul_body(count, more, start_ref, w_ref, *refs):
    out = nn(w_ref[...], stack_pair(refs[:count]))
    o_ref = refs[-1]
    for h in range(2):
        part = out[:, h * BLK : (h + 1) * BLK]
        if more:
            part = part + refs[count][h].astype(f32)
        o_ref[h] = part.astype(o_ref.dtype)


def mul_rows(w, arrays, start, many, dtype=bf16, extra=None):
    width, deep = w.shape
    ch = arrays[0].shape[2]
    count = len(arrays)
    out = pl.BlockSpec((2, width, BLK), lambda i, at: (i, 0, 0))
    return pl.pallas_call(
        partial(mul_body, count, extra is not None),
        grid_spec=pltpu.PrefetchScalarGridSpec(
            num_scalar_prefetch=1,
            grid=(many // 2,),
            in_specs=[pl.BlockSpec((width, deep), lambda i, at: (0, 0))]
            + [pl.BlockSpec((2, 2, ch, BLK), lambda i, at: (0, at[0] + i, 0, 0))] * count
            + ([] if extra is None else [out]),
            out_specs=out,
        ),
        out_shape=jax.ShapeDtypeStruct((many, width, BLK), dtype),
        compiler_params=params(40),
        cost_estimate=cost(2 * many * BLK * width * deep, 2 * many * BLK * (2 * width + deep)),
    )(start // 2, w, *arrays, *([] if extra is None else [extra]))


def outer_body(ch, many, cuts, at_ref, x_ref, g_ref, gp_ref, gpg_ref, mix_ref, *refs):
    step = pl.program_id(0)
    acc_s = refs[-1]

    def flat(ref):
        return jnp.concatenate([ref[b] for b in range(many)], axis=1)

    def part(ref, k):
        return jnp.concatenate([ref[k, b] for b in range(many)], axis=1)

    @pl.when(step == 0)
    def _():
        acc_s[...] = jnp.zeros_like(acc_s)

    x = flat(x_ref)
    g = flat(g_ref)
    for at, (left, ref, k) in enumerate(
        [(x, gp_ref, 0), (x, gp_ref, 1), (x, gpg_ref, 0), (x, gpg_ref, 1), (g, mix_ref, 0), (g, mix_ref, 1)]
    ):
        acc_s[at] += nt(left, part(ref, k))

    @pl.when(step == pl.num_programs(0) - 1)
    def _():
        deep = acc_s.shape[1] // cuts
        for cut in range(cuts):
            start = pl.multiple_of(at_ref[pl.num_programs(0) + cut] * deep, 8)
            for at in range(6):
                refs[cut][at] = acc_s[at, pl.ds(start, deep), :].astype(bf16)


def outer_sums(order, cuts, xt, gt, gp, gpg, mix):
    nb, width, _ = xt.shape
    ch = gp.shape[2]
    many = 8
    rows = pl.BlockSpec((many, width, BLK), lambda i, at: (i, 0, 0))
    chan = pl.BlockSpec((2, many, ch, BLK), lambda i, at: (0, at[i], 0, 0))
    tok = nb * BLK
    return pl.pallas_call(
        partial(outer_body, ch, many, cuts),
        grid_spec=pltpu.PrefetchScalarGridSpec(
            num_scalar_prefetch=1,
            grid=(nb // many,),
            in_specs=[rows, rows, chan, chan, chan],
            out_specs=[pl.BlockSpec((6, width // cuts, ch), lambda i, at: (0, 0, 0))] * cuts,
            scratch_shapes=[pltpu.VMEM((6, width, ch), f32)],
        ),
        out_shape=[jax.ShapeDtypeStruct((6, width // cuts, ch), bf16)] * cuts,
        compiler_params=params(56),
        cost_estimate=cost(12 * tok * width * ch, tok * (4 * width + 12 * ch)),
    )(order, xt, gt, gp, gpg, mix)


def sequence_tables(lens, nb):
    nseq = lens.shape[0]
    blocks = (lens + BLK - 1) // BLK
    start = jnp.cumsum(blocks) - blocks
    bigs = (blocks + 1) // 2
    first_big = jnp.cumsum(bigs) - bigs
    h = jnp.arange((nb + nseq) // 2, dtype=jnp.int32)
    owner = (h[:, None] >= first_big[None, :]).astype(jnp.int32).sum(axis=1) - 1
    mine = owner[:, None] == jnp.arange(nseq, dtype=jnp.int32)[None, :]

    def at_owner(values):
        return jnp.sum(jnp.where(mine, values[None, :], 0), axis=1)

    rel = h - at_owner(first_big)
    first = jnp.minimum(at_owner(start) + 2 * rel, nb - 1)
    whole = (2 * rel + 1 < at_owner(blocks)).astype(jnp.int32)
    tab = jnp.stack([first, whole]).astype(jnp.int32)
    seq = jnp.stack(
        [jnp.append(first_big, jnp.sum(blocks)), jnp.append(bigs, jnp.sum(bigs))]
    ).astype(jnp.int32)
    return tab, seq


def live_rows(lens, rows):
    slot = (lens + BLK - 1) // BLK * BLK
    begin = jnp.cumsum(slot) - slot
    pos = jnp.arange(rows, dtype=jnp.int32)
    inside = (pos[:, None] >= begin[None, :]) & (pos[:, None] < (begin + lens)[None, :])
    return jnp.sum(inside.astype(f32), axis=1)


def rank_of(keys):
    return jnp.sum((keys[None, :] < keys[:, None]).astype(jnp.int32), axis=1)


class Line:
    def __init__(self, n_dp, n_t):
        self.n_dp, self.n_t = n_dp, n_t
        self.axes = {"dp": n_dp, "tensor": n_t}
        self.both = ("dp", "tensor")
        self.cuts = 1

    def place_of_group(self):
        return lax.axis_index("tensor")

    def regroup(self, x):
        return x

    def deal(self, x):
        return lax.all_to_all(x, "dp", split_axis=0, concat_axis=0, tiled=True)

    def undeal(self, x):
        return self.deal(x)

    def gather_rows(self, x):
        return [(lax.all_gather(x, "tensor", axis=0, tiled=True), jnp.zeros((1,), jnp.int32))]

    def scatter_rows(self, w, arrays, many):
        whole = mul_rows(w, arrays, jnp.zeros((1,), jnp.int32), many * self.n_t)
        return [lax.psum_scatter(whole, "tensor", scatter_dimension=0, tiled=True)]

    def order(self, pieces):
        return jnp.append(jnp.arange(pieces * self.n_t, dtype=jnp.int32), 0)

    def gather_channels(self, chan, norm):
        perm = [(f, (f % self.n_dp) * self.n_t + f // self.n_dp) for f in range(self.n_dp * self.n_t)]
        chan = lax.ppermute(chan, self.both, perm)
        norm = lax.all_gather(norm, self.both, axis=1, tiled=True)
        return lax.all_gather(chan, "dp", axis=0, tiled=True), norm

    def gather_weights(self, pack):
        return lax.all_gather(pack, "dp", axis=0, tiled=True)

    def scatter_weights(self, gw):
        six, width, ch = gw[0].shape
        gw = gw[0].reshape(six, self.n_dp, width // self.n_dp, ch).transpose(1, 0, 2, 3)
        return lax.psum_scatter(gw, "dp", scatter_dimension=0, tiled=True)[0].astype(f32)

    def scatter_channels(self, sums):
        sums = lax.psum_scatter(sums, "dp", scatter_dimension=0, tiled=True)
        perm = [((f % self.n_dp) * self.n_t + f // self.n_dp, f) for f in range(self.n_dp * self.n_t)]
        return lax.ppermute(sums, self.both, perm)

    def scatter_norm(self, sums):
        return lax.psum_scatter(sums, self.both, scatter_dimension=1, tiled=True)


class Pairs:
    def __init__(self, n_dp, n_t):
        self.quads = n_dp // 2
        self.axes = {"q": self.quads, "c": 2, "h": 2, "w": 2}
        self.both = ("q", "c", "h", "w")
        self.cuts = self.quads
        self.other = [(0, 1), (1, 0)]
        self.crossed = [(2 * c + h, 2 * h + c) for c in range(2) for h in range(2)]

    def flip(self, x, axis, bit=1):
        return lax.ppermute(x, axis, [(i, i ^ bit) for i in range(self.axes[axis])])

    def place_of_group(self):
        return 2 * lax.axis_index("c") + lax.axis_index("w")

    def regroup(self, x):
        return lax.ppermute(x, ("c", "h"), self.crossed)

    def deal(self, x):
        return self.regroup(lax.all_to_all(x, ("q", "c"), split_axis=0, concat_axis=0, tiled=True))

    def undeal(self, x):
        return lax.all_to_all(self.regroup(x), ("q", "c"), split_axis=0, concat_axis=0, tiled=True)

    def places(self):
        c, w = lax.axis_index("c"), lax.axis_index("w")
        return [2 * c + w, 2 * (1 - c) + w, 2 * c + 1 - w, 2 * (1 - c) + 1 - w]

    def starts(self, many):
        return [(place * many).astype(jnp.int32).reshape(1) for place in self.places()]

    def gather_rows(self, x):
        beside = self.flip(x, "c")
        near = self.flip(x, "w")
        far = self.flip(near, "c")
        return list(zip([x, beside, near, far], self.starts(x.shape[0])))

    def scatter_rows(self, w, arrays, many):
        own, beside, near, far = self.starts(many)
        give = self.flip(mul_rows(w, arrays, far, many), "c")
        send = self.flip(mul_rows(w, arrays, near, many, extra=give), "w")
        give = self.flip(mul_rows(w, arrays, beside, many), "c")
        return [mul_rows(w, arrays, own, many, dtype=f32), give, send]

    def order(self, pieces):
        place = jnp.stack(self.places())[:, None] * pieces + jnp.arange(pieces)[None, :]
        cut = lax.axis_index("q") ^ jnp.arange(self.quads)
        return jnp.concatenate([place.reshape(-1), cut]).astype(jnp.int32)

    def steps(self):
        bit = self.quads // 2
        while bit:
            yield "q", bit
            bit //= 2
        yield "h", 1

    def spot(self):
        return 2 * lax.axis_index("q") + lax.axis_index("h")

    def gather_channels(self, chan, norm):
        count = 2 * self.quads
        perm = []
        for f in range(4 * count):
            place, at = f // count, f % count
            q, h, c, w = at // 2, at % 2, place // 2, place % 2
            perm.append((f, ((2 * q + c) * 2 + h) * 2 + w))
        chan = lax.ppermute(chan, self.both, perm)
        norm = norm.reshape(1, -1)
        for axis in ("c", "w"):
            norm = jnp.concatenate([norm, self.flip(norm, axis)], axis=0)
        c, w = lax.axis_index("c"), lax.axis_index("w")
        at = jnp.arange(4)
        norm = jnp.take(norm, 2 * ((at % 2) ^ w) + ((at // 2) ^ c), axis=0)
        flat = jnp.concatenate([chan.reshape(1, -1), norm.reshape(1, -1)], axis=1)
        for axis, bit in reversed(list(self.steps())):
            flat = jnp.concatenate([flat, self.flip(flat, axis, bit)], axis=0)
        flat = jnp.take(flat, jnp.arange(count) ^ self.spot(), axis=0)
        rows, wide = chan.shape
        chan = flat[:, : rows * wide].reshape(count * rows, wide)
        norm = flat[:, rows * wide :].reshape(self.quads, 2, 2, 2, 3, -1)
        norm = norm.transpose(4, 0, 2, 1, 3, 5).reshape(3, -1)
        return chan, norm

    def gather_weights(self, pack):
        h = lax.axis_index("h")
        first = self.regroup(pack)
        back = [(2 * (1 - h) + c, 2 * c + h) for c in range(2) for h in range(2)]
        second = lax.ppermute(pack, ("c", "h"), back)
        pair = jnp.concatenate([jnp.where(h == 0, first, second), jnp.where(h == 0, second, first)], axis=0)
        deep, wide = pair.shape
        q = lax.axis_index("q")
        whole = jnp.zeros((self.quads * deep, wide), pack.dtype)
        for bit in range(self.quads):
            part = self.flip(pair, "q", bit) if bit else pair
            whole = lax.dynamic_update_slice_in_dim(whole, part, (q ^ bit) * deep, 0)
        return whole

    def scatter_weights(self, gw):
        total = gw[0].astype(f32)
        for bit in range(1, self.quads):
            total = total + self.flip(gw[bit], "q", bit).astype(f32)
        total = total.astype(bf16)
        six, deep, ch = total.shape
        total = total.reshape(six, 2, deep // 2, ch)
        h = lax.axis_index("h")
        first = jnp.where(h == 0, total[:, 0], total[:, 1])
        second = jnp.where(h == 0, total[:, 1], total[:, 0])
        there = [(2 * c + h, 2 * (1 - h) + c) for c in range(2) for h in range(2)]
        return self.regroup(first).astype(f32) + lax.ppermute(second, ("c", "h"), there).astype(f32)

    def scatter_channels(self, sums):
        count = 2 * self.quads
        rows, wide = sums.shape
        part = jnp.take(sums.reshape(count, rows // count * wide), jnp.arange(count) ^ self.spot(), axis=0)
        for axis, bit in self.steps():
            half = part.shape[0] // 2
            part = part[:half] + self.flip(part[half:], axis, bit)
        perm = []
        for f in range(4 * count):
            place, at = f // count, f % count
            q, h, c, w = at // 2, at % 2, place // 2, place % 2
            perm.append((((2 * q + c) * 2 + h) * 2 + w, f))
        return lax.ppermute(part.reshape(rows // count, wide), self.both, perm)

    def scatter_norm(self, sums):
        count = 8 * self.quads
        mine = lax.axis_index(self.both)
        part = jnp.take(sums.reshape(3, count, -1), jnp.arange(count) ^ mine, axis=1)
        bits = [("q", 1 << at) for at in reversed(range(self.quads.bit_length() - 1))]
        for axis, bit in bits + [("c", 1), ("h", 1), ("w", 1)]:
            half = part.shape[1] // 2
            part = part[:, :half] + self.flip(part[:, half:], axis, bit)
        return part[:, 0]


def local(
    net, wave, tokens, cotangent, source, target, lengths, ln_gain, ln_bias, w_fwd, b_fwd, w_bwd, b_bwd,
    w_gate, b_gate, w_out, b_out, log_dt, log_rate, ssm_b, ssm_c, ssm_d,
):
    rows, width = tokens.shape
    many = rows // BLK
    n_t = net.n_t
    group = rows * n_t
    nb = group // BLK
    ch = w_fwd.shape[1]
    back = (wave.T / BIG).astype(bf16)
    wave = wave.astype(bf16)

    rank = rank_of(target)
    sender = source // group
    place = rank_of(sender * rows + jnp.arange(rows, dtype=jnp.int32))
    (sent_x,) = permute_to(rank, [tokens])
    got_x = net.deal(sent_x)
    (sent_g,) = permute_to(rank, [cotangent])
    got_g = net.deal(sent_g)
    table = net.regroup(jnp.concatenate([place, lengths[0]]))
    place, lens = table[:rows], table[rows:]

    chan = jnp.concatenate(
        [log_rate[0], log_rate[1], ssm_b[0], ssm_b[1], ssm_c[0], ssm_c[1]]
        + [jnp.stack([log_dt[0], log_dt[1], ssm_d[0], ssm_d[1], b_fwd, b_bwd, b_gate[0], b_gate[1]], axis=1)],
        axis=1,
    )
    chan_all, norm_all = net.gather_channels(chan, jnp.stack([ln_gain, ln_bias, b_out]))

    def lanes(column):
        return jnp.broadcast_to(column[..., None], column.shape + (BLK,))

    gain = lanes(norm_all[0])
    shift = lanes(norm_all[1])
    bias_out = lanes(norm_all[2])
    small = chan_all[:, 6 * STATE :]
    bias_in = lanes(small[:, 4:8].T.reshape(-1))

    def pick(at):
        return jnp.stack([chan_all[:, at * STATE : (at + 1) * STATE], chan_all[:, (at + 1) * STATE : (at + 2) * STATE]])

    def decays(log_dt, log_rate, ssm_b):
        rate = jnp.exp(log_rate)
        ld = -jnp.exp(log_dt)[..., None] * rate
        return rate, ld, (1.0 - jnp.exp(ld)) / rate * ssm_b

    _, ld_all, drive_all = decays(small[:, 0:2].T, pick(0), pick(2))
    ld_pairs = (ld_all * log2e).reshape(2, ch // 2, 2 * STATE)
    w_pairs = (pick(4) * drive_all).reshape(2, ch // 2, 2 * STATE)
    kh = spectra(ld_pairs, w_pairs, lanes(small[:, 2:4].T), wave)

    pack = jnp.concatenate(
        [w_fwd, w_bwd, w_gate.reshape(-1, 2 * ch), w_out.transpose(2, 0, 1).reshape(-1, 2 * ch)], axis=1
    )
    w_all = net.gather_weights(pack)
    w_in, w_back = w_all[:, : 4 * ch], w_all[:, 4 * ch :]
    w_in_t, w_back_t = w_in.T, w_back.T

    live = live_rows(lens, group)
    live_own = lax.dynamic_slice_in_dim(live, net.place_of_group() * rows, rows, 0).reshape(many, 1, BLK)
    live = live.reshape(nb // 2, 1, BIG)
    tab, seq = sequence_tables(lens, nb)

    xt, xd = deal_x(place, got_x, gain, shift)
    xs = net.gather_rows(xt)
    kept = None
    for part, start in xs:
        kept = project(part, start, nb, live, w_in_t, bias_in, kept)
    a, da, gg, dg = kept
    y, mix = ssm_scan(tab, seq, a, kh, wave, back, gg)

    gt, gd, g_bias_out = deal_g(place, got_g, live_own)
    gs = net.gather_rows(gt)
    kept = None
    for part, start in gs:
        kept = gate_grad(part, start, nb, w_back_t, kept)
    (gm,) = kept

    branch = net.scatter_rows(w_back, [mix], many)
    sent_out = layer_rows(place, branch, xd, live_own, bias_out)
    layer_out = permute_from(rank, net.undeal(sent_out))

    gpg, gp, gh, bsum = ssm_back(tab, seq, a, gm, kh, wave, back, gg, y, dg, da)
    g_normed = net.scatter_rows(w_in, [gp, gpg], many)
    gw = outer_sums(
        net.order(many // 8),
        net.cuts,
        jnp.concatenate([part for part, _ in xs], axis=0),
        jnp.concatenate([part for part, _ in gs], axis=0),
        gp,
        gpg,
        mix,
    )
    gw = net.scatter_weights(gw)
    s0, s1, g0 = moments(ld_pairs, gh, back)

    sent_in, norm_sums = input_rows(place, g_normed, xd, gd, gain)
    in_grad = permute_from(rank, net.undeal(sent_in))

    s0 = s0.reshape(2, ch, STATE)
    s1 = s1.reshape(2, ch, STATE)
    gb_gate = jnp.sum(bsum[:, :, :BLK], axis=2)
    gb_in = jnp.sum(bsum[:, :, BLK:], axis=2)
    sums = jnp.concatenate(
        [s0[0], s0[1], s1[0], s1[1], jnp.concatenate([g0[:, :, 0], gb_gate, gb_in], axis=0).T], axis=1
    )
    sums = net.scatter_channels(sums)
    norm_sums = net.scatter_norm(jnp.sum(jnp.concatenate([norm_sums, g_bias_out[None]], axis=0), axis=2))
    s0 = jnp.stack([sums[:, :STATE], sums[:, STATE : 2 * STATE]])
    s1 = jnp.stack([sums[:, 2 * STATE : 3 * STATE], sums[:, 3 * STATE : 4 * STATE]])
    tail = sums[:, 4 * STATE :].T
    step = jnp.exp(log_dt)[..., None]
    rate, ld, drive = decays(log_dt, log_rate, ssm_b)
    g_c = s0 * drive
    g_drive = s0 * ssm_c
    g_b = g_drive * (1.0 - jnp.exp(ld)) / rate
    g_ld = s1 * ssm_c * drive - g_drive * ssm_b / rate * jnp.exp(ld)
    g_rate = -g_drive * drive / rate - g_ld * step
    g_dt = jnp.sum(g_ld * ld, axis=2)
    return (
        layer_out,
        in_grad,
        norm_sums[0],
        norm_sums[1],
        gw[0],
        tail[4],
        gw[1],
        tail[5],
        jnp.stack([gw[2], gw[3]], axis=1),
        tail[2:4],
        jnp.stack([gw[4].T, gw[5].T]),
        norm_sums[2],
        g_dt,
        g_rate * rate,
        g_b,
        g_c,
        tail[0:2],
    )


def solution(mesh):
    n_dp, n_t = mesh.shape["dp"], mesh.shape["tensor"]
    if n_t == 4 and n_dp == 8:
        net = Pairs(n_dp, n_t)
        dp, tensor = ("q", "c"), ("h", "w")
    else:
        net = Line(n_dp, n_t)
        dp, tensor = ("dp",), ("tensor",)
    net.n_t = n_t
    mesh = jax.sharding.Mesh(mesh.devices.reshape(tuple(net.axes.values())), tuple(net.axes))
    both = P(dp + tensor)
    rows = P(dp + tensor, None)
    pair = P(None, dp + tensor)
    state = P(None, dp + tensor, None)
    proj = P(dp, tensor)
    gate = P(dp, None, tensor)
    out = P(None, tensor, dp)
    wave = wave_table()

    def run(*args):
        return local(net, jnp.asarray(wave), *args)

    return jax.shard_map(
        run,
        mesh=mesh,
        in_specs=(
            rows, rows, both, both, P(dp, None), both, both, proj, both, proj, both, gate, pair, out, both,
            pair, state, state, state, pair,
        ),
        out_specs=(
            rows, rows, both, both, proj, both, proj, both, gate, pair, out, both, pair, state, state, state, pair,
        ),
        check_vma=False,
    )
```

time: 925 us -> 724 us (0.78)
  waiting for transfers between devices: 469 us -> 126 us
  starting transfers between devices: 23.8 us -> 150 us
  Pallas kernels: 265 us -> 320 us
  blocking collectives: 48.4 us -> 0 us
  other arithmetic: 17.7 us -> 36.1 us
  between operations: 16.5 us -> 2.48 us
    all_gather x3 -> x0, waiting for transfers between devices: 199 us -> none  [the longest x1 116 us: local(): xt_all = lax.all_gather(xt, 'tensor', axis=0, tiled=True)]
    reduce_scatter x3 -> x0, waiting for transfers between devices: 185 us -> none  [the longest x2 185 us: to_owner(): return lax.psum_scatter(x, 'tensor', scatter_dimension=0, tiled=True)]
    ppermute x2 -> x42, starting transfers between devices: 8.24 us -> 128 us  [the longest x31 76.9 us: flip(): return lax.ppermute(x, axis, [(i, i ^ bit) for i in range(self.axes[axis])])]
    ppermute x2 -> x42, waiting for transfers between devices: 0.01 us -> 79.7 us  [the longest x31 71.8 us: flip(): return lax.ppermute(x, axis, [(i, i ^ bit) for i in range(self.axes[axis])])]
    unnamed x10 -> x0, waiting for transfers between devices: 75.1 us -> none
    pallas_call x6 -> x21, Pallas kernels: 185 us -> 234 us  [the longest x1 67.4 us: ssm_back(): pl.pallas_call(partial(back_body, nb, nseq, cc, 16), grid=(2, ch // cc),...]
    all_to_all x3 -> x4, waiting for transfers between devices: 9.43 us -> 46.4 us  [the longest x2 40.7 us: deal(): lax.all_to_all(x, ('q', 'c'), split_axis=0, concat_axis=0, tiled=True)]
    all_to_all x1 -> x0, blocking collectives: 28.2 us -> none  [swap(): return lax.all_to_all(x, 'dp', split_axis=0, concat_axis=0, tiled=True)]
  transfers between devices with their start and end apart: 13 -> 46, of which waited for: 7 -> 13; matrix products, arithmetic and copies ran while one was open for 6% -> 11% of each run, Pallas kernels for 12% -> 29%
where the time goes in v2:
time: 724 us; the launch traced here: 711 us
  Pallas kernels  320 us (44%)
  starting transfers between devices  150 us (21%)
  waiting for transfers between devices  126 us (17%)
  local copies, waits for them, and re-layouts  76.3 us (11%)
  other arithmetic  36.1 us (5%)
    ppermute x31, starting transfers between devices, flip(): return lax.ppermute(x, axis, [(i, i ^ bit) for i in range(self.axes[axis])])  76.9 us
    ppermute x31, waiting for transfers between devices, flip(): return lax.ppermute(x, axis, [(i, i ^ bit) for i in range(self.axes[axis])])  71.8 us
    pallas_call x1, Pallas kernels, ssm_back(): pl.pallas_call(partial(back_body, nb, nseq, cc, 16), grid=(2, ch // cc),...  67.4 us
    pallas_call x8, Pallas kernels, chained(): pl.pallas_call(body, grid_spec=pltpu.PrefetchScalarGridSpec(num_scalar_pr...  54.6 us
    ppermute x7, starting transfers between devices, regroup(): return lax.ppermute(x, ('c', 'h'), self.crossed)  42 us
    all_to_all x2, waiting for transfers between devices, deal(): lax.all_to_all(x, ('q', 'c'), split_axis=0, concat_axis=0, tiled=True)  40.7 us
    pallas_call x1, Pallas kernels, ssm_scan(): pl.pallas_call(partial(scan_body, nb, nseq, cc, 32), grid=(2, ch // cc),...  36.9 us
    unnamed x154, local copies, waits for them, and re-layouts  36 us
  transfers between devices with their start and end apart: 46, of which 13 were waited for; matrix products, arithmetic and copies ran while one was open for 11% of the time, Pallas kernels for 29%

profile of v2, /device:TPU:1, one launch (start us, length us, event | category | flops | bytes accessed | tf_op | source)
XLA Modules:
  0.0 711.2 jit_solution(8575765760721400999)
XLA Ops:
  4.4 5.6 collective-permute-start.8
  19.7 4.4 all-to-all-start.2
  46.8 4.0 collective-permute-done.5
  66.0 7.9 %all-to-all-start = ((bf16[8,128,768]{2,1,0:T(8,128)(2,1)}), bf16[8,128,768]{2,1,0:T(8,128)(2,1)}, u32[]{:S(2)}, u32[]{:S(2)}) async-start(bf16[8,128,768]{2,1,0:T(8,128)(2,1)} %bitcast.5), calls=%async_computation | async-start | bytes 3145728 | tf_op jit(solution)/shard_map/all_to_all | solution.py:890
  79.1 40.7 %all-to-all-done = bf16[8,128,768]{2,1,0:T(8,128)(2,1)} async-done(((bf16[8,128,768]{2,1,0:T(8,128)(2,1)}), bf16[8,128,768]{2,1,0:T(8,128)(2,1)}, u32[]{:S(2)}, u32[]{:S(2)}) %all-to-all-start) | async-done | bytes 1572896 | tf_op jit(solution)/shard_map/all_to_all | solution.py:890
  123.1 33.1 %shard_map.338.kh_ref = f32[2,8,384,512]{3,2,1,0:T(8,128)S(1)} custom-call(f32[2,192,128]{2,1,0:T(8,128)S(1)} %get-tuple-element.193.ld_ref, f32[2,192,128]{2,1,0:T(8,128)S(1)} %get-tuple-element.192.w_ref, f32[2,384,128]{2,1,0:T(8,128)S(1)} %broadcast_in_dim.136.d_ref, bf16[256,512]{1,0:T(8,128)(2,1)S(1)} %copy-done.30), custom_call_target="tpu_custom_call" | custom-call | flops 30720000000 | bytes 12582912 | tf_op jit(solution)/shard_map/pallas_call | solution.py:384
  156.2 4.6 copy-done.31
  161.5 8.3 %shard_map.333 = (bf16[8,768,128]{2,1,0:T(8,128)(2,1)}, bf16[8,768,128]{2,1,0:T(8,128)(2,1)S(1)}) custom-call(s32[1024,1]{1,0:T(8,128)S(1)} %copy.177.place_ref, bf16[1024,768]{1,0:T(8,128)(2,1)} %collective-permute-done.1.x_ref, f32[768,128]{1,0:T(8,128)S(1)} %broadcast_in_dim.125.gain_ref, f32[768,128]{1,0:T(8,128)S(1)} %broadcast_in_dim.127.shift_ref), custom_call_target="tpu_custom_call" | custom-call | flops 1610612736 | bytes 4718592 | tf_op jit(solution)/shard_map/pallas_call | solution.py:134
  180.6 5.6 shard_map.347
  186.2 9.0 %collective-permute-start.23 = (bf16[8,768,128]{2,1,0:T(8,128)(2,1)}, bf16[8,768,128]{2,1,0:T(8,128)(2,1)}, u32[]{:S(2)}, u32[]{:S(2)}) collective-permute-start(bf16[8,768,128]{2,1,0:T(8,128)(2,1)} %get-tuple-element.71.g_ref), channel_id=1, source_target_pairs={{0,4},{4,0},{1,5},{5,1},{2,6},{6,2},{3,7},{7,3},{8,12},{12,8},{9,1... | collective-permute-start | bytes 4718600 | tf_op jit(solution)/shard_map/ppermute | solution.py:881
  202.6 18.5 %collective-permute-start.14 = (bf16[8,768,128]{2,1,0:T(8,128)(2,1)}, bf16[8,768,128]{2,1,0:T(8,128)(2,1)}, u32[]{:S(2)}, u32[]{:S(2)}) collective-permute-start(bf16[8,768,128]{2,1,0:T(8,128)(2,1)} %collective-permute-done.13.x_ref), channel_id=1, source_target_pairs={{0,4},{4,0},{1,5},{5,1},{2,6},{6,2},{3,7},{7,3},{8,12},{12,8},{9,1... | collective-permute-start | bytes 4718600 | tf_op jit(solution)/shard_map/ppermute | solution.py:881
  221.1 4.1 fusion.29
  225.2 4.3 copy.184.wt_ref
  229.5 3.7 shard_map.348.refs_0_
  233.4 10.1 %shard_map.334 = (bf16[2,32,384,128]{3,2,1,0:T(8,128)(2,1)}, bf16[2,32,384,128]{3,2,1,0:T(8,128)(2,1)}, bf16[2,32,384,128]{3,2,1,0:T(8,128)(2,1)}, bf16[2,32,384,128]{3,2,1,0:T(8,128)(2,1)}) custom-call(s32[1]{0:T(128)S(6)} %select_n.218.start_ref, bf16[8,768,128]{2,1,0:T(8,128)(2,1)} %get-tuple-element.54.x_ref, f32[16,1,256]{2,1,0:T(1,128)S(1)} %bitcast.175, ...), custom_call_target="tpu_custom_call" | custom-call | flops 2415919104 | bytes 7864320 | tf_op jit(solution)/shard_map/pallas_call | solution.py:276
  250.9 10.1 %shard_map.335 = (bf16[2,32,384,128]{3,2,1,0:T(8,128)(2,1)}, bf16[2,32,384,128]{3,2,1,0:T(8,128)(2,1)}, bf16[2,32,384,128]{3,2,1,0:T(8,128)(2,1)}, bf16[2,32,384,128]{3,2,1,0:T(8,128)(2,1)}) custom-call(s32[1]{0:T(128)S(6)} %select_n.232.start_ref, ...), custom_call_target="tpu_custom_call", output_to_operand_aliasing={{0}: (5, {}), {1}: (6, {}), {2}: (7, {}), {3}: (8, {})} | custom-call | flops 2415919104 | bytes 7864320 | tf_op jit(solution)/shard_map/pallas_call | solution.py:276
  261.0 10.1 %shard_map.336 = (bf16[2,32,384,128]{3,2,1,0:T(8,128)(2,1)}, bf16[2,32,384,128]{3,2,1,0:T(8,128)(2,1)}, bf16[2,32,384,128]{3,2,1,0:T(8,128)(2,1)}, bf16[2,32,384,128]{3,2,1,0:T(8,128)(2,1)}) custom-call(s32[1]{0:T(128)S(6)} %select_n.231.start_ref, ...), custom_call_target="tpu_custom_call", output_to_operand_aliasing={{0}: (5, {}), {1}: (6, {}), {2}: (7, {}), {3}: (8, {})} | custom-call | flops 2415919104 | bytes 7864320 | tf_op jit(solution)/shard_map/pallas_call | solution.py:276
  271.1 10.1 %shard_map.337 = (bf16[2,32,384,128]{3,2,1,0:T(8,128)(2,1)}, bf16[2,32,384,128]{3,2,1,0:T(8,128)(2,1)}, bf16[2,32,384,128]{3,2,1,0:T(8,128)(2,1)}, bf16[2,32,384,128]{3,2,1,0:T(8,128)(2,1)}) custom-call(s32[1]{0:T(128)S(6)} %select_n.230.start_ref, ...), custom_call_target="tpu_custom_call", output_to_operand_aliasing={{0}: (5, {}), {1}: (6, {}), {2}: (7, {}), {3}: (8, {})} | custom-call | flops 2415919104 | bytes 7864320 | tf_op jit(solution)/shard_map/pallas_call | solution.py:276
  281.1 36.9 %shard_map.339 = (bf16[2,32,384,128]{3,2,1,0:T(8,128)(2,1)}, bf16[2,32,384,128]{3,2,1,0:T(8,128)(2,1)}) custom-call(s32[2,17]{1,0:T(2,128)} %pad_add_fusion.1.tab_ref, s32[2,4]{1,0:T(2,128)} %pad_add_fusion.2.seq_ref, bf16[2,32,384,128]{3,2,1,0:T(8,128)(2,1)} %get-tuple-element.67.a_ref, f32[2,8,384,512]{3,2,1,0:T(8,128)} %copy-done.31, ...), custom_call_target="tpu_custom_call" | custom-call | flops 38400000000 | bytes 25165824 | tf_op jit(solution)/shard_map/pallas_call | solution.py:654
  324.2 67.4 %shard_map.352 = (bf16[2,32,384,128]{3,2,1,0:T(8,128)(2,1)}, bf16[2,32,384,128]{3,2,1,0:T(8,128)(2,1)}, f32[2,8,384,512]{3,2,1,0:T(8,128)}, f32[2,384,256]{2,1,0:T(8,128)}) custom-call(s32[2,17]{1,0:T(2,128)} %pad_add_fusion.1.tab_ref, s32[2,4]{1,0:T(2,128)} %pad_add_fusion.2.seq_ref, bf16[2,32,384,128]{3,2,1,0:T(8,128)(2,1)} %get-tuple-element.67.a_ref, ...), custom_call_target="tpu_custom_call" | custom-call | flops 61440000000 | bytes 50331648 | tf_op jit(solution)/shard_map/pallas_call | solution.py:673
  394.4 5.5 shard_map.355
  399.9 5.5 shard_map.354
  411.6 4.6 copy-done.32
  416.2 25.4 %shard_map.360 = (f32[2,192,128]{2,1,0:T(8,128)S(1)}, f32[2,192,128]{2,1,0:T(8,128)S(1)}, f32[2,384,128]{2,1,0:T(8,128)S(1)}) custom-call(f32[2,192,128]{2,1,0:T(8,128)S(1)} %copy-done.22, f32[2,8,384,512]{3,2,1,0:T(8,128)S(1)} %copy-done.32, bf16[512,256]{1,0:T(8,128)(2,1)S(1)} %copy-done.29), custom_call_target="tpu_custom_call" | custom-call | flops 30720000000 | bytes 12582912 | tf_op jit(solution)/shard_map/pallas_call | solution.py:442
  445.3 6.6 pad_maximum_fusion.x_ref
  451.9 6.9 pad_maximum_fusion.1.g_ref
  458.8 27.7 %shard_map.359 = (bf16[6,192,384]{2,1,0:T(8,128)(2,1)}, bf16[6,192,384]{2,1,0:T(8,128)(2,1)}, bf16[6,192,384]{2,1,0:T(8,128)(2,1)}, bf16[6,192,384]{2,1,0:T(8,128)(2,1)}) custom-call(s32[8]{0:T(128)} %concatenate.75.at_ref, bf16[32,768,128]{2,1,0:T(8,128)(2,1)} %pad_maximum_fusion.x_ref, bf16[32,768,128]{2,1,0:T(8,128)(2,1)} %pad_maximum_fusion.1.g_ref, ...), custom_call_target="tpu_custom_call" | custom-call | flops 14495514624 | bytes 31457280 | tf_op jit(solution)/shard_map/pallas_call | solution.py:769
  488.2 4.7 shard_map.353.refs_0_
  495.7 10.2 %collective-permute-start.39 = (f32[2,12576]{1,0:T(2,128)S(1)}, f32[2,12576]{1,0:T(2,128)S(1)}, u32[]{:S(2)}, u32[]{:S(2)}) collective-permute-start(f32[2,12576]{1,0:T(2,128)S(1)} %slice.350), channel_id=1, source_target_pairs={{0,8},{8,0},{16,24},{24,16},{1,9},{9,1},{17,25},{25,17},{2,10},{10... | collective-permute-start | bytes 301832 | tf_op jit(solution)/shard_map/ppermute | solution.py:881
  505.9 4.8 shard_map.356
  512.4 4.7 shard_map.343
  517.5 4.1 collective-permute-start.40
  521.5 26.1 %collective-permute-done.26.refs_2_ = bf16[8,768,128]{2,1,0:T(8,128)(2,1)S(1)} collective-permute-done((bf16[8,768,128]{2,1,0:T(8,128)(2,1)S(1)}, bf16[8,768,128]{2,1,0:T(8,128)(2,1)S(1)}, u32[]{:S(2)}, u32[]{:S(2)}) %collective-permute-start.26) | collective-permute-done | bytes 1572896 | tf_op jit(solution)/shard_map/ppermute | solution.py:881
  548.9 9.3 %shard_map.357 = (bf16[1024,768]{1,0:T(8,128)(2,1)}, f32[2,768,128]{2,1,0:T(8,128)S(1)}) custom-call(s32[1,1024]{1,0:T(1,128)S(1)} %bitcast.180, bf16[8,768,128]{2,1,0:T(8,128)(2,1)S(1)} %copy-done.12, bf16[8,768,128]{2,1,0:T(8,128)(2,1)S(1)} %copy-done.16, f32[768,128]{1,0:T(8,128)S(1)} %copy-done.14, f32[8,768,128]{2,1,0:T(8,128)} %copy-done.10, ...), custom_call_target="tpu_custom_call" | custom-call | flops 1610612736 | bytes 6291456 | tf_op jit(solution)/shard_map/pallas_call | solution.py:222
  558.1 7.1 collective-permute-start.27
  565.2 15.3 %collective-permute-done.40 = f32[1,12576]{1,0:T(1,128)S(1)} collective-permute-done((f32[1,12576]{1,0:T(1,128)S(1)}, f32[1,12576]{1,0:T(1,128)S(1)}, u32[]{:S(2)}, u32[]{:S(2)}) %collective-permute-start.40) | collective-permute-done | bytes 50336 | tf_op jit(solution)/shard_map/ppermute | solution.py:881
  584.6 5.4 collective-permute-start.41
  596.6 4.1 collective-permute-start.33
  600.7 4.4 collective-permute-start.35
  607.2 6.4 shard_map.344
  613.6 10.7 %collective-permute-start.19 = (bf16[1024,768]{1,0:T(8,128)(2,1)}, bf16[1024,768]{1,0:T(8,128)(2,1)}, u32[]{:S(2)}, u32[]{:S(2)}) collective-permute-start(bf16[1024,768]{1,0:T(8,128)(2,1)} %shard_map.344), channel_id=1, source_target_pairs={{0,0},{2,4},{4,2},{6,6},{1,1},{3,5},{5,3},{7,7},{8,8},{10,12},{12,... | collective-permute-start | bytes 4718600 | tf_op jit(solution)/shard_map/ppermute | solution.py:887
  624.3 16.6 %collective-permute-done.34 = bf16[6,192,384]{2,1,0:T(8,128)(2,1)S(1)} collective-permute-done((bf16[6,192,384]{2,1,0:T(8,128)(2,1)S(1)}, bf16[6,192,384]{2,1,0:T(8,128)(2,1)S(1)}, u32[]{:S(2)}, u32[]{:S(2)}) %collective-permute-start.34) | collective-permute-done | bytes 884768 | tf_op jit(solution)/shard_map/ppermute | solution.py:881
  642.3 5.7 all-to-all-start.3
  650.2 11.7 %collective-permute-start.36 = (bf16[6,96,384]{2,1,0:T(8,128)(2,1)}, bf16[6,96,384]{2,1,0:T(8,128)(2,1)S(1)}, u32[]{:S(2)}, u32[]{:S(2)}) collective-permute-start(bf16[6,96,384]{2,1,0:T(8,128)(2,1)} %get-tuple-element.178), channel_id=1, source_target_pairs={{0,0},{2,4},{4,2},{6,6},{1,1},{3,5},{5,3},{7,7},{8,8},{10,12},{12,... | collective-permute-start | bytes 1327112 | tf_op jit(solution)/shard_map/ppermute | solution.py:887
  669.6 7.9 %collective-permute-done.36 = bf16[6,96,384]{2,1,0:T(8,128)(2,1)S(1)} collective-permute-done((bf16[6,96,384]{2,1,0:T(8,128)(2,1)}, bf16[6,96,384]{2,1,0:T(8,128)(2,1)S(1)}, u32[]{:S(2)}, u32[]{:S(2)}) %collective-permute-start.36) | collective-permute-done | bytes 442400 | tf_op jit(solution)/shard_map/ppermute | solution.py:887
  679.5 5.6 collective-permute-start.30
  685.1 4.2 all-to-all-start.1
  701.1 5.8 all-to-all-done.1
  (390 shorter events, 153.5 us)
Async XLA Ops:
  4.4 53.0 %collective-permute-start.8 = (bf16[96,2304]{1,0:T(8,128)(2,1)S(1)}, bf16[96,2304]{1,0:T(8,128)(2,1)S(1)}, u32[]{:S(2)}, u32[]{:S(2)}) collective-permute-start(bf16[96,2304]{1,0:T(8,128)(2,1)S(1)} %constant_dynamic-update-slice_fusion.2), channel_id=1, source_target_pairs={{0,0},{2,4},{4,2},{6,6},{1,1},{3,5},{5,3},{7,7},{8,8},{10,12},{12,... | collective-permute-start | bytes 1327112 | tf_op jit(solution)/shard_map/ppermute | solution.py:887
  10.0 47.4 %collective-permute-start.9 = (bf16[96,2304]{1,0:T(8,128)(2,1)S(1)}, bf16[96,2304]{1,0:T(8,128)(2,1)S(1)}, u32[]{:S(2)}, u32[]{:S(2)}) collective-permute-start(bf16[96,2304]{1,0:T(8,128)(2,1)S(1)} %constant_dynamic-update-slice_fusion.2), channel_id=1, source_target_pairs={{4,0},{0,2},{6,4},{2,6},{5,1},{1,3},{7,5},{3,7},{12,8},{8,10},{14,... | collective-permute-start | bytes 1327112 | tf_op jit(solution)/shard_map/ppermute | solution.py:958
  12.0 29.7 %collective-permute-start = (s32[1027]{0:T(1024)S(1)}, s32[1027]{0:T(1024)S(1)}, u32[]{:S(2)}, u32[]{:S(2)}) collective-permute-start(s32[1027]{0:T(1024)S(1)} %pad_add_fusion), channel_id=1, source_target_pairs={{0,0},{2,4},{4,2},{6,6},{1,1},{3,5},{5,3},{7,7},{8,8},{10,12},{12,... | collective-permute-start | bytes 12332 | tf_op jit(solution)/shard_map/ppermute | solution.py:887
  19.7 46.3 %all-to-all-start.2 = ((bf16[8,128,768]{2,1,0:T(8,128)(2,1)}), bf16[8,128,768]{2,1,0:T(8,128)(2,1)}, u32[]{:S(2)}, u32[]{:S(2)}) async-start(bf16[8,128,768]{2,1,0:T(8,128)(2,1)} %bitcast.53), calls=%async_computation.2 | async-start | bytes 3145728 | tf_op jit(solution)/shard_map/all_to_all | solution.py:890
  24.2 12.5 %collective-permute-start.3 = (f32[1,72]{1,0:T(1,128)S(1)}, f32[1,72]{1,0:T(1,128)S(1)}, u32[]{:S(2)}, u32[]{:S(2)}) collective-permute-start(f32[1,72]{1,0:T(1,128)S(1)} %reshape.474), channel_id=1, source_target_pairs={{0,4},{4,0},{1,5},{5,1},{2,6},{6,2},{3,7},{7,3},{8,12},{12,8},{9,1... | collective-permute-start | bytes 872 | tf_op jit(solution)/shard_map/ppermute | solution.py:881
  25.2 18.6 %collective-permute-start.2 = (f32[48,392]{1,0:T(8,128)S(1)}, f32[48,392]{1,0:T(8,128)S(1)}, u32[]{:S(2)}, u32[]{:S(2)}) collective-permute-start(f32[48,392]{1,0:T(8,128)S(1)} %concatenate.63), channel_id=1, source_target_pairs={{0,0},{1,2},{2,8},{3,10},{4,16},{5,18},{6,24},{7,26},{8,1},{9,3},{... | collective-permute-start | bytes 225800 | tf_op jit(solution)/shard_map/ppermute | solution.py:937
  36.7 4.3 collective-permute-start.4
  44.1 6.8 collective-permute-start.5
  51.0 6.1 collective-permute-start.6
  54.8 125.8 %copy-start.25 = (f32[1024]{0:T(1024)}, f32[1024]{0:T(1024)S(1)}, u32[]{:S(2)}) copy-start(f32[1024]{0:T(1024)S(1)} %dynamic_slice.3) | copy-start | bytes 12292
  57.2 7.7 %collective-permute-start.7 = (f32[4,19104]{1,0:T(4,128)S(1)}, f32[4,19104]{1,0:T(4,128)S(1)}, u32[]{:S(2)}, u32[]{:S(2)}) collective-permute-start(f32[4,19104]{1,0:T(4,128)S(1)} %pad_maximum_fusion.4), channel_id=1, source_target_pairs={{0,16},{8,24},{16,0},{24,8},{1,17},{9,25},{17,1},{25,9},{2,18},{10... | collective-permute-start | bytes 917000 | tf_op jit(solution)/shard_map/ppermute | solution.py:881
  60.7 115.6 %collective-permute-start.10 = (bf16[192,2304]{1,0:T(8,128)(2,1)}, bf16[192,2304]{1,0:T(8,128)(2,1)}, u32[]{:S(2)}, u32[]{:S(2)}) collective-permute-start(bf16[192,2304]{1,0:T(8,128)(2,1)} %get-tuple-element.180), channel_id=1, source_target_pairs={{0,8},{8,0},{16,24},{24,16},{1,9},{9,1},{17,25},{25,17},{2,10},{10... | collective-permute-start | bytes 2654216 | tf_op jit(solution)/shard_map/ppermute | solution.py:881
  61.9 116.6 %collective-permute-start.11 = (bf16[192,2304]{1,0:T(8,128)(2,1)}, bf16[192,2304]{1,0:T(8,128)(2,1)}, u32[]{:S(2)}, u32[]{:S(2)}) collective-permute-start(bf16[192,2304]{1,0:T(8,128)(2,1)} %get-tuple-element.180), channel_id=1, source_target_pairs={{0,16},{8,24},{16,0},{24,8},{1,17},{9,25},{17,1},{25,9},{2,18},{10... | collective-permute-start | bytes 2654216 | tf_op jit(solution)/shard_map/ppermute | solution.py:881
  63.3 134.0 %collective-permute-start.12 = (bf16[192,2304]{1,0:T(8,128)(2,1)}, bf16[192,2304]{1,0:T(8,128)(2,1)}, u32[]{:S(2)}, u32[]{:S(2)}) collective-permute-start(bf16[192,2304]{1,0:T(8,128)(2,1)} %get-tuple-element.180), channel_id=1, source_target_pairs={{0,24},{8,16},{16,8},{24,0},{1,25},{9,17},{17,9},{25,1},{2,26},{10... | collective-permute-start | bytes 2654216 | tf_op jit(solution)/shard_map/ppermute | solution.py:881
  66.0 53.8 %all-to-all-start = ((bf16[8,128,768]{2,1,0:T(8,128)(2,1)}), bf16[8,128,768]{2,1,0:T(8,128)(2,1)}, u32[]{:S(2)}, u32[]{:S(2)}) async-start(bf16[8,128,768]{2,1,0:T(8,128)(2,1)} %bitcast.5), calls=%async_computation | async-start | bytes 3145728 | tf_op jit(solution)/shard_map/all_to_all | solution.py:890
  77.2 79.0 %copy-start.21 = (f32[2,192,128]{2,1,0:T(8,128)}, f32[2,192,128]{2,1,0:T(8,128)S(1)}, u32[]{:S(2)}) copy-start(f32[2,192,128]{2,1,0:T(8,128)S(1)} %get-tuple-element.193.ld_ref) | copy-start | bytes 589828
  77.2 103.4 %collective-permute-start.20 = (bf16[1024,768]{1,0:T(8,128)(2,1)}, bf16[1024,768]{1,0:T(8,128)(2,1)S(1)}, u32[]{:S(2)}, u32[]{:S(2)}) collective-permute-start(bf16[1024,768]{1,0:T(8,128)(2,1)} %bitcast.54), channel_id=1, source_target_pairs={{0,0},{2,4},{4,2},{6,6},{1,1},{3,5},{5,3},{7,7},{8,8},{10,12},{12,... | collective-permute-start | bytes 4718600 | tf_op jit(solution)/shard_map/ppermute | solution.py:887
  119.8 41.4 %collective-permute-start.1 = (bf16[1024,768]{1,0:T(8,128)(2,1)}, bf16[1024,768]{1,0:T(8,128)(2,1)}, u32[]{:S(2)}, u32[]{:S(2)}) collective-permute-start(bf16[1024,768]{1,0:T(8,128)(2,1)} %bitcast.6), channel_id=1, source_target_pairs={{0,0},{2,4},{4,2},{6,6},{1,1},{3,5},{5,3},{7,7},{8,8},{10,12},{12,... | collective-permute-start | bytes 4718600 | tf_op jit(solution)/shard_map/ppermute | solution.py:887
  170.9 31.6 %collective-permute-start.13 = (bf16[8,768,128]{2,1,0:T(8,128)(2,1)}, bf16[8,768,128]{2,1,0:T(8,128)(2,1)}, u32[]{:S(2)}, u32[]{:S(2)}) collective-permute-start(bf16[8,768,128]{2,1,0:T(8,128)(2,1)} %get-tuple-element.54.x_ref), channel_id=1, source_target_pairs={{0,1},{1,0},{2,3},{3,2},{4,5},{5,4},{6,7},{7,6},{8,9},{9,8},{10,11... | collective-permute-start | bytes 4718600 | tf_op jit(solution)/shard_map/ppermute | solution.py:881
  186.2 57.6 %collective-permute-start.23 = (bf16[8,768,128]{2,1,0:T(8,128)(2,1)}, bf16[8,768,128]{2,1,0:T(8,128)(2,1)}, u32[]{:S(2)}, u32[]{:S(2)}) collective-permute-start(bf16[8,768,128]{2,1,0:T(8,128)(2,1)} %get-tuple-element.71.g_ref), channel_id=1, source_target_pairs={{0,4},{4,0},{1,5},{5,1},{2,6},{6,2},{3,7},{7,3},{8,12},{12,8},{9,1... | collective-permute-start | bytes 4718600 | tf_op jit(solution)/shard_map/ppermute | solution.py:881
  195.2 48.3 %collective-permute-start.21 = (bf16[8,768,128]{2,1,0:T(8,128)(2,1)}, bf16[8,768,128]{2,1,0:T(8,128)(2,1)}, u32[]{:S(2)}, u32[]{:S(2)}) collective-permute-start(bf16[8,768,128]{2,1,0:T(8,128)(2,1)} %get-tuple-element.71.g_ref), channel_id=1, source_target_pairs={{0,1},{1,0},{2,3},{3,2},{4,5},{5,4},{6,7},{7,6},{8,9},{9,8},{10,11... | collective-permute-start | bytes 4718600 | tf_op jit(solution)/shard_map/ppermute | solution.py:881
  197.0 53.9 %collective-permute-start.15 = (bf16[8,768,128]{2,1,0:T(8,128)(2,1)}, bf16[8,768,128]{2,1,0:T(8,128)(2,1)}, u32[]{:S(2)}, u32[]{:S(2)}) collective-permute-start(bf16[8,768,128]{2,1,0:T(8,128)(2,1)} %get-tuple-element.54.x_ref), channel_id=1, source_target_pairs={{0,4},{4,0},{1,5},{5,1},{2,6},{6,2},{3,7},{7,3},{8,12},{12,8},{9,1... | collective-permute-start | bytes 4718600 | tf_op jit(solution)/shard_map/ppermute | solution.py:881
  202.6 68.5 %collective-permute-start.14 = (bf16[8,768,128]{2,1,0:T(8,128)(2,1)}, bf16[8,768,128]{2,1,0:T(8,128)(2,1)}, u32[]{:S(2)}, u32[]{:S(2)}) collective-permute-start(bf16[8,768,128]{2,1,0:T(8,128)(2,1)} %collective-permute-done.13.x_ref), channel_id=1, source_target_pairs={{0,4},{4,0},{1,5},{5,1},{2,6},{6,2},{3,7},{7,3},{8,12},{12,8},{9,1... | collective-permute-start | bytes 4718600 | tf_op jit(solution)/shard_map/ppermute | solution.py:881
  243.5 74.5 %collective-permute-start.22 = (bf16[8,768,128]{2,1,0:T(8,128)(2,1)}, bf16[8,768,128]{2,1,0:T(8,128)(2,1)}, u32[]{:S(2)}, u32[]{:S(2)}) collective-permute-start(bf16[8,768,128]{2,1,0:T(8,128)(2,1)} %collective-permute-done.21.g_ref), channel_id=1, source_target_pairs={{0,4},{4,0},{1,5},{5,1},{2,6},{6,2},{3,7},{7,3},{8,12},{12,8},{9,1... | collective-permute-start | bytes 4718600 | tf_op jit(solution)/shard_map/ppermute | solution.py:881
  444.1 50.4 %collective-permute-start.38 = (f32[4,12576]{1,0:T(4,128)S(1)}, f32[4,12576]{1,0:T(4,128)}, u32[]{:S(2)}, u32[]{:S(2)}) collective-permute-start(f32[4,12576]{1,0:T(4,128)S(1)} %slice.348), channel_id=1, source_target_pairs={{0,16},{8,24},{16,0},{24,8},{1,17},{9,25},{17,1},{25,9},{2,18},{10... | collective-permute-start | bytes 603656 | tf_op jit(solution)/shard_map/ppermute | solution.py:881
  444.2 61.7 %collective-permute-start.25 = (bf16[8,768,128]{2,1,0:T(8,128)(2,1)}, bf16[8,768,128]{2,1,0:T(8,128)(2,1)}, u32[]{:S(2)}, u32[]{:S(2)}) collective-permute-start(bf16[8,768,128]{2,1,0:T(8,128)(2,1)} %shard_map.355), channel_id=1, source_target_pairs={{0,4},{4,0},{1,5},{5,1},{2,6},{6,2},{3,7},{7,3},{8,12},{12,8},{9,1... | collective-permute-start | bytes 4718600 | tf_op jit(solution)/shard_map/ppermute | solution.py:881
  444.5 77.1 %collective-permute-start.24 = (bf16[8,768,128]{2,1,0:T(8,128)(2,1)}, bf16[8,768,128]{2,1,0:T(8,128)(2,1)}, u32[]{:S(2)}, u32[]{:S(2)}) collective-permute-start(bf16[8,768,128]{2,1,0:T(8,128)(2,1)} %shard_map.354), channel_id=1, source_target_pairs={{0,4},{4,0},{1,5},{5,1},{2,6},{6,2},{3,7},{7,3},{8,12},{12,8},{9,1... | collective-permute-start | bytes 4718600 | tf_op jit(solution)/shard_map/ppermute | solution.py:881
  444.7 67.6 %collective-permute-start.17 = (bf16[8,768,128]{2,1,0:T(8,128)(2,1)}, bf16[8,768,128]{2,1,0:T(8,128)(2,1)}, u32[]{:S(2)}, u32[]{:S(2)}) collective-permute-start(bf16[8,768,128]{2,1,0:T(8,128)(2,1)} %shard_map.342), channel_id=1, source_target_pairs={{0,4},{4,0},{1,5},{5,1},{2,6},{6,2},{3,7},{7,3},{8,12},{12,8},{9,1... | collective-permute-start | bytes 4718600 | tf_op jit(solution)/shard_map/ppermute | solution.py:881
  445.0 155.7 %collective-permute-start.16 = (bf16[8,768,128]{2,1,0:T(8,128)(2,1)}, bf16[8,768,128]{2,1,0:T(8,128)(2,1)}, u32[]{:S(2)}, u32[]{:S(2)}) collective-permute-start(bf16[8,768,128]{2,1,0:T(8,128)(2,1)} %shard_map.341), channel_id=1, source_target_pairs={{0,4},{4,0},{1,5},{5,1},{2,6},{6,2},{3,7},{7,3},{8,12},{12,8},{9,1... | collective-permute-start | bytes 4718600 | tf_op jit(solution)/shard_map/ppermute | solution.py:881
  495.7 21.6 %collective-permute-start.39 = (f32[2,12576]{1,0:T(2,128)S(1)}, f32[2,12576]{1,0:T(2,128)S(1)}, u32[]{:S(2)}, u32[]{:S(2)}) collective-permute-start(f32[2,12576]{1,0:T(2,128)S(1)} %slice.350), channel_id=1, source_target_pairs={{0,8},{8,0},{16,24},{24,16},{1,9},{9,1},{17,25},{25,17},{2,10},{10... | collective-permute-start | bytes 301832 | tf_op jit(solution)/shard_map/ppermute | solution.py:881
  510.8 36.8 %collective-permute-start.26 = (bf16[8,768,128]{2,1,0:T(8,128)(2,1)S(1)}, bf16[8,768,128]{2,1,0:T(8,128)(2,1)S(1)}, u32[]{:S(2)}, u32[]{:S(2)}) collective-permute-start(bf16[8,768,128]{2,1,0:T(8,128)(2,1)S(1)} %shard_map.356), channel_id=1, source_target_pairs={{0,1},{1,0},{2,3},{3,2},{4,5},{5,4},{6,7},{7,6},{8,9},{9,8},{10,11... | collective-permute-start | bytes 4718600 | tf_op jit(solution)/shard_map/ppermute | solution.py:881
  517.1 90.0 %collective-permute-start.18 = (bf16[8,768,128]{2,1,0:T(8,128)(2,1)}, bf16[8,768,128]{2,1,0:T(8,128)(2,1)}, u32[]{:S(2)}, u32[]{:S(2)}) collective-permute-start(bf16[8,768,128]{2,1,0:T(8,128)(2,1)} %shard_map.343), channel_id=1, source_target_pairs={{0,1},{1,0},{2,3},{3,2},{4,5},{5,4},{6,7},{7,6},{8,9},{9,8},{10,11... | collective-permute-start | bytes 4718600 | tf_op jit(solution)/shard_map/ppermute | solution.py:881
  517.5 63.1 %collective-permute-start.40 = (f32[1,12576]{1,0:T(1,128)S(1)}, f32[1,12576]{1,0:T(1,128)S(1)}, u32[]{:S(2)}, u32[]{:S(2)}) collective-permute-start(f32[1,12576]{1,0:T(1,128)S(1)} %slice.352), channel_id=1, source_target_pairs={{0,2},{2,0},{1,3},{3,1},{4,6},{6,4},{5,7},{7,5},{8,10},{10,8},{9,1... | collective-permute-start | bytes 150920 | tf_op jit(solution)/shard_map/ppermute | solution.py:881
  558.1 84.2 %collective-permute-start.27 = (bf16[1024,768]{1,0:T(8,128)(2,1)}, bf16[1024,768]{1,0:T(8,128)(2,1)}, u32[]{:S(2)}, u32[]{:S(2)}) collective-permute-start(bf16[1024,768]{1,0:T(8,128)(2,1)} %get-tuple-element.77), channel_id=1, source_target_pairs={{0,0},{2,4},{4,2},{6,6},{1,1},{3,5},{5,3},{7,7},{8,8},{10,12},{12,... | collective-permute-start | bytes 4718600 | tf_op jit(solution)/shard_map/ppermute | solution.py:887
  584.6 16.1 %collective-permute-start.41 = (f32[48,262]{0,1:T(8,128)}, f32[48,262]{0,1:T(8,128)S(1)}, u32[]{:S(2)}, u32[]{:S(2)}) collective-permute-start(f32[48,262]{0,1:T(8,128)} %copy.198), channel_id=1, source_target_pairs={{0,0},{2,1},{8,2},{10,3},{16,4},{18,5},{24,6},{26,7},{1,8},{3,9},{... | collective-permute-start | bytes 150920 | tf_op jit(solution)/shard_map/ppermute | solution.py:993
  596.6 27.7 %collective-permute-start.33 = (bf16[6,192,384]{2,1,0:T(8,128)(2,1)S(1)}, bf16[6,192,384]{2,1,0:T(8,128)(2,1)S(1)}, u32[]{:S(2)}, u32[]{:S(2)}) collective-permute-start(bf16[6,192,384]{2,1,0:T(8,128)(2,1)S(1)} %copy-done.64), channel_id=1, source_target_pairs={{0,8},{8,0},{16,24},{24,16},{1,9},{9,1},{17,25},{25,17},{2,10},{10... | collective-permute-start | bytes 2654216 | tf_op jit(solution)/shard_map/ppermute | solution.py:881
  600.7 40.2 %collective-permute-start.34 = (bf16[6,192,384]{2,1,0:T(8,128)(2,1)S(1)}, bf16[6,192,384]{2,1,0:T(8,128)(2,1)S(1)}, u32[]{:S(2)}, u32[]{:S(2)}) collective-permute-start(bf16[6,192,384]{2,1,0:T(8,128)(2,1)S(1)} %copy-done.63), channel_id=1, source_target_pairs={{0,16},{8,24},{16,0},{24,8},{1,17},{9,25},{17,1},{25,9},{2,18},{10... | collective-permute-start | bytes 2654216 | tf_op jit(solution)/shard_map/ppermute | solution.py:881
  600.7 40.2 %collective-permute-start.35 = (bf16[6,192,384]{2,1,0:T(8,128)(2,1)S(1)}, bf16[6,192,384]{2,1,0:T(8,128)(2,1)S(1)}, u32[]{:S(2)}, u32[]{:S(2)}) collective-permute-start(bf16[6,192,384]{2,1,0:T(8,128)(2,1)S(1)} %copy-done.62), channel_id=1, source_target_pairs={{0,24},{8,16},{16,8},{24,0},{1,25},{9,17},{17,9},{25,1},{2,26},{10... | collective-permute-start | bytes 2654216 | tf_op jit(solution)/shard_map/ppermute | solution.py:881
  613.6 71.5 %collective-permute-start.19 = (bf16[1024,768]{1,0:T(8,128)(2,1)}, bf16[1024,768]{1,0:T(8,128)(2,1)}, u32[]{:S(2)}, u32[]{:S(2)}) collective-permute-start(bf16[1024,768]{1,0:T(8,128)(2,1)} %shard_map.344), channel_id=1, source_target_pairs={{0,0},{2,4},{4,2},{6,6},{1,1},{3,5},{5,3},{7,7},{8,8},{10,12},{12,... | collective-permute-start | bytes 4718600 | tf_op jit(solution)/shard_map/ppermute | solution.py:887
  642.3 42.8 %all-to-all-start.3 = ((bf16[8,128,768]{2,1,0:T(8,128)(2,1)}), bf16[8,128,768]{2,1,0:T(8,128)(2,1)S(1)}, u32[]{:S(2)}, u32[]{:S(2)}) async-start(bf16[8,128,768]{2,1,0:T(8,128)(2,1)} %bitcast.56), calls=%async_computation.3 | async-start | bytes 3145728 | tf_op jit(solution)/shard_map/all_to_all | solution.py:893
  650.2 27.3 %collective-permute-start.36 = (bf16[6,96,384]{2,1,0:T(8,128)(2,1)}, bf16[6,96,384]{2,1,0:T(8,128)(2,1)S(1)}, u32[]{:S(2)}, u32[]{:S(2)}) collective-permute-start(bf16[6,96,384]{2,1,0:T(8,128)(2,1)} %get-tuple-element.178), channel_id=1, source_target_pairs={{0,0},{2,4},{4,2},{6,6},{1,1},{3,5},{5,3},{7,7},{8,8},{10,12},{12,... | collective-permute-start | bytes 1327112 | tf_op jit(solution)/shard_map/ppermute | solution.py:887
  661.9 15.6 %collective-permute-start.37 = (bf16[6,96,384]{2,1,0:T(8,128)(2,1)}, bf16[6,96,384]{2,1,0:T(8,128)(2,1)}, u32[]{:S(2)}, u32[]{:S(2)}) collective-permute-start(bf16[6,96,384]{2,1,0:T(8,128)(2,1)} %get-tuple-element.179), channel_id=1, source_target_pairs={{0,4},{2,0},{4,6},{6,2},{1,5},{3,1},{5,7},{7,3},{8,12},{10,8},{12,... | collective-permute-start | bytes 1327112 | tf_op jit(solution)/shard_map/ppermute | solution.py:979
  663.4 5.8 collective-permute-start.28
  669.3 10.3 %collective-permute-start.29 = (f32[3,8,24]{2,0,1:T(4,128)S(1)}, f32[3,8,24]{2,0,1:T(4,128)S(1)}, u32[]{:S(2)}, u32[]{:S(2)}) collective-permute-start(f32[3,8,24]{2,0,1:T(4,128)S(1)} %slice.337), channel_id=1, source_target_pairs={{0,8},{8,0},{16,24},{24,16},{1,9},{9,1},{17,25},{25,17},{2,10},{10... | collective-permute-start | bytes 6920 | tf_op jit(solution)/shard_map/ppermute | solution.py:881
  679.5 11.9 %collective-permute-start.30 = (f32[3,4,24]{2,0,1:T(4,128)S(1)}, f32[3,4,24]{2,0,1:T(4,128)S(1)}, u32[]{:S(2)}, u32[]{:S(2)}) collective-permute-start(f32[3,4,24]{2,0,1:T(4,128)S(1)} %slice.339), channel_id=1, source_target_pairs={{0,4},{4,0},{1,5},{5,1},{2,6},{6,2},{3,7},{7,3},{8,12},{12,8},{9,1... | collective-permute-start | bytes 3464 | tf_op jit(solution)/shard_map/ppermute | solution.py:881
  685.1 21.8 %all-to-all-start.1 = ((bf16[8,128,768]{2,1,0:T(8,128)(2,1)}), bf16[8,128,768]{2,1,0:T(8,128)(2,1)S(1)}, u32[]{:S(2)}, u32[]{:S(2)}) async-start(bf16[8,128,768]{2,1,0:T(8,128)(2,1)} %bitcast.51), calls=%async_computation.1 | async-start | bytes 3145728 | tf_op jit(solution)/shard_map/all_to_all | solution.py:893
  691.5 3.4 collective-permute-start.31
  694.9 2.7 collective-permute-start.32
  (70 other events, 989.2 us)

commit v3 on v2

--- a/solution.py
+++ b/solution.py
@@ -729,12 +729,26 @@
     )(start // 2, w, *arrays, *([] if extra is None else [extra]))
 
 
-def outer_body(ch, many, cuts, at_ref, x_ref, g_ref, gp_ref, gpg_ref, mix_ref, *refs):
+def outer_body(ch, many, cuts, parts, at_ref, *refs):
     step = pl.program_id(0)
-    acc_s = refs[-1]
-
-    def flat(ref):
-        return jnp.concatenate([ref[b] for b in range(many)], axis=1)
+    xs, gs = refs[:parts], refs[parts : 2 * parts]
+    gp_ref, gpg_ref, mix_ref = refs[2 * parts : 2 * parts + 3]
+    outs = refs[2 * parts + 3 : 2 * parts + 3 + cuts]
+    acc_s, x_s, g_s = refs[-3:]
+
+    def fill(at):
+        for b in range(many):
+            x_s[:, b * BLK : (b + 1) * BLK] = xs[at][b]
+            g_s[:, b * BLK : (b + 1) * BLK] = gs[at][b]
+
+    if parts == 1:
+        fill(0)
+    else:
+        for at in range(parts):
+
+            @pl.when(step == at)
+            def _(at=at):
+                fill(at)
 
     def part(ref, k):
         return jnp.concatenate([ref[k, b] for b in range(many)], axis=1)
@@ -743,12 +757,10 @@
     def _():
         acc_s[...] = jnp.zeros_like(acc_s)
 
-    x = flat(x_ref)
-    g = flat(g_ref)
     for at, (left, ref, k) in enumerate(
-        [(x, gp_ref, 0), (x, gp_ref, 1), (x, gpg_ref, 0), (x, gpg_ref, 1), (g, mix_ref, 0), (g, mix_ref, 1)]
+        [(x_s, gp_ref, 0), (x_s, gp_ref, 1), (x_s, gpg_ref, 0), (x_s, gpg_ref, 1), (g_s, mix_ref, 0), (g_s, mix_ref, 1)]
     ):
-        acc_s[at] += nt(left, part(ref, k))
+        acc_s[at] += nt(left[...], part(ref, k))
 
     @pl.when(step == pl.num_programs(0) - 1)
     def _():
@@ -756,29 +768,178 @@
         for cut in range(cuts):
             start = pl.multiple_of(at_ref[pl.num_programs(0) + cut] * deep, 8)
             for at in range(6):
-                refs[cut][at] = acc_s[at, pl.ds(start, deep), :].astype(bf16)
-
-
-def outer_sums(order, cuts, xt, gt, gp, gpg, mix):
-    nb, width, _ = xt.shape
-    ch = gp.shape[2]
+                outs[cut][at] = acc_s[at, pl.ds(start, deep), :].astype(bf16)
+
+
+def outer_sums(order, cuts, xs, gs, gp, gpg, mix):
+    width = xs[0].shape[1]
+    _, nb, ch, _ = gp.shape
     many = 8
-    rows = pl.BlockSpec((many, width, BLK), lambda i, at: (i, 0, 0))
+    parts = len(xs)
+    if parts == 1:
+        rows = pl.BlockSpec((many, width, BLK), lambda i, at: (i, 0, 0))
+    else:
+        rows = pl.BlockSpec((many, width, BLK), lambda i, at: (0, 0, 0), pipeline_mode=pl.Buffered(1))
     chan = pl.BlockSpec((2, many, ch, BLK), lambda i, at: (0, at[i], 0, 0))
     tok = nb * BLK
     return pl.pallas_call(
-        partial(outer_body, ch, many, cuts),
+        partial(outer_body, ch, many, cuts, parts),
         grid_spec=pltpu.PrefetchScalarGridSpec(
             num_scalar_prefetch=1,
             grid=(nb // many,),
-            in_specs=[rows, rows, chan, chan, chan],
+            in_specs=[rows] * (2 * parts) + [chan, chan, chan],
             out_specs=[pl.BlockSpec((6, width // cuts, ch), lambda i, at: (0, 0, 0))] * cuts,
-            scratch_shapes=[pltpu.VMEM((6, width, ch), f32)],
+            scratch_shapes=[
+                pltpu.VMEM((6, width, ch), f32),
+                pltpu.VMEM((width, many * BLK), bf16),
+                pltpu.VMEM((width, many * BLK), bf16),
+            ],
         ),
         out_shape=[jax.ShapeDtypeStruct((6, width // cuts, ch), bf16)] * cuts,
-        compiler_params=params(56),
+        compiler_params=params(60),
         cost_estimate=cost(12 * tok * width * ch, tok * (4 * width + 12 * ch)),
-    )(order, xt, gt, gp, gpg, mix)
+    )(order, *xs, *gs, gp, gpg, mix)
+
+
+def meet_body(axes, rank_ref, x_ref, chan_ref, norm_ref, got_ref, call_ref, nall_ref, send_s, *sems):
+    xs_sem, xr_sem, cs_sem, cr_sem, ns_sem, nr_sem, own_sem = sems
+    q, c, h, w = (lax.axis_index(name) for name in axes)
+    rows = x_ref.shape[0]
+    piece = rows // 8
+    flat = ((2 * q + c) * 2 + h) * 2 + w
+
+    def peer(bits):
+        return (q ^ (bits // 8), c ^ (bits // 4 % 2), h ^ (bits // 2 % 2), w ^ (bits % 2))
+
+    barrier = pltpu.get_barrier_semaphore()
+    for bits in range(1, 32):
+        pl.semaphore_signal(barrier, inc=1, device_id=peer(bits), device_id_type=pl.DeviceIdType.MESH)
+    pl.semaphore_wait(barrier, 31)
+
+    def remote(src, dst, send, recv, to):
+        return pltpu.make_async_remote_copy(
+            src_ref=src, dst_ref=dst, send_sem=send, recv_sem=recv, device_id=to, device_id_type=pl.DeviceIdType.MESH
+        )
+
+    nall_ref[flat] = norm_ref[...]
+
+    def norm_copy(bits):
+        return remote(norm_ref, nall_ref.at[flat], ns_sem.at[bits], nr_sem.at[bits], peer(bits))
+
+    for bits in range(1, 32):
+        norm_copy(bits).start()
+
+    pieces = [(kq, kh) for kh in (1, 0) for kq in (1, 2, 3, 0)]
+    spot = lax.broadcasted_iota(jnp.int32, (piece, rows), 0)
+
+    def row_copy(kq, kh):
+        at = 2 * kq + kh
+        return remote(
+            send_s.at[at], got_ref.at[2 * q + c], xs_sem.at[at], xr_sem.at[2 * kq + c], (q ^ kq, h, h ^ kh, w)
+        )
+
+    def own_copy():
+        return pltpu.make_async_copy(send_s.at[0], got_ref.at[2 * q + c], own_sem.at[0])
+
+    for kq, kh in pieces:
+        chunk = 2 * (q ^ kq) + (h ^ kh)
+        pick = jnp.where(spot + chunk * piece == rank_ref[...], 1.0, 0.0).astype(bf16)
+        send_s[2 * kq + kh] = nn(pick, x_ref[...]).astype(bf16)
+        if (kq, kh) == (0, 0):
+
+            @pl.when(c == h)
+            def _():
+                own_copy().start()
+
+            @pl.when(c != h)
+            def _():
+                row_copy(0, 0).start()
+
+        else:
+            row_copy(kq, kh).start()
+
+    place = 2 * c + w
+    spot_c = 4 * c + 2 * h + w
+
+    def chan_copy(kq, kh):
+        at = 2 * kq + kh
+        return remote(
+            chan_ref, call_ref.at[spot_c], cs_sem.at[at], cr_sem.at[spot_c], (q ^ kq, q // 2, h ^ kh, q % 2)
+        )
+
+    def own_chan():
+        return pltpu.make_async_copy(chan_ref, call_ref.at[spot_c], own_sem.at[1])
+
+    for kq, kh in pieces:
+        if (kq, kh) == (0, 0):
+
+            @pl.when(place == q)
+            def _():
+                own_chan().start()
+
+            @pl.when(place != q)
+            def _():
+                chan_copy(0, 0).start()
+
+        else:
+            chan_copy(kq, kh).start()
+
+    for bits in range(1, 32):
+        norm_copy(bits).wait()
+    for at in range(8):
+
+        @pl.when((c == h) & (at == c))
+        def _():
+            own_copy().wait()
+
+        @pl.when(jnp.logical_not((c == h) & (at == c)))
+        def _(at=at):
+            remote(send_s.at[at], got_ref.at[at], xs_sem.at[at], xr_sem.at[at], peer(1)).wait_recv()
+
+    for at in range(8):
+
+        @pl.when((place == q) & (at == spot_c))
+        def _():
+            own_chan().wait()
+
+        @pl.when(jnp.logical_not((place == q) & (at == spot_c)))
+        def _(at=at):
+            remote(chan_ref, call_ref.at[at], cs_sem.at[at], cr_sem.at[at], peer(1)).wait_recv()
+
+    for kq, kh in pieces:
+        if (kq, kh) == (0, 0):
+
+            @pl.when(c != h)
+            def _():
+                row_copy(0, 0).wait_send()
+
+            @pl.when(place != q)
+            def _():
+                chan_copy(0, 0).wait_send()
+
+        else:
+            row_copy(kq, kh).wait_send()
+            chan_copy(kq, kh).wait_send()
+
+
+def meet(axes, rank, x, chan, norm):
+    rows, width = x.shape
+    vmem = pl.BlockSpec(memory_space=pltpu.VMEM)
+    sem = pltpu.SemaphoreType.DMA
+    return pl.pallas_call(
+        partial(meet_body, axes),
+        in_specs=[vmem] * 4,
+        out_specs=[vmem] * 3,
+        out_shape=[
+            jax.ShapeDtypeStruct((8, rows // 8, width), bf16),
+            jax.ShapeDtypeStruct((8,) + chan.shape, f32),
+            jax.ShapeDtypeStruct((32,) + norm.shape, f32),
+        ],
+        scratch_shapes=[pltpu.VMEM((8, rows // 8, width), bf16)]
+        + [sem((8,)), sem((8,)), sem((8,)), sem((8,)), sem((32,)), sem((32,)), sem((2,))],
+        compiler_params=pltpu.CompilerParams(collective_id=1, has_side_effects=True, vmem_limit_bytes=32 * MIB),
+        cost_estimate=cost(2 * rows * rows * width, 100 * rows * width),
+    )(rank.reshape(1, rows), x, chan, norm)
 
 
 def sequence_tables(lens, nb):
@@ -812,6 +973,10 @@
     return jnp.sum(inside.astype(f32), axis=1)
 
 
+def after(values):
+    return lax.optimization_barrier(values)
+
+
 def rank_of(keys):
     return jnp.sum((keys[None, :] < keys[:, None]).astype(jnp.int32), axis=1)
 
@@ -844,6 +1009,10 @@
 
     def order(self, pieces):
         return jnp.append(jnp.arange(pieces * self.n_t, dtype=jnp.int32), 0)
+
+    def enter(self, rank, x, chan, norm):
+        (sent,) = permute_to(rank, [x])
+        return (self.deal(sent),) + self.gather_channels(chan, norm)
 
     def gather_channels(self, chan, norm):
         perm = [(f, (f % self.n_dp) * self.n_t + f // self.n_dp) for f in range(self.n_dp * self.n_t)]
@@ -907,10 +1076,15 @@
 
     def scatter_rows(self, w, arrays, many):
         own, beside, near, far = self.starts(many)
-        give = self.flip(mul_rows(w, arrays, far, many), "c")
-        send = self.flip(mul_rows(w, arrays, near, many, extra=give), "w")
-        give = self.flip(mul_rows(w, arrays, beside, many), "c")
-        return [mul_rows(w, arrays, own, many, dtype=f32), give, send]
+        first = mul_rows(w, arrays, far, many)
+        give = self.flip(first, "c")
+        beside, first = after((beside, first))
+        second = mul_rows(w, arrays, beside, many)
+        second, give = after((second, give))
+        third = mul_rows(w, arrays, near, many, extra=give)
+        send = self.flip(third, "w")
+        own, third = after((own, third))
+        return [mul_rows(w, arrays, own, many, dtype=f32), self.flip(second, "c"), send]
 
     def order(self, pieces):
         place = jnp.stack(self.places())[:, None] * pieces + jnp.arange(pieces)[None, :]
@@ -927,29 +1101,16 @@
     def spot(self):
         return 2 * lax.axis_index("q") + lax.axis_index("h")
 
-    def gather_channels(self, chan, norm):
-        count = 2 * self.quads
-        perm = []
-        for f in range(4 * count):
-            place, at = f // count, f % count
-            q, h, c, w = at // 2, at % 2, place // 2, place % 2
-            perm.append((f, ((2 * q + c) * 2 + h) * 2 + w))
-        chan = lax.ppermute(chan, self.both, perm)
-        norm = norm.reshape(1, -1)
-        for axis in ("c", "w"):
-            norm = jnp.concatenate([norm, self.flip(norm, axis)], axis=0)
-        c, w = lax.axis_index("c"), lax.axis_index("w")
-        at = jnp.arange(4)
-        norm = jnp.take(norm, 2 * ((at % 2) ^ w) + ((at // 2) ^ c), axis=0)
-        flat = jnp.concatenate([chan.reshape(1, -1), norm.reshape(1, -1)], axis=1)
-        for axis, bit in reversed(list(self.steps())):
-            flat = jnp.concatenate([flat, self.flip(flat, axis, bit)], axis=0)
-        flat = jnp.take(flat, jnp.arange(count) ^ self.spot(), axis=0)
-        rows, wide = chan.shape
-        chan = flat[:, : rows * wide].reshape(count * rows, wide)
-        norm = flat[:, rows * wide :].reshape(self.quads, 2, 2, 2, 3, -1)
-        norm = norm.transpose(4, 0, 2, 1, 3, 5).reshape(3, -1)
-        return chan, norm
+    def enter(self, rank, x, chan, norm):
+        own, wide = chan.shape
+        small = norm.shape[1]
+        rows = -(-own * wide // 1024) * 8
+        chan = jnp.pad(chan.reshape(-1), (0, rows * BLK - own * wide)).reshape(rows, BLK)
+        norm = jnp.pad(norm, ((0, 5), (0, BLK - small)))
+        got, chan, norm = meet(self.both, rank, x, chan, norm)
+        chan = chan.reshape(8, -1)[:, : own * wide].reshape(8 * own, wide)
+        norm = norm[:, :3, :small].transpose(1, 0, 2).reshape(3, -1)
+        return got.reshape(x.shape), chan, norm
 
     def gather_weights(self, pack):
         h = lax.axis_index("h")
@@ -1019,10 +1180,6 @@
     rank = rank_of(target)
     sender = source // group
     place = rank_of(sender * rows + jnp.arange(rows, dtype=jnp.int32))
-    (sent_x,) = permute_to(rank, [tokens])
-    got_x = net.deal(sent_x)
-    (sent_g,) = permute_to(rank, [cotangent])
-    got_g = net.deal(sent_g)
     table = net.regroup(jnp.concatenate([place, lengths[0]]))
     place, lens = table[:rows], table[rows:]
 
@@ -1031,7 +1188,7 @@
         + [jnp.stack([log_dt[0], log_dt[1], ssm_d[0], ssm_d[1], b_fwd, b_bwd, b_gate[0], b_gate[1]], axis=1)],
         axis=1,
     )
-    chan_all, norm_all = net.gather_channels(chan, jnp.stack([ln_gain, ln_bias, b_out]))
+    got_x, chan_all, norm_all = net.enter(rank, tokens, chan, jnp.stack([ln_gain, ln_bias, b_out]))
 
     def lanes(column):
         return jnp.broadcast_to(column[..., None], column.shape + (BLK,))
@@ -1058,7 +1215,10 @@
     pack = jnp.concatenate(
         [w_fwd, w_bwd, w_gate.reshape(-1, 2 * ch), w_out.transpose(2, 0, 1).reshape(-1, 2 * ch)], axis=1
     )
+    pack, cotangent, got_x = after((pack, cotangent, got_x))
     w_all = net.gather_weights(pack)
+    (sent_g,) = permute_to(rank, [cotangent])
+    got_g = net.deal(sent_g)
     w_in, w_back = w_all[:, : 4 * ch], w_all[:, 4 * ch :]
     w_in_t, w_back_t = w_in.T, w_back.T
 
@@ -1088,19 +1248,15 @@
 
     gpg, gp, gh, bsum = ssm_back(tab, seq, a, gm, kh, wave, back, gg, y, dg, da)
     g_normed = net.scatter_rows(w_in, [gp, gpg], many)
-    gw = outer_sums(
-        net.order(many // 8),
-        net.cuts,
-        jnp.concatenate([part for part, _ in xs], axis=0),
-        jnp.concatenate([part for part, _ in gs], axis=0),
-        gp,
-        gpg,
-        mix,
-    )
+    mix, own_part = after((mix, g_normed[0]))
+    g_normed[0] = own_part
+    gw = outer_sums(net.order(many // 8), net.cuts, [part for part, _ in xs], [part for part, _ in gs], gp, gpg, mix)
+    gh, gw = after((gh, gw))
     gw = net.scatter_weights(gw)
+
+    sent_in, norm_sums = input_rows(place, g_normed, xd, gd, gain)
+    gh, sent_in = after((gh, sent_in))
     s0, s1, g0 = moments(ld_pairs, gh, back)
-
-    sent_in, norm_sums = input_rows(place, g_normed, xd, gd, gain)
     in_grad = permute_from(rank, net.undeal(sent_in))
 
     s0 = s0.reshape(2, ch, STATE)

time: 724 us -> 692 us (0.956); the launches traced: 711 us -> 687 us
  Pallas kernels: 320 us -> 396 us
  starting transfers between devices: 150 us -> 83 us
  waiting for transfers between devices: 126 us -> 101 us
  other arithmetic: 36.1 us -> 18.3 us
  local copies, waits for them, and re-layouts: 76.3 us -> 86 us
    pallas_call x1 -> x2, Pallas kernels: 27.7 us -> 89.9 us  [the longest x1 55.8 us: meet(): pl.pallas_call(partial(meet_body, axes), in_specs=[vmem] * 4, out_specs=[...]
    ppermute x31 -> x26, starting transfers between devices: 76.9 us -> 36.1 us  [flip(): return lax.ppermute(x, axis, [(i, i ^ bit) for i in range(self.axes[axis])])]
    all_to_all x2 -> x1, waiting for transfers between devices: 40.7 us -> 0.01 us  [deal(): lax.all_to_all(x, ('q', 'c'), split_axis=0, concat_axis=0, tiled=True)]
    ppermute x7 -> x6, starting transfers between devices: 42 us -> 24.6 us  [regroup(): return lax.ppermute(x, ('c', 'h'), self.crossed)]
    ppermute x1, waiting for transfers between devices: 0.01 us -> 16.4 us  [scatter_channels(): return lax.ppermute(part.reshape(rows // count, wide), self.both, perm)]
    pallas_call x1, Pallas kernels: 67.4 us -> 80.9 us  [ssm_back(): pl.pallas_call(partial(back_body, nb, nseq, cc, 16), grid=(2, ch // cc),...]
    concatenate x7 -> x1, other arithmetic: 14.2 us -> 0.8 us  [local(): jnp.concatenate([w_fwd, w_bwd, w_gate.reshape(-1, 2 * ch), w_out.transpos...]
    ppermute x7 -> x6, waiting for transfers between devices: 7.93 us -> 20.1 us  [regroup(): return lax.ppermute(x, ('c', 'h'), self.crossed)]
  transfers between devices with their start and end apart: 46 -> 38, of which waited for: 13 -> 10; matrix products, arithmetic and copies ran while one was open for 11% -> 8% of each run, Pallas kernels for 29% -> 49%
where the time goes in v3:
time: 692 us; the launch traced here: 687 us
  Pallas kernels  396 us (57%)
  waiting for transfers between devices  101 us (15%)
  local copies, waits for them, and re-layouts  86 us (12%)
  starting transfers between devices  83 us (12%)
  other arithmetic  18.3 us (3%)
    pallas_call x1, Pallas kernels, ssm_back(): pl.pallas_call(partial(back_body, nb, nseq, cc, 16), grid=(2, ch // cc),...  80.9 us
    ppermute x26, waiting for transfers between devices, flip(): return lax.ppermute(x, axis, [(i, i ^ bit) for i in range(self.axes[axis])])  60.2 us
    pallas_call x1, Pallas kernels, meet(): pl.pallas_call(partial(meet_body, axes), in_specs=[vmem] * 4, out_specs=[...  55.8 us
    pallas_call x8, Pallas kernels, chained(): pl.pallas_call(body, grid_spec=pltpu.PrefetchScalarGridSpec(num_scalar_pr...  54.6 us
    pallas_call x1, Pallas kernels, ssm_scan(): pl.pallas_call(partial(scan_body, nb, nseq, cc, 32), grid=(2, ch // cc),...  43.4 us
    unnamed x121, local copies, waits for them, and re-layouts  40.7 us
    ppermute x26, starting transfers between devices, flip(): return lax.ppermute(x, axis, [(i, i ^ bit) for i in range(self.axes[axis])])  36.1 us
    pallas_call x1, Pallas kernels, outer_sums(): pl.pallas_call(partial(outer_body, ch, many, cuts, parts), grid_spec=pltp...  34.1 us
  transfers between devices with their start and end apart: 38, of which 10 were waited for; matrix products, arithmetic and copies ran while one was open for 8% of the time, Pallas kernels for 49%

profile of v3, /device:TPU:1, one launch (start us, length us, event | category | flops | bytes accessed | tf_op | source)
XLA Modules:
  0.0 687.0 jit_solution(243017523745587823)
XLA Ops:
  12.2 55.8 %shard_map.332 = (bf16[8,128,768]{2,1,0:T(8,128)(2,1)S(1)}, f32[8,152,128]{2,1,0:T(8,128)S(1)}, f32[32,8,128]{2,1,0:T(8,128)S(1)}) custom-call(s32[1,1024]{1,0:T(1,128)S(1)} %bitcast.182, bf16[1024,768]{1,0:T(8,128)(2,1)S(1)} %copy-done.33, f32[152,128]{1,0:T(8,128)S(1)} %pad_bitcast_fusion.chan_ref, f32[8,128]{1,0:T(8,128)S(1)} %select_maximum_fusion.norm_ref), custom_call_target="tpu_custom_call" | custom-call | flops 1610612736 | bytes 78643200 | tf_op jit(solution)/shard_map/pallas_call | solution.py:929
  68.8 6.8 collective-permute-start.1
  83.2 4.7 all-to-all-start.1
  97.3 33.1 %shard_map.338.kh_ref = f32[2,8,384,512]{3,2,1,0:T(8,128)S(1)} custom-call(f32[2,192,128]{2,1,0:T(8,128)S(1)} %get-tuple-element.242.ld_ref, f32[2,192,128]{2,1,0:T(8,128)S(1)} %get-tuple-element.241.w_ref, f32[2,384,128]{2,1,0:T(8,128)S(1)} %broadcast_in_dim.112.d_ref, bf16[256,512]{1,0:T(8,128)(2,1)S(1)} %copy-done.38), custom_call_target="tpu_custom_call" | custom-call | flops 30720000000 | bytes 12582912 | tf_op jit(solution)/shard_map/pallas_call | solution.py:384
  130.4 4.6 copy-done.39
  137.5 6.8 shard_map.333
  155.8 3.9 collective-permute-start.13
  161.7 12.5 %collective-permute-done.3 = bf16[192,2304]{1,0:T(8,128)(2,1)} collective-permute-done((bf16[192,2304]{1,0:T(8,128)(2,1)S(1)}, bf16[192,2304]{1,0:T(8,128)(2,1)}, u32[]{:S(2)}, u32[]{:S(2)}) %collective-permute-start.3) | collective-permute-done | bytes 884768 | tf_op jit(solution)/shard_map/ppermute | solution.py:1050
  178.5 13.7 %collective-permute-done.5 = bf16[192,2304]{1,0:T(8,128)(2,1)} collective-permute-done((bf16[192,2304]{1,0:T(8,128)(2,1)S(1)}, bf16[192,2304]{1,0:T(8,128)(2,1)}, u32[]{:S(2)}, u32[]{:S(2)}) %collective-permute-start.5) | collective-permute-done | bytes 884768 | tf_op jit(solution)/shard_map/ppermute | solution.py:1050
  198.8 3.9 collective-permute-start.7
  202.7 5.6 shard_map.347
  208.3 4.8 fusion.20
  217.0 10.0 %shard_map.334 = (bf16[2,32,384,128]{3,2,1,0:T(8,128)(2,1)}, bf16[2,32,384,128]{3,2,1,0:T(8,128)(2,1)}, bf16[2,32,384,128]{3,2,1,0:T(8,128)(2,1)}, bf16[2,32,384,128]{3,2,1,0:T(8,128)(2,1)}) custom-call(s32[1]{0:T(128)S(6)} %select_n.160.start_ref, bf16[8,768,128]{2,1,0:T(8,128)(2,1)} %get-tuple-element.81.x_ref.refs_0_, f32[16,1,256]{2,1,0:T(1,128)S(1)} %bitcast.175, ...), custom_call_target="tpu_custom_call" | custom-call | flops 2415919104 | bytes 7864320 | tf_op jit(solution)/shard_map/pallas_call | solution.py:276
  227.0 10.1 %shard_map.335 = (bf16[2,32,384,128]{3,2,1,0:T(8,128)(2,1)}, bf16[2,32,384,128]{3,2,1,0:T(8,128)(2,1)}, bf16[2,32,384,128]{3,2,1,0:T(8,128)(2,1)}, bf16[2,32,384,128]{3,2,1,0:T(8,128)(2,1)}) custom-call(s32[1]{0:T(128)S(6)} %select_n.159.start_ref, ...), custom_call_target="tpu_custom_call", output_to_operand_aliasing={{0}: (5, {}), {1}: (6, {}), {2}: (7, {}), {3}: (8, {})} | custom-call | flops 2415919104 | bytes 7864320 | tf_op jit(solution)/shard_map/pallas_call | solution.py:276
  237.1 10.0 %shard_map.336 = (bf16[2,32,384,128]{3,2,1,0:T(8,128)(2,1)}, bf16[2,32,384,128]{3,2,1,0:T(8,128)(2,1)}, bf16[2,32,384,128]{3,2,1,0:T(8,128)(2,1)}, bf16[2,32,384,128]{3,2,1,0:T(8,128)(2,1)}) custom-call(s32[1]{0:T(128)S(6)} %select_n.146.start_ref, ...), custom_call_target="tpu_custom_call", output_to_operand_aliasing={{0}: (5, {}), {1}: (6, {}), {2}: (7, {}), {3}: (8, {})} | custom-call | flops 2415919104 | bytes 7864320 | tf_op jit(solution)/shard_map/pallas_call | solution.py:276
  247.2 3.7 shard_map.348.refs_0_
  250.9 10.1 %shard_map.337 = (bf16[2,32,384,128]{3,2,1,0:T(8,128)(2,1)}, bf16[2,32,384,128]{3,2,1,0:T(8,128)(2,1)}, bf16[2,32,384,128]{3,2,1,0:T(8,128)(2,1)}, bf16[2,32,384,128]{3,2,1,0:T(8,128)(2,1)}) custom-call(s32[1]{0:T(128)S(6)} %select_n.158.start_ref, ...), custom_call_target="tpu_custom_call", output_to_operand_aliasing={{0}: (5, {}), {1}: (6, {}), {2}: (7, {}), {3}: (8, {})} | custom-call | flops 2415919104 | bytes 7864320 | tf_op jit(solution)/shard_map/pallas_call | solution.py:276
  261.4 43.4 %shard_map.339 = (bf16[2,32,384,128]{3,2,1,0:T(8,128)(2,1)}, bf16[2,32,384,128]{3,2,1,0:T(8,128)(2,1)}) custom-call(s32[2,17]{1,0:T(2,128)} %pad_add_fusion.1.tab_ref, s32[2,4]{1,0:T(2,128)} %pad_add_fusion.2.seq_ref, bf16[2,32,384,128]{3,2,1,0:T(8,128)(2,1)} %get-tuple-element.95.a_ref, f32[2,8,384,512]{3,2,1,0:T(8,128)} %copy-done.39, ...), custom_call_target="tpu_custom_call" | custom-call | flops 38400000000 | bytes 25165824 | tf_op jit(solution)/shard_map/pallas_call | solution.py:654
  308.9 3.1 shard_map.340
  312.1 3.5 shard_map.349.refs_0_
  315.7 3.6 shard_map.350.refs_0_
  319.2 3.6 shard_map.351.gm_ref
  325.4 80.9 %shard_map.352 = (bf16[2,32,384,128]{3,2,1,0:T(8,128)(2,1)}, bf16[2,32,384,128]{3,2,1,0:T(8,128)(2,1)}, f32[2,8,384,512]{3,2,1,0:T(8,128)}, f32[2,384,256]{2,1,0:T(8,128)}) custom-call(s32[2,17]{1,0:T(2,128)} %pad_add_fusion.1.tab_ref, s32[2,4]{1,0:T(2,128)} %pad_add_fusion.2.seq_ref, bf16[2,32,384,128]{3,2,1,0:T(8,128)(2,1)} %get-tuple-element.95.a_ref, ...), custom_call_target="tpu_custom_call" | custom-call | flops 61440000000 | bytes 50331648 | tf_op jit(solution)/shard_map/pallas_call | solution.py:673
  410.7 5.5 shard_map.353
  420.1 3.1 shard_map.341
  425.9 4.7 shard_map.342
  432.1 4.6 shard_map.354
  437.8 5.7 shard_map.355
  443.6 4.5 shard_map.356.refs_0_
  449.8 34.1 %shard_map.357 = (bf16[6,192,384]{2,1,0:T(8,128)(2,1)}, bf16[6,192,384]{2,1,0:T(8,128)(2,1)}, bf16[6,192,384]{2,1,0:T(8,128)(2,1)}, bf16[6,192,384]{2,1,0:T(8,128)(2,1)}) custom-call(s32[8]{0:T(128)} %concatenate.41.at_ref, bf16[8,768,128]{2,1,0:T(8,128)(2,1)} %get-tuple-element.81.x_ref.refs_0_, bf16[8,768,128]{2,1,0:T(8,128)(2,1)} %collective-permute-done.8.x_ref.refs_1_, ...), custom_call_target="tpu_custom_call" | custom-call | flops 14495514624 | bytes 31457280 | tf_op jit(solution)/shard_map/pallas_call | solution.py:785
  494.7 5.3 shard_map.344
  500.1 3.9 collective-permute-start.12
  506.7 17.8 %collective-permute-done.27 = bf16[6,192,384]{2,1,0:T(8,128)(2,1)} collective-permute-done((bf16[6,192,384]{2,1,0:T(8,128)(2,1)}, bf16[6,192,384]{2,1,0:T(8,128)(2,1)}, u32[]{:S(2)}, u32[]{:S(2)}) %collective-permute-start.27) | collective-permute-done | bytes 884768 | tf_op jit(solution)/shard_map/ppermute | solution.py:1050
  527.7 5.0 collective-permute-start.29
  535.3 4.3 collective-permute-done.12
  539.6 4.3 all-to-all-start
  543.8 15.8 %collective-permute-done.29 = bf16[6,96,384]{2,1,0:T(8,128)(2,1)} collective-permute-done((bf16[6,96,384]{2,1,0:T(8,128)(2,1)}, bf16[6,96,384]{2,1,0:T(8,128)(2,1)}, u32[]{:S(2)}, u32[]{:S(2)}) %collective-permute-start.29) | collective-permute-done | bytes 442400 | tf_op jit(solution)/shard_map/ppermute | solution.py:1056
  559.7 4.7 collective-permute-done.30
  568.2 7.9 %shard_map.358 = (bf16[1024,768]{1,0:T(8,128)(2,1)S(1)}, f32[2,768,128]{2,1,0:T(8,128)S(1)}) custom-call(s32[1,1024]{1,0:T(1,128)S(1)} %bitcast.181, bf16[8,768,128]{2,1,0:T(8,128)(2,1)S(1)} %copy-done.15, bf16[8,768,128]{2,1,0:T(8,128)(2,1)S(1)} %copy-done.21, f32[768,128]{1,0:T(8,128)S(1)} %copy-done.17, f32[8,768,128]{2,1,0:T(8,128)} %copy-done.13, ...), custom_call_target="tpu_custom_call" | custom-call | flops 1610612736 | bytes 6291456 | tf_op jit(solution)/shard_map/pallas_call | solution.py:222
  576.2 5.1 copy-done.40
  581.3 25.0 %shard_map.360 = (f32[2,192,128]{2,1,0:T(8,128)S(1)}, f32[2,192,128]{2,1,0:T(8,128)S(1)}, f32[2,384,128]{2,1,0:T(8,128)S(1)}) custom-call(f32[2,192,128]{2,1,0:T(8,128)S(1)} %copy-done.26, f32[2,8,384,512]{3,2,1,0:T(8,128)S(1)} %copy-done.40, bf16[512,256]{1,0:T(8,128)(2,1)S(1)} %copy-done.37), custom_call_target="tpu_custom_call" | custom-call | flops 30720000000 | bytes 12582912 | tf_op jit(solution)/shard_map/pallas_call | solution.py:442
  614.9 4.4 shard_map.345
  622.3 15.0 %collective-permute-done.24 = f32[3,2,24]{2,0,1:T(4,128)S(1)} collective-permute-done((f32[3,2,24]{2,0,1:T(4,128)S(1)}, f32[3,2,24]{2,0,1:T(4,128)S(1)}, u32[]{:S(2)}, u32[]{:S(2)}) %collective-permute-start.24) | collective-permute-done | bytes 608 | tf_op jit(solution)/shard_map/ppermute | solution.py:1050
  637.3 13.0 %collective-permute-start.25 = (f32[3,1,24]{2,0,1:T(4,128)S(1)}, f32[3,1,24]{2,0,1:T(4,128)S(1)}, u32[]{:S(2)}, u32[]{:S(2)}) collective-permute-start(f32[3,1,24]{2,0,1:T(4,128)S(1)} %slice.338), channel_id=1, source_target_pairs={{0,1},{1,0},{2,3},{3,2},{4,5},{5,4},{6,7},{7,6},{8,9},{9,8},{10,11... | collective-permute-start | bytes 872 | tf_op jit(solution)/shard_map/ppermute | solution.py:1050
  650.4 3.2 collective-permute-start.33
  653.7 5.4 all-to-all-start.2
  659.5 3.6 collective-permute-start.34
  663.6 16.4 %collective-permute-done.34 = f32[48,262]{0,1:T(8,128)S(1)} collective-permute-done((f32[48,262]{0,1:T(8,128)S(1)}, f32[48,262]{0,1:T(8,128)S(1)}, u32[]{:S(2)}, u32[]{:S(2)}) %collective-permute-start.34) | collective-permute-done | bytes 50336 | tf_op jit(solution)/shard_map/ppermute | solution.py:1154
  (318 shorter events, 124.4 us)
Async XLA Ops:
  8.1 72.0 %copy-start.29 = (s32[1024]{0:T(1024)}, s32[1024]{0:T(1024)S(1)}, u32[]{:S(2)}) copy-start(s32[1024]{0:T(1024)S(1)} %convert_reduce_fusion.1) | copy-start | bytes 12292
  12.1 55.8 %copy-start.48 = (bf16[96,384]{1,0:T(8,128)(2,1)S(1)}, bf16[96,384]{1,0:T(8,128)(2,1)}, u32[]{:S(2)}) copy-start(bf16[96,384]{1,0:T(8,128)(2,1)} %param.30) | copy-start | bytes 221188
  12.1 55.8 %copy-start.49 = (bf16[96,384]{1,0:T(8,128)(2,1)S(1)}, bf16[96,384]{1,0:T(8,128)(2,1)}, u32[]{:S(2)}) copy-start(bf16[96,384]{1,0:T(8,128)(2,1)} %param.28) | copy-start | bytes 221188
  12.1 65.5 %copy-start.52 = (s32[1024]{0:T(1024)S(1)}, s32[1024]{0:T(1024)}, u32[]{:S(2)}) copy-start(s32[1024]{0:T(1024)} %param.23) | copy-start | bytes 12292
  12.1 66.1 %copy-start.53 = (s32[1,3]{1,0:T(1,128)S(1)}, s32[1,3]{1,0:T(1,128)}, u32[]{:S(2)}) copy-start(s32[1,3]{1,0:T(1,128)} %param.25) | copy-start | bytes 40
  12.1 68.1 %copy-start.34 = (bf16[1024,768]{1,0:T(8,128)(2,1)S(1)}, bf16[1024,768]{1,0:T(8,128)(2,1)}, u32[]{:S(2)}) copy-start(bf16[1024,768]{1,0:T(8,128)(2,1)} %refs_0_) | copy-start | bytes 4718596
  68.8 79.4 %collective-permute-start.1 = (bf16[96,2304]{1,0:T(8,128)(2,1)}, bf16[96,2304]{1,0:T(8,128)(2,1)}, u32[]{:S(2)}, u32[]{:S(2)}) collective-permute-start(bf16[96,2304]{1,0:T(8,128)(2,1)} %pad_maximum_fusion.1), channel_id=1, source_target_pairs={{0,0},{2,4},{4,2},{6,6},{1,1},{3,5},{5,3},{7,7},{8,8},{10,12},{12,... | collective-permute-start | bytes 1327112 | tf_op jit(solution)/shard_map/ppermute | solution.py:1056
  75.5 72.7 %collective-permute-start.2 = (bf16[96,2304]{1,0:T(8,128)(2,1)}, bf16[96,2304]{1,0:T(8,128)(2,1)}, u32[]{:S(2)}, u32[]{:S(2)}) collective-permute-start(bf16[96,2304]{1,0:T(8,128)(2,1)} %pad_maximum_fusion.1), channel_id=1, source_target_pairs={{4,0},{0,2},{6,4},{2,6},{5,1},{1,3},{7,5},{3,7},{12,8},{8,10},{14,... | collective-permute-start | bytes 1327112 | tf_op jit(solution)/shard_map/ppermute | solution.py:1119
  78.3 57.6 %collective-permute-start = (s32[1027]{0:T(1024)S(1)}, s32[1027]{0:T(1024)S(1)}, u32[]{:S(2)}, u32[]{:S(2)}) collective-permute-start(s32[1027]{0:T(1024)S(1)} %pad_add_fusion), channel_id=1, source_target_pairs={{0,0},{2,4},{4,2},{6,6},{1,1},{3,5},{5,3},{7,7},{8,8},{10,12},{12,... | collective-permute-start | bytes 12332 | tf_op jit(solution)/shard_map/ppermute | solution.py:1056
  83.2 72.7 %all-to-all-start.1 = ((bf16[8,128,768]{2,1,0:T(8,128)(2,1)}), bf16[8,128,768]{2,1,0:T(8,128)(2,1)}, u32[]{:S(2)}, u32[]{:S(2)}) async-start(bf16[8,128,768]{2,1,0:T(8,128)(2,1)} %bitcast.51), calls=%async_computation.1 | async-start | bytes 3145728 | tf_op jit(solution)/shard_map/all_to_all | solution.py:1059
  97.3 37.9 %copy-start.43 = (f32[4,384]{0,1:T(8,128)S(1)}, f32[4,384]{0,1:T(8,128)}, u32[]{:S(2)}) copy-start(f32[4,384]{0,1:T(8,128)} %slice_bitcast_fusion.3) | copy-start | bytes 18436
  145.4 53.3 %collective-permute-start.6 = (bf16[8,768,128]{2,1,0:T(8,128)(2,1)}, bf16[8,768,128]{2,1,0:T(8,128)(2,1)}, u32[]{:S(2)}, u32[]{:S(2)}) collective-permute-start(bf16[8,768,128]{2,1,0:T(8,128)(2,1)} %get-tuple-element.81.x_ref.refs_0_), channel_id=1, source_target_pairs={{0,1},{1,0},{2,3},{3,2},{4,5},{5,4},{6,7},{7,6},{8,9},{9,8},{10,11... | collective-permute-start | bytes 4718600 | tf_op jit(solution)/shard_map/ppermute | solution.py:1050
  152.4 21.8 %collective-permute-start.3 = (bf16[192,2304]{1,0:T(8,128)(2,1)S(1)}, bf16[192,2304]{1,0:T(8,128)(2,1)}, u32[]{:S(2)}, u32[]{:S(2)}) collective-permute-start(bf16[192,2304]{1,0:T(8,128)(2,1)S(1)} %get-tuple-element.229), channel_id=1, source_target_pairs={{0,8},{8,0},{16,24},{24,16},{1,9},{9,1},{17,25},{25,17},{2,10},{10... | collective-permute-start | bytes 2654216 | tf_op jit(solution)/shard_map/ppermute | solution.py:1050
  152.8 23.6 %collective-permute-start.4 = (bf16[192,2304]{1,0:T(8,128)(2,1)S(1)}, bf16[192,2304]{1,0:T(8,128)(2,1)}, u32[]{:S(2)}, u32[]{:S(2)}) collective-permute-start(bf16[192,2304]{1,0:T(8,128)(2,1)S(1)} %get-tuple-element.229), channel_id=1, source_target_pairs={{0,16},{8,24},{16,0},{24,8},{1,17},{9,25},{17,1},{25,9},{2,18},{10... | collective-permute-start | bytes 2654216 | tf_op jit(solution)/shard_map/ppermute | solution.py:1050
  154.9 37.3 %collective-permute-start.5 = (bf16[192,2304]{1,0:T(8,128)(2,1)S(1)}, bf16[192,2304]{1,0:T(8,128)(2,1)}, u32[]{:S(2)}, u32[]{:S(2)}) collective-permute-start(bf16[192,2304]{1,0:T(8,128)(2,1)S(1)} %get-tuple-element.229), channel_id=1, source_target_pairs={{0,24},{8,16},{16,8},{24,0},{1,25},{9,17},{17,9},{25,1},{2,26},{10... | collective-permute-start | bytes 2654216 | tf_op jit(solution)/shard_map/ppermute | solution.py:1050
  155.8 46.9 %collective-permute-start.13 = (bf16[1024,768]{1,0:T(8,128)(2,1)}, bf16[1024,768]{1,0:T(8,128)(2,1)S(1)}, u32[]{:S(2)}, u32[]{:S(2)}) collective-permute-start(bf16[1024,768]{1,0:T(8,128)(2,1)} %bitcast.52), channel_id=1, source_target_pairs={{0,0},{2,4},{4,2},{6,6},{1,1},{3,5},{5,3},{7,7},{8,8},{10,12},{12,... | collective-permute-start | bytes 4718600 | tf_op jit(solution)/shard_map/ppermute | solution.py:1056
  161.1 41.6 %copy-start.31 = (f32[1024]{0:T(1024)}, f32[1024]{0:T(1024)S(1)}, u32[]{:S(2)}) copy-start(f32[1024]{0:T(1024)S(1)} %dynamic_slice.3) | copy-start | bytes 12292
  174.2 52.8 %collective-permute-start.8 = (bf16[8,768,128]{2,1,0:T(8,128)(2,1)}, bf16[8,768,128]{2,1,0:T(8,128)(2,1)}, u32[]{:S(2)}, u32[]{:S(2)}) collective-permute-start(bf16[8,768,128]{2,1,0:T(8,128)(2,1)} %get-tuple-element.81.x_ref.refs_0_), channel_id=1, source_target_pairs={{0,4},{4,0},{1,5},{5,1},{2,6},{6,2},{3,7},{7,3},{8,12},{12,8},{9,1... | collective-permute-start | bytes 4718600 | tf_op jit(solution)/shard_map/ppermute | solution.py:1050
  198.8 52.1 %collective-permute-start.7 = (bf16[8,768,128]{2,1,0:T(8,128)(2,1)}, bf16[8,768,128]{2,1,0:T(8,128)(2,1)}, u32[]{:S(2)}, u32[]{:S(2)}) collective-permute-start(bf16[8,768,128]{2,1,0:T(8,128)(2,1)} %collective-permute-done.6.x_ref.refs_2_), channel_id=1, source_target_pairs={{0,4},{4,0},{1,5},{5,1},{2,6},{6,2},{3,7},{7,3},{8,12},{12,8},{9,1... | collective-permute-start | bytes 4718600 | tf_op jit(solution)/shard_map/ppermute | solution.py:1050
  208.3 52.7 %collective-permute-start.14 = (bf16[8,768,128]{2,1,0:T(8,128)(2,1)}, bf16[8,768,128]{2,1,0:T(8,128)(2,1)}, u32[]{:S(2)}, u32[]{:S(2)}) collective-permute-start(bf16[8,768,128]{2,1,0:T(8,128)(2,1)} %get-tuple-element.103.g_ref.refs_4_), channel_id=1, source_target_pairs={{0,1},{1,0},{2,3},{3,2},{4,5},{5,4},{6,7},{7,6},{8,9},{9,8},{10,11... | collective-permute-start | bytes 4718600 | tf_op jit(solution)/shard_map/ppermute | solution.py:1050
  247.1 65.0 %collective-permute-start.16 = (bf16[8,768,128]{2,1,0:T(8,128)(2,1)}, bf16[8,768,128]{2,1,0:T(8,128)(2,1)}, u32[]{:S(2)}, u32[]{:S(2)}) collective-permute-start(bf16[8,768,128]{2,1,0:T(8,128)(2,1)} %get-tuple-element.103.g_ref.refs_4_), channel_id=1, source_target_pairs={{0,4},{4,0},{1,5},{5,1},{2,6},{6,2},{3,7},{7,3},{8,12},{12,8},{9,1... | collective-permute-start | bytes 4718600 | tf_op jit(solution)/shard_map/ppermute | solution.py:1050
  261.0 58.2 %collective-permute-start.15 = (bf16[8,768,128]{2,1,0:T(8,128)(2,1)}, bf16[8,768,128]{2,1,0:T(8,128)(2,1)}, u32[]{:S(2)}, u32[]{:S(2)}) collective-permute-start(bf16[8,768,128]{2,1,0:T(8,128)(2,1)} %collective-permute-done.14.g_ref.refs_6_), channel_id=1, source_target_pairs={{0,4},{4,0},{1,5},{5,1},{2,6},{6,2},{3,7},{7,3},{8,12},{12,8},{9,1... | collective-permute-start | bytes 4718600 | tf_op jit(solution)/shard_map/ppermute | solution.py:1050
  312.0 111.2 %collective-permute-start.9 = (bf16[8,768,128]{2,1,0:T(8,128)(2,1)}, bf16[8,768,128]{2,1,0:T(8,128)(2,1)}, u32[]{:S(2)}, u32[]{:S(2)}) collective-permute-start(bf16[8,768,128]{2,1,0:T(8,128)(2,1)} %shard_map.340), channel_id=1, source_target_pairs={{0,4},{4,0},{1,5},{5,1},{2,6},{6,2},{3,7},{7,3},{8,12},{12,8},{9,1... | collective-permute-start | bytes 4718600 | tf_op jit(solution)/shard_map/ppermute | solution.py:1050
  416.3 21.6 %collective-permute-start.17 = (bf16[8,768,128]{2,1,0:T(8,128)(2,1)}, bf16[8,768,128]{2,1,0:T(8,128)(2,1)}, u32[]{:S(2)}, u32[]{:S(2)}) collective-permute-start(bf16[8,768,128]{2,1,0:T(8,128)(2,1)} %shard_map.353), channel_id=1, source_target_pairs={{0,4},{4,0},{1,5},{5,1},{2,6},{6,2},{3,7},{7,3},{8,12},{12,8},{9,1... | collective-permute-start | bytes 4718600 | tf_op jit(solution)/shard_map/ppermute | solution.py:1050
  430.6 63.9 %collective-permute-start.11 = (bf16[8,768,128]{2,1,0:T(8,128)(2,1)}, bf16[8,768,128]{2,1,0:T(8,128)(2,1)}, u32[]{:S(2)}, u32[]{:S(2)}) collective-permute-start(bf16[8,768,128]{2,1,0:T(8,128)(2,1)} %shard_map.342), channel_id=1, source_target_pairs={{0,1},{1,0},{2,3},{3,2},{4,5},{5,4},{6,7},{7,6},{8,9},{9,8},{10,11... | collective-permute-start | bytes 4718600 | tf_op jit(solution)/shard_map/ppermute | solution.py:1050
  431.4 63.1 %collective-permute-start.10 = (bf16[8,768,128]{2,1,0:T(8,128)(2,1)}, bf16[8,768,128]{2,1,0:T(8,128)(2,1)}, u32[]{:S(2)}, u32[]{:S(2)}) collective-permute-start(bf16[8,768,128]{2,1,0:T(8,128)(2,1)} %shard_map.341), channel_id=1, source_target_pairs={{0,4},{4,0},{1,5},{5,1},{2,6},{6,2},{3,7},{7,3},{8,12},{12,8},{9,1... | collective-permute-start | bytes 4718600 | tf_op jit(solution)/shard_map/ppermute | solution.py:1050
  449.7 37.0 %copy-start.30 = (s32[1024]{0:T(1024)S(1)}, s32[1024]{0:T(1024)}, u32[]{:S(2)}) copy-start(s32[1024]{0:T(1024)} %copy-done.29) | copy-start | bytes 12292
  449.8 38.1 %copy-start.50 = (f32[32,24]{1,0:T(8,128)S(1)}, f32[32,24]{1,0:T(8,128)}, u32[]{:S(2)}) copy-start(f32[32,24]{1,0:T(8,128)} %get-tuple-element.205) | copy-start | bytes 9220
  483.9 21.6 %collective-permute-start.26 = (bf16[6,192,384]{2,1,0:T(8,128)(2,1)}, bf16[6,192,384]{2,1,0:T(8,128)(2,1)}, u32[]{:S(2)}, u32[]{:S(2)}) collective-permute-start(bf16[6,192,384]{2,1,0:T(8,128)(2,1)} %get-tuple-element.127), channel_id=1, source_target_pairs={{0,8},{8,0},{16,24},{24,16},{1,9},{9,1},{17,25},{25,17},{2,10},{10... | collective-permute-start | bytes 2654216 | tf_op jit(solution)/shard_map/ppermute | solution.py:1050
  483.9 40.6 %collective-permute-start.27 = (bf16[6,192,384]{2,1,0:T(8,128)(2,1)}, bf16[6,192,384]{2,1,0:T(8,128)(2,1)}, u32[]{:S(2)}, u32[]{:S(2)}) collective-permute-start(bf16[6,192,384]{2,1,0:T(8,128)(2,1)} %get-tuple-element.128), channel_id=1, source_target_pairs={{0,16},{8,24},{16,0},{24,8},{1,17},{9,25},{17,1},{25,9},{2,18},{10... | collective-permute-start | bytes 2654216 | tf_op jit(solution)/shard_map/ppermute | solution.py:1050
  484.0 40.5 %collective-permute-start.28 = (bf16[6,192,384]{2,1,0:T(8,128)(2,1)}, bf16[6,192,384]{2,1,0:T(8,128)(2,1)}, u32[]{:S(2)}, u32[]{:S(2)}) collective-permute-start(bf16[6,192,384]{2,1,0:T(8,128)(2,1)} %get-tuple-element.129), channel_id=1, source_target_pairs={{0,24},{8,16},{16,8},{24,0},{1,25},{9,17},{17,9},{25,1},{2,26},{10... | collective-permute-start | bytes 2654216 | tf_op jit(solution)/shard_map/ppermute | solution.py:1050
  500.1 39.5 %collective-permute-start.12 = (bf16[1024,768]{1,0:T(8,128)(2,1)S(1)}, bf16[1024,768]{1,0:T(8,128)(2,1)}, u32[]{:S(2)}, u32[]{:S(2)}) collective-permute-start(bf16[1024,768]{1,0:T(8,128)(2,1)S(1)} %shard_map.344), channel_id=1, source_target_pairs={{0,0},{2,4},{4,2},{6,6},{1,1},{3,5},{5,3},{7,7},{8,8},{10,12},{12,... | collective-permute-start | bytes 4718600 | tf_op jit(solution)/shard_map/ppermute | solution.py:1056
  504.1 64.1 %collective-permute-start.19 = (bf16[8,768,128]{2,1,0:T(8,128)(2,1)}, bf16[8,768,128]{2,1,0:T(8,128)(2,1)}, u32[]{:S(2)}, u32[]{:S(2)}) collective-permute-start(bf16[8,768,128]{2,1,0:T(8,128)(2,1)} %shard_map.355), channel_id=1, source_target_pairs={{0,1},{1,0},{2,3},{3,2},{4,5},{5,4},{6,7},{7,6},{8,9},{9,8},{10,11... | collective-permute-start | bytes 4718600 | tf_op jit(solution)/shard_map/ppermute | solution.py:1050
  505.5 62.7 %collective-permute-start.18 = (bf16[8,768,128]{2,1,0:T(8,128)(2,1)S(1)}, bf16[8,768,128]{2,1,0:T(8,128)(2,1)}, u32[]{:S(2)}, u32[]{:S(2)}) collective-permute-start(bf16[8,768,128]{2,1,0:T(8,128)(2,1)S(1)} %copy-done.19), channel_id=1, source_target_pairs={{0,4},{4,0},{1,5},{5,1},{2,6},{6,2},{3,7},{7,3},{8,12},{12,8},{9,1... | collective-permute-start | bytes 4718600 | tf_op jit(solution)/shard_map/ppermute | solution.py:1050
  527.7 32.0 %collective-permute-start.29 = (bf16[6,96,384]{2,1,0:T(8,128)(2,1)}, bf16[6,96,384]{2,1,0:T(8,128)(2,1)}, u32[]{:S(2)}, u32[]{:S(2)}) collective-permute-start(bf16[6,96,384]{2,1,0:T(8,128)(2,1)} %get-tuple-element.227), channel_id=1, source_target_pairs={{0,0},{2,4},{4,2},{6,6},{1,1},{3,5},{5,3},{7,7},{8,8},{10,12},{12,... | collective-permute-start | bytes 1327112 | tf_op jit(solution)/shard_map/ppermute | solution.py:1056
  532.7 31.7 %collective-permute-start.30 = (bf16[6,96,384]{2,1,0:T(8,128)(2,1)}, bf16[6,96,384]{2,1,0:T(8,128)(2,1)}, u32[]{:S(2)}, u32[]{:S(2)}) collective-permute-start(bf16[6,96,384]{2,1,0:T(8,128)(2,1)} %get-tuple-element.228), channel_id=1, source_target_pairs={{0,4},{2,0},{4,6},{6,2},{1,5},{3,1},{5,7},{7,3},{8,12},{10,8},{12,... | collective-permute-start | bytes 1327112 | tf_op jit(solution)/shard_map/ppermute | solution.py:1140
  539.6 75.3 %all-to-all-start = ((bf16[8,128,768]{2,1,0:T(8,128)(2,1)}), bf16[8,128,768]{2,1,0:T(8,128)(2,1)}, u32[]{:S(2)}, u32[]{:S(2)}) async-start(bf16[8,128,768]{2,1,0:T(8,128)(2,1)} %bitcast.49), calls=%async_computation | async-start | bytes 3145728 | tf_op jit(solution)/shard_map/all_to_all | solution.py:1062
  607.8 2.8 collective-permute-start.21
  610.6 4.1 collective-permute-start.22
  611.1 9.9 %collective-permute-start.31 = (f32[4,12576]{1,0:T(4,128)S(1)}, f32[4,12576]{1,0:T(4,128)S(1)}, u32[]{:S(2)}, u32[]{:S(2)}) collective-permute-start(f32[4,12576]{1,0:T(4,128)S(1)} %slice.343), channel_id=1, source_target_pairs={{0,16},{8,24},{16,0},{24,8},{1,17},{9,25},{17,1},{25,9},{2,18},{10... | collective-permute-start | bytes 603656 | tf_op jit(solution)/shard_map/ppermute | solution.py:1050
  611.6 42.0 %collective-permute-start.20 = (bf16[1024,768]{1,0:T(8,128)(2,1)S(1)}, bf16[1024,768]{1,0:T(8,128)(2,1)}, u32[]{:S(2)}, u32[]{:S(2)}) collective-permute-start(bf16[1024,768]{1,0:T(8,128)(2,1)S(1)} %copy-done.36), channel_id=1, source_target_pairs={{0,0},{2,4},{4,2},{6,6},{1,1},{3,5},{5,3},{7,7},{8,8},{10,12},{12,... | collective-permute-start | bytes 4718600 | tf_op jit(solution)/shard_map/ppermute | solution.py:1056
  614.8 4.5 collective-permute-start.23
  619.3 18.0 %collective-permute-start.24 = (f32[3,2,24]{2,0,1:T(4,128)S(1)}, f32[3,2,24]{2,0,1:T(4,128)S(1)}, u32[]{:S(2)}, u32[]{:S(2)}) collective-permute-start(f32[3,2,24]{2,0,1:T(4,128)S(1)} %slice.336), channel_id=1, source_target_pairs={{0,2},{2,0},{1,3},{3,1},{4,6},{6,4},{5,7},{7,5},{8,10},{10,8},{9,1... | collective-permute-start | bytes 1736 | tf_op jit(solution)/shard_map/ppermute | solution.py:1050
  621.1 29.2 %collective-permute-start.32 = (f32[2,12576]{1,0:T(2,128)S(1)}, f32[2,12576]{1,0:T(2,128)S(1)}, u32[]{:S(2)}, u32[]{:S(2)}) collective-permute-start(f32[2,12576]{1,0:T(2,128)S(1)} %slice.345), channel_id=1, source_target_pairs={{0,8},{8,0},{16,24},{24,16},{1,9},{9,1},{17,25},{25,17},{2,10},{10... | collective-permute-start | bytes 301832 | tf_op jit(solution)/shard_map/ppermute | solution.py:1050
  637.3 16.3 %collective-permute-start.25 = (f32[3,1,24]{2,0,1:T(4,128)S(1)}, f32[3,1,24]{2,0,1:T(4,128)S(1)}, u32[]{:S(2)}, u32[]{:S(2)}) collective-permute-start(f32[3,1,24]{2,0,1:T(4,128)S(1)} %slice.338), channel_id=1, source_target_pairs={{0,1},{1,0},{2,3},{3,2},{4,5},{5,4},{6,7},{7,6},{8,9},{9,8},{10,11... | collective-permute-start | bytes 872 | tf_op jit(solution)/shard_map/ppermute | solution.py:1050
  650.4 8.7 %collective-permute-start.33 = (f32[1,12576]{1,0:T(1,128)S(1)}, f32[1,12576]{1,0:T(1,128)S(1)}, u32[]{:S(2)}, u32[]{:S(2)}) collective-permute-start(f32[1,12576]{1,0:T(1,128)S(1)} %slice.347), channel_id=1, source_target_pairs={{0,2},{2,0},{1,3},{3,1},{4,6},{6,4},{5,7},{7,5},{8,10},{10,8},{9,1... | collective-permute-start | bytes 150920 | tf_op jit(solution)/shard_map/ppermute | solution.py:1050
  653.7 30.2 %all-to-all-start.2 = ((bf16[8,128,768]{2,1,0:T(8,128)(2,1)}), bf16[8,128,768]{2,1,0:T(8,128)(2,1)S(1)}, u32[]{:S(2)}, u32[]{:S(2)}) async-start(bf16[8,128,768]{2,1,0:T(8,128)(2,1)} %bitcast.58), calls=%async_computation.2 | async-start | bytes 3145728 | tf_op jit(solution)/shard_map/all_to_all | solution.py:1062
  659.5 20.4 %collective-permute-start.34 = (f32[48,262]{0,1:T(8,128)S(1)}, f32[48,262]{0,1:T(8,128)S(1)}, u32[]{:S(2)}, u32[]{:S(2)}) collective-permute-start(f32[48,262]{0,1:T(8,128)S(1)} %copy.189), channel_id=1, source_target_pairs={{0,0},{2,1},{8,2},{10,3},{16,4},{18,5},{24,6},{26,7},{1,8},{3,9},{... | collective-permute-start | bytes 150920 | tf_op jit(solution)/shard_map/ppermute | solution.py:1154
  (46 other events, 528.5 us)

commit v4 on v3

--- a/solution.py
+++ b/solution.py
@@ -33,7 +33,10 @@
 
 
 def cost(flops, moved, trans=0):
-    return pl.CostEstimate(flops=int(flops), bytes_accessed=int(moved), transcendentals=int(trans))
+    scale = 0.05
+    return pl.CostEstimate(
+        flops=int(scale * flops), bytes_accessed=int(scale * moved), transcendentals=int(scale * trans)
+    )
 
 
 def halves(x):
@@ -435,24 +438,24 @@
     lax.fori_loop(0, cc // 2, one, 0, unroll=4)
 
 
-def moments(ld, gh, back):
+def moments(k, ld, gh, back):
     ch = gh.shape[2]
     cc = chunk_of(ch, 128)
-    row = pl.BlockSpec((1, cc // 2, BLK), lambda k, i: (k, i, 0))
+    row = pl.BlockSpec((1, cc // 2, BLK), lambda i: (0, i, 0))
     return pl.pallas_call(
         partial(moments_body, cc),
-        grid=(2, ch // cc),
+        grid=(ch // cc,),
         in_specs=[
-            row,
-            pl.BlockSpec((1, LAGS, cc, 2 * BIG), lambda k, i: (k, 0, i, 0)),
-            pl.BlockSpec((2 * BIG, BIG), lambda k, i: (0, 0)),
+            pl.BlockSpec((1, cc // 2, BLK), lambda i: (k, i, 0)),
+            pl.BlockSpec((1, LAGS, cc, 2 * BIG), lambda i: (0, 0, i, 0)),
+            pl.BlockSpec((2 * BIG, BIG), lambda i: (0, 0)),
         ],
-        out_specs=[row, row, pl.BlockSpec((1, cc, BLK), lambda k, i: (k, i, 0))],
-        out_shape=[jax.ShapeDtypeStruct((2, ch // 2, BLK), f32)] * 2
-        + [jax.ShapeDtypeStruct((2, ch, BLK), f32)],
+        out_specs=[row, row, pl.BlockSpec((1, cc, BLK), lambda i: (0, i, 0))],
+        out_shape=[jax.ShapeDtypeStruct((1, ch // 2, BLK), f32)] * 2
+        + [jax.ShapeDtypeStruct((1, ch, BLK), f32)],
         scratch_shapes=[pltpu.VMEM((2 * LAGS * cc, BLK), f32)],
         compiler_params=params(40),
-        cost_estimate=cost(2 * ch * 40e6, 2 * ch * LAGS * 2 * BIG * 4),
+        cost_estimate=cost(ch * 40e6, ch * LAGS * 2 * BIG * 4),
     )(ld, gh, back)
 
 
@@ -552,7 +555,7 @@
 
 
 def back_body(
-    nb, nseq, cc, rg, tab_ref, seq_ref, a_ref, gm_ref, kh_ref, wave_ref, back_ref, gg_ref, y_ref, dg_ref, da_ref,
+    nb, nseq, cc, rg, flip, tab_ref, seq_ref, a_ref, gm_ref, kh_ref, wave_ref, back_ref, gg_ref, y_ref, dg_ref, da_ref,
     gpg_ref, gp_ref, gh_ref, bs_ref, in_s, ah_s, gh_s, xh_s, x_s,
 ):
     pieces = (nb + nseq) // 2
@@ -563,41 +566,32 @@
     gh_ref[...] = jnp.zeros_like(gh_ref)
     zero = jnp.zeros((rg, BIG), f32)
 
-    def products(flip):
-        def piece(i, count, base, off):
-            at = pl.ds(pl.multiple_of((base + i) * cc + off, rg), rg)
-            ac = ah_s[at, :BIG]
-            as_ = ah_s[at, BIG:]
-
-            def inner(j, acc):
-                xc, xs = acc
-                other = (base + i - j) if flip else (base + i + j)
-                m = pl.ds(pl.multiple_of(other * cc + off, rg), rg)
-                rows = pl.ds(off, rg)
-                gc = gh_s[m, :BIG]
-                gs = gh_s[m, BIG:]
-                kc = kh_ref[0, j, rows, :BIG]
-                ks = kh_ref[0, j, rows, BIG:]
-                gh_ref[0, j, rows, :BIG] += ac * gc + as_ * gs
-                if flip:
-                    gh_ref[0, j, rows, BIG:] += gc * as_ - gs * ac
-                    return (xc + kc * gc - ks * gs, xs + kc * gs + ks * gc)
-                gh_ref[0, j, rows, BIG:] += ac * gs - as_ * gc
-                return (xc + kc * gc + ks * gs, xs + kc * gs - ks * gc)
-
-            xc, xs = lax.fori_loop(0, (i + 1) if flip else (count - i), inner, (zero, zero))
-            xh_s[at, :BIG] = xc.astype(bf16)
-            xh_s[at, BIG:] = xs.astype(bf16)
-
-        over_pieces(nseq, cc, rg, seq_ref, piece)
-
-    @pl.when(pl.program_id(0) == 0)
-    def _():
-        products(False)
-
-    @pl.when(pl.program_id(0) == 1)
-    def _():
-        products(True)
+    def piece(i, count, base, off):
+        at = pl.ds(pl.multiple_of((base + i) * cc + off, rg), rg)
+        ac = ah_s[at, :BIG]
+        as_ = ah_s[at, BIG:]
+
+        def inner(j, acc):
+            xc, xs = acc
+            other = (base + i - j) if flip else (base + i + j)
+            m = pl.ds(pl.multiple_of(other * cc + off, rg), rg)
+            rows = pl.ds(off, rg)
+            gc = gh_s[m, :BIG]
+            gs = gh_s[m, BIG:]
+            kc = kh_ref[0, j, rows, :BIG]
+            ks = kh_ref[0, j, rows, BIG:]
+            gh_ref[0, j, rows, :BIG] += ac * gc + as_ * gs
+            if flip:
+                gh_ref[0, j, rows, BIG:] += gc * as_ - gs * ac
+                return (xc + kc * gc - ks * gs, xs + kc * gs + ks * gc)
+            gh_ref[0, j, rows, BIG:] += ac * gs - as_ * gc
+            return (xc + kc * gc + ks * gs, xs + kc * gs - ks * gc)
+
+        xc, xs = lax.fori_loop(0, (i + 1) if flip else (count - i), inner, (zero, zero))
+        xh_s[at, :BIG] = xc.astype(bf16)
+        xh_s[at, BIG:] = xs.astype(bf16)
+
+    over_pieces(nseq, cc, rg, seq_ref, piece)
 
     for h in range(pieces):
         at = pl.ds(h * cc, cc)
@@ -668,17 +662,25 @@
     )(tab, seq, a, kh, wave, back, gg)
 
 
-def ssm_back(tab, seq, a, gm, kh, wave, back, gg, y, dg, da):
-    nb, nseq, ch, cc, size, big, spec, head, tables = ssm_specs(a.shape, seq)
+def ssm_back(k, tab, seq, a, gm, kh, wave, back, gg, y, dg, da):
+    nb, nseq, ch, cc, size, _, _, head, tables = ssm_specs(a.shape, seq)
+    big = pl.BlockSpec((1, nb, cc, BLK), lambda i: (k, 0, i, 0))
+    spec = pl.BlockSpec((1, LAGS, cc, 2 * BIG), lambda i: (k, 0, i, 0))
+    out = pl.BlockSpec((1, nb, cc, BLK), lambda i: (0, 0, i, 0))
+    out_spec = pl.BlockSpec((1, LAGS, cc, 2 * BIG), lambda i: (0, 0, i, 0))
+    tables = [
+        pl.BlockSpec((BIG, 2 * BIG), lambda i: (0, 0)),
+        pl.BlockSpec((2 * BIG, BIG), lambda i: (0, 0)),
+    ]
     return pl.pallas_call(
-        partial(back_body, nb, nseq, cc, 16),
-        grid=(2, ch // cc),
+        partial(back_body, nb, nseq, cc, 16, k == 1),
+        grid=(ch // cc,),
         in_specs=head + [big, big, spec] + tables + [big] * 4,
-        out_specs=[big, big, spec, pl.BlockSpec((1, cc, 2 * BLK), lambda k, i: (k, i, 0))],
-        out_shape=[jax.ShapeDtypeStruct(a.shape, bf16)] * 2
+        out_specs=[out, out, out_spec, pl.BlockSpec((1, cc, 2 * BLK), lambda i: (0, i, 0))],
+        out_shape=[jax.ShapeDtypeStruct((1,) + a.shape[1:], bf16)] * 2
         + [
-            jax.ShapeDtypeStruct((2, LAGS, ch, 2 * BIG), f32),
-            jax.ShapeDtypeStruct((2, ch, 2 * BLK), f32),
+            jax.ShapeDtypeStruct((1, LAGS, ch, 2 * BIG), f32),
+            jax.ShapeDtypeStruct((1, ch, 2 * BLK), f32),
         ],
         scratch_shapes=[
             pltpu.VMEM((size, BIG), bf16),
@@ -688,13 +690,13 @@
             pltpu.VMEM((size, BIG), f32),
         ],
         compiler_params=params(60),
-        cost_estimate=cost(2 * ch * 80e6, 2 * ch * nb * BLK * 16),
+        cost_estimate=cost(ch * 80e6, ch * nb * BLK * 16),
     )(tab, seq, a, gm, kh, wave, back, gg, y, dg, da)
 
 
 def stack_pair(refs):
     return jnp.concatenate(
-        [jnp.concatenate([ref[k, 0], ref[k, 1]], axis=1) for ref in refs for k in range(2)], axis=0
+        [jnp.concatenate([ref[k, 0], ref[k, 1]], axis=1) for ref in refs for k in range(ref.shape[0])], axis=0
     )
 
 
@@ -719,7 +721,7 @@
             num_scalar_prefetch=1,
             grid=(many // 2,),
             in_specs=[pl.BlockSpec((width, deep), lambda i, at: (0, 0))]
-            + [pl.BlockSpec((2, 2, ch, BLK), lambda i, at: (0, at[0] + i, 0, 0))] * count
+            + [pl.BlockSpec((x.shape[0], 2, ch, BLK), lambda i, at: (0, at[0] + i, 0, 0)) for x in arrays]
             + ([] if extra is None else [out]),
             out_specs=out,
         ),
@@ -732,8 +734,8 @@
 def outer_body(ch, many, cuts, parts, at_ref, *refs):
     step = pl.program_id(0)
     xs, gs = refs[:parts], refs[parts : 2 * parts]
-    gp_ref, gpg_ref, mix_ref = refs[2 * parts : 2 * parts + 3]
-    outs = refs[2 * parts + 3 : 2 * parts + 3 + cuts]
+    gp_refs, gpg_refs, mix_ref = refs[2 * parts : 2 * parts + 2], refs[2 * parts + 2 : 2 * parts + 4], refs[2 * parts + 4]
+    outs = refs[2 * parts + 5 : 2 * parts + 5 + cuts]
     acc_s, x_s, g_s = refs[-3:]
 
     def fill(at):
@@ -758,7 +760,8 @@
         acc_s[...] = jnp.zeros_like(acc_s)
 
     for at, (left, ref, k) in enumerate(
-        [(x_s, gp_ref, 0), (x_s, gp_ref, 1), (x_s, gpg_ref, 0), (x_s, gpg_ref, 1), (g_s, mix_ref, 0), (g_s, mix_ref, 1)]
+        [(x_s, gp_refs[0], 0), (x_s, gp_refs[1], 0), (x_s, gpg_refs[0], 0), (x_s, gpg_refs[1], 0)]
+        + [(g_s, mix_ref, 0), (g_s, mix_ref, 1)]
     ):
         acc_s[at] += nt(left[...], part(ref, k))
 
@@ -773,7 +776,7 @@
 
 def outer_sums(order, cuts, xs, gs, gp, gpg, mix):
     width = xs[0].shape[1]
-    _, nb, ch, _ = gp.shape
+    _, nb, ch, _ = mix.shape
     many = 8
     parts = len(xs)
     if parts == 1:
@@ -781,13 +784,14 @@
     else:
         rows = pl.BlockSpec((many, width, BLK), lambda i, at: (0, 0, 0), pipeline_mode=pl.Buffered(1))
     chan = pl.BlockSpec((2, many, ch, BLK), lambda i, at: (0, at[i], 0, 0))
+    one = pl.BlockSpec((1, many, ch, BLK), lambda i, at: (0, at[i], 0, 0))
     tok = nb * BLK
     return pl.pallas_call(
         partial(outer_body, ch, many, cuts, parts),
         grid_spec=pltpu.PrefetchScalarGridSpec(
             num_scalar_prefetch=1,
             grid=(nb // many,),
-            in_specs=[rows] * (2 * parts) + [chan, chan, chan],
+            in_specs=[rows] * (2 * parts) + [one] * 4 + [chan],
             out_specs=[pl.BlockSpec((6, width // cuts, ch), lambda i, at: (0, 0, 0))] * cuts,
             scratch_shapes=[
                 pltpu.VMEM((6, width, ch), f32),
@@ -798,7 +802,7 @@
         out_shape=[jax.ShapeDtypeStruct((6, width // cuts, ch), bf16)] * cuts,
         compiler_params=params(60),
         cost_estimate=cost(12 * tok * width * ch, tok * (4 * width + 12 * ch)),
-    )(order, *xs, *gs, gp, gpg, mix)
+    )(order, *xs, *gs, *gp, *gpg, mix)
 
 
 def meet_body(axes, rank_ref, x_ref, chan_ref, norm_ref, got_ref, call_ref, nall_ref, send_s, *sems):
@@ -994,25 +998,33 @@
     def regroup(self, x):
         return x
 
-    def deal(self, x):
+    def gather_first(self, x):
+        return [lax.all_gather(x, "tensor", axis=0, tiled=True)]
+
+    def gather_last(self, x, got):
+        return [(got[0], jnp.zeros((1,), jnp.int32))]
+
+    def scatter_first(self, w, arrays, many):
+        return [mul_rows(w, arrays, jnp.zeros((1,), jnp.int32), many * self.n_t)]
+
+    def scatter_send(self, parts):
+        return [lax.psum_scatter(parts[0], "tensor", scatter_dimension=0, tiled=True)]
+
+    def scatter_own(self, w, arrays, many):
+        return []
+
+    def swap(self, x):
+        return x
+
+    def spread(self, x):
         return lax.all_to_all(x, "dp", split_axis=0, concat_axis=0, tiled=True)
-
-    def undeal(self, x):
-        return self.deal(x)
-
-    def gather_rows(self, x):
-        return [(lax.all_gather(x, "tensor", axis=0, tiled=True), jnp.zeros((1,), jnp.int32))]
-
-    def scatter_rows(self, w, arrays, many):
-        whole = mul_rows(w, arrays, jnp.zeros((1,), jnp.int32), many * self.n_t)
-        return [lax.psum_scatter(whole, "tensor", scatter_dimension=0, tiled=True)]
 
     def order(self, pieces):
         return jnp.append(jnp.arange(pieces * self.n_t, dtype=jnp.int32), 0)
 
     def enter(self, rank, x, chan, norm):
         (sent,) = permute_to(rank, [x])
-        return (self.deal(sent),) + self.gather_channels(chan, norm)
+        return (self.spread(sent),) + self.gather_channels(chan, norm)
 
     def gather_channels(self, chan, norm):
         perm = [(f, (f % self.n_dp) * self.n_t + f // self.n_dp) for f in range(self.n_dp * self.n_t)]
@@ -1020,13 +1032,22 @@
         norm = lax.all_gather(norm, self.both, axis=1, tiled=True)
         return lax.all_gather(chan, "dp", axis=0, tiled=True), norm
 
-    def gather_weights(self, pack):
-        return lax.all_gather(pack, "dp", axis=0, tiled=True)
-
-    def scatter_weights(self, gw):
+    def weights_first(self, pack):
+        return [pack]
+
+    def weights_send(self, packs):
+        return [lax.all_gather(packs[0], "dp", axis=0, tiled=True)]
+
+    def weights_last(self, parts):
+        return parts[0]
+
+    def grads_send(self, gw):
         six, width, ch = gw[0].shape
         gw = gw[0].reshape(six, self.n_dp, width // self.n_dp, ch).transpose(1, 0, 2, 3)
-        return lax.psum_scatter(gw, "dp", scatter_dimension=0, tiled=True)[0].astype(f32)
+        return [lax.psum_scatter(gw, "dp", scatter_dimension=0, tiled=True)[0]]
+
+    def grads_last(self, parts):
+        return parts[0].astype(f32)
 
     def scatter_channels(self, sums):
         sums = lax.psum_scatter(sums, "dp", scatter_dimension=0, tiled=True)
@@ -1055,11 +1076,11 @@
     def regroup(self, x):
         return lax.ppermute(x, ("c", "h"), self.crossed)
 
-    def deal(self, x):
-        return self.regroup(lax.all_to_all(x, ("q", "c"), split_axis=0, concat_axis=0, tiled=True))
-
-    def undeal(self, x):
-        return lax.all_to_all(self.regroup(x), ("q", "c"), split_axis=0, concat_axis=0, tiled=True)
+    def swap(self, x):
+        return self.regroup(x)
+
+    def spread(self, x):
+        return lax.all_to_all(x, ("q", "c"), split_axis=0, concat_axis=0, tiled=True)
 
     def places(self):
         c, w = lax.axis_index("c"), lax.axis_index("w")
@@ -1068,23 +1089,27 @@
     def starts(self, many):
         return [(place * many).astype(jnp.int32).reshape(1) for place in self.places()]
 
-    def gather_rows(self, x):
-        beside = self.flip(x, "c")
-        near = self.flip(x, "w")
-        far = self.flip(near, "c")
-        return list(zip([x, beside, near, far], self.starts(x.shape[0])))
-
-    def scatter_rows(self, w, arrays, many):
-        own, beside, near, far = self.starts(many)
+    def gather_first(self, x):
+        return [self.flip(x, "c"), self.flip(x, "w")]
+
+    def gather_last(self, x, got):
+        beside, near = got
+        return list(zip([x, beside, near, self.flip(near, "c")], self.starts(x.shape[0])))
+
+    def scatter_first(self, w, arrays, many):
+        _, beside, near, far = self.starts(many)
         first = mul_rows(w, arrays, far, many)
         give = self.flip(first, "c")
         beside, first = after((beside, first))
         second = mul_rows(w, arrays, beside, many)
         second, give = after((second, give))
-        third = mul_rows(w, arrays, near, many, extra=give)
-        send = self.flip(third, "w")
-        own, third = after((own, third))
-        return [mul_rows(w, arrays, own, many, dtype=f32), self.flip(second, "c"), send]
+        return [second, mul_rows(w, arrays, near, many, extra=give)]
+
+    def scatter_send(self, parts):
+        return [self.flip(parts[0], "c"), self.flip(parts[1], "w")]
+
+    def scatter_own(self, w, arrays, many):
+        return [mul_rows(w, arrays, self.starts(many)[0], many, dtype=f32)]
 
     def order(self, pieces):
         place = jnp.stack(self.places())[:, None] * pieces + jnp.arange(pieces)[None, :]
@@ -1112,24 +1137,31 @@
         norm = norm[:, :3, :small].transpose(1, 0, 2).reshape(3, -1)
         return got.reshape(x.shape), chan, norm
 
-    def gather_weights(self, pack):
+    def weights_first(self, pack):
+        back = [(2 * (1 - h) + c, 2 * c + h) for c in range(2) for h in range(2)]
+        return [self.regroup(pack), lax.ppermute(pack, ("c", "h"), back)]
+
+    def weights_send(self, packs):
         h = lax.axis_index("h")
-        first = self.regroup(pack)
-        back = [(2 * (1 - h) + c, 2 * c + h) for c in range(2) for h in range(2)]
-        second = lax.ppermute(pack, ("c", "h"), back)
+        first, second = packs
         pair = jnp.concatenate([jnp.where(h == 0, first, second), jnp.where(h == 0, second, first)], axis=0)
-        deep, wide = pair.shape
+        return [pair] + [self.flip(pair, "q", bit) for bit in range(1, self.quads)]
+
+    def weights_last(self, parts):
+        deep, wide = parts[0].shape
         q = lax.axis_index("q")
-        whole = jnp.zeros((self.quads * deep, wide), pack.dtype)
+        whole = jnp.zeros((self.quads * deep, wide), parts[0].dtype)
         for bit in range(self.quads):
-            part = self.flip(pair, "q", bit) if bit else pair
-            whole = lax.dynamic_update_slice_in_dim(whole, part, (q ^ bit) * deep, 0)
+            whole = lax.dynamic_update_slice_in_dim(whole, parts[bit], (q ^ bit) * deep, 0)
         return whole
 
-    def scatter_weights(self, gw):
-        total = gw[0].astype(f32)
-        for bit in range(1, self.quads):
-            total = total + self.flip(gw[bit], "q", bit).astype(f32)
+    def grads_send(self, gw):
+        return [gw[0]] + [self.flip(gw[bit], "q", bit) for bit in range(1, self.quads)]
+
+    def grads_last(self, parts):
+        total = parts[0].astype(f32)
+        for part in parts[1:]:
+            total = total + part.astype(f32)
         total = total.astype(bf16)
         six, deep, ch = total.shape
         total = total.reshape(six, 2, deep // 2, ch)
@@ -1177,90 +1209,115 @@
     back = (wave.T / BIG).astype(bf16)
     wave = wave.astype(bf16)
 
-    rank = rank_of(target)
-    sender = source // group
-    place = rank_of(sender * rows + jnp.arange(rows, dtype=jnp.int32))
-    table = net.regroup(jnp.concatenate([place, lengths[0]]))
-    place, lens = table[:rows], table[rows:]
-
-    chan = jnp.concatenate(
-        [log_rate[0], log_rate[1], ssm_b[0], ssm_b[1], ssm_c[0], ssm_c[1]]
-        + [jnp.stack([log_dt[0], log_dt[1], ssm_d[0], ssm_d[1], b_fwd, b_bwd, b_gate[0], b_gate[1]], axis=1)],
-        axis=1,
-    )
-    got_x, chan_all, norm_all = net.enter(rank, tokens, chan, jnp.stack([ln_gain, ln_bias, b_out]))
-
     def lanes(column):
         return jnp.broadcast_to(column[..., None], column.shape + (BLK,))
-
-    gain = lanes(norm_all[0])
-    shift = lanes(norm_all[1])
-    bias_out = lanes(norm_all[2])
-    small = chan_all[:, 6 * STATE :]
-    bias_in = lanes(small[:, 4:8].T.reshape(-1))
-
-    def pick(at):
-        return jnp.stack([chan_all[:, at * STATE : (at + 1) * STATE], chan_all[:, (at + 1) * STATE : (at + 2) * STATE]])
 
     def decays(log_dt, log_rate, ssm_b):
         rate = jnp.exp(log_rate)
         ld = -jnp.exp(log_dt)[..., None] * rate
         return rate, ld, (1.0 - jnp.exp(ld)) / rate * ssm_b
 
-    _, ld_all, drive_all = decays(small[:, 0:2].T, pick(0), pick(2))
-    ld_pairs = (ld_all * log2e).reshape(2, ch // 2, 2 * STATE)
-    w_pairs = (pick(4) * drive_all).reshape(2, ch // 2, 2 * STATE)
-    kh = spectra(ld_pairs, w_pairs, lanes(small[:, 2:4].T), wave)
-
+    rank = rank_of(target)
+    sender = source // group
+    place = rank_of(sender * rows + jnp.arange(rows, dtype=jnp.int32))
     pack = jnp.concatenate(
         [w_fwd, w_bwd, w_gate.reshape(-1, 2 * ch), w_out.transpose(2, 0, 1).reshape(-1, 2 * ch)], axis=1
     )
-    pack, cotangent, got_x = after((pack, cotangent, got_x))
-    w_all = net.gather_weights(pack)
-    (sent_g,) = permute_to(rank, [cotangent])
-    got_g = net.deal(sent_g)
-    w_in, w_back = w_all[:, : 4 * ch], w_all[:, 4 * ch :]
-    w_in_t, w_back_t = w_in.T, w_back.T
-
+    packs = net.weights_first(pack)
+    table = net.regroup(jnp.concatenate([place, lengths[0]]))
+    rate, ld, drive = decays(log_dt, log_rate, ssm_b)
+    scale = ssm_c * drive
+    chan = jnp.concatenate(
+        [ld[0] * log2e, ld[1] * log2e, scale[0], scale[1]]
+        + [jnp.stack([ssm_d[0], ssm_d[1], b_fwd, b_bwd, b_gate[0], b_gate[1]], axis=1)],
+        axis=1,
+    )
+    got_x, chan_all, norm_all = net.enter(rank, tokens, chan, jnp.stack([ln_gain, ln_bias, b_out]))
+    got_x, chan_all, norm_all, packs, table, cotangent = after((got_x, chan_all, norm_all, packs, table, cotangent))
+
+    place, lens = table[:rows], table[rows:]
+    gain = lanes(norm_all[0])
+    shift = lanes(norm_all[1])
+    bias_out = lanes(norm_all[2])
+    small = chan_all[:, 4 * STATE :]
+    bias_in = lanes(small[:, 2:6].T.reshape(-1))
+
+    def pairs(at):
+        both = jnp.stack([chan_all[:, (at + k) * STATE : (at + k + 1) * STATE] for k in range(2)])
+        return both.reshape(2, ch // 2, 2 * STATE)
+
+    ld_pairs = pairs(0)
+    w_pairs = pairs(2)
+    skip = lanes(small[:, 0:2].T)
     live = live_rows(lens, group)
     live_own = lax.dynamic_slice_in_dim(live, net.place_of_group() * rows, rows, 0).reshape(many, 1, BLK)
     live = live.reshape(nb // 2, 1, BIG)
     tab, seq = sequence_tables(lens, nb)
 
+    w_parts = net.weights_send(packs)
     xt, xd = deal_x(place, got_x, gain, shift)
-    xs = net.gather_rows(xt)
+    xt, ld_pairs, cotangent = after((xt, ld_pairs, cotangent))
+    x_got = net.gather_first(xt)
+    (sent_g,) = permute_to(rank, [cotangent])
+    got_g = net.spread(sent_g)
+    kh = spectra(ld_pairs, w_pairs, skip, wave)
+    w_parts, x_got, kh = after((w_parts, x_got, kh))
+
+    w_all = net.weights_last(w_parts)
+    w_in, w_back = w_all[:, : 4 * ch], w_all[:, 4 * ch :]
+    w_in_t, w_back_t = w_in.T, w_back.T
+    xs = net.gather_last(xt, x_got)
+    got_g = net.swap(got_g)
     kept = None
     for part, start in xs:
         kept = project(part, start, nb, live, w_in_t, bias_in, kept)
+    kept, got_g = after((kept, got_g))
     a, da, gg, dg = kept
+    gt, gd, g_bias_out = deal_g(place, got_g, live_own)
+    gt, a = after((gt, a))
+    g_got = net.gather_first(gt)
     y, mix = ssm_scan(tab, seq, a, kh, wave, back, gg)
-
-    gt, gd, g_bias_out = deal_g(place, got_g, live_own)
-    gs = net.gather_rows(gt)
+    g_got, y, mix = after((g_got, y, mix))
+    gs = net.gather_last(gt, g_got)
     kept = None
     for part, start in gs:
         kept = gate_grad(part, start, nb, w_back_t, kept)
     (gm,) = kept
-
-    branch = net.scatter_rows(w_back, [mix], many)
+    branch = net.scatter_first(w_back, [mix], many)
+    branch, gm = after((branch, gm))
+
+    branch = net.scatter_send(branch)
+    branch = net.scatter_own(w_back, [mix], many) + branch
+    first = ssm_back(0, tab, seq, a, gm, kh, wave, back, gg, y, dg, da)
+    branch, first, a = after((branch, first, a))
     sent_out = layer_rows(place, branch, xd, live_own, bias_out)
-    layer_out = permute_from(rank, net.undeal(sent_out))
-
-    gpg, gp, gh, bsum = ssm_back(tab, seq, a, gm, kh, wave, back, gg, y, dg, da)
-    g_normed = net.scatter_rows(w_in, [gp, gpg], many)
-    mix, own_part = after((mix, g_normed[0]))
-    g_normed[0] = own_part
+    sent_out, a = after((sent_out, a))
+    sent_out = net.swap(sent_out)
+    second = ssm_back(1, tab, seq, a, gm, kh, wave, back, gg, y, dg, da)
+    sent_out, first, second = after((sent_out, first, second))
+    gpg, gp, gh, bsum = zip(first, second)
+    sent_out = net.spread(sent_out)
+    back_list = [gp[0], gp[1], gpg[0], gpg[1]]
+    g_normed = net.scatter_first(w_in, back_list, many)
+    g_normed, back_list, mix = after((g_normed, back_list, mix))
+    gp, gpg = back_list[:2], back_list[2:]
+    g_normed = net.scatter_send(g_normed)
+    g_normed = net.scatter_own(w_in, back_list, many) + g_normed
     gw = outer_sums(net.order(many // 8), net.cuts, [part for part, _ in xs], [part for part, _ in gs], gp, gpg, mix)
-    gh, gw = after((gh, gw))
-    gw = net.scatter_weights(gw)
-
+    g_normed, gw, gh, sent_out = after((g_normed, gw, gh, sent_out))
     sent_in, norm_sums = input_rows(place, g_normed, xd, gd, gain)
-    gh, sent_in = after((gh, sent_in))
-    s0, s1, g0 = moments(ld_pairs, gh, back)
-    in_grad = permute_from(rank, net.undeal(sent_in))
+    sent_in, gh, gw, norm_sums = after((sent_in, gh, gw, norm_sums))
+    sent_in = net.swap(sent_in)
+    gw = net.grads_send(gw)
+    s0, s1, g0 = [jnp.concatenate(part) for part in zip(*[moments(k, ld_pairs, gh[k], back) for k in range(2)])]
+    layer_out = permute_from(rank, sent_out)
+    sent_in, gw, s0, s1, g0 = after((sent_in, gw, s0, s1, g0))
+    gw = net.grads_last(gw)
+    in_grad = permute_from(rank, net.spread(sent_in))
 
     s0 = s0.reshape(2, ch, STATE)
     s1 = s1.reshape(2, ch, STATE)
+    bsum = jnp.concatenate(bsum)
     gb_gate = jnp.sum(bsum[:, :, :BLK], axis=2)
     gb_in = jnp.sum(bsum[:, :, BLK:], axis=2)
     sums = jnp.concatenate(
@@ -1272,7 +1329,6 @@
     s1 = jnp.stack([sums[:, 2 * STATE : 3 * STATE], sums[:, 3 * STATE : 4 * STATE]])
     tail = sums[:, 4 * STATE :].T
     step = jnp.exp(log_dt)[..., None]
-    rate, ld, drive = decays(log_dt, log_rate, ssm_b)
     g_c = s0 * drive
     g_drive = s0 * ssm_c
     g_b = g_drive * (1.0 - jnp.exp(ld)) / rate

time: 692 us -> 638 us (0.922)
  the two profiles are of different devices: /device:TPU:1 before, /device:TPU:0 now
where the time goes in v4:
time: 638 us; the launch traced here: 625 us
  Pallas kernels  385 us (60%)
  starting transfers between devices  98.7 us (15%)
  local copies, waits for them, and re-layouts  83.8 us (13%)
  waiting for transfers between devices  30.7 us (5%)
  other arithmetic  24.2 us (4%)
    pallas_call x2, Pallas kernels, ssm_back(): pl.pallas_call(partial(back_body, nb, nseq, cc, 16, k == 1), grid=(ch //...  76 us
    pallas_call x1, Pallas kernels, meet(): pl.pallas_call(partial(meet_body, axes), in_specs=[vmem] * 4, out_specs=[...  59.4 us
    pallas_call x8, Pallas kernels, chained(): pl.pallas_call(body, grid_spec=pltpu.PrefetchScalarGridSpec(num_scalar_pr...  49.4 us
    unnamed x173, local copies, waits for them, and re-layouts  46.1 us
    ppermute x26, starting transfers between devices, flip(): return lax.ppermute(x, axis, [(i, i ^ bit) for i in range(self.axes[axis])])  38.9 us
    pallas_call x1, Pallas kernels, ssm_scan(): pl.pallas_call(partial(scan_body, nb, nseq, cc, 32), grid=(2, ch // cc),...  38.7 us
    pallas_call x1, Pallas kernels, outer_sums(): pl.pallas_call(partial(outer_body, ch, many, cuts, parts), grid_spec=pltp...  34 us
    pallas_call x1, Pallas kernels, spectra(): pl.pallas_call(partial(spectra_body, cc), grid=(2, ch // cc), in_specs=[p...  33.1 us
  transfers between devices with their start and end apart: 38, of which 6 were waited for; matrix products, arithmetic and copies ran while one was open for 10% of the time, Pallas kernels for 54%

profile of v4, /device:TPU:0, one launch (start us, length us, event | category | flops | bytes accessed | tf_op | source)
XLA Modules:
  0.0 625.2 jit_solution(12374436519478487367)
XLA Ops:
  5.3 5.3 collective-permute-start.1
  18.3 59.4 %shard_map.332 = (bf16[8,128,768]{2,1,0:T(8,128)(2,1)S(1)}, f32[8,104,128]{2,1,0:T(8,128)S(1)}, f32[32,8,128]{2,1,0:T(8,128)S(1)}) custom-call(s32[1,1024]{1,0:T(1,128)S(1)} %bitcast.171, bf16[1024,768]{1,0:T(8,128)(2,1)S(1)} %copy-done.36, f32[104,128]{1,0:T(8,128)S(1)} %pad_bitcast_fusion.chan_ref, f32[8,128]{1,0:T(8,128)S(1)} %select_maximum_fusion.norm_ref), custom_call_target="tpu_custom_call" | custom-call | flops 80530640 | bytes 3932160 | tf_op jit(solution)/shard_map/pallas_call | solution.py:933
  84.4 6.3 %shard_map.333 = (bf16[8,768,128]{2,1,0:T(8,128)(2,1)S(1)}, bf16[8,768,128]{2,1,0:T(8,128)(2,1)S(1)}) custom-call(s32[1024,1]{1,0:T(8,128)S(1)} %copy.147.place_ref, bf16[1024,768]{1,0:T(8,128)(2,1)S(1)} %bitcast.164, f32[768,128]{1,0:T(8,128)S(1)} %broadcast_in_dim.101.gain_ref, f32[768,128]{1,0:T(8,128)S(1)} %broadcast_in_dim.103.shift_ref), custom_call_target="tpu_custom_call" | custom-call | flops 80530640 | bytes 235929 | tf_op jit(solution)/shard_map/pallas_call | solution.py:137
  101.3 4.4 all-to-all-start
  122.5 33.1 %shard_map.334.kh_ref = f32[2,8,384,512]{3,2,1,0:T(8,128)S(1)} custom-call(f32[2,192,128]{2,1,0:T(8,128)S(1)} %copy-done.34, f32[2,192,128]{2,1,0:T(8,128)S(1)} %pad_maximum_fusion.5.w_ref, f32[2,384,128]{2,1,0:T(8,128)S(1)} %broadcast_in_dim.104.d_ref, bf16[256,512]{1,0:T(8,128)(2,1)S(1)} %copy-done.31), custom_call_target="tpu_custom_call" | custom-call | flops 1536000000 | bytes 629145 | tf_op jit(solution)/shard_map/pallas_call | solution.py:387
  155.6 4.6 copy-done.1
  160.2 13.3 %collective-permute-start.9 = (bf16[1024,768]{1,0:T(8,128)(2,1)}, bf16[1024,768]{1,0:T(8,128)(2,1)}, u32[]{:S(2)}, u32[]{:S(2)}) collective-permute-start(bf16[1024,768]{1,0:T(8,128)(2,1)} %bitcast.34), channel_id=1, source_target_pairs={{0,0},{2,4},{4,2},{6,6},{1,1},{3,5},{5,3},{7,7},{8,8},{10,12},{12,... | collective-permute-start | bytes 4718600 | tf_op jit(solution)/shard_map/ppermute | solution.py:1077
  179.1 2.7 slice_bitcast_fusion.28
  182.6 3.0 copy.153.wt_ref
  187.3 9.0 %shard_map.335 = (bf16[2,32,384,128]{3,2,1,0:T(8,128)(2,1)}, bf16[2,32,384,128]{3,2,1,0:T(8,128)(2,1)}, bf16[2,32,384,128]{3,2,1,0:T(8,128)(2,1)}, bf16[2,32,384,128]{3,2,1,0:T(8,128)(2,1)}) custom-call(s32[1]{0:T(128)S(6)} %select_n.139.start_ref, bf16[8,768,128]{2,1,0:T(8,128)(2,1)S(1)} %copy-done.18, f32[16,1,256]{2,1,0:T(1,128)S(1)} %bitcast.165, ...), custom_call_target="tpu_custom_call" | custom-call | flops 120795952 | bytes 393216 | tf_op jit(solution)/shard_map/pallas_call | solution.py:279
  196.3 9.1 %shard_map.336 = (bf16[2,32,384,128]{3,2,1,0:T(8,128)(2,1)}, bf16[2,32,384,128]{3,2,1,0:T(8,128)(2,1)}, bf16[2,32,384,128]{3,2,1,0:T(8,128)(2,1)}, bf16[2,32,384,128]{3,2,1,0:T(8,128)(2,1)}) custom-call(s32[1]{0:T(128)S(6)} %select_n.152.start_ref, ...), custom_call_target="tpu_custom_call", output_to_operand_aliasing={{0}: (5, {}), {1}: (6, {}), {2}: (7, {}), {3}: (8, {})} | custom-call | flops 120795952 | bytes 393216 | tf_op jit(solution)/shard_map/pallas_call | solution.py:279
  205.4 10.0 %shard_map.337 = (bf16[2,32,384,128]{3,2,1,0:T(8,128)(2,1)}, bf16[2,32,384,128]{3,2,1,0:T(8,128)(2,1)}, bf16[2,32,384,128]{3,2,1,0:T(8,128)(2,1)}, bf16[2,32,384,128]{3,2,1,0:T(8,128)(2,1)}) custom-call(s32[1]{0:T(128)S(6)} %select_n.151.start_ref, ...), custom_call_target="tpu_custom_call", output_to_operand_aliasing={{0}: (5, {}), {1}: (6, {}), {2}: (7, {}), {3}: (8, {})} | custom-call | flops 120795952 | bytes 393216 | tf_op jit(solution)/shard_map/pallas_call | solution.py:279
  215.5 10.1 %shard_map.338 = (bf16[2,32,384,128]{3,2,1,0:T(8,128)(2,1)}, bf16[2,32,384,128]{3,2,1,0:T(8,128)(2,1)}, bf16[2,32,384,128]{3,2,1,0:T(8,128)(2,1)}, bf16[2,32,384,128]{3,2,1,0:T(8,128)(2,1)}) custom-call(s32[1]{0:T(128)S(6)} %select_n.148.start_ref, ...), custom_call_target="tpu_custom_call", output_to_operand_aliasing={{0}: (5, {}), {1}: (6, {}), {2}: (7, {}), {3}: (8, {})} | custom-call | flops 120795952 | bytes 393216 | tf_op jit(solution)/shard_map/pallas_call | solution.py:279
  225.6 6.0 shard_map.340
  234.8 2.5 slice_bitcast_fusion.27
  237.3 38.7 %shard_map.341 = (bf16[2,32,384,128]{3,2,1,0:T(8,128)(2,1)}, bf16[2,32,384,128]{3,2,1,0:T(8,128)(2,1)}) custom-call(s32[2,17]{1,0:T(2,128)} %pad_add_fusion.1.tab_ref, s32[2,4]{1,0:T(2,128)} %pad_add_fusion.2.seq_ref, bf16[2,32,384,128]{3,2,1,0:T(8,128)(2,1)} %get-tuple-element.223.a_ref, f32[2,8,384,512]{3,2,1,0:T(8,128)} %copy-done.1, ...), custom_call_target="tpu_custom_call" | custom-call | flops 1920000000 | bytes 1258291 | tf_op jit(solution)/shard_map/pallas_call | solution.py:648
  276.1 3.3 copy-done.2
  279.4 3.1 shard_map.343
  288.8 3.6 shard_map.348.refs_0_
  292.5 3.1 shard_map.344
  295.6 4.6 shard_map.345
  300.2 3.5 shard_map.349.gm_ref
  303.8 2.6 copy-done
  311.8 38.6 %shard_map.350 = (bf16[1,32,384,128]{3,2,1,0:T(8,128)(2,1)}, bf16[1,32,384,128]{3,2,1,0:T(8,128)(2,1)}, f32[1,8,384,512]{3,2,1,0:T(8,128)}, f32[1,384,256]{2,1,0:T(8,128)}) custom-call(s32[2,17]{1,0:T(2,128)} %pad_add_fusion.1.tab_ref, s32[2,4]{1,0:T(2,128)} %pad_add_fusion.2.seq_ref, bf16[2,32,384,128]{3,2,1,0:T(8,128)(2,1)} %get-tuple-element.223.a_ref, ...), custom_call_target="tpu_custom_call" | custom-call | flops 1536000000 | bytes 1258291 | tf_op jit(solution)/shard_map/pallas_call | solution.py:675
  350.6 6.0 shard_map.351
  356.5 13.6 %collective-permute-start.16 = (bf16[1024,768]{1,0:T(8,128)(2,1)}, bf16[1024,768]{1,0:T(8,128)(2,1)}, u32[]{:S(2)}, u32[]{:S(2)}) collective-permute-start(bf16[1024,768]{1,0:T(8,128)(2,1)} %shard_map.351), channel_id=1, source_target_pairs={{0,0},{2,4},{4,2},{6,6},{1,1},{3,5},{5,3},{7,7},{8,8},{10,12},{12,... | collective-permute-start | bytes 4718600 | tf_op jit(solution)/shard_map/ppermute | solution.py:1077
  370.2 37.3 %shard_map.352 = (bf16[1,32,384,128]{3,2,1,0:T(8,128)(2,1)}, bf16[1,32,384,128]{3,2,1,0:T(8,128)(2,1)}, f32[1,8,384,512]{3,2,1,0:T(8,128)}, f32[1,384,256]{2,1,0:T(8,128)}) custom-call(s32[2,17]{1,0:T(2,128)} %pad_add_fusion.1.tab_ref, s32[2,4]{1,0:T(2,128)} %pad_add_fusion.2.seq_ref, bf16[2,32,384,128]{3,2,1,0:T(8,128)(2,1)} %get-tuple-element.223.a_ref, ...), custom_call_target="tpu_custom_call" | custom-call | flops 1536000000 | bytes 1258291 | tf_op jit(solution)/shard_map/pallas_call | solution.py:675
  413.0 4.3 shard_map.353
  417.3 5.2 shard_map.354
  422.5 5.5 shard_map.355
  429.0 10.4 %all-to-all-start.1 = ((bf16[8,128,768]{2,1,0:T(8,128)(2,1)}), bf16[8,128,768]{2,1,0:T(8,128)(2,1)}, u32[]{:S(2)}, u32[]{:S(2)}) async-start(bf16[8,128,768]{2,1,0:T(8,128)(2,1)} %bitcast.51), calls=%async_computation.1 | async-start | bytes 3145728 | tf_op jit(solution)/shard_map/all_to_all | solution.py:1083
  447.5 4.5 shard_map.356.refs_0_
  453.7 34.0 %shard_map.357 = (bf16[6,192,384]{2,1,0:T(8,128)(2,1)}, bf16[6,192,384]{2,1,0:T(8,128)(2,1)}, bf16[6,192,384]{2,1,0:T(8,128)(2,1)}, bf16[6,192,384]{2,1,0:T(8,128)(2,1)}) custom-call(s32[8]{0:T(128)} %concatenate.51.at_ref, bf16[8,768,128]{2,1,0:T(8,128)(2,1)} %copy-done.17, bf16[8,768,128]{2,1,0:T(8,128)(2,1)} %copy-done.15, ...), custom_call_target="tpu_custom_call" | custom-call | flops 724775744 | bytes 1572864 | tf_op jit(solution)/shard_map/pallas_call | solution.py:789
  489.2 9.3 %shard_map.359 = (bf16[1024,768]{1,0:T(8,128)(2,1)}, f32[2,768,128]{2,1,0:T(8,128)S(1)}) custom-call(s32[1,1024]{1,0:T(1,128)S(1)} %bitcast.176, bf16[8,768,128]{2,1,0:T(8,128)(2,1)S(1)} %copy-done.27, bf16[8,768,128]{2,1,0:T(8,128)(2,1)S(1)} %copy-done.41, f32[768,128]{1,0:T(8,128)S(1)} %copy-done.33, f32[8,768,128]{2,1,0:T(8,128)} %copy-done.13, ...), custom_call_target="tpu_custom_call" | custom-call | flops 80530640 | bytes 314572 | tf_op jit(solution)/shard_map/pallas_call | solution.py:225
  507.5 2.8 copy-done.22
  510.3 12.5 %shard_map.360 = (f32[1,192,128]{2,1,0:T(8,128)S(1)}, f32[1,192,128]{2,1,0:T(8,128)S(1)}, f32[1,384,128]{2,1,0:T(8,128)S(1)}) custom-call(f32[2,192,128]{2,1,0:T(8,128)S(1)} %copy-done.35, f32[1,8,384,512]{3,2,1,0:T(8,128)S(1)} %copy-done.22, bf16[512,256]{1,0:T(8,128)(2,1)S(1)} %copy-done.14), custom_call_target="tpu_custom_call" | custom-call | flops 768000000 | bytes 314572 | tf_op jit(solution)/shard_map/pallas_call | solution.py:445
  522.8 2.8 copy-done.23
  525.6 12.5 %shard_map.361 = (f32[1,192,128]{2,1,0:T(8,128)S(1)}, f32[1,192,128]{2,1,0:T(8,128)S(1)}, f32[1,384,128]{2,1,0:T(8,128)S(1)}) custom-call(f32[2,192,128]{2,1,0:T(8,128)S(1)} %copy-done.35, f32[1,8,384,512]{3,2,1,0:T(8,128)S(1)} %copy-done.23, bf16[512,256]{1,0:T(8,128)(2,1)S(1)} %copy-done.14), custom_call_target="tpu_custom_call" | custom-call | flops 768000000 | bytes 314572 | tf_op jit(solution)/shard_map/pallas_call | solution.py:445
  542.3 10.3 %collective-permute-start.26 = (f32[3,4,24]{2,0,1:T(4,128)S(1)}, f32[3,4,24]{2,0,1:T(4,128)S(1)}, u32[]{:S(2)}, u32[]{:S(2)}) collective-permute-start(f32[3,4,24]{2,0,1:T(4,128)S(1)} %slice.292), channel_id=1, source_target_pairs={{0,4},{4,0},{1,5},{5,1},{2,6},{6,2},{3,7},{7,3},{8,12},{12,8},{9,1... | collective-permute-start | bytes 3464 | tf_op jit(solution)/shard_map/ppermute | solution.py:1071
  553.5 8.2 %collective-permute-start.27 = (f32[3,2,24]{2,0,1:T(4,128)S(1)}, f32[3,2,24]{2,0,1:T(4,128)S(1)}, u32[]{:S(2)}, u32[]{:S(2)}) collective-permute-start(f32[3,2,24]{2,0,1:T(4,128)S(1)} %slice.294), channel_id=1, source_target_pairs={{0,2},{2,0},{1,3},{3,1},{4,6},{6,4},{5,7},{7,5},{8,10},{10,8},{9,1... | collective-permute-start | bytes 1736 | tf_op jit(solution)/shard_map/ppermute | solution.py:1071
  561.7 4.4 shard_map.358
  573.4 5.0 collective-permute-done.31
  579.5 3.8 collective-permute-done.32
  586.0 2.9 collective-permute-done.33
  592.9 3.2 collective-permute-start.30
  596.0 3.6 all-to-all-start.2
  603.6 15.6 %collective-permute-done.30 = bf16[6,96,384]{2,1,0:T(8,128)(2,1)S(1)} collective-permute-done((bf16[6,96,384]{2,1,0:T(8,128)(2,1)}, bf16[6,96,384]{2,1,0:T(8,128)(2,1)S(1)}, u32[]{:S(2)}, u32[]{:S(2)}) %collective-permute-start.30) | collective-permute-done | bytes 442400 | tf_op jit(solution)/shard_map/ppermute | solution.py:1172
  621.8 3.0 shard_map.362
  (364 shorter events, 121.4 us)
Async XLA Ops:
  4.6 75.1 %collective-permute-start = (bf16[96,2304]{1,0:T(8,128)(2,1)S(1)}, bf16[96,2304]{1,0:T(8,128)(2,1)S(1)}, u32[]{:S(2)}, u32[]{:S(2)}) collective-permute-start(bf16[96,2304]{1,0:T(8,128)(2,1)S(1)} %constant_dynamic-update-slice_fusion), channel_id=1, source_target_pairs={{0,0},{2,4},{4,2},{6,6},{1,1},{3,5},{5,3},{7,7},{8,8},{10,12},{12,... | collective-permute-start | bytes 1327112 | tf_op jit(solution)/shard_map/ppermute | solution.py:1077
  5.3 74.4 %collective-permute-start.1 = (bf16[96,2304]{1,0:T(8,128)(2,1)S(1)}, bf16[96,2304]{1,0:T(8,128)(2,1)S(1)}, u32[]{:S(2)}, u32[]{:S(2)}) collective-permute-start(bf16[96,2304]{1,0:T(8,128)(2,1)S(1)} %constant_dynamic-update-slice_fusion), channel_id=1, source_target_pairs={{4,0},{0,2},{6,4},{2,6},{5,1},{1,3},{7,5},{3,7},{12,8},{8,10},{14,... | collective-permute-start | bytes 1327112 | tf_op jit(solution)/shard_map/ppermute | solution.py:1142
  12.5 67.1 %collective-permute-start.2 = (s32[1027]{0:T(1024)S(1)}, s32[1027]{0:T(1024)S(1)}, u32[]{:S(2)}, u32[]{:S(2)}) collective-permute-start(s32[1027]{0:T(1024)S(1)} %pad_add_fusion), channel_id=1, source_target_pairs={{0,0},{2,4},{4,2},{6,6},{1,1},{3,5},{5,3},{7,7},{8,8},{10,12},{12,... | collective-permute-start | bytes 12332 | tf_op jit(solution)/shard_map/ppermute | solution.py:1077
  90.7 82.8 %collective-permute-start.6 = (bf16[8,768,128]{2,1,0:T(8,128)(2,1)S(1)}, bf16[8,768,128]{2,1,0:T(8,128)(2,1)S(1)}, u32[]{:S(2)}, u32[]{:S(2)}) collective-permute-start(bf16[8,768,128]{2,1,0:T(8,128)(2,1)S(1)} %get-tuple-element.163.x_ref.refs_0_), channel_id=1, source_target_pairs={{0,4},{4,0},{1,5},{5,1},{2,6},{6,2},{3,7},{7,3},{8,12},{12,8},{9,1... | collective-permute-start | bytes 4718600 | tf_op jit(solution)/shard_map/ppermute | solution.py:1071
  90.8 82.7 %collective-permute-start.7 = (bf16[8,768,128]{2,1,0:T(8,128)(2,1)S(1)}, bf16[8,768,128]{2,1,0:T(8,128)(2,1)}, u32[]{:S(2)}, u32[]{:S(2)}) collective-permute-start(bf16[8,768,128]{2,1,0:T(8,128)(2,1)S(1)} %get-tuple-element.163.x_ref.refs_0_), channel_id=1, source_target_pairs={{0,1},{1,0},{2,3},{3,2},{4,5},{5,4},{6,7},{7,6},{8,9},{9,8},{10,11... | collective-permute-start | bytes 4718600 | tf_op jit(solution)/shard_map/ppermute | solution.py:1071
  93.5 66.6 %collective-permute-start.3 = (bf16[192,2304]{1,0:T(8,128)(2,1)}, bf16[192,2304]{1,0:T(8,128)(2,1)}, u32[]{:S(2)}, u32[]{:S(2)}) collective-permute-start(bf16[192,2304]{1,0:T(8,128)(2,1)} %pad_maximum_fusion), channel_id=1, source_target_pairs={{0,8},{8,0},{16,24},{24,16},{1,9},{9,1},{17,25},{25,17},{2,10},{10... | collective-permute-start | bytes 2654216 | tf_op jit(solution)/shard_map/ppermute | solution.py:1071
  94.0 79.5 %collective-permute-start.4 = (bf16[192,2304]{1,0:T(8,128)(2,1)}, bf16[192,2304]{1,0:T(8,128)(2,1)}, u32[]{:S(2)}, u32[]{:S(2)}) collective-permute-start(bf16[192,2304]{1,0:T(8,128)(2,1)} %pad_maximum_fusion), channel_id=1, source_target_pairs={{0,16},{8,24},{16,0},{24,8},{1,17},{9,25},{17,1},{25,9},{2,18},{10... | collective-permute-start | bytes 2654216 | tf_op jit(solution)/shard_map/ppermute | solution.py:1071
  95.4 78.1 %collective-permute-start.5 = (bf16[192,2304]{1,0:T(8,128)(2,1)}, bf16[192,2304]{1,0:T(8,128)(2,1)}, u32[]{:S(2)}, u32[]{:S(2)}) collective-permute-start(bf16[192,2304]{1,0:T(8,128)(2,1)} %pad_maximum_fusion), channel_id=1, source_target_pairs={{0,24},{8,16},{16,8},{24,0},{1,25},{9,17},{17,9},{25,1},{2,26},{10... | collective-permute-start | bytes 2654216 | tf_op jit(solution)/shard_map/ppermute | solution.py:1071
  101.3 20.2 %copy-start.31 = (bf16[256,512]{1,0:T(8,128)(2,1)S(1)}, bf16[256,512]{1,0:T(8,128)(2,1)}, u32[]{:S(2)}) copy-start(bf16[256,512]{1,0:T(8,128)(2,1)} %constant.236.wave_ref) | copy-start | bytes 786436
  101.3 58.8 %all-to-all-start = ((bf16[8,128,768]{2,1,0:T(8,128)(2,1)}), bf16[8,128,768]{2,1,0:T(8,128)(2,1)}, u32[]{:S(2)}, u32[]{:S(2)}) async-start(bf16[8,128,768]{2,1,0:T(8,128)(2,1)} %bitcast.163), calls=%async_computation | async-start | bytes 3145728 | tf_op jit(solution)/shard_map/all_to_all | solution.py:1083
  118.5 37.0 %copy-start.69 = (s32[3]{0:T(128)}, s32[3]{0:T(128)S(1)}, u32[]{:S(2)}) copy-start(s32[3]{0:T(128)S(1)} %bitcast_subtract_fusion.2) | copy-start | bytes 40
  160.2 65.4 %collective-permute-start.9 = (bf16[1024,768]{1,0:T(8,128)(2,1)}, bf16[1024,768]{1,0:T(8,128)(2,1)}, u32[]{:S(2)}, u32[]{:S(2)}) collective-permute-start(bf16[1024,768]{1,0:T(8,128)(2,1)} %bitcast.34), channel_id=1, source_target_pairs={{0,0},{2,4},{4,2},{6,6},{1,1},{3,5},{5,3},{7,7},{8,8},{10,12},{12,... | collective-permute-start | bytes 4718600 | tf_op jit(solution)/shard_map/ppermute | solution.py:1077
  173.5 41.9 %collective-permute-start.8 = (bf16[8,768,128]{2,1,0:T(8,128)(2,1)}, bf16[8,768,128]{2,1,0:T(8,128)(2,1)}, u32[]{:S(2)}, u32[]{:S(2)}) collective-permute-start(bf16[8,768,128]{2,1,0:T(8,128)(2,1)} %collective-permute-done.7.x_ref.refs_2_), channel_id=1, source_target_pairs={{0,4},{4,0},{1,5},{5,1},{2,6},{6,2},{3,7},{7,3},{8,12},{12,8},{9,1... | collective-permute-start | bytes 4718600 | tf_op jit(solution)/shard_map/ppermute | solution.py:1071
  215.4 18.7 %copy-start.62 = (s32[3]{0:T(128)S(1)}, s32[3]{0:T(128)}, u32[]{:S(2)}) copy-start(s32[3]{0:T(128)} %copy-done.61) | copy-start | bytes 40
  232.8 51.9 %copy-start.19 = (bf16[8,768,128]{2,1,0:T(8,128)(2,1)}, bf16[8,768,128]{2,1,0:T(8,128)(2,1)S(1)}, u32[]{:S(2)}) copy-start(bf16[8,768,128]{2,1,0:T(8,128)(2,1)S(1)} %get-tuple-element.192.g_ref.refs_4_) | copy-start | bytes 4718596
  232.8 43.3 %collective-permute-start.10 = (bf16[8,768,128]{2,1,0:T(8,128)(2,1)S(1)}, bf16[8,768,128]{2,1,0:T(8,128)(2,1)S(1)}, u32[]{:S(2)}, u32[]{:S(2)}) collective-permute-start(bf16[8,768,128]{2,1,0:T(8,128)(2,1)S(1)} %get-tuple-element.192.g_ref.refs_4_), channel_id=1, source_target_pairs={{0,4},{4,0},{1,5},{5,1},{2,6},{6,2},{3,7},{7,3},{8,12},{12,8},{9,1... | collective-permute-start | bytes 4718600 | tf_op jit(solution)/shard_map/ppermute | solution.py:1071
  233.1 43.0 %collective-permute-start.11 = (bf16[8,768,128]{2,1,0:T(8,128)(2,1)S(1)}, bf16[8,768,128]{2,1,0:T(8,128)(2,1)}, u32[]{:S(2)}, u32[]{:S(2)}) collective-permute-start(bf16[8,768,128]{2,1,0:T(8,128)(2,1)S(1)} %get-tuple-element.192.g_ref.refs_4_), channel_id=1, source_target_pairs={{0,1},{1,0},{2,3},{3,2},{4,5},{5,4},{6,7},{7,6},{8,9},{9,8},{10,11... | collective-permute-start | bytes 4718600 | tf_op jit(solution)/shard_map/ppermute | solution.py:1071
  237.3 38.7 %copy-start.10 = (bf16[768,768]{1,0:T(8,128)(2,1)}, bf16[768,768]{1,0:T(8,128)(2,1)S(1)}, u32[]{:S(2)}) copy-start(bf16[768,768]{1,0:T(8,128)(2,1)S(1)} %get-tuple-element.370.w_ref) | copy-start | bytes 3538948
  282.5 13.1 %collective-permute-start.12 = (bf16[8,768,128]{2,1,0:T(8,128)(2,1)}, bf16[8,768,128]{2,1,0:T(8,128)(2,1)}, u32[]{:S(2)}, u32[]{:S(2)}) collective-permute-start(bf16[8,768,128]{2,1,0:T(8,128)(2,1)} %shard_map.343), channel_id=1, source_target_pairs={{0,4},{4,0},{1,5},{5,1},{2,6},{6,2},{3,7},{7,3},{8,12},{12,8},{9,1... | collective-permute-start | bytes 4718600 | tf_op jit(solution)/shard_map/ppermute | solution.py:1071
  282.6 17.6 %collective-permute-start.13 = (bf16[8,768,128]{2,1,0:T(8,128)(2,1)}, bf16[8,768,128]{2,1,0:T(8,128)(2,1)}, u32[]{:S(2)}, u32[]{:S(2)}) collective-permute-start(bf16[8,768,128]{2,1,0:T(8,128)(2,1)} %collective-permute-done.11.g_ref.refs_6_), channel_id=1, source_target_pairs={{0,4},{4,0},{1,5},{5,1},{2,6},{6,2},{3,7},{7,3},{8,12},{12,8},{9,1... | collective-permute-start | bytes 4718600 | tf_op jit(solution)/shard_map/ppermute | solution.py:1071
  306.3 44.0 %collective-permute-start.14 = (bf16[8,768,128]{2,1,0:T(8,128)(2,1)}, bf16[8,768,128]{2,1,0:T(8,128)(2,1)S(1)}, u32[]{:S(2)}, u32[]{:S(2)}) collective-permute-start(bf16[8,768,128]{2,1,0:T(8,128)(2,1)} %shard_map.344), channel_id=1, source_target_pairs={{0,4},{4,0},{1,5},{5,1},{2,6},{6,2},{3,7},{7,3},{8,12},{12,8},{9,1... | collective-permute-start | bytes 4718600 | tf_op jit(solution)/shard_map/ppermute | solution.py:1071
  306.4 44.0 %collective-permute-start.15 = (bf16[8,768,128]{2,1,0:T(8,128)(2,1)}, bf16[8,768,128]{2,1,0:T(8,128)(2,1)}, u32[]{:S(2)}, u32[]{:S(2)}) collective-permute-start(bf16[8,768,128]{2,1,0:T(8,128)(2,1)} %shard_map.345), channel_id=1, source_target_pairs={{0,1},{1,0},{2,3},{3,2},{4,5},{5,4},{6,7},{7,6},{8,9},{9,8},{10,11... | collective-permute-start | bytes 4718600 | tf_op jit(solution)/shard_map/ppermute | solution.py:1071
  311.8 38.8 %copy-start.26 = (bf16[8,768,128]{2,1,0:T(8,128)(2,1)S(1)}, bf16[8,768,128]{2,1,0:T(8,128)(2,1)}, u32[]{:S(2)}) copy-start(bf16[8,768,128]{2,1,0:T(8,128)(2,1)} %copy-done.25) | copy-start | bytes 4718596
  356.5 51.0 %copy-start.3 = (bf16[1,32,384,128]{3,2,1,0:T(8,128)(2,1)S(1)}, bf16[1,32,384,128]{3,2,1,0:T(8,128)(2,1)}, u32[]{:S(2)}) copy-start(bf16[1,32,384,128]{3,2,1,0:T(8,128)(2,1)} %get-tuple-element.237.refs_2_.refs_10_) | copy-start | bytes 9437188
  356.5 51.0 %collective-permute-start.16 = (bf16[1024,768]{1,0:T(8,128)(2,1)}, bf16[1024,768]{1,0:T(8,128)(2,1)}, u32[]{:S(2)}, u32[]{:S(2)}) collective-permute-start(bf16[1024,768]{1,0:T(8,128)(2,1)} %shard_map.351), channel_id=1, source_target_pairs={{0,0},{2,4},{4,2},{6,6},{1,1},{3,5},{5,3},{7,7},{8,8},{10,12},{12,... | collective-permute-start | bytes 4718600 | tf_op jit(solution)/shard_map/ppermute | solution.py:1077
  417.3 5.3 collective-permute-start.17
  428.0 59.7 %collective-permute-start.18 = (bf16[8,768,128]{2,1,0:T(8,128)(2,1)}, bf16[8,768,128]{2,1,0:T(8,128)(2,1)}, u32[]{:S(2)}, u32[]{:S(2)}) collective-permute-start(bf16[8,768,128]{2,1,0:T(8,128)(2,1)} %shard_map.354), channel_id=1, source_target_pairs={{0,4},{4,0},{1,5},{5,1},{2,6},{6,2},{3,7},{7,3},{8,12},{12,8},{9,1... | collective-permute-start | bytes 4718600 | tf_op jit(solution)/shard_map/ppermute | solution.py:1071
  428.5 59.3 %collective-permute-start.19 = (bf16[8,768,128]{2,1,0:T(8,128)(2,1)}, bf16[8,768,128]{2,1,0:T(8,128)(2,1)}, u32[]{:S(2)}, u32[]{:S(2)}) collective-permute-start(bf16[8,768,128]{2,1,0:T(8,128)(2,1)} %shard_map.355), channel_id=1, source_target_pairs={{0,1},{1,0},{2,3},{3,2},{4,5},{5,4},{6,7},{7,6},{8,9},{9,8},{10,11... | collective-permute-start | bytes 4718600 | tf_op jit(solution)/shard_map/ppermute | solution.py:1071
  429.0 58.7 %all-to-all-start.1 = ((bf16[8,128,768]{2,1,0:T(8,128)(2,1)}), bf16[8,128,768]{2,1,0:T(8,128)(2,1)}, u32[]{:S(2)}, u32[]{:S(2)}) async-start(bf16[8,128,768]{2,1,0:T(8,128)(2,1)} %bitcast.51), calls=%async_computation.1 | async-start | bytes 3145728 | tf_op jit(solution)/shard_map/all_to_all | solution.py:1083
  453.7 34.1 %copy-start.27 = (bf16[8,768,128]{2,1,0:T(8,128)(2,1)S(1)}, bf16[8,768,128]{2,1,0:T(8,128)(2,1)}, u32[]{:S(2)}) copy-start(bf16[8,768,128]{2,1,0:T(8,128)(2,1)} %copy-done.25) | copy-start | bytes 4718596
  453.7 34.1 %copy-start.33 = (f32[768,128]{1,0:T(8,128)S(1)}, f32[768,128]{1,0:T(8,128)}, u32[]{:S(2)}) copy-start(f32[768,128]{1,0:T(8,128)} %copy-done.32) | copy-start | bytes 1179652
  498.5 69.5 %collective-permute-start.20 = (bf16[1024,768]{1,0:T(8,128)(2,1)}, bf16[1024,768]{1,0:T(8,128)(2,1)S(1)}, u32[]{:S(2)}, u32[]{:S(2)}) collective-permute-start(bf16[1024,768]{1,0:T(8,128)(2,1)} %get-tuple-element.262), channel_id=1, source_target_pairs={{0,0},{2,4},{4,2},{6,6},{1,1},{3,5},{5,3},{7,7},{8,8},{10,12},{12,... | collective-permute-start | bytes 4718600 | tf_op jit(solution)/shard_map/ppermute | solution.py:1077
  500.5 67.4 %collective-permute-start.21 = (bf16[6,192,384]{2,1,0:T(8,128)(2,1)}, bf16[6,192,384]{2,1,0:T(8,128)(2,1)}, u32[]{:S(2)}, u32[]{:S(2)}) collective-permute-start(bf16[6,192,384]{2,1,0:T(8,128)(2,1)} %get-tuple-element.264), channel_id=1, source_target_pairs={{0,8},{8,0},{16,24},{24,16},{1,9},{9,1},{17,25},{25,17},{2,10},{10... | collective-permute-start | bytes 2654216 | tf_op jit(solution)/shard_map/ppermute | solution.py:1071
  502.5 65.4 %collective-permute-start.22 = (bf16[6,192,384]{2,1,0:T(8,128)(2,1)}, bf16[6,192,384]{2,1,0:T(8,128)(2,1)}, u32[]{:S(2)}, u32[]{:S(2)}) collective-permute-start(bf16[6,192,384]{2,1,0:T(8,128)(2,1)} %get-tuple-element.265), channel_id=1, source_target_pairs={{0,16},{8,24},{16,0},{24,8},{1,17},{9,25},{17,1},{25,9},{2,18},{10... | collective-permute-start | bytes 2654216 | tf_op jit(solution)/shard_map/ppermute | solution.py:1071
  504.0 63.9 %collective-permute-start.23 = (bf16[6,192,384]{2,1,0:T(8,128)(2,1)}, bf16[6,192,384]{2,1,0:T(8,128)(2,1)}, u32[]{:S(2)}, u32[]{:S(2)}) collective-permute-start(bf16[6,192,384]{2,1,0:T(8,128)(2,1)} %get-tuple-element.266), channel_id=1, source_target_pairs={{0,24},{8,16},{16,8},{24,0},{1,25},{9,17},{17,9},{25,1},{2,26},{10... | collective-permute-start | bytes 2654216 | tf_op jit(solution)/shard_map/ppermute | solution.py:1071
  505.4 32.8 %collective-permute-start.24 = (f32[3,16,24]{2,0,1:T(4,128)S(1)}, f32[3,16,24]{2,0,1:T(4,128)S(1)}, u32[]{:S(2)}, u32[]{:S(2)}) collective-permute-start(f32[3,16,24]{2,0,1:T(4,128)S(1)} %slice.288), channel_id=1, source_target_pairs={{0,16},{8,24},{16,0},{24,8},{1,17},{9,25},{17,1},{25,9},{2,18},{10... | collective-permute-start | bytes 13832 | tf_op jit(solution)/shard_map/ppermute | solution.py:1071
  525.6 36.1 %copy-start.28 = (s32[1024,1]{1,0:T(8,128)S(1)}, s32[1024,1]{1,0:T(8,128)}, u32[]{:S(2)}) copy-start(s32[1024,1]{1,0:T(8,128)} %copy.159.rank_ref) | copy-start | bytes 12292
  538.2 4.0 collective-permute-start.25
  542.3 11.2 %collective-permute-start.26 = (f32[3,4,24]{2,0,1:T(4,128)S(1)}, f32[3,4,24]{2,0,1:T(4,128)S(1)}, u32[]{:S(2)}, u32[]{:S(2)}) collective-permute-start(f32[3,4,24]{2,0,1:T(4,128)S(1)} %slice.292), channel_id=1, source_target_pairs={{0,4},{4,0},{1,5},{5,1},{2,6},{6,2},{3,7},{7,3},{8,12},{12,8},{9,1... | collective-permute-start | bytes 3464 | tf_op jit(solution)/shard_map/ppermute | solution.py:1071
  553.5 12.6 %collective-permute-start.27 = (f32[3,2,24]{2,0,1:T(4,128)S(1)}, f32[3,2,24]{2,0,1:T(4,128)S(1)}, u32[]{:S(2)}, u32[]{:S(2)}) collective-permute-start(f32[3,2,24]{2,0,1:T(4,128)S(1)} %slice.294), channel_id=1, source_target_pairs={{0,2},{2,0},{1,3},{3,1},{4,6},{6,4},{5,7},{7,5},{8,10},{10,8},{9,1... | collective-permute-start | bytes 1736 | tf_op jit(solution)/shard_map/ppermute | solution.py:1071
  566.1 7.3 %collective-permute-start.28 = (f32[3,1,24]{2,0,1:T(4,128)S(1)}, f32[3,1,24]{2,0,1:T(4,128)S(1)}, u32[]{:S(2)}, u32[]{:S(2)}) collective-permute-start(f32[3,1,24]{2,0,1:T(4,128)S(1)} %slice.296), channel_id=1, source_target_pairs={{0,1},{1,0},{2,3},{3,2},{4,5},{5,4},{6,7},{7,6},{8,9},{9,8},{10,11... | collective-permute-start | bytes 872 | tf_op jit(solution)/shard_map/ppermute | solution.py:1071
  571.9 6.6 %collective-permute-start.31 = (f32[4,12576]{1,0:T(4,128)S(1)}, f32[4,12576]{1,0:T(4,128)S(1)}, u32[]{:S(2)}, u32[]{:S(2)}) collective-permute-start(f32[4,12576]{1,0:T(4,128)S(1)} %slice.303), channel_id=1, source_target_pairs={{0,16},{8,24},{16,0},{24,8},{1,17},{9,25},{17,1},{25,9},{2,18},{10... | collective-permute-start | bytes 603656 | tf_op jit(solution)/shard_map/ppermute | solution.py:1071
  578.6 4.7 collective-permute-start.32
  583.4 5.4 collective-permute-start.33
  589.2 10.4 %collective-permute-start.34 = (f32[48,262]{0,1:T(8,128)S(1)}, f32[48,262]{0,1:T(8,128)S(1)}, u32[]{:S(2)}, u32[]{:S(2)}) collective-permute-start(f32[48,262]{0,1:T(8,128)S(1)} %copy.165), channel_id=1, source_target_pairs={{0,0},{2,1},{8,2},{10,3},{16,4},{18,5},{24,6},{26,7},{1,8},{3,9},{... | collective-permute-start | bytes 150920 | tf_op jit(solution)/shard_map/ppermute | solution.py:1186
  591.2 12.4 %collective-permute-start.29 = (bf16[6,96,384]{2,1,0:T(8,128)(2,1)}, bf16[6,96,384]{2,1,0:T(8,128)(2,1)S(1)}, u32[]{:S(2)}, u32[]{:S(2)}) collective-permute-start(bf16[6,96,384]{2,1,0:T(8,128)(2,1)} %get-tuple-element.379), channel_id=1, source_target_pairs={{0,0},{2,4},{4,2},{6,6},{1,1},{3,5},{5,3},{7,7},{8,8},{10,12},{12,... | collective-permute-start | bytes 1327112 | tf_op jit(solution)/shard_map/ppermute | solution.py:1077
  592.9 26.3 %collective-permute-start.30 = (bf16[6,96,384]{2,1,0:T(8,128)(2,1)}, bf16[6,96,384]{2,1,0:T(8,128)(2,1)S(1)}, u32[]{:S(2)}, u32[]{:S(2)}) collective-permute-start(bf16[6,96,384]{2,1,0:T(8,128)(2,1)} %get-tuple-element.380), channel_id=1, source_target_pairs={{0,4},{2,0},{4,6},{6,2},{1,5},{3,1},{5,7},{7,3},{8,12},{10,8},{12,... | collective-permute-start | bytes 1327112 | tf_op jit(solution)/shard_map/ppermute | solution.py:1172
  596.0 25.7 %all-to-all-start.2 = ((bf16[8,128,768]{2,1,0:T(8,128)(2,1)}), bf16[8,128,768]{2,1,0:T(8,128)(2,1)S(1)}, u32[]{:S(2)}, u32[]{:S(2)}) async-start(bf16[8,128,768]{2,1,0:T(8,128)(2,1)} %bitcast.181), calls=%async_computation.2 | async-start | bytes 3145728 | tf_op jit(solution)/shard_map/all_to_all | solution.py:1083
  (70 other events, 540.7 us)

commit v5 on v4

--- a/solution.py
+++ b/solution.py
@@ -673,7 +673,7 @@
         pl.BlockSpec((2 * BIG, BIG), lambda i: (0, 0)),
     ]
     return pl.pallas_call(
-        partial(back_body, nb, nseq, cc, 16, k == 1),
+        partial(back_body, nb, nseq, cc, 64, k == 1),
         grid=(ch // cc,),
         in_specs=head + [big, big, spec] + tables + [big] * 4,
         out_specs=[out, out, out_spec, pl.BlockSpec((1, cc, 2 * BLK), lambda i: (0, i, 0))],
@@ -759,19 +759,17 @@
     def _():
         acc_s[...] = jnp.zeros_like(acc_s)
 
-    for at, (left, ref, k) in enumerate(
-        [(x_s, gp_refs[0], 0), (x_s, gp_refs[1], 0), (x_s, gpg_refs[0], 0), (x_s, gpg_refs[1], 0)]
-        + [(g_s, mix_ref, 0), (g_s, mix_ref, 1)]
-    ):
-        acc_s[at] += nt(left[...], part(ref, k))
+    split = 4 * ch
+    left = jnp.concatenate([part(ref, 0) for ref in (*gp_refs, *gpg_refs)], axis=0)
+    acc_s[:, :split] += nt(x_s[...], left)
+    acc_s[:, split:] += nt(g_s[...], jnp.concatenate([part(mix_ref, 0), part(mix_ref, 1)], axis=0))
 
     @pl.when(step == pl.num_programs(0) - 1)
     def _():
-        deep = acc_s.shape[1] // cuts
+        deep = acc_s.shape[0] // cuts
         for cut in range(cuts):
             start = pl.multiple_of(at_ref[pl.num_programs(0) + cut] * deep, 8)
-            for at in range(6):
-                outs[cut][at] = acc_s[at, pl.ds(start, deep), :].astype(bf16)
+            outs[cut][...] = acc_s[pl.ds(start, deep), :].astype(bf16)
 
 
 def outer_sums(order, cuts, xs, gs, gp, gpg, mix):
@@ -792,17 +790,46 @@
             num_scalar_prefetch=1,
             grid=(nb // many,),
             in_specs=[rows] * (2 * parts) + [one] * 4 + [chan],
-            out_specs=[pl.BlockSpec((6, width // cuts, ch), lambda i, at: (0, 0, 0))] * cuts,
+            out_specs=[pl.BlockSpec((width // cuts, 6 * ch), lambda i, at: (0, 0))] * cuts,
             scratch_shapes=[
-                pltpu.VMEM((6, width, ch), f32),
+                pltpu.VMEM((width, 6 * ch), f32),
                 pltpu.VMEM((width, many * BLK), bf16),
                 pltpu.VMEM((width, many * BLK), bf16),
             ],
         ),
-        out_shape=[jax.ShapeDtypeStruct((6, width // cuts, ch), bf16)] * cuts,
+        out_shape=[jax.ShapeDtypeStruct((width // cuts, 6 * ch), bf16)] * cuts,
         compiler_params=params(60),
         cost_estimate=cost(12 * tok * width * ch, tok * (4 * width + 12 * ch)),
     )(order, *xs, *gs, *gp, *gpg, mix)
+
+
+def join_body(parts, split, at_ref, *refs):
+    head_ref, tail_ref, head_t_ref, tail_t_ref = refs[parts:]
+    deep = refs[0].shape[0]
+    for at in range(parts):
+        rows = pl.ds(pl.multiple_of(at_ref[at] * deep, 16), deep)
+        head_ref[rows, :] = refs[at][:, :split]
+        tail_ref[rows, :] = refs[at][:, split:]
+    head_t_ref[...] = head_ref[...].T
+    tail_t_ref[...] = tail_ref[...].T
+
+
+def join_weights(order, parts, split):
+    count = len(parts)
+    deep, wide = parts[0].shape
+    rows = deep * count
+    vmem = pl.BlockSpec(memory_space=pltpu.VMEM)
+    return pl.pallas_call(
+        partial(join_body, count, split),
+        in_specs=[pl.BlockSpec(memory_space=pltpu.SMEM)] + [vmem] * count,
+        out_specs=[vmem] * 4,
+        out_shape=[
+            jax.ShapeDtypeStruct(shape, bf16)
+            for shape in ((rows, split), (rows, wide - split), (split, rows), (wide - split, rows))
+        ],
+        compiler_params=params(48),
+        cost_estimate=cost(0, 6 * rows * wide),
+    )(order, *parts)
 
 
 def meet_body(axes, rank_ref, x_ref, chan_ref, norm_ref, got_ref, call_ref, nall_ref, send_s, *sems):
@@ -839,7 +866,7 @@
     def row_copy(kq, kh):
         at = 2 * kq + kh
         return remote(
-            send_s.at[at], got_ref.at[2 * q + c], xs_sem.at[at], xr_sem.at[2 * kq + c], (q ^ kq, h, h ^ kh, w)
+            send_s.at[at], got_ref.at[2 * q + c], xs_sem.at[at], xr_sem.at[2 * kq + c], (q ^ kq, 1 - h, h ^ kh, w)
         )
 
     def own_copy():
@@ -851,24 +878,24 @@
         send_s[2 * kq + kh] = nn(pick, x_ref[...]).astype(bf16)
         if (kq, kh) == (0, 0):
 
+            @pl.when(c != h)
+            def _():
+                own_copy().start()
+
             @pl.when(c == h)
             def _():
-                own_copy().start()
-
-            @pl.when(c != h)
-            def _():
                 row_copy(0, 0).start()
 
         else:
             row_copy(kq, kh).start()
 
-    place = 2 * c + w
+    place = 2 * (1 - c) + w
     spot_c = 4 * c + 2 * h + w
 
     def chan_copy(kq, kh):
         at = 2 * kq + kh
         return remote(
-            chan_ref, call_ref.at[spot_c], cs_sem.at[at], cr_sem.at[spot_c], (q ^ kq, q // 2, h ^ kh, q % 2)
+            chan_ref, call_ref.at[spot_c], cs_sem.at[at], cr_sem.at[spot_c], (q ^ kq, 1 - q // 2, h ^ kh, q % 2)
         )
 
     def own_chan():
@@ -892,11 +919,11 @@
         norm_copy(bits).wait()
     for at in range(8):
 
-        @pl.when((c == h) & (at == c))
+        @pl.when((c != h) & (at == c))
         def _():
             own_copy().wait()
 
-        @pl.when(jnp.logical_not((c == h) & (at == c)))
+        @pl.when(jnp.logical_not((c != h) & (at == c)))
         def _(at=at):
             remote(send_s.at[at], got_ref.at[at], xs_sem.at[at], xr_sem.at[at], peer(1)).wait_recv()
 
@@ -913,7 +940,7 @@
     for kq, kh in pieces:
         if (kq, kh) == (0, 0):
 
-            @pl.when(c != h)
+            @pl.when(c == h)
             def _():
                 row_copy(0, 0).wait_send()
 
@@ -1013,7 +1040,7 @@
     def scatter_own(self, w, arrays, many):
         return []
 
-    def swap(self, x):
+    def ungroup(self, x):
         return x
 
     def spread(self, x):
@@ -1030,7 +1057,7 @@
         perm = [(f, (f % self.n_dp) * self.n_t + f // self.n_dp) for f in range(self.n_dp * self.n_t)]
         chan = lax.ppermute(chan, self.both, perm)
         norm = lax.all_gather(norm, self.both, axis=1, tiled=True)
-        return lax.all_gather(chan, "dp", axis=0, tiled=True), norm
+        return lax.all_gather(chan[None], "dp", axis=0, tiled=True), norm
 
     def weights_first(self, pack):
         return [pack]
@@ -1038,13 +1065,11 @@
     def weights_send(self, packs):
         return [lax.all_gather(packs[0], "dp", axis=0, tiled=True)]
 
-    def weights_last(self, parts):
-        return parts[0]
+    def cut_order(self):
+        return jnp.zeros((1,), jnp.int32)
 
     def grads_send(self, gw):
-        six, width, ch = gw[0].shape
-        gw = gw[0].reshape(six, self.n_dp, width // self.n_dp, ch).transpose(1, 0, 2, 3)
-        return [lax.psum_scatter(gw, "dp", scatter_dimension=0, tiled=True)[0]]
+        return [lax.psum_scatter(gw[0], "dp", scatter_dimension=0, tiled=True)]
 
     def grads_last(self, parts):
         return parts[0].astype(f32)
@@ -1065,26 +1090,28 @@
         self.both = ("q", "c", "h", "w")
         self.cuts = self.quads
         self.other = [(0, 1), (1, 0)]
-        self.crossed = [(2 * c + h, 2 * h + c) for c in range(2) for h in range(2)]
+        self.there = [(2 * c + h, 2 * (1 - h) + c) for c in range(2) for h in range(2)]
+        self.back = [(b, a) for a, b in self.there]
+        self.turned = [(2 * c + h, 2 * (1 - h) + 1 - c) for c in range(2) for h in range(2)]
 
     def flip(self, x, axis, bit=1):
         return lax.ppermute(x, axis, [(i, i ^ bit) for i in range(self.axes[axis])])
 
     def place_of_group(self):
-        return 2 * lax.axis_index("c") + lax.axis_index("w")
+        return 2 * (1 - lax.axis_index("c")) + lax.axis_index("w")
 
     def regroup(self, x):
-        return lax.ppermute(x, ("c", "h"), self.crossed)
-
-    def swap(self, x):
-        return self.regroup(x)
+        return lax.ppermute(x, ("c", "h"), self.there)
+
+    def ungroup(self, x):
+        return lax.ppermute(x, ("c", "h"), self.back)
 
     def spread(self, x):
         return lax.all_to_all(x, ("q", "c"), split_axis=0, concat_axis=0, tiled=True)
 
     def places(self):
         c, w = lax.axis_index("c"), lax.axis_index("w")
-        return [2 * c + w, 2 * (1 - c) + w, 2 * c + 1 - w, 2 * (1 - c) + 1 - w]
+        return [2 * (1 - c) + w, 2 * c + w, 2 * (1 - c) + 1 - w, 2 * c + 1 - w]
 
     def starts(self, many):
         return [(place * many).astype(jnp.int32).reshape(1) for place in self.places()]
@@ -1113,8 +1140,7 @@
 
     def order(self, pieces):
         place = jnp.stack(self.places())[:, None] * pieces + jnp.arange(pieces)[None, :]
-        cut = lax.axis_index("q") ^ jnp.arange(self.quads)
-        return jnp.concatenate([place.reshape(-1), cut]).astype(jnp.int32)
+        return jnp.concatenate([place.reshape(-1).astype(jnp.int32), self.cut_order()])
 
     def steps(self):
         bit = self.quads // 2
@@ -1127,19 +1153,14 @@
         return 2 * lax.axis_index("q") + lax.axis_index("h")
 
     def enter(self, rank, x, chan, norm):
-        own, wide = chan.shape
         small = norm.shape[1]
-        rows = -(-own * wide // 1024) * 8
-        chan = jnp.pad(chan.reshape(-1), (0, rows * BLK - own * wide)).reshape(rows, BLK)
         norm = jnp.pad(norm, ((0, 5), (0, BLK - small)))
         got, chan, norm = meet(self.both, rank, x, chan, norm)
-        chan = chan.reshape(8, -1)[:, : own * wide].reshape(8 * own, wide)
         norm = norm[:, :3, :small].transpose(1, 0, 2).reshape(3, -1)
         return got.reshape(x.shape), chan, norm
 
     def weights_first(self, pack):
-        back = [(2 * (1 - h) + c, 2 * c + h) for c in range(2) for h in range(2)]
-        return [self.regroup(pack), lax.ppermute(pack, ("c", "h"), back)]
+        return [self.regroup(pack), lax.ppermute(pack, ("c", "h"), self.turned)]
 
     def weights_send(self, packs):
         h = lax.axis_index("h")
@@ -1147,14 +1168,6 @@
         pair = jnp.concatenate([jnp.where(h == 0, first, second), jnp.where(h == 0, second, first)], axis=0)
         return [pair] + [self.flip(pair, "q", bit) for bit in range(1, self.quads)]
 
-    def weights_last(self, parts):
-        deep, wide = parts[0].shape
-        q = lax.axis_index("q")
-        whole = jnp.zeros((self.quads * deep, wide), parts[0].dtype)
-        for bit in range(self.quads):
-            whole = lax.dynamic_update_slice_in_dim(whole, parts[bit], (q ^ bit) * deep, 0)
-        return whole
-
     def grads_send(self, gw):
         return [gw[0]] + [self.flip(gw[bit], "q", bit) for bit in range(1, self.quads)]
 
@@ -1163,13 +1176,14 @@
         for part in parts[1:]:
             total = total + part.astype(f32)
         total = total.astype(bf16)
-        six, deep, ch = total.shape
-        total = total.reshape(six, 2, deep // 2, ch)
+        half = total.shape[0] // 2
         h = lax.axis_index("h")
-        first = jnp.where(h == 0, total[:, 0], total[:, 1])
-        second = jnp.where(h == 0, total[:, 1], total[:, 0])
-        there = [(2 * c + h, 2 * (1 - h) + c) for c in range(2) for h in range(2)]
-        return self.regroup(first).astype(f32) + lax.ppermute(second, ("c", "h"), there).astype(f32)
+        first = jnp.where(h == 0, total[:half], total[half:])
+        second = jnp.where(h == 0, total[half:], total[:half])
+        return self.ungroup(first).astype(f32) + lax.ppermute(second, ("c", "h"), self.turned).astype(f32)
+
+    def cut_order(self):
+        return (lax.axis_index("q") ^ jnp.arange(self.quads)).astype(jnp.int32)
 
     def scatter_channels(self, sums):
         count = 2 * self.quads
@@ -1181,7 +1195,7 @@
         perm = []
         for f in range(4 * count):
             place, at = f // count, f % count
-            q, h, c, w = at // 2, at % 2, place // 2, place % 2
+            q, h, c, w = at // 2, at % 2, 1 - place // 2, place % 2
             perm.append((((2 * q + c) * 2 + h) * 2 + w, f))
         return lax.ppermute(part.reshape(rows // count, wide), self.both, perm)
 
@@ -1223,51 +1237,51 @@
     pack = jnp.concatenate(
         [w_fwd, w_bwd, w_gate.reshape(-1, 2 * ch), w_out.transpose(2, 0, 1).reshape(-1, 2 * ch)], axis=1
     )
-    packs = net.weights_first(pack)
     table = net.regroup(jnp.concatenate([place, lengths[0]]))
     rate, ld, drive = decays(log_dt, log_rate, ssm_b)
-    scale = ssm_c * drive
+    own = b_fwd.shape[0]
+    small = jnp.concatenate([ssm_d, b_fwd[None], b_bwd[None], b_gate])
     chan = jnp.concatenate(
-        [ld[0] * log2e, ld[1] * log2e, scale[0], scale[1]]
-        + [jnp.stack([ssm_d[0], ssm_d[1], b_fwd, b_bwd, b_gate[0], b_gate[1]], axis=1)],
-        axis=1,
+        [
+            (ld * log2e).reshape(own, 2 * STATE),
+            (ssm_c * drive).reshape(own, 2 * STATE),
+            jnp.pad(small, ((0, -(2 * own + 6) % 8 + 0), (0, 2 * STATE - own))),
+        ]
     )
     got_x, chan_all, norm_all = net.enter(rank, tokens, chan, jnp.stack([ln_gain, ln_bias, b_out]))
-    got_x, chan_all, norm_all, packs, table, cotangent = after((got_x, chan_all, norm_all, packs, table, cotangent))
-
+    got_x, chan_all, norm_all, table, cotangent, pack = after((got_x, chan_all, norm_all, table, cotangent, pack))
+
+    packs = net.weights_first(pack)
     place, lens = table[:rows], table[rows:]
     gain = lanes(norm_all[0])
     shift = lanes(norm_all[1])
-    bias_out = lanes(norm_all[2])
-    small = chan_all[:, 4 * STATE :]
-    bias_in = lanes(small[:, 2:6].T.reshape(-1))
+    small = chan_all[:, 2 * own : 2 * own + 6, :own].transpose(1, 0, 2).reshape(6, ch)
 
     def pairs(at):
-        both = jnp.stack([chan_all[:, (at + k) * STATE : (at + k + 1) * STATE] for k in range(2)])
-        return both.reshape(2, ch // 2, 2 * STATE)
+        both = chan_all[:, at : at + own].reshape(-1, 2, own // 2, 2 * STATE)
+        return both.transpose(1, 0, 2, 3).reshape(2, ch // 2, 2 * STATE)
 
     ld_pairs = pairs(0)
-    w_pairs = pairs(2)
-    skip = lanes(small[:, 0:2].T)
+    w_pairs = pairs(own)
+    skip = lanes(small[0:2])
     live = live_rows(lens, group)
     live_own = lax.dynamic_slice_in_dim(live, net.place_of_group() * rows, rows, 0).reshape(many, 1, BLK)
     live = live.reshape(nb // 2, 1, BIG)
     tab, seq = sequence_tables(lens, nb)
 
+    xt, xd = deal_x(place, got_x, gain, shift)
+    xt, cotangent, packs, ld_pairs, w_pairs, skip = after((xt, cotangent, packs, ld_pairs, w_pairs, skip))
+    x_got = net.gather_first(xt)
     w_parts = net.weights_send(packs)
-    xt, xd = deal_x(place, got_x, gain, shift)
-    xt, ld_pairs, cotangent = after((xt, ld_pairs, cotangent))
-    x_got = net.gather_first(xt)
     (sent_g,) = permute_to(rank, [cotangent])
     got_g = net.spread(sent_g)
     kh = spectra(ld_pairs, w_pairs, skip, wave)
-    w_parts, x_got, kh = after((w_parts, x_got, kh))
-
-    w_all = net.weights_last(w_parts)
-    w_in, w_back = w_all[:, : 4 * ch], w_all[:, 4 * ch :]
-    w_in_t, w_back_t = w_in.T, w_back.T
+    w_parts, x_got, kh, norm_all, small = after((w_parts, x_got, kh, norm_all, small))
+    bias_in = lanes(small[2:6].reshape(-1))
+    bias_out = lanes(norm_all[2])
+    w_in, w_back, w_in_t, w_back_t = join_weights(net.cut_order(), w_parts, 4 * ch)
     xs = net.gather_last(xt, x_got)
-    got_g = net.swap(got_g)
+    got_g = net.regroup(got_g)
     kept = None
     for part, start in xs:
         kept = project(part, start, nb, live, w_in_t, bias_in, kept)
@@ -1292,7 +1306,7 @@
     branch, first, a = after((branch, first, a))
     sent_out = layer_rows(place, branch, xd, live_own, bias_out)
     sent_out, a = after((sent_out, a))
-    sent_out = net.swap(sent_out)
+    sent_out = net.ungroup(sent_out)
     second = ssm_back(1, tab, seq, a, gm, kh, wave, back, gg, y, dg, da)
     sent_out, first, second = after((sent_out, first, second))
     gpg, gp, gh, bsum = zip(first, second)
@@ -1304,16 +1318,14 @@
     g_normed = net.scatter_send(g_normed)
     g_normed = net.scatter_own(w_in, back_list, many) + g_normed
     gw = outer_sums(net.order(many // 8), net.cuts, [part for part, _ in xs], [part for part, _ in gs], gp, gpg, mix)
-    g_normed, gw, gh, sent_out = after((g_normed, gw, gh, sent_out))
+    first = moments(0, ld_pairs, gh[0], back)
+    g_normed, gw, gh, sent_out, first = after((g_normed, gw, gh, sent_out, first))
     sent_in, norm_sums = input_rows(place, g_normed, xd, gd, gain)
-    sent_in, gh, gw, norm_sums = after((sent_in, gh, gw, norm_sums))
-    sent_in = net.swap(sent_in)
+    sent_in, gh, gw, norm_sums, sent_out = after((sent_in, gh, gw, norm_sums, sent_out))
+    sent_in = net.ungroup(sent_in)
     gw = net.grads_send(gw)
-    s0, s1, g0 = [jnp.concatenate(part) for part in zip(*[moments(k, ld_pairs, gh[k], back) for k in range(2)])]
+    s0, s1, g0 = [jnp.concatenate(part) for part in zip(first, moments(1, ld_pairs, gh[1], back))]
     layer_out = permute_from(rank, sent_out)
-    sent_in, gw, s0, s1, g0 = after((sent_in, gw, s0, s1, g0))
-    gw = net.grads_last(gw)
-    in_grad = permute_from(rank, net.spread(sent_in))
 
     s0 = s0.reshape(2, ch, STATE)
     s1 = s1.reshape(2, ch, STATE)
@@ -1325,6 +1337,9 @@
     )
     sums = net.scatter_channels(sums)
     norm_sums = net.scatter_norm(jnp.sum(jnp.concatenate([norm_sums, g_bias_out[None]], axis=0), axis=2))
+    sent_in, gw, sums, norm_sums, layer_out = after((sent_in, gw, sums, norm_sums, layer_out))
+    in_grad = permute_from(rank, net.spread(sent_in))
+    gw = net.grads_last(gw)
     s0 = jnp.stack([sums[:, :STATE], sums[:, STATE : 2 * STATE]])
     s1 = jnp.stack([sums[:, 2 * STATE : 3 * STATE], sums[:, 3 * STATE : 4 * STATE]])
     tail = sums[:, 4 * STATE :].T
@@ -1340,13 +1355,13 @@
         in_grad,
         norm_sums[0],
         norm_sums[1],
-        gw[0],
+        gw[:, :ch],
         tail[4],
-        gw[1],
+        gw[:, ch : 2 * ch],
         tail[5],
-        jnp.stack([gw[2], gw[3]], axis=1),
+        gw[:, 2 * ch : 4 * ch].reshape(-1, 2, ch),
         tail[2:4],
-        jnp.stack([gw[4].T, gw[5].T]),
+        gw[:, 4 * ch :].T.reshape(2, ch, -1),
         norm_sums[2],
         g_dt,
         g_rate * rate,

time: 638 us -> 588 us (0.922)
  the two profiles are of different devices: /device:TPU:0 before, /device:TPU:1 now
where the time goes in v5:
time: 588 us; the launch traced here: 580 us
  Pallas kernels  349 us (59%)
  starting transfers between devices  74.8 us (13%)
  waiting for transfers between devices  68.3 us (12%)
  local copies, waits for them, and re-layouts  62.6 us (11%)
  other arithmetic  22.5 us (4%)
    pallas_call x2, Pallas kernels, ssm_back(): pl.pallas_call(partial(back_body, nb, nseq, cc, 64, k == 1), grid=(ch //...  56.1 us
    pallas_call x1, Pallas kernels, meet(): pl.pallas_call(partial(meet_body, axes), in_specs=[vmem] * 4, out_specs=[...  52 us
    pallas_call x8, Pallas kernels, chained(): pl.pallas_call(body, grid_spec=pltpu.PrefetchScalarGridSpec(num_scalar_pr...  47.6 us
    unnamed x146, local copies, waits for them, and re-layouts  46.9 us
    ppermute x26, waiting for transfers between devices, flip(): return lax.ppermute(x, axis, [(i, i ^ bit) for i in range(self.axes[axis])])  41.9 us
    ppermute x26, starting transfers between devices, flip(): return lax.ppermute(x, axis, [(i, i ^ bit) for i in range(self.axes[axis])])  36.9 us
    pallas_call x1, Pallas kernels, ssm_scan(): pl.pallas_call(partial(scan_body, nb, nseq, cc, 32), grid=(2, ch // cc),...  35.3 us
    pallas_call x1, Pallas kernels, spectra(): pl.pallas_call(partial(spectra_body, cc), grid=(2, ch // cc), in_specs=[p...  33.1 us
  transfers between devices with their start and end apart: 38, of which 12 were waited for; matrix products, arithmetic and copies ran while one was open for 6% of the time, Pallas kernels for 54%

profile of v5, /device:TPU:1, one launch (start us, length us, event | category | flops | bytes accessed | tf_op | source)
XLA Modules:
  0.0 579.7 jit_solution(6002314171201015751)
XLA Ops:
  2.6 3.1 collective-permute-start
  14.2 52.0 %shard_map.332 = (bf16[8,128,768]{2,1,0:T(8,128)(2,1)S(1)}, f32[8,104,128]{2,1,0:T(8,128)S(1)}, f32[32,8,128]{2,1,0:T(8,128)S(1)}) custom-call(s32[1,1024]{1,0:T(1,128)S(1)} %bitcast.120, bf16[1024,768]{1,0:T(8,128)(2,1)S(1)} %copy-done.39, f32[104,128]{1,0:T(8,128)S(1)} %pad_maximum_fusion.3.chan_ref, f32[8,128]{1,0:T(8,128)S(1)} %select_maximum_fusion.norm_ref), custom_call_target="tpu_custom_call" | custom-call | flops 80530640 | bytes 3932160 | tf_op jit(solution)/shard_map/pallas_call | solution.py:960
  73.1 6.1 %shard_map.333 = (bf16[8,768,128]{2,1,0:T(8,128)(2,1)S(1)}, bf16[8,768,128]{2,1,0:T(8,128)(2,1)S(1)}) custom-call(s32[1024,1]{1,0:T(8,128)S(1)} %copy.162.place_ref, bf16[1024,768]{1,0:T(8,128)(2,1)S(1)} %bitcast.113, f32[768,128]{1,0:T(8,128)S(1)} %broadcast_in_dim.107.gain_ref, f32[768,128]{1,0:T(8,128)S(1)} %broadcast_in_dim.109.shift_ref), custom_call_target="tpu_custom_call" | custom-call | flops 80530640 | bytes 235929 | tf_op jit(solution)/shard_map/pallas_call | solution.py:137
  82.3 9.3 %collective-permute-start.6 = (bf16[8,768,128]{2,1,0:T(8,128)(2,1)S(1)}, bf16[8,768,128]{2,1,0:T(8,128)(2,1)S(1)}, u32[]{:S(2)}, u32[]{:S(2)}) collective-permute-start(bf16[8,768,128]{2,1,0:T(8,128)(2,1)S(1)} %get-tuple-element.176.x_ref.refs_0_), channel_id=1, source_target_pairs={{0,4},{4,0},{1,5},{5,1},{2,6},{6,2},{3,7},{7,3},{8,12},{12,8},{9,1... | collective-permute-start | bytes 4718600 | tf_op jit(solution)/shard_map/ppermute | solution.py:1098
  94.7 4.2 all-to-all-start
  107.1 33.1 %shard_map.334.kh_ref = f32[2,8,384,512]{3,2,1,0:T(8,128)S(1)} custom-call(f32[2,192,128]{2,1,0:T(8,128)S(1)} %bitcast.110, f32[2,192,128]{2,1,0:T(8,128)S(1)} %bitcast.114, f32[2,384,128]{2,1,0:T(8,128)S(1)} %copy-done.45, bf16[256,512]{1,0:T(8,128)(2,1)S(1)} %copy-done.34), custom_call_target="tpu_custom_call" | custom-call | flops 1536000000 | bytes 629145 | tf_op jit(solution)/shard_map/pallas_call | solution.py:387
  140.2 4.6 copy-done.1
  144.8 12.3 %collective-permute-done.5.refs_3_ = bf16[192,2304]{1,0:T(8,128)(2,1)} collective-permute-done((bf16[192,2304]{1,0:T(8,128)(2,1)}, bf16[192,2304]{1,0:T(8,128)(2,1)}, u32[]{:S(2)}, u32[]{:S(2)}) %collective-permute-start.5) | collective-permute-done | bytes 884768 | tf_op jit(solution)/shard_map/ppermute | solution.py:1098
  162.4 5.0 shard_map.335
  169.5 9.0 %shard_map.336 = (bf16[2,32,384,128]{3,2,1,0:T(8,128)(2,1)}, bf16[2,32,384,128]{3,2,1,0:T(8,128)(2,1)}, bf16[2,32,384,128]{3,2,1,0:T(8,128)(2,1)}, bf16[2,32,384,128]{3,2,1,0:T(8,128)(2,1)}) custom-call(s32[1]{0:T(128)S(6)} %select_n.125.start_ref, bf16[8,768,128]{2,1,0:T(8,128)(2,1)S(1)} %copy-done.20, f32[16,1,256]{2,1,0:T(1,128)S(1)} %bitcast.115, ...), custom_call_target="tpu_custom_call" | custom-call | flops 120795952 | bytes 393216 | tf_op jit(solution)/shard_map/pallas_call | solution.py:279
  178.5 9.0 %shard_map.337 = (bf16[2,32,384,128]{3,2,1,0:T(8,128)(2,1)}, bf16[2,32,384,128]{3,2,1,0:T(8,128)(2,1)}, bf16[2,32,384,128]{3,2,1,0:T(8,128)(2,1)}, bf16[2,32,384,128]{3,2,1,0:T(8,128)(2,1)}) custom-call(s32[1]{0:T(128)S(6)} %select_n.124.start_ref, ...), custom_call_target="tpu_custom_call", output_to_operand_aliasing={{0}: (5, {}), {1}: (6, {}), {2}: (7, {}), {3}: (8, {})} | custom-call | flops 120795952 | bytes 393216 | tf_op jit(solution)/shard_map/pallas_call | solution.py:279
  187.5 10.0 %shard_map.338 = (bf16[2,32,384,128]{3,2,1,0:T(8,128)(2,1)}, bf16[2,32,384,128]{3,2,1,0:T(8,128)(2,1)}, bf16[2,32,384,128]{3,2,1,0:T(8,128)(2,1)}, bf16[2,32,384,128]{3,2,1,0:T(8,128)(2,1)}) custom-call(s32[1]{0:T(128)S(6)} %select_n.123.start_ref, ...), custom_call_target="tpu_custom_call", output_to_operand_aliasing={{0}: (5, {}), {1}: (6, {}), {2}: (7, {}), {3}: (8, {})} | custom-call | flops 120795952 | bytes 393216 | tf_op jit(solution)/shard_map/pallas_call | solution.py:279
  197.5 10.1 %shard_map.339 = (bf16[2,32,384,128]{3,2,1,0:T(8,128)(2,1)}, bf16[2,32,384,128]{3,2,1,0:T(8,128)(2,1)}, bf16[2,32,384,128]{3,2,1,0:T(8,128)(2,1)}, bf16[2,32,384,128]{3,2,1,0:T(8,128)(2,1)}) custom-call(s32[1]{0:T(128)S(6)} %select_n.118.start_ref, ...), custom_call_target="tpu_custom_call", output_to_operand_aliasing={{0}: (5, {}), {1}: (6, {}), {2}: (7, {}), {3}: (8, {})} | custom-call | flops 120795952 | bytes 393216 | tf_op jit(solution)/shard_map/pallas_call | solution.py:279
  207.6 4.6 shard_map.341
  217.5 35.3 %shard_map.342 = (bf16[2,32,384,128]{3,2,1,0:T(8,128)(2,1)}, bf16[2,32,384,128]{3,2,1,0:T(8,128)(2,1)}) custom-call(s32[2,17]{1,0:T(2,128)} %pad_add_fusion.1.tab_ref, s32[2,4]{1,0:T(2,128)} %pad_add_fusion.2.seq_ref, bf16[2,32,384,128]{3,2,1,0:T(8,128)(2,1)} %get-tuple-element.244.a_ref, f32[2,8,384,512]{3,2,1,0:T(8,128)} %copy-done.1, ...), custom_call_target="tpu_custom_call" | custom-call | flops 1920000000 | bytes 1258291 | tf_op jit(solution)/shard_map/pallas_call | solution.py:648
  254.0 2.8 copy-done.2
  265.8 3.6 shard_map.349.refs_0_
  269.3 4.6 shard_map.346
  276.0 2.6 copy-done
  283.9 28.1 %shard_map.351 = (bf16[1,32,384,128]{3,2,1,0:T(8,128)(2,1)}, bf16[1,32,384,128]{3,2,1,0:T(8,128)(2,1)}, f32[1,8,384,512]{3,2,1,0:T(8,128)}, f32[1,384,256]{2,1,0:T(8,128)}) custom-call(s32[2,17]{1,0:T(2,128)} %pad_add_fusion.1.tab_ref, s32[2,4]{1,0:T(2,128)} %pad_add_fusion.2.seq_ref, bf16[2,32,384,128]{3,2,1,0:T(8,128)(2,1)} %get-tuple-element.244.a_ref, ...), custom_call_target="tpu_custom_call" | custom-call | flops 1536000000 | bytes 1258291 | tf_op jit(solution)/shard_map/pallas_call | solution.py:675
  312.0 3.0 collective-permute-done.15.refs_2_
  315.2 6.4 %shard_map.352 = bf16[1024,768]{1,0:T(8,128)(2,1)} custom-call(s32[1,1024]{1,0:T(1,128)S(1)} %bitcast.124, bf16[8,768,128]{2,1,0:T(8,128)(2,1)S(1)} %copy-done.30, f32[8,1,128]{2,1,0:T(1,128)S(1)} %bitcast.127, f32[768,128]{1,0:T(8,128)S(1)} %broadcast_in_dim.115.bias_ref, f32[8,768,128]{2,1,0:T(8,128)} %copy-done.14, ...), custom_call_target="tpu_custom_call" | custom-call | flops 80530640 | bytes 235929 | tf_op jit(solution)/shard_map/pallas_call | solution.py:189
  322.6 28.0 %shard_map.353 = (bf16[1,32,384,128]{3,2,1,0:T(8,128)(2,1)}, bf16[1,32,384,128]{3,2,1,0:T(8,128)(2,1)}, f32[1,8,384,512]{3,2,1,0:T(8,128)}, f32[1,384,256]{2,1,0:T(8,128)}) custom-call(s32[2,17]{1,0:T(2,128)} %pad_add_fusion.1.tab_ref, s32[2,4]{1,0:T(2,128)} %pad_add_fusion.2.seq_ref, bf16[2,32,384,128]{3,2,1,0:T(8,128)(2,1)} %get-tuple-element.244.a_ref, ...), custom_call_target="tpu_custom_call" | custom-call | flops 1536000000 | bytes 1258291 | tf_op jit(solution)/shard_map/pallas_call | solution.py:675
  350.5 10.5 %collective-permute-done.16 = bf16[1024,768]{1,0:T(8,128)(2,1)} collective-permute-done((bf16[1024,768]{1,0:T(8,128)(2,1)}, bf16[1024,768]{1,0:T(8,128)(2,1)}, u32[]{:S(2)}, u32[]{:S(2)}) %collective-permute-start.16) | collective-permute-done | bytes 1572896 | tf_op jit(solution)/shard_map/ppermute | solution.py:1107
  366.4 4.3 shard_map.354
  370.8 5.2 shard_map.355
  376.0 5.4 shard_map.356
  383.1 9.3 %all-to-all-start.1 = ((bf16[8,128,768]{2,1,0:T(8,128)(2,1)}), bf16[8,128,768]{2,1,0:T(8,128)(2,1)}, u32[]{:S(2)}, u32[]{:S(2)}) async-start(bf16[8,128,768]{2,1,0:T(8,128)(2,1)} %bitcast.44), calls=%async_computation.1 | async-start | bytes 3145728 | tf_op jit(solution)/shard_map/all_to_all | solution.py:1110
  395.0 2.8 copy-done.27
  397.8 12.7 %shard_map.359 = (f32[1,192,128]{2,1,0:T(8,128)S(1)}, f32[1,192,128]{2,1,0:T(8,128)S(1)}, f32[1,384,128]{2,1,0:T(8,128)S(1)}) custom-call(f32[2,192,128]{2,1,0:T(8,128)S(1)} %bitcast.111, f32[1,8,384,512]{3,2,1,0:T(8,128)S(1)} %copy-done.27, bf16[512,256]{1,0:T(8,128)(2,1)S(1)} %copy-done.16), custom_call_target="tpu_custom_call" | custom-call | flops 768000000 | bytes 314572 | tf_op jit(solution)/shard_map/pallas_call | solution.py:445
  412.2 4.5 shard_map.357.refs_0_
  418.4 29.1 %shard_map.358 = (bf16[192,2304]{1,0:T(8,128)(2,1)}, bf16[192,2304]{1,0:T(8,128)(2,1)}, bf16[192,2304]{1,0:T(8,128)(2,1)}, bf16[192,2304]{1,0:T(8,128)(2,1)}) custom-call(s32[8]{0:T(128)} %concatenate.49.at_ref, bf16[8,768,128]{2,1,0:T(8,128)(2,1)} %copy-done.19, bf16[8,768,128]{2,1,0:T(8,128)(2,1)} %copy-done.17, ...), custom_call_target="tpu_custom_call" | custom-call | flops 724775744 | bytes 1572864 | tf_op jit(solution)/shard_map/pallas_call | solution.py:787
  448.9 9.2 %shard_map.360 = (bf16[1024,768]{1,0:T(8,128)(2,1)}, f32[2,768,128]{2,1,0:T(8,128)S(1)}) custom-call(s32[1,1024]{1,0:T(1,128)S(1)} %bitcast.125, bf16[8,768,128]{2,1,0:T(8,128)(2,1)S(1)} %copy-done.31, bf16[8,768,128]{2,1,0:T(8,128)(2,1)S(1)} %copy-done.44, f32[768,128]{1,0:T(8,128)S(1)} %copy-done.36, f32[8,768,128]{2,1,0:T(8,128)} %copy-done.15, ...), custom_call_target="tpu_custom_call" | custom-call | flops 80530640 | bytes 314572 | tf_op jit(solution)/shard_map/pallas_call | solution.py:225
  462.9 2.8 copy-done.26
  465.6 12.7 %shard_map.361 = (f32[1,192,128]{2,1,0:T(8,128)S(1)}, f32[1,192,128]{2,1,0:T(8,128)S(1)}, f32[1,384,128]{2,1,0:T(8,128)S(1)}) custom-call(f32[2,192,128]{2,1,0:T(8,128)S(1)} %bitcast.112, f32[1,8,384,512]{3,2,1,0:T(8,128)S(1)} %copy-done.26, bf16[512,256]{1,0:T(8,128)(2,1)S(1)} %copy-done.16), custom_call_target="tpu_custom_call" | custom-call | flops 768000000 | bytes 314572 | tf_op jit(solution)/shard_map/pallas_call | solution.py:445
  483.6 16.0 %collective-permute-done.28 = f32[3,16,24]{2,0,1:T(4,128)S(1)} collective-permute-done((f32[3,16,24]{2,0,1:T(4,128)S(1)}, f32[3,16,24]{2,0,1:T(4,128)S(1)}, u32[]{:S(2)}, u32[]{:S(2)}) %collective-permute-start.28) | collective-permute-done | bytes 4640 | tf_op jit(solution)/shard_map/ppermute | solution.py:1098
  500.9 4.4 shard_map.362
  505.4 2.5 collective-permute-start.24
  507.9 3.4 collective-permute-done.24
  511.4 2.5 collective-permute-start.30
  515.5 3.3 collective-permute-done.25
  518.8 3.4 collective-permute-start.31
  523.2 2.4 collective-permute-start.26
  529.9 4.3 collective-permute-start.27
  535.2 7.5 %all-to-all-start.2 = ((bf16[8,128,768]{2,1,0:T(8,128)(2,1)}), bf16[8,128,768]{2,1,0:T(8,128)(2,1)S(1)}, u32[]{:S(2)}, u32[]{:S(2)}) async-start(bf16[8,128,768]{2,1,0:T(8,128)(2,1)} %bitcast.53), calls=%async_computation.2 | async-start | bytes 3145728 | tf_op jit(solution)/shard_map/all_to_all | solution.py:1110
  547.5 3.7 collective-permute-start.33
  555.9 15.0 %collective-permute-done.33 = bf16[96,2304]{1,0:T(8,128)(2,1)} collective-permute-done((bf16[96,2304]{1,0:T(8,128)(2,1)S(1)}, bf16[96,2304]{1,0:T(8,128)(2,1)}, u32[]{:S(2)}, u32[]{:S(2)}) %collective-permute-start.33) | collective-permute-done | bytes 442400 | tf_op jit(solution)/shard_map/ppermute | solution.py:1107
  576.3 3.0 shard_map.363
  (318 shorter events, 110.9 us)
Async XLA Ops:
  0.7 66.6 %copy-start.61 = (bf16[96,384]{1,0:T(8,128)(2,1)S(1)}, bf16[96,384]{1,0:T(8,128)(2,1)}, u32[]{:S(2)}) copy-start(bf16[96,384]{1,0:T(8,128)(2,1)} %param.30) | copy-start | bytes 221188
  0.7 66.6 %copy-start.62 = (bf16[96,384]{1,0:T(8,128)(2,1)S(1)}, bf16[96,384]{1,0:T(8,128)(2,1)}, u32[]{:S(2)}) copy-start(bf16[96,384]{1,0:T(8,128)(2,1)} %param.28) | copy-start | bytes 221188
  2.6 64.8 %collective-permute-start = (s32[1027]{0:T(1024)S(1)}, s32[1027]{0:T(1024)S(1)}, u32[]{:S(2)}, u32[]{:S(2)}) collective-permute-start(s32[1027]{0:T(1024)S(1)} %pad_add_fusion), channel_id=1, source_target_pairs={{0,4},{2,0},{4,6},{6,2},{1,5},{3,1},{5,7},{7,3},{8,12},{10,8},{12,... | collective-permute-start | bytes 12332 | tf_op jit(solution)/shard_map/ppermute | solution.py:1104
  67.5 12.9 %collective-permute-start.1 = (bf16[96,2304]{1,0:T(8,128)(2,1)S(1)}, bf16[96,2304]{1,0:T(8,128)(2,1)S(1)}, u32[]{:S(2)}, u32[]{:S(2)}) collective-permute-start(bf16[96,2304]{1,0:T(8,128)(2,1)S(1)} %pad_maximum_fusion.1), channel_id=1, source_target_pairs={{0,4},{2,0},{4,6},{6,2},{1,5},{3,1},{5,7},{7,3},{8,12},{10,8},{12,... | collective-permute-start | bytes 1327112 | tf_op jit(solution)/shard_map/ppermute | solution.py:1104
  68.5 11.9 %collective-permute-start.2 = (bf16[96,2304]{1,0:T(8,128)(2,1)S(1)}, bf16[96,2304]{1,0:T(8,128)(2,1)S(1)}, u32[]{:S(2)}, u32[]{:S(2)}) collective-permute-start(bf16[96,2304]{1,0:T(8,128)(2,1)S(1)} %pad_maximum_fusion.1), channel_id=1, source_target_pairs={{0,6},{2,2},{4,4},{6,0},{1,7},{3,3},{5,5},{7,1},{8,14},{10,10},{12... | collective-permute-start | bytes 1327112 | tf_op jit(solution)/shard_map/ppermute | solution.py:1163
  71.2 20.4 %copy-start.40 = (bf16[1024,768]{1,0:T(8,128)(2,1)S(1)}, bf16[1024,768]{1,0:T(8,128)(2,1)}, u32[]{:S(2)}) copy-start(bf16[1024,768]{1,0:T(8,128)(2,1)} %refs_0_) | copy-start | bytes 4718596
  82.3 74.8 %collective-permute-start.6 = (bf16[8,768,128]{2,1,0:T(8,128)(2,1)S(1)}, bf16[8,768,128]{2,1,0:T(8,128)(2,1)S(1)}, u32[]{:S(2)}, u32[]{:S(2)}) collective-permute-start(bf16[8,768,128]{2,1,0:T(8,128)(2,1)S(1)} %get-tuple-element.176.x_ref.refs_0_), channel_id=1, source_target_pairs={{0,4},{4,0},{1,5},{5,1},{2,6},{6,2},{3,7},{7,3},{8,12},{12,8},{9,1... | collective-permute-start | bytes 4718600 | tf_op jit(solution)/shard_map/ppermute | solution.py:1098
  91.7 66.6 %collective-permute-start.7 = (bf16[8,768,128]{2,1,0:T(8,128)(2,1)S(1)}, bf16[8,768,128]{2,1,0:T(8,128)(2,1)}, u32[]{:S(2)}, u32[]{:S(2)}) collective-permute-start(bf16[8,768,128]{2,1,0:T(8,128)(2,1)S(1)} %get-tuple-element.176.x_ref.refs_0_), channel_id=1, source_target_pairs={{0,1},{1,0},{2,3},{3,2},{4,5},{5,4},{6,7},{7,6},{8,9},{9,8},{10,11... | collective-permute-start | bytes 4718600 | tf_op jit(solution)/shard_map/ppermute | solution.py:1098
  94.7 64.5 %all-to-all-start = ((bf16[8,128,768]{2,1,0:T(8,128)(2,1)}), bf16[8,128,768]{2,1,0:T(8,128)(2,1)}, u32[]{:S(2)}, u32[]{:S(2)}) async-start(bf16[8,128,768]{2,1,0:T(8,128)(2,1)} %bitcast.109), calls=%async_computation | async-start | bytes 3145728 | tf_op jit(solution)/shard_map/all_to_all | solution.py:1110
  101.2 43.6 %collective-permute-start.3 = (bf16[192,2304]{1,0:T(8,128)(2,1)}, bf16[192,2304]{1,0:T(8,128)(2,1)}, u32[]{:S(2)}, u32[]{:S(2)}) collective-permute-start(bf16[192,2304]{1,0:T(8,128)(2,1)} %pad_maximum_fusion.refs_0_), channel_id=1, source_target_pairs={{0,8},{8,0},{16,24},{24,16},{1,9},{9,1},{17,25},{25,17},{2,10},{10... | collective-permute-start | bytes 2654216 | tf_op jit(solution)/shard_map/ppermute | solution.py:1098
  102.9 41.8 %collective-permute-start.4 = (bf16[192,2304]{1,0:T(8,128)(2,1)}, bf16[192,2304]{1,0:T(8,128)(2,1)}, u32[]{:S(2)}, u32[]{:S(2)}) collective-permute-start(bf16[192,2304]{1,0:T(8,128)(2,1)} %pad_maximum_fusion.refs_0_), channel_id=1, source_target_pairs={{0,16},{8,24},{16,0},{24,8},{1,17},{9,25},{17,1},{25,9},{2,18},{10... | collective-permute-start | bytes 2654216 | tf_op jit(solution)/shard_map/ppermute | solution.py:1098
  103.7 53.4 %collective-permute-start.5 = (bf16[192,2304]{1,0:T(8,128)(2,1)}, bf16[192,2304]{1,0:T(8,128)(2,1)}, u32[]{:S(2)}, u32[]{:S(2)}) collective-permute-start(bf16[192,2304]{1,0:T(8,128)(2,1)} %pad_maximum_fusion.refs_0_), channel_id=1, source_target_pairs={{0,24},{8,16},{16,8},{24,0},{1,25},{9,17},{17,9},{25,1},{2,26},{10... | collective-permute-start | bytes 2654216 | tf_op jit(solution)/shard_map/ppermute | solution.py:1098
  158.3 39.2 %collective-permute-start.8 = (bf16[8,768,128]{2,1,0:T(8,128)(2,1)}, bf16[8,768,128]{2,1,0:T(8,128)(2,1)}, u32[]{:S(2)}, u32[]{:S(2)}) collective-permute-start(bf16[8,768,128]{2,1,0:T(8,128)(2,1)} %collective-permute-done.7.x_ref.refs_2_), channel_id=1, source_target_pairs={{0,4},{4,0},{1,5},{5,1},{2,6},{6,2},{3,7},{7,3},{8,12},{12,8},{9,1... | collective-permute-start | bytes 4718600 | tf_op jit(solution)/shard_map/ppermute | solution.py:1098
  159.1 48.4 %collective-permute-start.9 = (bf16[1024,768]{1,0:T(8,128)(2,1)}, bf16[1024,768]{1,0:T(8,128)(2,1)S(1)}, u32[]{:S(2)}, u32[]{:S(2)}) collective-permute-start(bf16[1024,768]{1,0:T(8,128)(2,1)} %bitcast.27), channel_id=1, source_target_pairs={{0,4},{2,0},{4,6},{6,2},{1,5},{3,1},{5,7},{7,3},{8,12},{10,8},{12,... | collective-permute-start | bytes 4718600 | tf_op jit(solution)/shard_map/ppermute | solution.py:1104
  167.4 86.6 %copy-start.12 = (bf16[768,768]{1,0:T(8,128)(2,1)}, bf16[768,768]{1,0:T(8,128)(2,1)S(1)}, u32[]{:S(2)}) copy-start(bf16[768,768]{1,0:T(8,128)(2,1)S(1)} %get-tuple-element.209.w_ref) | copy-start | bytes 3538948
  213.3 39.5 %copy-start.21 = (bf16[8,768,128]{2,1,0:T(8,128)(2,1)}, bf16[8,768,128]{2,1,0:T(8,128)(2,1)S(1)}, u32[]{:S(2)}) copy-start(bf16[8,768,128]{2,1,0:T(8,128)(2,1)S(1)} %get-tuple-element.212.g_ref.refs_4_) | copy-start | bytes 4718596
  213.3 39.5 %collective-permute-start.10 = (bf16[8,768,128]{2,1,0:T(8,128)(2,1)S(1)}, bf16[8,768,128]{2,1,0:T(8,128)(2,1)S(1)}, u32[]{:S(2)}, u32[]{:S(2)}) collective-permute-start(bf16[8,768,128]{2,1,0:T(8,128)(2,1)S(1)} %get-tuple-element.212.g_ref.refs_4_), channel_id=1, source_target_pairs={{0,4},{4,0},{1,5},{5,1},{2,6},{6,2},{3,7},{7,3},{8,12},{12,8},{9,1... | collective-permute-start | bytes 4718600 | tf_op jit(solution)/shard_map/ppermute | solution.py:1098
  213.3 40.7 %collective-permute-start.11 = (bf16[8,768,128]{2,1,0:T(8,128)(2,1)S(1)}, bf16[8,768,128]{2,1,0:T(8,128)(2,1)}, u32[]{:S(2)}, u32[]{:S(2)}) collective-permute-start(bf16[8,768,128]{2,1,0:T(8,128)(2,1)S(1)} %get-tuple-element.212.g_ref.refs_4_), channel_id=1, source_target_pairs={{0,1},{1,0},{2,3},{3,2},{4,5},{5,4},{6,7},{7,6},{8,9},{9,8},{10,11... | collective-permute-start | bytes 4718600 | tf_op jit(solution)/shard_map/ppermute | solution.py:1098
  258.9 10.4 %collective-permute-start.12 = (bf16[8,768,128]{2,1,0:T(8,128)(2,1)S(1)}, bf16[8,768,128]{2,1,0:T(8,128)(2,1)}, u32[]{:S(2)}, u32[]{:S(2)}) collective-permute-start(bf16[8,768,128]{2,1,0:T(8,128)(2,1)S(1)} %shard_map.344), channel_id=1, source_target_pairs={{0,4},{4,0},{1,5},{5,1},{2,6},{6,2},{3,7},{7,3},{8,12},{12,8},{9,1... | collective-permute-start | bytes 4718600 | tf_op jit(solution)/shard_map/ppermute | solution.py:1098
  259.3 14.6 %collective-permute-start.13 = (bf16[8,768,128]{2,1,0:T(8,128)(2,1)}, bf16[8,768,128]{2,1,0:T(8,128)(2,1)S(1)}, u32[]{:S(2)}, u32[]{:S(2)}) collective-permute-start(bf16[8,768,128]{2,1,0:T(8,128)(2,1)} %collective-permute-done.11.g_ref.refs_6_), channel_id=1, source_target_pairs={{0,4},{4,0},{1,5},{5,1},{2,6},{6,2},{3,7},{7,3},{8,12},{12,8},{9,1... | collective-permute-start | bytes 4718600 | tf_op jit(solution)/shard_map/ppermute | solution.py:1098
  278.5 33.5 %collective-permute-start.14 = (bf16[8,768,128]{2,1,0:T(8,128)(2,1)S(1)}, bf16[8,768,128]{2,1,0:T(8,128)(2,1)}, u32[]{:S(2)}, u32[]{:S(2)}) collective-permute-start(bf16[8,768,128]{2,1,0:T(8,128)(2,1)S(1)} %shard_map.345), channel_id=1, source_target_pairs={{0,4},{4,0},{1,5},{5,1},{2,6},{6,2},{3,7},{7,3},{8,12},{12,8},{9,1... | collective-permute-start | bytes 4718600 | tf_op jit(solution)/shard_map/ppermute | solution.py:1098
  278.9 36.1 %collective-permute-start.15 = (bf16[8,768,128]{2,1,0:T(8,128)(2,1)}, bf16[8,768,128]{2,1,0:T(8,128)(2,1)}, u32[]{:S(2)}, u32[]{:S(2)}) collective-permute-start(bf16[8,768,128]{2,1,0:T(8,128)(2,1)} %shard_map.346), channel_id=1, source_target_pairs={{0,1},{1,0},{2,3},{3,2},{4,5},{5,4},{6,7},{7,6},{8,9},{9,8},{10,11... | collective-permute-start | bytes 4718600 | tf_op jit(solution)/shard_map/ppermute | solution.py:1098
  283.9 31.3 %copy-start.30 = (bf16[8,768,128]{2,1,0:T(8,128)(2,1)S(1)}, bf16[8,768,128]{2,1,0:T(8,128)(2,1)}, u32[]{:S(2)}) copy-start(bf16[8,768,128]{2,1,0:T(8,128)(2,1)} %copy-done.29) | copy-start | bytes 4718596
  321.6 39.4 %collective-permute-start.16 = (bf16[1024,768]{1,0:T(8,128)(2,1)}, bf16[1024,768]{1,0:T(8,128)(2,1)}, u32[]{:S(2)}, u32[]{:S(2)}) collective-permute-start(bf16[1024,768]{1,0:T(8,128)(2,1)} %shard_map.352), channel_id=1, source_target_pairs={{4,0},{0,2},{6,4},{2,6},{5,1},{1,3},{7,5},{3,7},{12,8},{8,10},{14,... | collective-permute-start | bytes 4718600 | tf_op jit(solution)/shard_map/ppermute | solution.py:1107
  322.6 38.4 %copy-start.3 = (bf16[1,32,384,128]{3,2,1,0:T(8,128)(2,1)S(1)}, bf16[1,32,384,128]{3,2,1,0:T(8,128)(2,1)}, u32[]{:S(2)}) copy-start(bf16[1,32,384,128]{3,2,1,0:T(8,128)(2,1)} %get-tuple-element.258.refs_2_.refs_10_) | copy-start | bytes 9437188
  370.7 5.3 collective-permute-start.17
  381.4 66.0 %collective-permute-start.18 = (bf16[8,768,128]{2,1,0:T(8,128)(2,1)}, bf16[8,768,128]{2,1,0:T(8,128)(2,1)}, u32[]{:S(2)}, u32[]{:S(2)}) collective-permute-start(bf16[8,768,128]{2,1,0:T(8,128)(2,1)} %shard_map.355), channel_id=1, source_target_pairs={{0,4},{4,0},{1,5},{5,1},{2,6},{6,2},{3,7},{7,3},{8,12},{12,8},{9,1... | collective-permute-start | bytes 4718600 | tf_op jit(solution)/shard_map/ppermute | solution.py:1098
  381.9 65.6 %collective-permute-start.19 = (bf16[8,768,128]{2,1,0:T(8,128)(2,1)}, bf16[8,768,128]{2,1,0:T(8,128)(2,1)}, u32[]{:S(2)}, u32[]{:S(2)}) collective-permute-start(bf16[8,768,128]{2,1,0:T(8,128)(2,1)} %shard_map.356), channel_id=1, source_target_pairs={{0,1},{1,0},{2,3},{3,2},{4,5},{5,4},{6,7},{7,6},{8,9},{9,8},{10,11... | collective-permute-start | bytes 4718600 | tf_op jit(solution)/shard_map/ppermute | solution.py:1098
  383.1 27.4 %copy-start.57 = (f32[1,384,256]{2,1,0:T(8,128)S(1)}, f32[1,384,256]{2,1,0:T(8,128)}, u32[]{:S(2)}) copy-start(f32[1,384,256]{2,1,0:T(8,128)} %get-tuple-element.297) | copy-start | bytes 1179652
  383.1 64.3 %all-to-all-start.1 = ((bf16[8,128,768]{2,1,0:T(8,128)(2,1)}), bf16[8,128,768]{2,1,0:T(8,128)(2,1)}, u32[]{:S(2)}, u32[]{:S(2)}) async-start(bf16[8,128,768]{2,1,0:T(8,128)(2,1)} %bitcast.44), calls=%async_computation.1 | async-start | bytes 3145728 | tf_op jit(solution)/shard_map/all_to_all | solution.py:1110
  418.4 29.1 %copy-start.31 = (bf16[8,768,128]{2,1,0:T(8,128)(2,1)S(1)}, bf16[8,768,128]{2,1,0:T(8,128)(2,1)}, u32[]{:S(2)}) copy-start(bf16[8,768,128]{2,1,0:T(8,128)(2,1)} %copy-done.29) | copy-start | bytes 4718596
  418.4 29.1 %copy-start.36 = (f32[768,128]{1,0:T(8,128)S(1)}, f32[768,128]{1,0:T(8,128)}, u32[]{:S(2)}) copy-start(f32[768,128]{1,0:T(8,128)} %copy-done.35) | copy-start | bytes 1179652
  458.9 76.2 %collective-permute-start.20 = (bf16[1024,768]{1,0:T(8,128)(2,1)}, bf16[1024,768]{1,0:T(8,128)(2,1)}, u32[]{:S(2)}, u32[]{:S(2)}) collective-permute-start(bf16[1024,768]{1,0:T(8,128)(2,1)} %get-tuple-element.284), channel_id=1, source_target_pairs={{4,0},{0,2},{6,4},{2,6},{5,1},{1,3},{7,5},{3,7},{12,8},{8,10},{14,... | collective-permute-start | bytes 4718600 | tf_op jit(solution)/shard_map/ppermute | solution.py:1107
  458.9 76.2 %collective-permute-start.21 = (bf16[192,2304]{1,0:T(8,128)(2,1)}, bf16[192,2304]{1,0:T(8,128)(2,1)}, u32[]{:S(2)}, u32[]{:S(2)}) collective-permute-start(bf16[192,2304]{1,0:T(8,128)(2,1)} %get-tuple-element.286), channel_id=1, source_target_pairs={{0,8},{8,0},{16,24},{24,16},{1,9},{9,1},{17,25},{25,17},{2,10},{10... | collective-permute-start | bytes 2654216 | tf_op jit(solution)/shard_map/ppermute | solution.py:1098
  460.7 74.4 %collective-permute-start.22 = (bf16[192,2304]{1,0:T(8,128)(2,1)}, bf16[192,2304]{1,0:T(8,128)(2,1)}, u32[]{:S(2)}, u32[]{:S(2)}) collective-permute-start(bf16[192,2304]{1,0:T(8,128)(2,1)} %get-tuple-element.287), channel_id=1, source_target_pairs={{0,16},{8,24},{16,0},{24,8},{1,17},{9,25},{17,1},{25,9},{2,18},{10... | collective-permute-start | bytes 2654216 | tf_op jit(solution)/shard_map/ppermute | solution.py:1098
  461.9 73.3 %collective-permute-start.23 = (bf16[192,2304]{1,0:T(8,128)(2,1)}, bf16[192,2304]{1,0:T(8,128)(2,1)}, u32[]{:S(2)}, u32[]{:S(2)}) collective-permute-start(bf16[192,2304]{1,0:T(8,128)(2,1)} %get-tuple-element.288), channel_id=1, source_target_pairs={{0,24},{8,16},{16,8},{24,0},{1,25},{9,17},{17,9},{25,1},{2,26},{10... | collective-permute-start | bytes 2654216 | tf_op jit(solution)/shard_map/ppermute | solution.py:1098
  481.0 18.6 %collective-permute-start.28 = (f32[3,16,24]{2,0,1:T(4,128)S(1)}, f32[3,16,24]{2,0,1:T(4,128)S(1)}, u32[]{:S(2)}, u32[]{:S(2)}) collective-permute-start(f32[3,16,24]{2,0,1:T(4,128)S(1)} %slice.217), channel_id=1, source_target_pairs={{0,16},{8,24},{16,0},{24,8},{1,17},{9,25},{17,1},{25,9},{2,18},{10... | collective-permute-start | bytes 13832 | tf_op jit(solution)/shard_map/ppermute | solution.py:1098
  499.7 5.7 collective-permute-start.29
  505.4 6.0 %collective-permute-start.24 = (f32[4,12576]{1,0:T(4,128)S(1)}, f32[4,12576]{1,0:T(4,128)S(1)}, u32[]{:S(2)}, u32[]{:S(2)}) collective-permute-start(f32[4,12576]{1,0:T(4,128)S(1)} %slice.211), channel_id=1, source_target_pairs={{0,16},{8,24},{16,0},{24,8},{1,17},{9,25},{17,1},{25,9},{2,18},{10... | collective-permute-start | bytes 603656 | tf_op jit(solution)/shard_map/ppermute | solution.py:1098
  511.4 3.4 collective-permute-start.30
  514.7 4.1 collective-permute-start.25
  518.8 4.4 collective-permute-start.31
  523.2 3.9 collective-permute-start.26
  527.1 2.8 collective-permute-start.32
  529.9 5.2 collective-permute-start.27
  535.2 41.0 %all-to-all-start.2 = ((bf16[8,128,768]{2,1,0:T(8,128)(2,1)}), bf16[8,128,768]{2,1,0:T(8,128)(2,1)S(1)}, u32[]{:S(2)}, u32[]{:S(2)}) async-start(bf16[8,128,768]{2,1,0:T(8,128)(2,1)} %bitcast.53), calls=%async_computation.2 | async-start | bytes 3145728 | tf_op jit(solution)/shard_map/all_to_all | solution.py:1110
  545.8 9.3 %collective-permute-start.34 = (bf16[96,2304]{1,0:T(8,128)(2,1)}, bf16[96,2304]{1,0:T(8,128)(2,1)S(1)}, u32[]{:S(2)}, u32[]{:S(2)}) collective-permute-start(bf16[96,2304]{1,0:T(8,128)(2,1)} %get-tuple-element.431), channel_id=1, source_target_pairs={{0,6},{2,2},{4,4},{6,0},{1,7},{3,3},{5,5},{7,1},{8,14},{10,10},{12... | collective-permute-start | bytes 1327112 | tf_op jit(solution)/shard_map/ppermute | solution.py:1183
  547.5 23.5 %collective-permute-start.33 = (bf16[96,2304]{1,0:T(8,128)(2,1)S(1)}, bf16[96,2304]{1,0:T(8,128)(2,1)}, u32[]{:S(2)}, u32[]{:S(2)}) collective-permute-start(bf16[96,2304]{1,0:T(8,128)(2,1)S(1)} %get-tuple-element.430), channel_id=1, source_target_pairs={{4,0},{0,2},{6,4},{2,6},{5,1},{1,3},{7,5},{3,7},{12,8},{8,10},{14,... | collective-permute-start | bytes 1327112 | tf_op jit(solution)/shard_map/ppermute | solution.py:1107
  (61 other events, 264.7 us)

commit v6 on v5

--- a/solution.py
+++ b/solution.py
@@ -29,7 +29,7 @@
 
 
 def params(limit):
-    return pltpu.CompilerParams(vmem_limit_bytes=limit * MIB)
+    return pltpu.CompilerParams(vmem_limit_bytes=60 * MIB)
 
 
 def cost(flops, moved, trans=0):
@@ -235,41 +235,35 @@
 
 
 def project_body(ch, many, start_ref, x_ref, live_ref, wt_ref, bias_ref, *refs):
-    a_ref, da_ref, gg_ref, dg_ref, pre_s = refs[-5:]
+    a_ref, da_ref, gg_ref, dg_ref = refs[-4:]
     x = jnp.concatenate([x_ref[0], x_ref[1]], axis=1)
-    pre_s[...] = nn(wt_ref[...], x)
     live = live_ref[0]
-    step = 32
     root = 0.7978845608028654
+    step = 64 if ch % 128 else 128
 
     def act(pre):
         square = pre * pre
-        bent = jnp.tanh(root * pre * (1.0 + 0.044715 * square))
-        rise = 0.5 + 0.5 * bent
-        slope = rise + (0.5 * root) * pre * (1.0 - bent * bent) * (1.0 + 0.134145 * square)
-        return pre * rise, slope
+        rise = 0.5 + 0.5 * jnp.tanh(pre * (root + (0.044715 * root) * square))
+        value = pre * rise
+        slope = rise + rise * (pre - value) * (2.0 * root + (6.0 * 0.044715 * root) * square)
+        return value, slope
 
     def put(ref, k, at, value):
         value = value.astype(bf16)
         ref[k, 0, at, :] = value[:, :BLK]
         ref[k, 1, at, :] = value[:, BLK:]
 
-    def chunk(i, carry):
-        at = pl.ds(pl.multiple_of(i * step, step), step)
-        for k in range(2):
-            row = pl.ds(pl.multiple_of(k * ch + i * step, step), step)
-            gate = pl.ds(pl.multiple_of((2 + k) * ch + i * step, step), step)
-            bias = bias_ref[row, :]
-            value, slope = act(pre_s[row, :] + jnp.concatenate([bias, bias], axis=1))
-            put(a_ref, k, at, live * value)
-            put(da_ref, k, at, live * slope)
-            bias = bias_ref[gate, :]
-            value, slope = act(pre_s[gate, :] + jnp.concatenate([bias, bias], axis=1))
-            put(gg_ref, k, at, value)
-            put(dg_ref, k, at, slope)
-        return carry
-
-    lax.fori_loop(0, ch // step, chunk, 0)
+    for k in range(2):
+        for first, value_ref, slope_ref in ((k * ch, a_ref, da_ref), ((2 + k) * ch, gg_ref, dg_ref)):
+            for at in range(0, ch, step):
+                rows = pl.ds(first + at, step)
+                bias = bias_ref[rows, :]
+                pre = nn(wt_ref[rows, :], x) + jnp.concatenate([bias, bias], axis=1)
+                value, slope = act(pre)
+                if value_ref is a_ref:
+                    value, slope = live * value, live * slope
+                put(value_ref, k, pl.ds(at, step), value)
+                put(slope_ref, k, pl.ds(at, step), slope)
 
 
 def chained(body, grid, in_specs, out_specs, shapes, scratch, limit, estimate, start, operands, kept):
@@ -304,7 +298,7 @@
         ],
         [out] * 4,
         [jax.ShapeDtypeStruct((2, nb, ch, BLK), bf16)] * 4,
-        [pltpu.VMEM((4 * ch, BIG), f32)],
+        [],
         48,
         cost(8 * tok * width * ch, 2 * tok * width + 16 * tok * ch, 4 * tok * ch),
         start // 2,
@@ -355,14 +349,13 @@
         scale = w_ref[0, pl.ds(p, 1), :] * jnp.exp2(block * ld)
         lhs = jnp.concatenate([jnp.where(low, scale, 0.0), jnp.where(low, 0.0, scale)], axis=0)
         lhs_high, lhs_low = halves(lhs)
-        high, rest = halves(decay)
-        k = nt(jnp.concatenate([lhs_high, lhs_low], axis=0), high)
-        k = k[0 : 2 * count] + k[2 * count : 4 * count] + nt(lhs_high, rest)
+        k = nt(jnp.concatenate([lhs_high, lhs_low], axis=0), decay.astype(bf16))
+        k = k[0 : 2 * count] + k[2 * count : 4 * count]
         k_s[pl.ds(2 * p, count, stride=cc), :] = k[0:count]
         k_s[pl.ds(2 * p + 1, count, stride=cc), :] = k[count : 2 * count]
         return carry
 
-    lax.fori_loop(0, cc // 2, one, 0, unroll=4)
+    lax.fori_loop(0, cc // 2, one, 0, unroll=16)
     sign = jnp.where(lax.broadcasted_iota(jnp.int32, (cc, BIG), 1) % 2 == 0, 1.0, -1.0)
     before = None
     for big in range(LAGS):
@@ -435,7 +428,7 @@
         s1_ref[0, pl.ds(p, 1), :] = jnp.sum(far * m1, axis=0, keepdims=True)
         return carry
 
-    lax.fori_loop(0, cc // 2, one, 0, unroll=4)
+    lax.fori_loop(0, cc // 2, one, 0, unroll=16)
 
 
 def moments(k, ld, gh, back):
@@ -1075,7 +1068,9 @@
         return parts[0].astype(f32)
 
     def scatter_channels(self, sums):
-        sums = lax.psum_scatter(sums, "dp", scatter_dimension=0, tiled=True)
+        return lax.psum_scatter(sums, "dp", scatter_dimension=0, tiled=True)
+
+    def owner_channels(self, sums):
         perm = [((f % self.n_dp) * self.n_t + f // self.n_dp, f) for f in range(self.n_dp * self.n_t)]
         return lax.ppermute(sums, self.both, perm)
 
@@ -1187,27 +1182,27 @@
 
     def scatter_channels(self, sums):
         count = 2 * self.quads
-        rows, wide = sums.shape
-        part = jnp.take(sums.reshape(count, rows // count * wide), jnp.arange(count) ^ self.spot(), axis=0)
-        for axis, bit in self.steps():
-            half = part.shape[0] // 2
-            part = part[:half] + self.flip(part[half:], axis, bit)
+        rows, wide = sums.shape[0] // count, sums.shape[1]
+        part = jnp.pad(sums, ((0, 0), (0, -wide % 8))).reshape(count, -1, BLK)
+        part = lax.all_to_all(part, ("q", "h"), split_axis=0, concat_axis=0, tiled=True)
+        return jnp.sum(part, axis=0).reshape(rows, -1)[:, :wide]
+
+    def owner_channels(self, sums):
+        count = 2 * self.quads
         perm = []
         for f in range(4 * count):
             place, at = f // count, f % count
             q, h, c, w = at // 2, at % 2, 1 - place // 2, place % 2
             perm.append((((2 * q + c) * 2 + h) * 2 + w, f))
-        return lax.ppermute(part.reshape(rows // count, wide), self.both, perm)
+        return lax.ppermute(sums, self.both, perm)
 
     def scatter_norm(self, sums):
         count = 8 * self.quads
-        mine = lax.axis_index(self.both)
-        part = jnp.take(sums.reshape(3, count, -1), jnp.arange(count) ^ mine, axis=1)
-        bits = [("q", 1 << at) for at in reversed(range(self.quads.bit_length() - 1))]
-        for axis, bit in bits + [("c", 1), ("h", 1), ("w", 1)]:
-            half = part.shape[1] // 2
-            part = part[:, :half] + self.flip(part[:, half:], axis, bit)
-        return part[:, 0]
+        part = sums.reshape(3, count, -1).transpose(1, 0, 2)
+        wide = part.shape[2]
+        part = jnp.pad(part, ((0, 0), (0, 5), (0, BLK - wide)))
+        part = lax.all_to_all(part, self.both, split_axis=0, concat_axis=0, tiled=True)
+        return jnp.sum(part, axis=0)[:3, :wide]
 
 
 def local(
@@ -1318,13 +1313,12 @@
     g_normed = net.scatter_send(g_normed)
     g_normed = net.scatter_own(w_in, back_list, many) + g_normed
     gw = outer_sums(net.order(many // 8), net.cuts, [part for part, _ in xs], [part for part, _ in gs], gp, gpg, mix)
-    first = moments(0, ld_pairs, gh[0], back)
-    g_normed, gw, gh, sent_out, first = after((g_normed, gw, gh, sent_out, first))
+    g_normed, gw, gh, sent_out = after((g_normed, gw, gh, sent_out))
     sent_in, norm_sums = input_rows(place, g_normed, xd, gd, gain)
-    sent_in, gh, gw, norm_sums, sent_out = after((sent_in, gh, gw, norm_sums, sent_out))
+    sent_in, gh, gw, norm_sums, sent_out, bsum = after((sent_in, gh, gw, norm_sums, sent_out, bsum))
     sent_in = net.ungroup(sent_in)
     gw = net.grads_send(gw)
-    s0, s1, g0 = [jnp.concatenate(part) for part in zip(first, moments(1, ld_pairs, gh[1], back))]
+    s0, s1, g0 = [jnp.concatenate(part) for part in zip(*[moments(k, ld_pairs, gh[k], back) for k in range(2)])]
     layer_out = permute_from(rank, sent_out)
 
     s0 = s0.reshape(2, ch, STATE)
@@ -1340,6 +1334,7 @@
     sent_in, gw, sums, norm_sums, layer_out = after((sent_in, gw, sums, norm_sums, layer_out))
     in_grad = permute_from(rank, net.spread(sent_in))
     gw = net.grads_last(gw)
+    sums = net.owner_channels(sums)
     s0 = jnp.stack([sums[:, :STATE], sums[:, STATE : 2 * STATE]])
     s1 = jnp.stack([sums[:, 2 * STATE : 3 * STATE], sums[:, 3 * STATE : 4 * STATE]])
     tail = sums[:, 4 * STATE :].T

time: 588 us -> 570 us (0.969)
  local copies, waits for them, and re-layouts: 62.6 us -> 28.9 us
  Pallas kernels: 349 us -> 376 us
  starting transfers between devices: 74.8 us -> 58.3 us
    unnamed x146 -> x67, local copies, waits for them, and re-layouts: 46.9 us -> 8.39 us
    ppermute x26 -> x18, starting transfers between devices: 36.9 us -> 17.5 us  [flip(): return lax.ppermute(x, axis, [(i, i ^ bit) for i in range(self.axes[axis])])]
    pallas_call x8, Pallas kernels: 30.2 us -> 49 us  [mul_rows(): pl.pallas_call(partial(mul_body, count, extra is not None), grid_spec=plt...]
    pallas_call x1, Pallas kernels: 33.1 us -> 18.4 us  [spectra(): pl.pallas_call(partial(spectra_body, cc), grid=(2, ch // cc), in_specs=[p...]
    all_to_all x0 -> x2, waiting for transfers between devices: none -> 14.6 us  [the longest x1 8.58 us: scatter_channels(): lax.all_to_all(part, ('q', 'h'), split_axis=0, concat_axis=0, tiled=True)]
    all_to_all x0 -> x2, starting transfers between devices: none -> 11.6 us  [the longest x1 6.66 us: scatter_norm(): lax.all_to_all(part, self.both, split_axis=0, concat_axis=0, tiled=True)]
    ppermute x3, waiting for transfers between devices: 25.5 us -> 15.3 us  [ungroup(): return lax.ppermute(x, ('c', 'h'), self.back)]
    ppermute x1, waiting for transfers between devices: 0.91 us -> 9.31 us  [owner_channels(): return lax.ppermute(sums, self.both, perm)]
  transfers between devices with their start and end apart: 38 -> 32, of which waited for: 12 -> 7; matrix products, arithmetic and copies ran while one was open for 6% -> 7% of each run, Pallas kernels for 54% -> 57%
where the time goes in v6:
time: 570 us; the launch traced here: 560 us
  Pallas kernels  376 us (66%)
  waiting for transfers between devices  73.9 us (13%)
  starting transfers between devices  58.3 us (10%)
  local copies, waits for them, and re-layouts  28.9 us (5%)
  other arithmetic  20.9 us (4%)
    pallas_call x2, Pallas kernels, ssm_back(): pl.pallas_call(partial(back_body, nb, nseq, cc, 64, k == 1), grid=(ch //...  61.8 us
    pallas_call x8, Pallas kernels, chained(): pl.pallas_call(body, grid_spec=pltpu.PrefetchScalarGridSpec(num_scalar_pr...  53.8 us
    pallas_call x1, Pallas kernels, meet(): pl.pallas_call(partial(meet_body, axes), in_specs=[vmem] * 4, out_specs=[...  52 us
    pallas_call x8, Pallas kernels, mul_rows(): pl.pallas_call(partial(mul_body, count, extra is not None), grid_spec=plt...  49 us
    pallas_call x1, Pallas kernels, ssm_scan(): pl.pallas_call(partial(scan_body, nb, nseq, cc, 32), grid=(2, ch // cc),...  39.5 us
    ppermute x18, waiting for transfers between devices, flip(): return lax.ppermute(x, axis, [(i, i ^ bit) for i in range(self.axes[axis])])  34.6 us
    pallas_call x1, Pallas kernels, outer_sums(): pl.pallas_call(partial(outer_body, ch, many, cuts, parts), grid_spec=pltp...  28.7 us
    pallas_call x2, Pallas kernels, moments(): pl.pallas_call(partial(moments_body, cc), grid=(ch // cc,), in_specs=[pl....  19.5 us
  transfers between devices with their start and end apart: 32, of which 7 were waited for; matrix products, arithmetic and copies ran while one was open for 7% of the time, Pallas kernels for 57%

profile of v6, /device:TPU:1, one launch (start us, length us, event | category | flops | bytes accessed | tf_op | source)
XLA Modules:
  0.0 559.7 jit_solution(6857694159470477429)
XLA Ops:
  2.6 3.1 collective-permute-start
  13.6 52.0 %shard_map.332 = (bf16[8,128,768]{2,1,0:T(8,128)(2,1)S(1)}, f32[8,104,128]{2,1,0:T(8,128)S(1)}, f32[32,8,128]{2,1,0:T(8,128)S(1)}) custom-call(s32[1,1024]{1,0:T(1,128)S(1)} %bitcast.101, bf16[1024,768]{1,0:T(8,128)(2,1)S(1)} %copy-done, f32[104,128]{1,0:T(8,128)S(1)} %pad_maximum_fusion.3.chan_ref, f32[8,128]{1,0:T(8,128)S(1)} %select_maximum_fusion.norm_ref), custom_call_target="tpu_custom_call" | custom-call | flops 80530640 | bytes 3932160 | tf_op jit(solution)/shard_map/pallas_call | solution.py:953
  73.1 8.9 %shard_map.333 = (bf16[8,768,128]{2,1,0:T(8,128)(2,1)}, bf16[8,768,128]{2,1,0:T(8,128)(2,1)}) custom-call(s32[1024,1]{1,0:T(8,128)} %copy.114.place_ref, bf16[1024,768]{1,0:T(8,128)(2,1)} %bitcast.100, f32[768,128]{1,0:T(8,128)} %broadcast_in_dim.87.gain_ref, f32[768,128]{1,0:T(8,128)} %broadcast_in_dim.89.shift_ref), custom_call_target="tpu_custom_call" | custom-call | flops 80530640 | bytes 235929 | tf_op jit(solution)/shard_map/pallas_call | solution.py:137
  83.9 7.1 %collective-permute-start.6 = (bf16[8,768,128]{2,1,0:T(8,128)(2,1)}, bf16[8,768,128]{2,1,0:T(8,128)(2,1)S(1)}, u32[]{:S(2)}, u32[]{:S(2)}) collective-permute-start(bf16[8,768,128]{2,1,0:T(8,128)(2,1)} %get-tuple-element.177.x_ref.refs_0_), channel_id=1, source_target_pairs={{0,4},{4,0},{1,5},{5,1},{2,6},{6,2},{3,7},{7,3},{8,12},{12,8},{9,1... | collective-permute-start | bytes 4718600 | tf_op jit(solution)/shard_map/ppermute | solution.py:1093
  91.0 4.4 shard_map.340
  95.4 4.2 all-to-all-start
  104.9 18.4 %shard_map.334.kh_ref = f32[2,8,384,512]{3,2,1,0:T(8,128)} custom-call(f32[2,192,128]{2,1,0:T(8,128)} %bitcast.107, f32[2,192,128]{2,1,0:T(8,128)} %bitcast.115, f32[2,384,128]{2,1,0:T(8,128)} %broadcast_in_dim.91.d_ref, bf16[256,512]{1,0:T(8,128)(2,1)} %constant.204.wave_ref), custom_call_target="tpu_custom_call" | custom-call | flops 1536000000 | bytes 629145 | tf_op jit(solution)/shard_map/pallas_call | solution.py:380
  123.3 15.3 %collective-permute-done.3.refs_1_ = bf16[192,2304]{1,0:T(8,128)(2,1)} collective-permute-done((bf16[192,2304]{1,0:T(8,128)(2,1)}, bf16[192,2304]{1,0:T(8,128)(2,1)}, u32[]{:S(2)}, u32[]{:S(2)}) %collective-permute-start.3) | collective-permute-done | bytes 884768 | tf_op jit(solution)/shard_map/ppermute | solution.py:1093
  138.6 19.2 %collective-permute-done.5.refs_3_ = bf16[192,2304]{1,0:T(8,128)(2,1)} collective-permute-done((bf16[192,2304]{1,0:T(8,128)(2,1)}, bf16[192,2304]{1,0:T(8,128)(2,1)}, u32[]{:S(2)}, u32[]{:S(2)}) %collective-permute-start.5) | collective-permute-done | bytes 884768 | tf_op jit(solution)/shard_map/ppermute | solution.py:1093
  162.7 5.0 shard_map.335
  169.0 8.9 %shard_map.336 = (bf16[2,32,384,128]{3,2,1,0:T(8,128)(2,1)}, bf16[2,32,384,128]{3,2,1,0:T(8,128)(2,1)}, bf16[2,32,384,128]{3,2,1,0:T(8,128)(2,1)}, bf16[2,32,384,128]{3,2,1,0:T(8,128)(2,1)}) custom-call(s32[1]{0:T(128)S(6)} %select_n.85.start_ref, bf16[8,768,128]{2,1,0:T(8,128)(2,1)} %get-tuple-element.177.x_ref.refs_0_, f32[16,1,256]{2,1,0:T(1,128)} %bitcast.118, ...), custom_call_target="tpu_custom_call" | custom-call | flops 120795952 | bytes 393216 | tf_op jit(solution)/shard_map/pallas_call | solution.py:273
  177.8 8.4 %shard_map.337 = (bf16[2,32,384,128]{3,2,1,0:T(8,128)(2,1)}, bf16[2,32,384,128]{3,2,1,0:T(8,128)(2,1)}, bf16[2,32,384,128]{3,2,1,0:T(8,128)(2,1)}, bf16[2,32,384,128]{3,2,1,0:T(8,128)(2,1)}) custom-call(s32[1]{0:T(128)S(6)} %select_n.84.start_ref, ...), custom_call_target="tpu_custom_call", output_to_operand_aliasing={{0}: (5, {}), {1}: (6, {}), {2}: (7, {}), {3}: (8, {})} | custom-call | flops 120795952 | bytes 393216 | tf_op jit(solution)/shard_map/pallas_call | solution.py:273
  186.3 8.4 %shard_map.338 = (bf16[2,32,384,128]{3,2,1,0:T(8,128)(2,1)}, bf16[2,32,384,128]{3,2,1,0:T(8,128)(2,1)}, bf16[2,32,384,128]{3,2,1,0:T(8,128)(2,1)}, bf16[2,32,384,128]{3,2,1,0:T(8,128)(2,1)}) custom-call(s32[1]{0:T(128)S(6)} %select_n.83.start_ref, ...), custom_call_target="tpu_custom_call", output_to_operand_aliasing={{0}: (5, {}), {1}: (6, {}), {2}: (7, {}), {3}: (8, {})} | custom-call | flops 120795952 | bytes 393216 | tf_op jit(solution)/shard_map/pallas_call | solution.py:273
  194.7 8.5 %shard_map.339 = (bf16[2,32,384,128]{3,2,1,0:T(8,128)(2,1)}, bf16[2,32,384,128]{3,2,1,0:T(8,128)(2,1)}, bf16[2,32,384,128]{3,2,1,0:T(8,128)(2,1)}, bf16[2,32,384,128]{3,2,1,0:T(8,128)(2,1)}) custom-call(s32[1]{0:T(128)S(6)} %select_n.78.start_ref, ...), custom_call_target="tpu_custom_call", output_to_operand_aliasing={{0}: (5, {}), {1}: (6, {}), {2}: (7, {}), {3}: (8, {})} | custom-call | flops 120795952 | bytes 393216 | tf_op jit(solution)/shard_map/pallas_call | solution.py:273
  203.2 8.1 %shard_map.341 = (bf16[8,768,128]{2,1,0:T(8,128)(2,1)}, bf16[8,768,128]{2,1,0:T(8,128)(2,1)}, f32[768,128]{1,0:T(8,128)}) custom-call(s32[1024,1]{1,0:T(8,128)} %copy.114.place_ref, bf16[1024,768]{1,0:T(8,128)(2,1)} %collective-permute-done.9.g_ref, f32[8,1,128]{2,1,0:T(1,128)} %bitcast.131), custom_call_target="tpu_custom_call" | custom-call | flops 80530640 | bytes 235929 | tf_op jit(solution)/shard_map/pallas_call | solution.py:152
  216.1 39.5 %shard_map.342 = (bf16[2,32,384,128]{3,2,1,0:T(8,128)(2,1)}, bf16[2,32,384,128]{3,2,1,0:T(8,128)(2,1)}) custom-call(s32[2,17]{1,0:T(2,128)} %pad_add_fusion.1.tab_ref, s32[2,4]{1,0:T(2,128)} %pad_add_fusion.2.seq_ref, bf16[2,32,384,128]{3,2,1,0:T(8,128)(2,1)} %get-tuple-element.245.a_ref, f32[2,8,384,512]{3,2,1,0:T(8,128)} %shard_map.334.kh_ref, ...), custom_call_target="tpu_custom_call" | custom-call | flops 1920000000 | bytes 1258291 | tf_op jit(solution)/shard_map/pallas_call | solution.py:641
  255.6 6.0 %shard_map.344 = bf16[8,768,128]{2,1,0:T(8,128)(2,1)} custom-call(s32[1]{0:T(128)S(6)} %select_n.78.start_ref, bf16[768,768]{1,0:T(8,128)(2,1)} %get-tuple-element.210.w_ref, bf16[2,32,384,128]{3,2,1,0:T(8,128)(2,1)} %get-tuple-element.263.refs_0_.refs_12_), custom_call_target="tpu_custom_call" | custom-call | flops 60397976 | bytes 235929 | tf_op jit(solution)/shard_map/pallas_call | solution.py:711
  262.1 4.9 shard_map.347.refs_0_
  267.0 4.9 shard_map.345
  271.9 4.9 shard_map.348.refs_0_
  276.7 4.9 shard_map.349.refs_0_
  281.6 5.2 shard_map.346
  288.1 5.0 shard_map.350.gm_ref
  293.5 5.3 shard_map.343.refs_0_
  298.7 31.0 %shard_map.351 = (bf16[1,32,384,128]{3,2,1,0:T(8,128)(2,1)}, bf16[1,32,384,128]{3,2,1,0:T(8,128)(2,1)}, f32[1,8,384,512]{3,2,1,0:T(8,128)}, f32[1,384,256]{2,1,0:T(8,128)}) custom-call(s32[2,17]{1,0:T(2,128)} %pad_add_fusion.1.tab_ref, s32[2,4]{1,0:T(2,128)} %pad_add_fusion.2.seq_ref, bf16[2,32,384,128]{3,2,1,0:T(8,128)(2,1)} %get-tuple-element.245.a_ref, ...), custom_call_target="tpu_custom_call" | custom-call | flops 1536000000 | bytes 1258291 | tf_op jit(solution)/shard_map/pallas_call | solution.py:668
  331.0 6.8 %shard_map.352 = bf16[1024,768]{1,0:T(8,128)(2,1)} custom-call(s32[1,1024]{1,0:T(1,128)} %bitcast.129, bf16[8,768,128]{2,1,0:T(8,128)(2,1)} %get-tuple-element.170.xd_ref, f32[8,1,128]{2,1,0:T(1,128)} %bitcast.132, f32[768,128]{1,0:T(8,128)} %broadcast_in_dim.95.bias_ref, f32[8,768,128]{2,1,0:T(8,128)} %shard_map.343.refs_0_, ...), custom_call_target="tpu_custom_call" | custom-call | flops 80530640 | bytes 235929 | tf_op jit(solution)/shard_map/pallas_call | solution.py:189
  338.3 30.8 %shard_map.353 = (bf16[1,32,384,128]{3,2,1,0:T(8,128)(2,1)}, bf16[1,32,384,128]{3,2,1,0:T(8,128)(2,1)}, f32[1,8,384,512]{3,2,1,0:T(8,128)}, f32[1,384,256]{2,1,0:T(8,128)}) custom-call(s32[2,17]{1,0:T(2,128)} %pad_add_fusion.1.tab_ref, s32[2,4]{1,0:T(2,128)} %pad_add_fusion.2.seq_ref, bf16[2,32,384,128]{3,2,1,0:T(8,128)(2,1)} %get-tuple-element.245.a_ref, ...), custom_call_target="tpu_custom_call" | custom-call | flops 1536000000 | bytes 1258291 | tf_op jit(solution)/shard_map/pallas_call | solution.py:668
  369.1 5.9 %collective-permute-done.16 = bf16[1024,768]{1,0:T(8,128)(2,1)S(1)} collective-permute-done((bf16[1024,768]{1,0:T(8,128)(2,1)}, bf16[1024,768]{1,0:T(8,128)(2,1)S(1)}, u32[]{:S(2)}, u32[]{:S(2)}) %collective-permute-start.16) | collective-permute-done | bytes 1572896 | tf_op jit(solution)/shard_map/ppermute | solution.py:1102
  375.0 7.1 %shard_map.354 = bf16[8,768,128]{2,1,0:T(8,128)(2,1)} custom-call(s32[1]{0:T(128)S(6)} %select_n.78.start_ref, bf16[768,1536]{1,0:T(8,128)(2,1)} %get-tuple-element.208.w_ref, bf16[1,32,384,128]{3,2,1,0:T(8,128)(2,1)} %get-tuple-element.257.refs_0_.refs_8_, bf16[1,32,384,128]{3,2,1,0:T(8,128)(2,1)} %get-tuple-element.258.refs_1_.refs_9_, ...), custom_call_target="tpu_custom_call" | custom-call | flops 120795952 | bytes 314572 | tf_op jit(solution)/shard_map/pallas_call | solution.py:711
  382.2 6.6 %shard_map.355 = bf16[8,768,128]{2,1,0:T(8,128)(2,1)} custom-call(s32[1]{0:T(128)S(6)} %select_n.92.start_ref, bf16[768,1536]{1,0:T(8,128)(2,1)} %get-tuple-element.208.w_ref, bf16[1,32,384,128]{3,2,1,0:T(8,128)(2,1)} %get-tuple-element.257.refs_0_.refs_8_, bf16[1,32,384,128]{3,2,1,0:T(8,128)(2,1)} %get-tuple-element.258.refs_1_.refs_9_, ...), custom_call_target="tpu_custom_call" | custom-call | flops 120795952 | bytes 314572 | tf_op jit(solution)/shard_map/pallas_call | solution.py:711
  388.9 7.1 %shard_map.356 = bf16[8,768,128]{2,1,0:T(8,128)(2,1)} custom-call(s32[1]{0:T(128)S(6)} %select_n.83.start_ref, bf16[768,1536]{1,0:T(8,128)(2,1)} %get-tuple-element.208.w_ref, bf16[1,32,384,128]{3,2,1,0:T(8,128)(2,1)} %get-tuple-element.257.refs_0_.refs_8_, bf16[1,32,384,128]{3,2,1,0:T(8,128)(2,1)} %get-tuple-element.258.refs_1_.refs_9_, ...), custom_call_target="tpu_custom_call" | custom-call | flops 120795952 | bytes 314572 | tf_op jit(solution)/shard_map/pallas_call | solution.py:711
  396.4 10.5 %all-to-all-start.1 = ((bf16[8,128,768]{2,1,0:T(8,128)(2,1)}), bf16[8,128,768]{2,1,0:T(8,128)(2,1)S(1)}, u32[]{:S(2)}, u32[]{:S(2)}) async-start(bf16[8,128,768]{2,1,0:T(8,128)(2,1)} %bitcast.110), calls=%async_computation.1 | async-start | bytes 3145728 | tf_op jit(solution)/shard_map/all_to_all | solution.py:1105
  407.5 6.9 %shard_map.357.refs_0_ = f32[8,768,128]{2,1,0:T(8,128)} custom-call(s32[1]{0:T(128)S(6)} %select_n.85.start_ref, bf16[768,1536]{1,0:T(8,128)(2,1)} %get-tuple-element.208.w_ref, bf16[1,32,384,128]{3,2,1,0:T(8,128)(2,1)} %get-tuple-element.257.refs_0_.refs_8_, bf16[1,32,384,128]{3,2,1,0:T(8,128)(2,1)} %get-tuple-element.258.refs_1_.refs_9_, ...), custom_call_target="tpu_custom_call" | custom-call | flops 120795952 | bytes 314572 | tf_op jit(solution)/shard_map/pallas_call | solution.py:711
  414.4 28.7 %shard_map.358 = (bf16[192,2304]{1,0:T(8,128)(2,1)}, bf16[192,2304]{1,0:T(8,128)(2,1)}, bf16[192,2304]{1,0:T(8,128)(2,1)}, bf16[192,2304]{1,0:T(8,128)(2,1)}) custom-call(s32[8]{0:T(128)} %concatenate.49.at_ref, bf16[8,768,128]{2,1,0:T(8,128)(2,1)} %get-tuple-element.177.x_ref.refs_0_, bf16[8,768,128]{2,1,0:T(8,128)(2,1)} %copy-done.4, ...), custom_call_target="tpu_custom_call" | custom-call | flops 724775744 | bytes 1572864 | tf_op jit(solution)/shard_map/pallas_call | solution.py:780
  443.2 10.7 %shard_map.359 = (bf16[1024,768]{1,0:T(8,128)(2,1)}, f32[2,768,128]{2,1,0:T(8,128)}) custom-call(s32[1,1024]{1,0:T(1,128)} %bitcast.130, bf16[8,768,128]{2,1,0:T(8,128)(2,1)} %get-tuple-element.170.xd_ref, bf16[8,768,128]{2,1,0:T(8,128)(2,1)} %get-tuple-element.207.gd_ref, f32[768,128]{1,0:T(8,128)} %broadcast_in_dim.87.gain_ref, ...), custom_call_target="tpu_custom_call" | custom-call | flops 80530640 | bytes 314572 | tf_op jit(solution)/shard_map/pallas_call | solution.py:225
  459.6 6.7 %all-to-all-start.3 = ((f32[32,8,128]{2,1,0:T(8,128)}), f32[32,8,128]{2,1,0:T(8,128)S(1)}, u32[]{:S(2)}, u32[]{:S(2)}) async-start(f32[32,8,128]{2,1,0:T(8,128)} %pad.19.clone), calls=%async_computation.3 | async-start | bytes 262144 | tf_op jit(solution)/shard_map/all_to_all | solution.py:1204
  466.7 9.7 %shard_map.360 = (f32[1,192,128]{2,1,0:T(8,128)}, f32[1,192,128]{2,1,0:T(8,128)}, f32[1,384,128]{2,1,0:T(8,128)}) custom-call(f32[2,192,128]{2,1,0:T(8,128)} %bitcast.108, f32[1,8,384,512]{3,2,1,0:T(8,128)} %get-tuple-element.290.gh_ref, bf16[512,256]{1,0:T(8,128)(2,1)} %constant.207.back_ref), custom_call_target="tpu_custom_call" | custom-call | flops 768000000 | bytes 314572 | tf_op jit(solution)/shard_map/pallas_call | solution.py:438
  477.4 9.8 %shard_map.361 = (f32[1,192,128]{2,1,0:T(8,128)}, f32[1,192,128]{2,1,0:T(8,128)}, f32[1,384,128]{2,1,0:T(8,128)}) custom-call(f32[2,192,128]{2,1,0:T(8,128)} %bitcast.109, f32[1,8,384,512]{3,2,1,0:T(8,128)} %get-tuple-element.292.gh_ref, bf16[512,256]{1,0:T(8,128)(2,1)} %constant.207.back_ref), custom_call_target="tpu_custom_call" | custom-call | flops 768000000 | bytes 314572 | tf_op jit(solution)/shard_map/pallas_call | solution.py:438
  492.1 6.0 %all-to-all-done.3 = f32[32,8,128]{2,1,0:T(8,128)S(1)} async-done(((f32[32,8,128]{2,1,0:T(8,128)}), f32[32,8,128]{2,1,0:T(8,128)S(1)}, u32[]{:S(2)}, u32[]{:S(2)}) %all-to-all-start.3) | async-done | bytes 131104 | tf_op jit(solution)/shard_map/all_to_all | solution.py:1204
  498.1 4.9 all-to-all-start.2
  504.1 4.6 shard_map.362
  508.7 8.6 %all-to-all-done.2 = f32[8,99,128]{2,1,0:T(8,128)S(1)} async-done(((f32[8,99,128]{2,1,0:T(8,128)}), f32[8,99,128]{2,1,0:T(8,128)S(1)}, u32[]{:S(2)}, u32[]{:S(2)}) %all-to-all-start.2) | async-done | bytes 405536 | tf_op jit(solution)/shard_map/all_to_all | solution.py:1187
  517.5 4.0 all-to-all-start.4
  521.5 1.9 add_convert_fusion
  526.5 2.2 collective-permute-start.24
  528.7 9.3 %collective-permute-done.26 = f32[48,262]{1,0:T(8,128)S(1)} collective-permute-done((f32[48,262]{1,0:T(8,128)S(1)}, f32[48,262]{1,0:T(8,128)S(1)}, u32[]{:S(2)}, u32[]{:S(2)}) %collective-permute-start.26) | collective-permute-done | bytes 50336 | tf_op jit(solution)/shard_map/ppermute | solution.py:1197
  541.6 9.4 %collective-permute-done.24 = bf16[96,2304]{1,0:T(8,128)(2,1)S(1)} collective-permute-done((bf16[96,2304]{1,0:T(8,128)(2,1)S(1)}, bf16[96,2304]{1,0:T(8,128)(2,1)S(1)}, u32[]{:S(2)}, u32[]{:S(2)}) %collective-permute-start.24) | collective-permute-done | bytes 442400 | tf_op jit(solution)/shard_map/ppermute | solution.py:1102
  554.7 4.6 shard_map.363
  (205 shorter events, 63.6 us)
Async XLA Ops:
  0.7 66.1 %copy-start.27 = (bf16[96,384]{1,0:T(8,128)(2,1)S(1)}, bf16[96,384]{1,0:T(8,128)(2,1)}, u32[]{:S(2)}) copy-start(bf16[96,384]{1,0:T(8,128)(2,1)} %param.30) | copy-start | bytes 221188
  0.7 66.1 %copy-start.28 = (bf16[96,384]{1,0:T(8,128)(2,1)S(1)}, bf16[96,384]{1,0:T(8,128)(2,1)}, u32[]{:S(2)}) copy-start(bf16[96,384]{1,0:T(8,128)(2,1)} %param.28) | copy-start | bytes 221188
  2.6 64.3 %collective-permute-start = (s32[1027]{0:T(1024)S(1)}, s32[1027]{0:T(1024)S(1)}, u32[]{:S(2)}, u32[]{:S(2)}) collective-permute-start(s32[1027]{0:T(1024)S(1)} %pad_add_fusion), channel_id=1, source_target_pairs={{0,4},{2,0},{4,6},{6,2},{1,5},{3,1},{5,7},{7,3},{8,12},{10,8},{12,... | collective-permute-start | bytes 12332 | tf_op jit(solution)/shard_map/ppermute | solution.py:1099
  7.1 59.7 %copy-start.2 = (s32[1024]{0:T(1024)}, s32[1024]{0:T(1024)S(1)}, u32[]{:S(2)}) copy-start(s32[1024]{0:T(1024)S(1)} %convert_reduce_fusion.1) | copy-start | bytes 12292
  66.9 15.1 %collective-permute-start.1 = (bf16[96,2304]{1,0:T(8,128)(2,1)S(1)}, bf16[96,2304]{1,0:T(8,128)(2,1)S(1)}, u32[]{:S(2)}, u32[]{:S(2)}) collective-permute-start(bf16[96,2304]{1,0:T(8,128)(2,1)S(1)} %pad_maximum_fusion.1), channel_id=1, source_target_pairs={{0,4},{2,0},{4,6},{6,2},{1,5},{3,1},{5,7},{7,3},{8,12},{10,8},{12,... | collective-permute-start | bytes 1327112 | tf_op jit(solution)/shard_map/ppermute | solution.py:1099
  68.0 14.1 %collective-permute-start.2 = (bf16[96,2304]{1,0:T(8,128)(2,1)S(1)}, bf16[96,2304]{1,0:T(8,128)(2,1)S(1)}, u32[]{:S(2)}, u32[]{:S(2)}) collective-permute-start(bf16[96,2304]{1,0:T(8,128)(2,1)S(1)} %pad_maximum_fusion.1), channel_id=1, source_target_pairs={{0,6},{2,2},{4,4},{6,0},{1,7},{3,3},{5,5},{7,1},{8,14},{10,10},{12... | collective-permute-start | bytes 1327112 | tf_op jit(solution)/shard_map/ppermute | solution.py:1158
  68.7 13.4 %copy-start.29 = (s32[1024]{0:T(1024)}, s32[1024]{0:T(1024)S(1)}, u32[]{:S(2)}) copy-start(s32[1024]{0:T(1024)S(1)} %slice.114) | copy-start | bytes 12292
  83.9 74.0 %collective-permute-start.6 = (bf16[8,768,128]{2,1,0:T(8,128)(2,1)}, bf16[8,768,128]{2,1,0:T(8,128)(2,1)S(1)}, u32[]{:S(2)}, u32[]{:S(2)}) collective-permute-start(bf16[8,768,128]{2,1,0:T(8,128)(2,1)} %get-tuple-element.177.x_ref.refs_0_), channel_id=1, source_target_pairs={{0,4},{4,0},{1,5},{5,1},{2,6},{6,2},{3,7},{7,3},{8,12},{12,8},{9,1... | collective-permute-start | bytes 4718600 | tf_op jit(solution)/shard_map/ppermute | solution.py:1093
  91.0 66.9 %collective-permute-start.7 = (bf16[8,768,128]{2,1,0:T(8,128)(2,1)}, bf16[8,768,128]{2,1,0:T(8,128)(2,1)S(1)}, u32[]{:S(2)}, u32[]{:S(2)}) collective-permute-start(bf16[8,768,128]{2,1,0:T(8,128)(2,1)} %get-tuple-element.177.x_ref.refs_0_), channel_id=1, source_target_pairs={{0,1},{1,0},{2,3},{3,2},{4,5},{5,4},{6,7},{7,6},{8,9},{9,8},{10,11... | collective-permute-start | bytes 4718600 | tf_op jit(solution)/shard_map/ppermute | solution.py:1093
  95.4 63.4 %all-to-all-start = ((bf16[8,128,768]{2,1,0:T(8,128)(2,1)}), bf16[8,128,768]{2,1,0:T(8,128)(2,1)}, u32[]{:S(2)}, u32[]{:S(2)}) async-start(bf16[8,128,768]{2,1,0:T(8,128)(2,1)} %bitcast.106), calls=%async_computation | async-start | bytes 3145728 | tf_op jit(solution)/shard_map/all_to_all | solution.py:1105
  101.9 36.7 %collective-permute-start.3 = (bf16[192,2304]{1,0:T(8,128)(2,1)}, bf16[192,2304]{1,0:T(8,128)(2,1)}, u32[]{:S(2)}, u32[]{:S(2)}) collective-permute-start(bf16[192,2304]{1,0:T(8,128)(2,1)} %pad_maximum_fusion.refs_0_), channel_id=1, source_target_pairs={{0,8},{8,0},{16,24},{24,16},{1,9},{9,1},{17,25},{25,17},{2,10},{10... | collective-permute-start | bytes 2654216 | tf_op jit(solution)/shard_map/ppermute | solution.py:1093
  103.6 35.0 %collective-permute-start.4 = (bf16[192,2304]{1,0:T(8,128)(2,1)}, bf16[192,2304]{1,0:T(8,128)(2,1)}, u32[]{:S(2)}, u32[]{:S(2)}) collective-permute-start(bf16[192,2304]{1,0:T(8,128)(2,1)} %pad_maximum_fusion.refs_0_), channel_id=1, source_target_pairs={{0,16},{8,24},{16,0},{24,8},{1,17},{9,25},{17,1},{25,9},{2,18},{10... | collective-permute-start | bytes 2654216 | tf_op jit(solution)/shard_map/ppermute | solution.py:1093
  104.4 53.4 %collective-permute-start.5 = (bf16[192,2304]{1,0:T(8,128)(2,1)}, bf16[192,2304]{1,0:T(8,128)(2,1)}, u32[]{:S(2)}, u32[]{:S(2)}) collective-permute-start(bf16[192,2304]{1,0:T(8,128)(2,1)} %pad_maximum_fusion.refs_0_), channel_id=1, source_target_pairs={{0,24},{8,16},{16,8},{24,0},{1,25},{9,17},{17,9},{25,1},{2,26},{10... | collective-permute-start | bytes 2654216 | tf_op jit(solution)/shard_map/ppermute | solution.py:1093
  157.9 36.8 %collective-permute-start.8 = (bf16[8,768,128]{2,1,0:T(8,128)(2,1)S(1)}, bf16[8,768,128]{2,1,0:T(8,128)(2,1)}, u32[]{:S(2)}, u32[]{:S(2)}) collective-permute-start(bf16[8,768,128]{2,1,0:T(8,128)(2,1)S(1)} %collective-permute-done.7.x_ref.refs_2_), channel_id=1, source_target_pairs={{0,4},{4,0},{1,5},{5,1},{2,6},{6,2},{3,7},{7,3},{8,12},{12,8},{9,1... | collective-permute-start | bytes 4718600 | tf_op jit(solution)/shard_map/ppermute | solution.py:1093
  158.8 44.4 %collective-permute-start.9 = (bf16[1024,768]{1,0:T(8,128)(2,1)}, bf16[1024,768]{1,0:T(8,128)(2,1)}, u32[]{:S(2)}, u32[]{:S(2)}) collective-permute-start(bf16[1024,768]{1,0:T(8,128)(2,1)} %bitcast.27), channel_id=1, source_target_pairs={{0,4},{2,0},{4,6},{6,2},{1,5},{3,1},{5,7},{7,3},{8,12},{10,8},{12,... | collective-permute-start | bytes 4718600 | tf_op jit(solution)/shard_map/ppermute | solution.py:1099
  211.3 44.3 %collective-permute-start.10 = (bf16[8,768,128]{2,1,0:T(8,128)(2,1)}, bf16[8,768,128]{2,1,0:T(8,128)(2,1)S(1)}, u32[]{:S(2)}, u32[]{:S(2)}) collective-permute-start(bf16[8,768,128]{2,1,0:T(8,128)(2,1)} %get-tuple-element.213.g_ref.refs_4_), channel_id=1, source_target_pairs={{0,4},{4,0},{1,5},{5,1},{2,6},{6,2},{3,7},{7,3},{8,12},{12,8},{9,1... | collective-permute-start | bytes 4718600 | tf_op jit(solution)/shard_map/ppermute | solution.py:1093
  211.5 44.1 %collective-permute-start.11 = (bf16[8,768,128]{2,1,0:T(8,128)(2,1)}, bf16[8,768,128]{2,1,0:T(8,128)(2,1)S(1)}, u32[]{:S(2)}, u32[]{:S(2)}) collective-permute-start(bf16[8,768,128]{2,1,0:T(8,128)(2,1)} %get-tuple-element.213.g_ref.refs_4_), channel_id=1, source_target_pairs={{0,1},{1,0},{2,3},{3,2},{4,5},{5,4},{6,7},{7,6},{8,9},{9,8},{10,11... | collective-permute-start | bytes 4718600 | tf_op jit(solution)/shard_map/ppermute | solution.py:1093
  261.6 20.1 %collective-permute-start.12 = (bf16[8,768,128]{2,1,0:T(8,128)(2,1)}, bf16[8,768,128]{2,1,0:T(8,128)(2,1)}, u32[]{:S(2)}, u32[]{:S(2)}) collective-permute-start(bf16[8,768,128]{2,1,0:T(8,128)(2,1)} %shard_map.344), channel_id=1, source_target_pairs={{0,4},{4,0},{1,5},{5,1},{2,6},{6,2},{3,7},{7,3},{8,12},{12,8},{9,1... | collective-permute-start | bytes 4718600 | tf_op jit(solution)/shard_map/ppermute | solution.py:1093
  261.9 24.9 %collective-permute-start.13 = (bf16[8,768,128]{2,1,0:T(8,128)(2,1)S(1)}, bf16[8,768,128]{2,1,0:T(8,128)(2,1)S(1)}, u32[]{:S(2)}, u32[]{:S(2)}) collective-permute-start(bf16[8,768,128]{2,1,0:T(8,128)(2,1)S(1)} %collective-permute-done.11.g_ref.refs_6_), channel_id=1, source_target_pairs={{0,4},{4,0},{1,5},{5,1},{2,6},{6,2},{3,7},{7,3},{8,12},{12,8},{9,1... | collective-permute-start | bytes 4718600 | tf_op jit(solution)/shard_map/ppermute | solution.py:1093
  293.1 36.6 %collective-permute-start.14 = (bf16[8,768,128]{2,1,0:T(8,128)(2,1)S(1)}, bf16[8,768,128]{2,1,0:T(8,128)(2,1)S(1)}, u32[]{:S(2)}, u32[]{:S(2)}) collective-permute-start(bf16[8,768,128]{2,1,0:T(8,128)(2,1)S(1)} %copy-done.12), channel_id=1, source_target_pairs={{0,4},{4,0},{1,5},{5,1},{2,6},{6,2},{3,7},{7,3},{8,12},{12,8},{9,1... | collective-permute-start | bytes 4718600 | tf_op jit(solution)/shard_map/ppermute | solution.py:1093
  293.4 36.3 %collective-permute-start.15 = (bf16[8,768,128]{2,1,0:T(8,128)(2,1)}, bf16[8,768,128]{2,1,0:T(8,128)(2,1)}, u32[]{:S(2)}, u32[]{:S(2)}) collective-permute-start(bf16[8,768,128]{2,1,0:T(8,128)(2,1)} %shard_map.346), channel_id=1, source_target_pairs={{0,1},{1,0},{2,3},{3,2},{4,5},{5,4},{6,7},{7,6},{8,9},{9,8},{10,11... | collective-permute-start | bytes 4718600 | tf_op jit(solution)/shard_map/ppermute | solution.py:1093
  337.8 37.2 %collective-permute-start.16 = (bf16[1024,768]{1,0:T(8,128)(2,1)}, bf16[1024,768]{1,0:T(8,128)(2,1)S(1)}, u32[]{:S(2)}, u32[]{:S(2)}) collective-permute-start(bf16[1024,768]{1,0:T(8,128)(2,1)} %shard_map.352), channel_id=1, source_target_pairs={{4,0},{0,2},{6,4},{2,6},{5,1},{1,3},{7,5},{3,7},{12,8},{8,10},{14,... | collective-permute-start | bytes 4718600 | tf_op jit(solution)/shard_map/ppermute | solution.py:1102
  382.2 6.7 %collective-permute-start.17 = (bf16[8,768,128]{2,1,0:T(8,128)(2,1)}, bf16[8,768,128]{2,1,0:T(8,128)(2,1)}, u32[]{:S(2)}, u32[]{:S(2)}) collective-permute-start(bf16[8,768,128]{2,1,0:T(8,128)(2,1)} %shard_map.354), channel_id=1, source_target_pairs={{0,4},{4,0},{1,5},{5,1},{2,6},{6,2},{3,7},{7,3},{8,12},{12,8},{9,1... | collective-permute-start | bytes 4718600 | tf_op jit(solution)/shard_map/ppermute | solution.py:1093
  395.9 11.0 %copy-start.30 = (s32[4]{0:T(128)S(1)}, s32[4]{0:T(128)}, u32[]{:S(2)}) copy-start(s32[4]{0:T(128)} %iota_xor_fusion.at_ref) | copy-start | bytes 52
  395.9 47.2 %collective-permute-start.18 = (bf16[8,768,128]{2,1,0:T(8,128)(2,1)S(1)}, bf16[8,768,128]{2,1,0:T(8,128)(2,1)}, u32[]{:S(2)}, u32[]{:S(2)}) collective-permute-start(bf16[8,768,128]{2,1,0:T(8,128)(2,1)S(1)} %copy-done.11), channel_id=1, source_target_pairs={{0,4},{4,0},{1,5},{5,1},{2,6},{6,2},{3,7},{7,3},{8,12},{12,8},{9,1... | collective-permute-start | bytes 4718600 | tf_op jit(solution)/shard_map/ppermute | solution.py:1093
  396.4 46.7 %collective-permute-start.19 = (bf16[8,768,128]{2,1,0:T(8,128)(2,1)}, bf16[8,768,128]{2,1,0:T(8,128)(2,1)}, u32[]{:S(2)}, u32[]{:S(2)}) collective-permute-start(bf16[8,768,128]{2,1,0:T(8,128)(2,1)} %shard_map.356), channel_id=1, source_target_pairs={{0,1},{1,0},{2,3},{3,2},{4,5},{5,4},{6,7},{7,6},{8,9},{9,8},{10,11... | collective-permute-start | bytes 4718600 | tf_op jit(solution)/shard_map/ppermute | solution.py:1093
  396.4 46.7 %all-to-all-start.1 = ((bf16[8,128,768]{2,1,0:T(8,128)(2,1)}), bf16[8,128,768]{2,1,0:T(8,128)(2,1)S(1)}, u32[]{:S(2)}, u32[]{:S(2)}) async-start(bf16[8,128,768]{2,1,0:T(8,128)(2,1)} %bitcast.110), calls=%async_computation.1 | async-start | bytes 3145728 | tf_op jit(solution)/shard_map/all_to_all | solution.py:1105
  443.1 10.7 %copy-start.9 = (bf16[8,128,768]{2,1,0:T(8,128)(2,1)}, bf16[8,128,768]{2,1,0:T(8,128)(2,1)S(1)}, u32[]{:S(2)}) copy-start(bf16[8,128,768]{2,1,0:T(8,128)(2,1)S(1)} %all-to-all-done.1) | copy-start | bytes 4718596
  443.2 14.1 %copy-start.21 = (f32[768,128]{1,0:T(8,128)S(1)}, f32[768,128]{1,0:T(8,128)}, u32[]{:S(2)}) copy-start(f32[768,128]{1,0:T(8,128)} %get-tuple-element.301) | copy-start | bytes 1179652
  453.8 12.5 %copy-start.19 = (f32[1,384,256]{2,1,0:T(8,128)S(1)}, f32[1,384,256]{2,1,0:T(8,128)}, u32[]{:S(2)}) copy-start(f32[1,384,256]{2,1,0:T(8,128)} %get-tuple-element.298) | copy-start | bytes 1179652
  453.8 12.5 %copy-start.20 = (f32[1,384,256]{2,1,0:T(8,128)S(1)}, f32[1,384,256]{2,1,0:T(8,128)}, u32[]{:S(2)}) copy-start(f32[1,384,256]{2,1,0:T(8,128)} %get-tuple-element.299) | copy-start | bytes 1179652
  453.8 63.6 %collective-permute-start.20 = (bf16[1024,768]{1,0:T(8,128)(2,1)}, bf16[1024,768]{1,0:T(8,128)(2,1)}, u32[]{:S(2)}, u32[]{:S(2)}) collective-permute-start(bf16[1024,768]{1,0:T(8,128)(2,1)} %get-tuple-element.285), channel_id=1, source_target_pairs={{4,0},{0,2},{6,4},{2,6},{5,1},{1,3},{7,5},{3,7},{12,8},{8,10},{14,... | collective-permute-start | bytes 4718600 | tf_op jit(solution)/shard_map/ppermute | solution.py:1102
  454.2 63.3 %collective-permute-start.21 = (bf16[192,2304]{1,0:T(8,128)(2,1)}, bf16[192,2304]{1,0:T(8,128)(2,1)S(1)}, u32[]{:S(2)}, u32[]{:S(2)}) collective-permute-start(bf16[192,2304]{1,0:T(8,128)(2,1)} %get-tuple-element.287), channel_id=1, source_target_pairs={{0,8},{8,0},{16,24},{24,16},{1,9},{9,1},{17,25},{25,17},{2,10},{10... | collective-permute-start | bytes 2654216 | tf_op jit(solution)/shard_map/ppermute | solution.py:1093
  455.9 61.6 %collective-permute-start.22 = (bf16[192,2304]{1,0:T(8,128)(2,1)}, bf16[192,2304]{1,0:T(8,128)(2,1)}, u32[]{:S(2)}, u32[]{:S(2)}) collective-permute-start(bf16[192,2304]{1,0:T(8,128)(2,1)} %get-tuple-element.288), channel_id=1, source_target_pairs={{0,16},{8,24},{16,0},{24,8},{1,17},{9,25},{17,1},{25,9},{2,18},{10... | collective-permute-start | bytes 2654216 | tf_op jit(solution)/shard_map/ppermute | solution.py:1093
  457.1 60.4 %collective-permute-start.23 = (bf16[192,2304]{1,0:T(8,128)(2,1)}, bf16[192,2304]{1,0:T(8,128)(2,1)}, u32[]{:S(2)}, u32[]{:S(2)}) collective-permute-start(bf16[192,2304]{1,0:T(8,128)(2,1)} %get-tuple-element.289), channel_id=1, source_target_pairs={{0,24},{8,16},{16,8},{24,0},{1,25},{9,17},{17,9},{25,1},{2,26},{10... | collective-permute-start | bytes 2654216 | tf_op jit(solution)/shard_map/ppermute | solution.py:1093
  459.6 38.5 %all-to-all-start.3 = ((f32[32,8,128]{2,1,0:T(8,128)}), f32[32,8,128]{2,1,0:T(8,128)S(1)}, u32[]{:S(2)}, u32[]{:S(2)}) async-start(f32[32,8,128]{2,1,0:T(8,128)} %pad.19.clone), calls=%async_computation.3 | async-start | bytes 262144 | tf_op jit(solution)/shard_map/all_to_all | solution.py:1204
  477.4 10.8 %copy-start.26 = (f32[1,192,128]{2,1,0:T(8,128)S(1)}, f32[1,192,128]{2,1,0:T(8,128)}, u32[]{:S(2)}) copy-start(f32[1,192,128]{2,1,0:T(8,128)} %get-tuple-element.294) | copy-start | bytes 294916
  477.4 11.9 %copy-start.22 = (f32[1,384,128]{2,1,0:T(8,128)S(1)}, f32[1,384,128]{2,1,0:T(8,128)}, u32[]{:S(2)}) copy-start(f32[1,384,128]{2,1,0:T(8,128)} %get-tuple-element.296) | copy-start | bytes 589828
  490.8 12.3 %copy-start.3 = (s32[1024]{0:T(1024)S(1)}, s32[1024]{0:T(1024)}, u32[]{:S(2)}) copy-start(s32[1024]{0:T(1024)} %copy-done.2) | copy-start | bytes 12292
  498.1 19.2 %all-to-all-start.2 = ((f32[8,99,128]{2,1,0:T(8,128)}), f32[8,99,128]{2,1,0:T(8,128)S(1)}, u32[]{:S(2)}, u32[]{:S(2)}) async-start(f32[8,99,128]{2,1,0:T(8,128)} %reshape.345), calls=%async_computation.2 | async-start | bytes 851968 | tf_op jit(solution)/shard_map/all_to_all | solution.py:1187
  508.7 12.8 %copy-start.15 = (bf16[192,2304]{1,0:T(8,128)(2,1)S(1)}, bf16[192,2304]{1,0:T(8,128)(2,1)}, u32[]{:S(2)}) copy-start(bf16[192,2304]{1,0:T(8,128)(2,1)} %get-tuple-element.306) | copy-start | bytes 2654212
  517.5 36.0 %all-to-all-start.4 = ((bf16[8,128,768]{2,1,0:T(8,128)(2,1)}), bf16[8,128,768]{2,1,0:T(8,128)(2,1)S(1)}, u32[]{:S(2)}, u32[]{:S(2)}) async-start(bf16[8,128,768]{2,1,0:T(8,128)(2,1)} %bitcast.50), calls=%async_computation.4 | async-start | bytes 3145728 | tf_op jit(solution)/shard_map/all_to_all | solution.py:1105
  523.3 14.8 %copy-start.23 = (f32[2,48,64]{2,1,0:T(8,128)S(1)}, f32[2,48,64]{2,1,0:T(8,128)}, u32[]{:S(2)}) copy-start(f32[2,48,64]{2,1,0:T(8,128)} %param.37) | copy-start | bytes 73732
  523.3 14.8 %copy-start.24 = (f32[2,48,64]{2,1,0:T(8,128)S(1)}, f32[2,48,64]{2,1,0:T(8,128)}, u32[]{:S(2)}) copy-start(f32[2,48,64]{2,1,0:T(8,128)} %param.39) | copy-start | bytes 73732
  523.4 14.8 %copy-start.25 = (f32[2,48,64]{2,1,0:T(8,128)S(1)}, f32[2,48,64]{2,1,0:T(8,128)}, u32[]{:S(2)}) copy-start(f32[2,48,64]{2,1,0:T(8,128)} %param.38) | copy-start | bytes 73732
  524.2 13.9 %collective-permute-start.26 = (f32[48,262]{1,0:T(8,128)S(1)}, f32[48,262]{1,0:T(8,128)S(1)}, u32[]{:S(2)}, u32[]{:S(2)}) collective-permute-start(f32[48,262]{1,0:T(8,128)S(1)} %bitcast.127), channel_id=1, source_target_pairs={{4,0},{6,1},{12,2},{14,3},{20,4},{22,5},{28,6},{30,7},{5,8},{7,9},... | collective-permute-start | bytes 150920 | tf_op jit(solution)/shard_map/ppermute | solution.py:1197
  524.8 16.7 %collective-permute-start.25 = (bf16[96,2304]{1,0:T(8,128)(2,1)}, bf16[96,2304]{1,0:T(8,128)(2,1)S(1)}, u32[]{:S(2)}, u32[]{:S(2)}) collective-permute-start(bf16[96,2304]{1,0:T(8,128)(2,1)} %get-tuple-element.416), channel_id=1, source_target_pairs={{0,6},{2,2},{4,4},{6,0},{1,7},{3,3},{5,5},{7,1},{8,14},{10,10},{12... | collective-permute-start | bytes 1327112 | tf_op jit(solution)/shard_map/ppermute | solution.py:1178
  526.5 24.5 %collective-permute-start.24 = (bf16[96,2304]{1,0:T(8,128)(2,1)S(1)}, bf16[96,2304]{1,0:T(8,128)(2,1)S(1)}, u32[]{:S(2)}, u32[]{:S(2)}) collective-permute-start(bf16[96,2304]{1,0:T(8,128)(2,1)S(1)} %get-tuple-element.415), channel_id=1, source_target_pairs={{4,0},{0,2},{6,4},{2,6},{5,1},{1,3},{7,5},{3,7},{12,8},{8,10},{14,... | collective-permute-start | bytes 1327112 | tf_op jit(solution)/shard_map/ppermute | solution.py:1102
  (15 other events, 64.9 us)
